TPU v7x, 512 devices: a whole 4x4x16 slice. The times are simulated.
512 devices in a mesh: grp: 32 (over z_lo, y), blk: 16 (over z_hi, x, core).
Axes of the slice: x: 4, y: 4, z: 16 (z_hi: 2, z_lo: 8; z = z_hi * 8 + z_lo), core: 2. Of those that a mesh axis runs over, the one named last changes fastest.
Arguments:
- image: bfloat16 [4096, 1024], P(('blk', 'grp')), may hold values from -16 to 16
- text: bfloat16 [4096, 1024], P(('grp', 'blk')), may hold values from -16 to 16
- mimage: bfloat16 [4096, 1024], P(('blk', 'grp')), may hold values from -16 to 16
- mtext: bfloat16 [4096, 1024], P(('grp', 'blk')), may hold values from -16 to 16
Outputs:
- grad_image: float32 [4096, 1024], P(('blk', 'grp'))
- grad_text: float32 [4096, 1024], P(('grp', 'blk'))
- loss: float32 [], replicated
All inputs are finite; a program needn't handle non-finite values.
Results may differ from a plain program's by a relative error of at most 0.0037.
Values may be sent and summed in bfloat16 or wider, within the bound.
No kernel may reach another device: no remote copies, remote signals or barrier semaphores. Data moves between devices by JAX's collectives and lax.ppermute only.
A program may use at most 64 MiB of HBM per device.

v0:
```python
import jax
import jax.numpy as jnp
from jax import lax
from jax.sharding import PartitionSpec as P

mix_weight = 0.4
very_low = -1e30


def combined_all(value, axis, join):
    pieces = jax.tree.map(lambda part: lax.all_gather(part, axis), value)
    head = jax.tree.map(lambda part: part[0], pieces)
    tail = jax.tree.map(lambda part: part[1:], pieces)
    running, _ = lax.scan(lambda running, share: (join(running, share), None), head, tail)
    return running


def from_behind(value, axis, steps):
    count = lax.axis_size(axis)
    pairs = [(source, (source + steps) % count) for source in range(count)]
    return lax.ppermute(value, axis, pairs)


def logits_of(left_rows, right_rows):
    scale_factor = left_rows.shape[1] ** (-0.5)
    product = lax.dot_general(
        left_rows, right_rows, (((1,), (1,)), ((), ())), preferred_element_type=jnp.float32
    )
    return product * scale_factor


def fold_stats(run_max, run_total, scores, along):
    new_max = jnp.maximum(run_max, jnp.max(scores, axis=along))
    spread = jnp.exp(scores - jnp.expand_dims(new_max, along))
    new_total = run_total * jnp.exp(run_max - new_max) + jnp.sum(spread, axis=along)
    return (new_max, new_total)


def join_pair(max_a, total_a, max_b, total_b):
    top_max = jnp.maximum(max_a, max_b)
    return (top_max, total_a * jnp.exp(max_a - top_max) + total_b * jnp.exp(max_b - top_max))


def join_stats(earlier, later):
    on_max, on_total = join_pair(earlier[0], earlier[1], later[0], later[1])
    mom_max, mom_total = join_pair(earlier[2], earlier[3], later[2], later[3])
    return (on_max, on_total, mom_max, mom_total)


def merge_rows(row_stats):
    merged = combined_all(row_stats, "grp", join_stats)
    return (merged[0] + jnp.log(merged[1]), merged[2] + jnp.log(merged[3]))


def gradient_tile(
    score_on, score_mom, diagonal, row_online, row_momentum, col_online, col_momentum
):
    prob_row = jnp.exp(score_on - row_online[None, :])
    prob_col = jnp.exp(score_on - col_online[:, None])
    target_row = (
        mix_weight * jnp.exp(score_mom - row_momentum[None, :]) + (1.0 - mix_weight) * diagonal
    )
    target_col = (
        mix_weight * jnp.exp(score_mom - col_momentum[:, None]) + (1.0 - mix_weight) * diagonal
    )
    grad_tile = 0.5 * (prob_row - target_row + (prob_col - target_col))
    cross_term = jnp.sum((target_row + target_col) * score_on)
    return (grad_tile.astype(jnp.bfloat16), cross_term)


def local(image, text, mimage, mtext):
    tile_rows = image.shape[0]
    feat_width = image.shape[1]
    group_size = lax.axis_size("grp")
    cycle_size = lax.axis_size("blk")
    group_pos = lax.axis_index("grp")
    cycle_pos = lax.axis_index("blk")
    images, mimages = (
        lax.all_gather(image, "grp", axis=0, tiled=True),
        lax.all_gather(mimage, "grp", axis=0, tiled=True),
    )
    image_span = images.shape[0]
    image_ids = cycle_pos * image_span + lax.iota(jnp.int32, image_span)
    group_base = group_pos * cycle_size * tile_rows
    low_rows = jnp.full((image_span,), very_low, jnp.float32)
    zero_rows = jnp.zeros((image_span,), jnp.float32)
    low_cols = jnp.full((tile_rows,), very_low, jnp.float32)
    zero_cols = jnp.zeros((tile_rows,), jnp.float32)
    kept_init = ()

    def first_turn(turn_index, carry):
        moving_text, moving_stats, row_stats, kept = carry
        own_text, own_mtext = moving_text
        cmax_on, csum_on, cmax_mom, csum_mom = moving_stats
        score_on = logits_of(own_text, images)
        score_mom = logits_of(own_mtext, mimages)
        rmax_on, rsum_on = fold_stats(row_stats[0], row_stats[1], score_on, 0)
        rmax_mom, rsum_mom = fold_stats(row_stats[2], row_stats[3], score_mom, 0)
        cmax_on, csum_on = fold_stats(cmax_on, csum_on, score_on, 1)
        cmax_mom, csum_mom = fold_stats(cmax_mom, csum_mom, score_mom, 1)
        moving_text = from_behind((own_text, own_mtext), "blk", 1)
        moving_stats = from_behind((cmax_on, csum_on, cmax_mom, csum_mom), "blk", 1)
        return (moving_text, moving_stats, (rmax_on, rsum_on, rmax_mom, rsum_mom), kept)

    first_init = (
        (text, mtext),
        (low_cols, zero_cols, low_cols, zero_cols),
        (low_rows, zero_rows, low_rows, zero_rows),
        kept_init,
    )
    unused_text, col_stats, row_stats, kept = lax.fori_loop(0, cycle_size, first_turn, first_init)
    col_online = col_stats[0] + jnp.log(col_stats[1])
    col_momentum = col_stats[2] + jnp.log(col_stats[3])
    row_online, row_momentum = merge_rows(row_stats)

    def second_turn(turn_index, carry):
        moving_text, moving_grad, grad_all, seen_text, cross_sum = carry
        col_on, col_mom, grad_text_acc = moving_grad
        own_text, own_mtext = moving_text
        score_on = logits_of(own_text, images)
        score_mom = logits_of(own_mtext, mimages)
        source_pos = (cycle_pos - turn_index) % cycle_size
        text_ids = group_base + source_pos * tile_rows + lax.iota(jnp.int32, tile_rows)
        diagonal = (text_ids[:, None] == image_ids[None, :]).astype(jnp.float32)
        grad_tile, cross_term = gradient_tile(
            score_on, score_mom, diagonal, row_online, row_momentum, col_on, col_mom
        )
        grad_text_acc = grad_text_acc + jnp.dot(
            grad_tile, images, preferred_element_type=jnp.float32
        )
        grad_all = lax.dynamic_update_slice_in_dim(grad_all, grad_tile, source_pos * tile_rows, 0)
        seen_text = lax.dynamic_update_slice_in_dim(seen_text, own_text, source_pos * tile_rows, 0)
        outgoing = (own_text, own_mtext)
        moving_text = from_behind((outgoing[0], outgoing[1]), "blk", 1)
        moving_grad = from_behind((col_on, col_mom, grad_text_acc), "blk", 1)
        return (moving_text, moving_grad, grad_all, seen_text, cross_sum + cross_term)

    text_init = (text, mtext)
    second_init = (
        text_init,
        (col_online, col_momentum, jnp.zeros((tile_rows, feat_width), jnp.float32)),
        jnp.zeros((cycle_size * tile_rows, image_span), jnp.bfloat16),
        jnp.zeros((cycle_size * tile_rows, feat_width), jnp.bfloat16),
        jnp.zeros((), jnp.float32),
    )
    final_carry = lax.fori_loop(0, cycle_size, second_turn, second_init)
    grad_text = final_carry[1][2]
    grad_all = final_carry[2]
    seen_text = final_carry[3]
    cross_sum = final_carry[4]
    image_part = lax.dot_general(
        grad_all, seen_text, (((0,), (0,)), ((), ())), preferred_element_type=jnp.float32
    )
    grad_image = lax.psum_scatter(image_part, "grp", scatter_dimension=0, tiled=True)
    own_rows = lax.dynamic_slice_in_dim(row_online, group_pos * tile_rows, tile_rows, 0)
    local_loss = jnp.sum(own_rows) + jnp.sum(col_online) - cross_sum
    total_pairs = tile_rows * group_size * cycle_size
    loss = lax.psum(local_loss, ("grp", "blk")) / (2.0 * total_pairs)
    return (grad_image, grad_text, loss)


def solution(mesh):
    in_specs = (
        P(("blk", "grp"), None),
        P(("grp", "blk"), None),
        P(("blk", "grp"), None),
        P(("grp", "blk"), None),
    )
    out_specs = (P(("blk", "grp"), None), P(("grp", "blk"), None), P())
    return jax.shard_map(local, mesh=mesh, in_specs=in_specs, out_specs=out_specs, check_vma=False)
```

profile of v0, /device:TPU:2, one launch (start us, length us, event | category | flops | bytes accessed | tf_op | source)
XLA Modules:
  0.0 1886.4 jit_solution(8683298976857234309)
XLA Ops:
  9.3 127.8 %all_gather.30 = bf16[256,1024]{1,0:T(8,128)(2,1)S(1)} all-gather(bf16[8,1024]{1,0:T(8,128)(2,1)S(1)} %copy-done.10), channel_id=1, replica_groups=mesh['grp'=32,'blk'=16] {'grp'}, dimensions={0}, use_global_device_ids=true | all-gather | bytes 540672 | tf_op jit(solution)/shard_map/all_gather | solution.py:79
  137.1 114.1 %all_gather.31 = bf16[256,1024]{1,0:T(8,128)(2,1)S(1)} all-gather(bf16[8,1024]{1,0:T(8,128)(2,1)S(1)} %copy-done.11), channel_id=1, replica_groups=mesh['grp'=32,'blk'=16] {'grp'}, dimensions={0}, use_global_device_ids=true | all-gather | bytes 540672 | tf_op jit(solution)/shard_map/all_gather | solution.py:80
  251.2 528.1 %while.77 = (s32[]{:T(128)}, bf16[8,1024]{1,0:T(8,128)(2,1)S(1)}, bf16[8,1024]{1,0:T(8,128)(2,1)S(1)}, f32[8]{0:T(128)S(1)}, f32[8]{0:T(128)S(1)}, /*index=5*/f3...) while((s32[]{:T(128)}, bf16[8,1024]{1,0:T(8,128)(2,1)S(1)}, ...), condition=%wide.region_9.0_spmd.clone, body=%wide.region_0.0_spmd.clone.sunk | while | flops 8419875 | bytes 1339081 | solution.py:111
  292.2 15.0 collective-permute-start.8
  325.8 15.0 collective-permute-start.8
  359.5 15.0 collective-permute-start.8
  393.2 15.0 collective-permute-start.8
  426.8 15.0 collective-permute-start.8
  460.5 15.0 collective-permute-start.8
  494.2 15.0 collective-permute-start.8
  527.9 15.0 collective-permute-start.8
  628.9 15.0 collective-permute-start.8
  662.5 15.0 collective-permute-start.8
  696.2 15.0 collective-permute-start.8
  729.9 15.0 collective-permute-start.8
  763.5 15.0 collective-permute-start.8
  779.3 113.2 %all-gather.6 = f32[32,1,256]{2,1,0:T(1,128)S(1)} all-gather(f32[1,1,256]{2,1,0:T(1,128)S(1)} %bitcast.68), channel_id=4, replica_groups=mesh['grp'=32,'blk'=16] {'grp'}, dimensions={0}, use_global_device_ids=true | all-gather | bytes 33792 | tf_op jit(solution)/shard_map/all_gather | solution.py:11
  893.2 111.3 %all-gather.5 = f32[32,1,256]{2,1,0:T(1,128)S(1)} all-gather(f32[1,1,256]{2,1,0:T(1,128)S(1)} %bitcast.79), channel_id=3, replica_groups=mesh['grp'=32,'blk'=16] {'grp'}, dimensions={0}, use_global_device_ids=true | all-gather | bytes 33792 | tf_op jit(solution)/shard_map/all_gather | solution.py:11
  1005.1 113.2 %all-gather.7 = f32[32,1,256]{2,1,0:T(1,128)S(1)} all-gather(f32[1,1,256]{2,1,0:T(1,128)S(1)} %bitcast.78), channel_id=5, replica_groups=mesh['grp'=32,'blk'=16] {'grp'}, dimensions={0}, use_global_device_ids=true | all-gather | bytes 33792 | tf_op jit(solution)/shard_map/all_gather | solution.py:11
  1118.9 111.3 %all-gather.4 = f32[32,1,256]{2,1,0:T(1,128)S(1)} all-gather(f32[1,1,256]{2,1,0:T(1,128)S(1)} %bitcast.69), channel_id=2, replica_groups=mesh['grp'=32,'blk'=16] {'grp'}, dimensions={0}, use_global_device_ids=true | all-gather | bytes 33792 | tf_op jit(solution)/shard_map/all_gather | solution.py:11
  1238.2 391.1 %while.76 = (s32[]{:T(128)}, bf16[8,1024]{1,0:T(8,128)(2,1)S(1)}, bf16[8,1024]{1,0:T(8,128)(2,1)S(1)}, f32[8]{0:T(128)S(1)}, f32[8]{0:T(128)S(1)}, /*index=5*/f3...) while((s32[]{:T(128)}, bf16[8,1024]{1,0:T(8,128)(2,1)S(1)}, ...), condition=%wide.region_14.15_spmd.clone, body=%wide.region_12.14_spmd.clone.sunk | while | flops 12648731 | bytes 2093632 | solution.py:146
  1254.0 17.8 collective-permute-start.2
  1632.6 110.1 %psum.7 = f32[]{:T(128)} all-reduce(f32[]{:T(128)S(6)} %sub.193), channel_id=1, replica_groups=mesh['grp'=32,'blk'=16] {'grp','blk'}, use_global_device_ids=true, to_apply=%region_18.19 | all-reduce | flops 1 | bytes 8 | tf_op jit(solution)/shard_map/psum | solution.py:158
  1743.3 134.5 %reduce-scatter.2.cloned.1.call-done = f32[8,1024]{1,0:T(8,128)} async-done(((f32[256,1024]{1,0:T(8,128)}), f32[8,1024]{1,0:T(8,128)}) %reduce-scatter.2.cloned.1.call-update) | async-done | bytes 32784 | tf_op jit(solution)/shard_map/reduce_scatter | solution.py:154
  (977 shorter events, 709.1 us)
Async XLA Ops:
  7.2 1870.6 %reduce-scatter.2.cloned.1.call-start = ((), (), s32[]{:S(2)}) async-start(), calls=%async_computation.1 | async-start | bytes 1081344 | tf_op jit(solution)/shard_map/reduce_scatter | solution.py:154
  274.3 33.7 %collective-permute-start.6 = (bf16[8,1024]{1,0:T(8,128)(2,1)S(1)}, bf16[8,1024]{1,0:T(8,128)(2,1)S(1)}, u32[]{:S(2)}, u32[]{:S(2)}) collective-permute-start(bf16[8,1024]{1,0:T(8,128)(2,1)S(1)} %copy.34), channel_id=1, source_target_pairs={{0,1},{1,2},{2,3},{3,4},{4,5},{5,6},{6,7},{7,8},{8,9},{9,10},{10,1... | collective-permute-start | bytes 49160 | tf_op jit(solution)/shard_map/while/body/eval_jaxpr/ppermute | solution.py:21
  280.9 26.3 %collective-permute-start.10 = (f32[8]{0:T(128)S(1)}, f32[8]{0:T(128)S(1)}, u32[]{:S(2)}, u32[]{:S(2)}) collective-permute-start(f32[8]{0:T(128)S(1)} %multiply_add_fusion.11), channel_id=1, source_target_pairs={{0,1},{1,2},{2,3},{3,4},{4,5},{5,6},{6,7},{7,8},{8,9},{9,10},{10,1... | collective-permute-start | bytes 104 | tf_op jit(solution)/shard_map/while/body/eval_jaxpr/ppermute | solution.py:21
  308.0 33.7 %collective-permute-start.6 = (bf16[8,1024]{1,0:T(8,128)(2,1)S(1)}, bf16[8,1024]{1,0:T(8,128)(2,1)S(1)}, u32[]{:S(2)}, u32[]{:S(2)}) collective-permute-start(bf16[8,1024]{1,0:T(8,128)(2,1)S(1)} %copy.34), channel_id=1, source_target_pairs={{0,1},{1,2},{2,3},{3,4},{4,5},{5,6},{6,7},{7,8},{8,9},{9,10},{10,1... | collective-permute-start | bytes 49160 | tf_op jit(solution)/shard_map/while/body/eval_jaxpr/ppermute | solution.py:21
  341.6 33.7 %collective-permute-start.6 = (bf16[8,1024]{1,0:T(8,128)(2,1)S(1)}, bf16[8,1024]{1,0:T(8,128)(2,1)S(1)}, u32[]{:S(2)}, u32[]{:S(2)}) collective-permute-start(bf16[8,1024]{1,0:T(8,128)(2,1)S(1)} %copy.34), channel_id=1, source_target_pairs={{0,1},{1,2},{2,3},{3,4},{4,5},{5,6},{6,7},{7,8},{8,9},{9,10},{10,1... | collective-permute-start | bytes 49160 | tf_op jit(solution)/shard_map/while/body/eval_jaxpr/ppermute | solution.py:21
  375.3 33.7 %collective-permute-start.6 = (bf16[8,1024]{1,0:T(8,128)(2,1)S(1)}, bf16[8,1024]{1,0:T(8,128)(2,1)S(1)}, u32[]{:S(2)}, u32[]{:S(2)}) collective-permute-start(bf16[8,1024]{1,0:T(8,128)(2,1)S(1)} %copy.34), channel_id=1, source_target_pairs={{0,1},{1,2},{2,3},{3,4},{4,5},{5,6},{6,7},{7,8},{8,9},{9,10},{10,1... | collective-permute-start | bytes 49160 | tf_op jit(solution)/shard_map/while/body/eval_jaxpr/ppermute | solution.py:21
  409.0 33.7 %collective-permute-start.6 = (bf16[8,1024]{1,0:T(8,128)(2,1)S(1)}, bf16[8,1024]{1,0:T(8,128)(2,1)S(1)}, u32[]{:S(2)}, u32[]{:S(2)}) collective-permute-start(bf16[8,1024]{1,0:T(8,128)(2,1)S(1)} %copy.34), channel_id=1, source_target_pairs={{0,1},{1,2},{2,3},{3,4},{4,5},{5,6},{6,7},{7,8},{8,9},{9,10},{10,1... | collective-permute-start | bytes 49160 | tf_op jit(solution)/shard_map/while/body/eval_jaxpr/ppermute | solution.py:21
  442.6 33.7 %collective-permute-start.6 = (bf16[8,1024]{1,0:T(8,128)(2,1)S(1)}, bf16[8,1024]{1,0:T(8,128)(2,1)S(1)}, u32[]{:S(2)}, u32[]{:S(2)}) collective-permute-start(bf16[8,1024]{1,0:T(8,128)(2,1)S(1)} %copy.34), channel_id=1, source_target_pairs={{0,1},{1,2},{2,3},{3,4},{4,5},{5,6},{6,7},{7,8},{8,9},{9,10},{10,1... | collective-permute-start | bytes 49160 | tf_op jit(solution)/shard_map/while/body/eval_jaxpr/ppermute | solution.py:21
  449.2 26.3 %collective-permute-start.10 = (f32[8]{0:T(128)S(1)}, f32[8]{0:T(128)S(1)}, u32[]{:S(2)}, u32[]{:S(2)}) collective-permute-start(f32[8]{0:T(128)S(1)} %multiply_add_fusion.11), channel_id=1, source_target_pairs={{0,1},{1,2},{2,3},{3,4},{4,5},{5,6},{6,7},{7,8},{8,9},{9,10},{10,1... | collective-permute-start | bytes 104 | tf_op jit(solution)/shard_map/while/body/eval_jaxpr/ppermute | solution.py:21
  476.3 33.7 %collective-permute-start.6 = (bf16[8,1024]{1,0:T(8,128)(2,1)S(1)}, bf16[8,1024]{1,0:T(8,128)(2,1)S(1)}, u32[]{:S(2)}, u32[]{:S(2)}) collective-permute-start(bf16[8,1024]{1,0:T(8,128)(2,1)S(1)} %copy.34), channel_id=1, source_target_pairs={{0,1},{1,2},{2,3},{3,4},{4,5},{5,6},{6,7},{7,8},{8,9},{9,10},{10,1... | collective-permute-start | bytes 49160 | tf_op jit(solution)/shard_map/while/body/eval_jaxpr/ppermute | solution.py:21
  482.9 26.3 %collective-permute-start.10 = (f32[8]{0:T(128)S(1)}, f32[8]{0:T(128)S(1)}, u32[]{:S(2)}, u32[]{:S(2)}) collective-permute-start(f32[8]{0:T(128)S(1)} %multiply_add_fusion.11), channel_id=1, source_target_pairs={{0,1},{1,2},{2,3},{3,4},{4,5},{5,6},{6,7},{7,8},{8,9},{9,10},{10,1... | collective-permute-start | bytes 104 | tf_op jit(solution)/shard_map/while/body/eval_jaxpr/ppermute | solution.py:21
  510.0 33.7 %collective-permute-start.6 = (bf16[8,1024]{1,0:T(8,128)(2,1)S(1)}, bf16[8,1024]{1,0:T(8,128)(2,1)S(1)}, u32[]{:S(2)}, u32[]{:S(2)}) collective-permute-start(bf16[8,1024]{1,0:T(8,128)(2,1)S(1)} %copy.34), channel_id=1, source_target_pairs={{0,1},{1,2},{2,3},{3,4},{4,5},{5,6},{6,7},{7,8},{8,9},{9,10},{10,1... | collective-permute-start | bytes 49160 | tf_op jit(solution)/shard_map/while/body/eval_jaxpr/ppermute | solution.py:21
  516.6 26.3 %collective-permute-start.10 = (f32[8]{0:T(128)S(1)}, f32[8]{0:T(128)S(1)}, u32[]{:S(2)}, u32[]{:S(2)}) collective-permute-start(f32[8]{0:T(128)S(1)} %multiply_add_fusion.11), channel_id=1, source_target_pairs={{0,1},{1,2},{2,3},{3,4},{4,5},{5,6},{6,7},{7,8},{8,9},{9,10},{10,1... | collective-permute-start | bytes 104 | tf_op jit(solution)/shard_map/while/body/eval_jaxpr/ppermute | solution.py:21
  543.6 33.7 %collective-permute-start.6 = (bf16[8,1024]{1,0:T(8,128)(2,1)S(1)}, bf16[8,1024]{1,0:T(8,128)(2,1)S(1)}, u32[]{:S(2)}, u32[]{:S(2)}) collective-permute-start(bf16[8,1024]{1,0:T(8,128)(2,1)S(1)} %copy.34), channel_id=1, source_target_pairs={{0,1},{1,2},{2,3},{3,4},{4,5},{5,6},{6,7},{7,8},{8,9},{9,10},{10,1... | collective-permute-start | bytes 49160 | tf_op jit(solution)/shard_map/while/body/eval_jaxpr/ppermute | solution.py:21
  550.2 26.3 %collective-permute-start.10 = (f32[8]{0:T(128)S(1)}, f32[8]{0:T(128)S(1)}, u32[]{:S(2)}, u32[]{:S(2)}) collective-permute-start(f32[8]{0:T(128)S(1)} %multiply_add_fusion.11), channel_id=1, source_target_pairs={{0,1},{1,2},{2,3},{3,4},{4,5},{5,6},{6,7},{7,8},{8,9},{9,10},{10,1... | collective-permute-start | bytes 104 | tf_op jit(solution)/shard_map/while/body/eval_jaxpr/ppermute | solution.py:21
  577.3 33.7 %collective-permute-start.6 = (bf16[8,1024]{1,0:T(8,128)(2,1)S(1)}, bf16[8,1024]{1,0:T(8,128)(2,1)S(1)}, u32[]{:S(2)}, u32[]{:S(2)}) collective-permute-start(bf16[8,1024]{1,0:T(8,128)(2,1)S(1)} %copy.34), channel_id=1, source_target_pairs={{0,1},{1,2},{2,3},{3,4},{4,5},{5,6},{6,7},{7,8},{8,9},{9,10},{10,1... | collective-permute-start | bytes 49160 | tf_op jit(solution)/shard_map/while/body/eval_jaxpr/ppermute | solution.py:21
  583.9 26.3 %collective-permute-start.10 = (f32[8]{0:T(128)S(1)}, f32[8]{0:T(128)S(1)}, u32[]{:S(2)}, u32[]{:S(2)}) collective-permute-start(f32[8]{0:T(128)S(1)} %multiply_add_fusion.11), channel_id=1, source_target_pairs={{0,1},{1,2},{2,3},{3,4},{4,5},{5,6},{6,7},{7,8},{8,9},{9,10},{10,1... | collective-permute-start | bytes 104 | tf_op jit(solution)/shard_map/while/body/eval_jaxpr/ppermute | solution.py:21
  611.0 33.7 %collective-permute-start.6 = (bf16[8,1024]{1,0:T(8,128)(2,1)S(1)}, bf16[8,1024]{1,0:T(8,128)(2,1)S(1)}, u32[]{:S(2)}, u32[]{:S(2)}) collective-permute-start(bf16[8,1024]{1,0:T(8,128)(2,1)S(1)} %copy.34), channel_id=1, source_target_pairs={{0,1},{1,2},{2,3},{3,4},{4,5},{5,6},{6,7},{7,8},{8,9},{9,10},{10,1... | collective-permute-start | bytes 49160 | tf_op jit(solution)/shard_map/while/body/eval_jaxpr/ppermute | solution.py:21
  617.6 26.3 %collective-permute-start.10 = (f32[8]{0:T(128)S(1)}, f32[8]{0:T(128)S(1)}, u32[]{:S(2)}, u32[]{:S(2)}) collective-permute-start(f32[8]{0:T(128)S(1)} %multiply_add_fusion.11), channel_id=1, source_target_pairs={{0,1},{1,2},{2,3},{3,4},{4,5},{5,6},{6,7},{7,8},{8,9},{9,10},{10,1... | collective-permute-start | bytes 104 | tf_op jit(solution)/shard_map/while/body/eval_jaxpr/ppermute | solution.py:21
  644.7 33.7 %collective-permute-start.6 = (bf16[8,1024]{1,0:T(8,128)(2,1)S(1)}, bf16[8,1024]{1,0:T(8,128)(2,1)S(1)}, u32[]{:S(2)}, u32[]{:S(2)}) collective-permute-start(bf16[8,1024]{1,0:T(8,128)(2,1)S(1)} %copy.34), channel_id=1, source_target_pairs={{0,1},{1,2},{2,3},{3,4},{4,5},{5,6},{6,7},{7,8},{8,9},{9,10},{10,1... | collective-permute-start | bytes 49160 | tf_op jit(solution)/shard_map/while/body/eval_jaxpr/ppermute | solution.py:21
  678.3 33.7 %collective-permute-start.6 = (bf16[8,1024]{1,0:T(8,128)(2,1)S(1)}, bf16[8,1024]{1,0:T(8,128)(2,1)S(1)}, u32[]{:S(2)}, u32[]{:S(2)}) collective-permute-start(bf16[8,1024]{1,0:T(8,128)(2,1)S(1)} %copy.34), channel_id=1, source_target_pairs={{0,1},{1,2},{2,3},{3,4},{4,5},{5,6},{6,7},{7,8},{8,9},{9,10},{10,1... | collective-permute-start | bytes 49160 | tf_op jit(solution)/shard_map/while/body/eval_jaxpr/ppermute | solution.py:21
  712.0 33.7 %collective-permute-start.6 = (bf16[8,1024]{1,0:T(8,128)(2,1)S(1)}, bf16[8,1024]{1,0:T(8,128)(2,1)S(1)}, u32[]{:S(2)}, u32[]{:S(2)}) collective-permute-start(bf16[8,1024]{1,0:T(8,128)(2,1)S(1)} %copy.34), channel_id=1, source_target_pairs={{0,1},{1,2},{2,3},{3,4},{4,5},{5,6},{6,7},{7,8},{8,9},{9,10},{10,1... | collective-permute-start | bytes 49160 | tf_op jit(solution)/shard_map/while/body/eval_jaxpr/ppermute | solution.py:21
  745.7 33.7 %collective-permute-start.6 = (bf16[8,1024]{1,0:T(8,128)(2,1)S(1)}, bf16[8,1024]{1,0:T(8,128)(2,1)S(1)}, u32[]{:S(2)}, u32[]{:S(2)}) collective-permute-start(bf16[8,1024]{1,0:T(8,128)(2,1)S(1)} %copy.34), channel_id=1, source_target_pairs={{0,1},{1,2},{2,3},{3,4},{4,5},{5,6},{6,7},{7,8},{8,9},{9,10},{10,1... | collective-permute-start | bytes 49160 | tf_op jit(solution)/shard_map/while/body/eval_jaxpr/ppermute | solution.py:21
  1254.0 29.6 %collective-permute-start.2 = (f32[8]{0:T(128)S(1)}, f32[8]{0:T(128)S(1)}, u32[]{:S(2)}, u32[]{:S(2)}) collective-permute-start(f32[8]{0:T(128)S(1)} %copy.81), channel_id=1, source_target_pairs={{0,1},{1,2},{2,3},{3,4},{4,5},{5,6},{6,7},{7,8},{8,9},{9,10},{10,1... | collective-permute-start | bytes 104 | tf_op jit(solution)/shard_map/while/body/eval_jaxpr/ppermute | solution.py:21
  (174 other events, 2656.0 us)
Sparse Core Ops, SparseCore 0:
  1630.7 247.0 reduce-scatter.1
where the time goes:
time: 1890 us
  starting transfers between devices  819 us (43%)
  blocking collectives  801 us (42%)
  waiting for transfers between devices  179 us (9%)
  matrix products  24.1 us (1%)
  other arithmetic  20.6 us (1%)
    ppermute x176, starting transfers between devices, from_behind(): return lax.ppermute(value, axis, pairs)  819 us
    all_gather x4, blocking collectives, combined_all(): pieces = jax.tree.map(lambda part: lax.all_gather(part, axis), value)  449 us
    reduce_scatter x1, waiting for transfers between devices, local(): lax.psum_scatter(image_part, 'grp', scatter_dimension=0, tiled=True)  135 us
    all_gather x1, blocking collectives, local(): lax.all_gather(image, 'grp', axis=0, tiled=True)  128 us
    all_gather x1, blocking collectives, local(): lax.all_gather(mimage, 'grp', axis=0, tiled=True)  114 us
    psum x1, blocking collectives, local(): loss = lax.psum(local_loss, ('grp', 'blk')) / (2.0 * total_pairs)  110 us
    ppermute x176, waiting for transfers between devices, from_behind(): return lax.ppermute(value, axis, pairs)  44.6 us
  transfers between devices with their start and end apart: 177, of which 33 were waited for; matrix products, arithmetic and copies ran while one was open for 2% of the time, Pallas kernels for 0%

commit v1 on v0

v1 whole, which is shorter than its diff:
```python
import jax
import jax.numpy as jnp
from jax import lax
from jax.sharding import Mesh, PartitionSpec as P

mix_weight = 0.4
plane = ("x", "y", "c")
column = ("zh", "zl")


def share(block, axes, count):
    sent = jnp.broadcast_to(block[None], (count,) + block.shape)
    return lax.all_to_all(sent, axes, 0, 0, tiled=True)


def scores(left, right):
    product = lax.dot_general(left, right, (((1,), (1,)), ((), ())), preferred_element_type=jnp.float32)
    return product * left.shape[1] ** (-0.5)


def stats_of(score_on, score_mom, along):
    max_on = jnp.max(score_on, axis=along)
    sum_on = jnp.sum(jnp.exp(score_on - jnp.expand_dims(max_on, along)), axis=along)
    max_mom = jnp.max(score_mom, axis=along)
    weight = jnp.exp(score_mom - jnp.expand_dims(max_mom, along))
    return [max_on, sum_on, max_mom, jnp.sum(weight, axis=along), jnp.sum(weight * score_on, axis=along)]


def combine(parts):
    max_on, sum_on, max_mom, sum_mom, cross = (parts[:, k] for k in range(5))
    top_on = jnp.max(max_on, axis=0)
    lse_on = top_on + jnp.log(jnp.sum(sum_on * jnp.exp(max_on - top_on), axis=0))
    top_mom = jnp.max(max_mom, axis=0)
    rescale = jnp.exp(max_mom - top_mom)
    total = jnp.sum(sum_mom * rescale, axis=0)
    lse_mom = top_mom + jnp.log(total)
    loss = jnp.sum(lse_on - mix_weight * jnp.sum(cross * rescale, axis=0) / total)
    return lse_on, lse_mom, loss


def local(image, text, mimage, mtext):
    rows, width = image.shape
    n_plane = lax.axis_size(plane)
    n_column = lax.axis_size(column)
    got_i = share(jnp.concatenate([image, mimage], axis=0), plane, n_plane)
    got_t = share(jnp.concatenate([text, mtext], axis=0), column, n_column)
    images = got_i[:, :rows].reshape(n_plane * rows, width)
    mimages = got_i[:, rows:].reshape(n_plane * rows, width)
    texts = got_t[:, :rows].reshape(n_column * rows, width)
    mtexts = got_t[:, rows:].reshape(n_column * rows, width)

    score_on = scores(images, texts)
    score_mom = scores(mimages, mtexts)

    def ids(n, axes, other):
        pos = lax.iota(jnp.int32, n * rows)
        peer, row = pos // rows, pos % rows
        return peer, row

    peer, row = ids(n_plane, plane, None)
    px, py, pc = peer // 8, (peer // 2) % 4, peer % 2
    zh, zl = lax.axis_index("zh"), lax.axis_index("zl")
    image_ids = ((zh * 8 + px * 2 + pc) * 32 + zl * 4 + py) * rows + row
    peer, row = ids(n_column, column, None)
    qh, ql = peer // 8, peer % 8
    x, y, c = lax.axis_index("x"), lax.axis_index("y"), lax.axis_index("c")
    text_ids = ((ql * 4 + y) * 16 + qh * 8 + x * 2 + c) * rows + row
    diagonal = image_ids[:, None] == text_ids[None, :]

    row_parts = jnp.stack(stats_of(score_on, score_mom, 1))
    col_parts = jnp.stack(stats_of(score_on, score_mom, 0))
    own = jnp.sum(jnp.where(diagonal, score_on, 0.0), axis=0)
    col_parts = jnp.concatenate([col_parts, own[None]], axis=0)
    row_got = share(row_parts, plane, n_plane)
    col_got = share(col_parts, column, n_column)
    row_on, row_mom, row_loss = combine(row_got)
    col_on, col_mom, col_loss = combine(col_got)
    col_loss = col_loss - 2.0 * (1.0 - mix_weight) * jnp.sum(col_got[:, 5])

    delta = jnp.where(diagonal, 1.0 - mix_weight, 0.0)
    target_row = mix_weight * jnp.exp(score_mom - row_mom[:, None]) + delta
    target_col = mix_weight * jnp.exp(score_mom - col_mom[None, :]) + delta
    prob_row = jnp.exp(score_on - row_on[:, None])
    prob_col = jnp.exp(score_on - col_on[None, :])
    grad = (0.5 * ((prob_row - target_row) + (prob_col - target_col))).astype(jnp.bfloat16)

    part_image = jnp.dot(grad, texts, preferred_element_type=jnp.float32)
    part_text = lax.dot_general(grad, images, (((0,), (0,)), ((), ())), preferred_element_type=jnp.float32)
    got_image = lax.all_to_all(part_image.reshape(n_plane, rows, width), plane, 0, 0, tiled=True)
    got_text = lax.all_to_all(part_text.reshape(n_column, rows, width), column, 0, 0, tiled=True)
    grad_image = jnp.sum(got_image, axis=0)
    grad_text = jnp.sum(got_text, axis=0)

    row_losses = share(jnp.full((1, 128), row_loss), column, n_column)
    col_losses = share(jnp.full((1, 128), col_loss), plane, n_plane)
    total_pairs = rows * n_plane * n_column
    loss = (jnp.sum(row_losses[:, 0, 0]) + jnp.sum(col_losses[:, 0, 0])) / (2.0 * total_pairs)
    return grad_image, grad_text, loss


def solution(mesh):
    fine = Mesh(mesh.devices.reshape(8, 4, 2, 4, 2), ("zl", "y", "zh", "x", "c"))
    by_image = P(("zh", "x", "c", "zl", "y"), None)
    by_text = P(("zl", "y", "zh", "x", "c"), None)
    return jax.shard_map(
        local,
        mesh=fine,
        in_specs=(by_image, by_text, by_image, by_text),
        out_specs=(by_image, by_text, P()),
        check_vma=False,
    )
```

time: 1890 us -> 193 us (0.10)
  the two profiles are of different devices: /device:TPU:2 before, /device:TPU:32 now
where the time goes in v1:
time: 193 us; the launch traced here: 192 us
  waiting for transfers between devices  123 us (64%)
  starting transfers between devices  49.5 us (26%)
  other arithmetic  5.94 us (3%)
  local copies, waits for them, and re-layouts  5.37 us (3%)
  between operations  4.46 us (2%)
  matrix products  3.19 us (2%)
    all_to_all x6, waiting for transfers between devices, share(): return lax.all_to_all(sent, axes, 0, 0, tiled=True)  81.3 us
    all_to_all x6, starting transfers between devices, share(): return lax.all_to_all(sent, axes, 0, 0, tiled=True)  40.7 us
    all_to_all x1, waiting for transfers between devices, local(): lax.all_to_all(part_text.reshape(n_column, rows, width), column, 0, 0, ti...  26.6 us
    all_to_all x1, waiting for transfers between devices, local(): lax.all_to_all(part_image.reshape(n_plane, rows, width), plane, 0, 0, til...  15.4 us
    all_to_all x1, starting transfers between devices, local(): lax.all_to_all(part_text.reshape(n_column, rows, width), column, 0, 0, ti...  4.88 us
    all_to_all x1, starting transfers between devices, local(): lax.all_to_all(part_image.reshape(n_plane, rows, width), plane, 0, 0, til...  3.93 us
  transfers between devices with their start and end apart: 8, of which 8 were waited for; matrix products, arithmetic and copies ran while one was open for 4% of the time, Pallas kernels for 0%

profile of v1, /device:TPU:32, one launch (start us, length us, event | category | flops | bytes accessed | tf_op | source)
XLA Modules:
  0.0 191.7 jit_solution(16038863495605789231)
XLA Ops:
  0.6 0.7 pad_maximum_fusion
  1.4 1.1 broadcast_in_dim.22
  2.5 7.5 %all-to-all-start = ((bf16[32,16,1024]{2,1,0:T(8,128)(2,1)}), bf16[32,16,1024]{2,1,0:T(8,128)(2,1)S(1)}, u32[]{:S(2)}, u32[]{:S(2)}) async-start(bf16[32,16,1024]{2,1,0:T(8,128)(2,1)} %broadcast_in_dim.22), calls=%async_computation | async-start | bytes 2097152 | tf_op jit(solution)/shard_map/all_to_all | solution.py:13
  10.0 16.8 %all-to-all-done = bf16[32,16,1024]{2,1,0:T(8,128)(2,1)S(1)} async-done(((bf16[32,16,1024]{2,1,0:T(8,128)(2,1)}), bf16[32,16,1024]{2,1,0:T(8,128)(2,1)S(1)}, u32[]{:S(2)}, u32[]{:S(2)}) %all-to-all-start) | async-done | bytes 1048608 | tf_op jit(solution)/shard_map/all_to_all | solution.py:13
  26.8 0.8 broadcast_in_dim.23
  27.6 15.2 %all-to-all-start.1 = ((bf16[16,16,1024]{2,1,0:T(8,128)(2,1)}), bf16[16,16,1024]{2,1,0:T(8,128)(2,1)S(1)}, u32[]{:S(2)}, u32[]{:S(2)}) async-start(bf16[16,16,1024]{2,1,0:T(8,128)(2,1)} %broadcast_in_dim.23), calls=%async_computation.1 | async-start | bytes 1048576 | tf_op jit(solution)/shard_map/all_to_all | solution.py:13
  42.9 29.8 %all-to-all-done.1 = bf16[16,16,1024]{2,1,0:T(8,128)(2,1)S(1)} async-done(((bf16[16,16,1024]{2,1,0:T(8,128)(2,1)}), bf16[16,16,1024]{2,1,0:T(8,128)(2,1)S(1)}, u32[]{:S(2)}, u32[]{:S(2)}) %all-to-all-start.1) | async-done | bytes 524320 | tf_op jit(solution)/shard_map/all_to_all | solution.py:13
  73.8 0.7 broadcast_in_dim.24
  74.5 3.9 %all-to-all-start.2 = ((f32[32,5,256]{2,1,0:T(8,128)}), f32[32,5,256]{2,1,0:T(8,128)S(1)}, u32[]{:S(2)}, u32[]{:S(2)}) async-start(f32[32,5,256]{2,1,0:T(8,128)} %broadcast_in_dim.24), calls=%async_computation.2 | async-start | bytes 524288 | tf_op jit(solution)/shard_map/all_to_all | solution.py:13
  78.4 8.9 %all-to-all-done.2 = f32[32,5,256]{2,1,0:T(8,128)S(1)} async-done(((f32[32,5,256]{2,1,0:T(8,128)}), f32[32,5,256]{2,1,0:T(8,128)S(1)}, u32[]{:S(2)}, u32[]{:S(2)}) %all-to-all-start.2) | async-done | bytes 163872 | tf_op jit(solution)/shard_map/all_to_all | solution.py:13
  88.0 6.1 %all-to-all-start.3 = ((f32[16,6,128]{2,1,0:T(8,128)}), f32[16,6,128]{2,1,0:T(8,128)S(1)}, u32[]{:S(2)}, u32[]{:S(2)}) async-start(f32[16,6,128]{2,1,0:T(8,128)} %broadcast_in_dim.28), calls=%async_computation.3 | async-start | bytes 131072 | tf_op jit(solution)/shard_map/all_to_all | solution.py:13
  94.9 11.5 %all-to-all-done.3 = f32[16,6,128]{2,1,0:T(8,128)S(1)} async-done(((f32[16,6,128]{2,1,0:T(8,128)}), f32[16,6,128]{2,1,0:T(8,128)S(1)}, u32[]{:S(2)}, u32[]{:S(2)}) %all-to-all-start.3) | async-done | bytes 49184 | tf_op jit(solution)/shard_map/all_to_all | solution.py:13
  106.3 1.2 broadcast_in_dim_broadcast_in_dim_broadcast_in_dim.6
  107.6 4.2 %all-to-all-start.6 = ((f32[16,1,128]{2,1,0:T(1,128)}), f32[16,1,128]{2,1,0:T(1,128)S(1)}, u32[]{:S(2)}, u32[]{:S(2)}) async-start(f32[16,1,128]{2,1,0:T(1,128)} %broadcast_in_dim_broadcast_in_dim_broadcast_in_dim.6), calls=%async_computation.6 | async-start | bytes 16384 | tf_op jit(solution)/shard_map/all_to_all | solution.py:13
  114.4 8.4 %all-to-all-done.6 = f32[16,1,128]{2,1,0:T(1,128)S(1)} async-done(((f32[16,1,128]{2,1,0:T(1,128)}), f32[16,1,128]{2,1,0:T(1,128)S(1)}, u32[]{:S(2)}, u32[]{:S(2)}) %all-to-all-start.6) | async-done | bytes 8224 | tf_op jit(solution)/shard_map/all_to_all | solution.py:13
  123.4 3.8 %all-to-all-start.7 = ((f32[32,1,128]{2,1,0:T(1,128)}), f32[32,1,128]{2,1,0:T(1,128)S(1)}, u32[]{:S(2)}, u32[]{:S(2)}) async-start(f32[32,1,128]{2,1,0:T(1,128)} %broadcast_in_dim_broadcast_in_dim_broadcast_in_dim.7), calls=%async_computation.7 | async-start | bytes 32768 | tf_op jit(solution)/shard_map/all_to_all | solution.py:13
  127.2 1.4 fusion.5
  128.6 5.9 %all-to-all-done.7 = f32[32,1,128]{2,1,0:T(1,128)S(1)} async-done(((f32[32,1,128]{2,1,0:T(1,128)}), f32[32,1,128]{2,1,0:T(1,128)S(1)}, u32[]{:S(2)}, u32[]{:S(2)}) %all-to-all-start.7) | async-done | bytes 16416 | tf_op jit(solution)/shard_map/all_to_all | solution.py:13
  134.5 3.9 %all-to-all-start.4 = ((f32[32,8,1024]{2,1,0:T(8,128)}), f32[32,8,1024]{2,1,0:T(8,128)S(1)}, u32[]{:S(2)}, u32[]{:S(2)}) async-start(f32[32,8,1024]{2,1,0:T(8,128)} %fusion.5), calls=%async_computation.4 | async-start | bytes 2097152 | tf_op jit(solution)/shard_map/all_to_all | solution.py:89
  138.8 1.1 fusion
  139.8 15.4 %all-to-all-done.4 = f32[32,8,1024]{2,1,0:T(8,128)S(1)} async-done(((f32[32,8,1024]{2,1,0:T(8,128)}), f32[32,8,1024]{2,1,0:T(8,128)S(1)}, u32[]{:S(2)}, u32[]{:S(2)}) %all-to-all-start.4) | async-done | bytes 1048608 | tf_op jit(solution)/shard_map/all_to_all | solution.py:89
  155.2 4.9 %all-to-all-start.5 = ((f32[16,8,1024]{2,1,0:T(8,128)}), f32[16,8,1024]{2,1,0:T(8,128)S(1)}, u32[]{:S(2)}, u32[]{:S(2)}) async-start(f32[16,8,1024]{2,1,0:T(8,128)} %fusion), calls=%async_computation.5 | async-start | bytes 1048576 | tf_op jit(solution)/shard_map/all_to_all | solution.py:90
  162.7 0.7 reduce_sum.191
  163.4 26.6 %all-to-all-done.5 = f32[16,8,1024]{2,1,0:T(8,128)S(1)} async-done(((f32[16,8,1024]{2,1,0:T(8,128)}), f32[16,8,1024]{2,1,0:T(8,128)S(1)}, u32[]{:S(2)}, u32[]{:S(2)}) %all-to-all-start.5) | async-done | bytes 524320 | tf_op jit(solution)/shard_map/all_to_all | solution.py:90
  (28 shorter events, 6.7 us)
Async XLA Ops:
  2.5 7.5 %copy-start = (bf16[8,1024]{1,0:T(8,128)(2,1)S(1)}, bf16[8,1024]{1,0:T(8,128)(2,1)}, u32[]{:S(2)}) copy-start(bf16[8,1024]{1,0:T(8,128)(2,1)} %param.7) | copy-start | bytes 49156
  2.5 7.5 %copy-start.1 = (bf16[8,1024]{1,0:T(8,128)(2,1)S(1)}, bf16[8,1024]{1,0:T(8,128)(2,1)}, u32[]{:S(2)}) copy-start(bf16[8,1024]{1,0:T(8,128)(2,1)} %param.5) | copy-start | bytes 49156
  2.5 24.3 %all-to-all-start = ((bf16[32,16,1024]{2,1,0:T(8,128)(2,1)}), bf16[32,16,1024]{2,1,0:T(8,128)(2,1)S(1)}, u32[]{:S(2)}, u32[]{:S(2)}) async-start(bf16[32,16,1024]{2,1,0:T(8,128)(2,1)} %broadcast_in_dim.22), calls=%async_computation | async-start | bytes 2097152 | tf_op jit(solution)/shard_map/all_to_all | solution.py:13
  27.6 45.0 %all-to-all-start.1 = ((bf16[16,16,1024]{2,1,0:T(8,128)(2,1)}), bf16[16,16,1024]{2,1,0:T(8,128)(2,1)S(1)}, u32[]{:S(2)}, u32[]{:S(2)}) async-start(bf16[16,16,1024]{2,1,0:T(8,128)(2,1)} %broadcast_in_dim.23), calls=%async_computation.1 | async-start | bytes 1048576 | tf_op jit(solution)/shard_map/all_to_all | solution.py:13
  74.5 12.8 %all-to-all-start.2 = ((f32[32,5,256]{2,1,0:T(8,128)}), f32[32,5,256]{2,1,0:T(8,128)S(1)}, u32[]{:S(2)}, u32[]{:S(2)}) async-start(f32[32,5,256]{2,1,0:T(8,128)} %broadcast_in_dim.24), calls=%async_computation.2 | async-start | bytes 524288 | tf_op jit(solution)/shard_map/all_to_all | solution.py:13
  88.0 18.4 %all-to-all-start.3 = ((f32[16,6,128]{2,1,0:T(8,128)}), f32[16,6,128]{2,1,0:T(8,128)S(1)}, u32[]{:S(2)}, u32[]{:S(2)}) async-start(f32[16,6,128]{2,1,0:T(8,128)} %broadcast_in_dim.28), calls=%async_computation.3 | async-start | bytes 131072 | tf_op jit(solution)/shard_map/all_to_all | solution.py:13
  107.6 15.2 %all-to-all-start.6 = ((f32[16,1,128]{2,1,0:T(1,128)}), f32[16,1,128]{2,1,0:T(1,128)S(1)}, u32[]{:S(2)}, u32[]{:S(2)}) async-start(f32[16,1,128]{2,1,0:T(1,128)} %broadcast_in_dim_broadcast_in_dim_broadcast_in_dim.6), calls=%async_computation.6 | async-start | bytes 16384 | tf_op jit(solution)/shard_map/all_to_all | solution.py:13
  123.4 11.1 %all-to-all-start.7 = ((f32[32,1,128]{2,1,0:T(1,128)}), f32[32,1,128]{2,1,0:T(1,128)S(1)}, u32[]{:S(2)}, u32[]{:S(2)}) async-start(f32[32,1,128]{2,1,0:T(1,128)} %broadcast_in_dim_broadcast_in_dim_broadcast_in_dim.7), calls=%async_computation.7 | async-start | bytes 32768 | tf_op jit(solution)/shard_map/all_to_all | solution.py:13
  134.5 20.7 %all-to-all-start.4 = ((f32[32,8,1024]{2,1,0:T(8,128)}), f32[32,8,1024]{2,1,0:T(8,128)S(1)}, u32[]{:S(2)}, u32[]{:S(2)}) async-start(f32[32,8,1024]{2,1,0:T(8,128)} %fusion.5), calls=%async_computation.4 | async-start | bytes 2097152 | tf_op jit(solution)/shard_map/all_to_all | solution.py:89
  155.2 34.7 %all-to-all-start.5 = ((f32[16,8,1024]{2,1,0:T(8,128)}), f32[16,8,1024]{2,1,0:T(8,128)S(1)}, u32[]{:S(2)}, u32[]{:S(2)}) async-start(f32[16,8,1024]{2,1,0:T(8,128)} %fusion), calls=%async_computation.5 | async-start | bytes 1048576 | tf_op jit(solution)/shard_map/all_to_all | solution.py:90

commit v2 on v1

v2 whole, which is shorter than its diff:
```python
import jax
import jax.numpy as jnp
from jax import lax
from jax.sharding import Mesh, PartitionSpec as P

mix_weight = 0.4
column = ("zh", "zl")


def share(block, axes, count):
    sent = jnp.broadcast_to(block[None], (count,) + block.shape)
    return lax.all_to_all(sent, axes, 0, 0, tiled=True)


def swap(block):
    return lax.ppermute(block, "c", [(0, 1), (1, 0)])


def share_ring(block):
    return lax.all_gather(lax.all_gather(block, "x"), "y")


def scatter_ring(parts, axis, extra):
    here = lax.axis_index(axis)
    parts = parts.reshape(4, -1, parts.shape[-1])
    total = lax.dynamic_index_in_dim(parts, here, 0, False)
    tail = jnp.full((8, parts.shape[-1]), extra)
    rows = total.shape[0]
    got = []
    for k in (2, 1, 3):
        block = lax.dynamic_index_in_dim(parts, (here + k) % 4, 0, False)
        sent = jnp.concatenate([block, tail], axis=0)
        got.append(lax.ppermute(sent, axis, [(i, (i + k) % 4) for i in range(4)]))
    for piece in got:
        total = total + piece[:rows]
        extra = extra + piece[rows, 0]
    return total, extra


def scores(left, right):
    product = lax.dot_general(left, right, (((1,), (1,)), ((), ())), preferred_element_type=jnp.float32)
    return product * left.shape[1] ** (-0.5)


def stats_of(score_on, score_mom, along):
    max_on = jnp.max(score_on, axis=along)
    sum_on = jnp.sum(jnp.exp(score_on - jnp.expand_dims(max_on, along)), axis=along)
    max_mom = jnp.max(score_mom, axis=along)
    weight = jnp.exp(score_mom - jnp.expand_dims(max_mom, along))
    return [max_on, sum_on, max_mom, jnp.sum(weight, axis=along), jnp.sum(weight * score_on, axis=along)]


def combine(parts):
    max_on, sum_on, max_mom, sum_mom, cross = (parts[:, k] for k in range(5))
    top_on = jnp.max(max_on, axis=0)
    lse_on = top_on + jnp.log(jnp.sum(sum_on * jnp.exp(max_on - top_on), axis=0))
    top_mom = jnp.max(max_mom, axis=0)
    rescale = jnp.exp(max_mom - top_mom)
    total = jnp.sum(sum_mom * rescale, axis=0)
    lse_mom = top_mom + jnp.log(total)
    loss = jnp.sum(lse_on - mix_weight * jnp.sum(cross * rescale, axis=0) / total)
    return lse_on, lse_mom, loss


def local(image, text, mimage, mtext):
    rows, width = image.shape
    x, y, c, zh, zl = (lax.axis_index(a) for a in ("x", "y", "c", "zh", "zl"))
    n_plane, n_column = 32, 16
    half = n_plane // 2 * rows
    got_t = share(jnp.concatenate([text, mtext], axis=0), column, n_column)
    mine = share_ring(jnp.concatenate([image, mimage], axis=0)).reshape(16, 2 * rows, width)
    got_i = jnp.concatenate([mine, swap(mine)], axis=0)
    images = got_i[:, :rows].reshape(n_plane * rows, width)
    mimages = got_i[:, rows:].reshape(n_plane * rows, width)
    texts = got_t[:, :rows].reshape(n_column * rows, width)
    mtexts = got_t[:, rows:].reshape(n_column * rows, width)

    score_on = scores(images, texts)
    score_mom = scores(mimages, mtexts)

    pos = lax.iota(jnp.int32, n_plane * rows)
    peer, row = pos // rows, pos % rows
    pc, py, px = peer // 16, (peer // 4) % 4, peer % 4
    pc = jnp.where(pc == 0, c, 1 - c)
    image_ids = ((zh * 8 + px * 2 + pc) * 32 + zl * 4 + py) * rows + row
    pos = lax.iota(jnp.int32, n_column * rows)
    peer, row = pos // rows, pos % rows
    text_ids = (((peer % 8) * 4 + y) * 16 + (peer // 8) * 8 + x * 2 + c) * rows + row
    diagonal = image_ids[:, None] == text_ids[None, :]

    none = jnp.zeros((n_plane * rows,), jnp.float32)
    row_parts = jnp.stack(stats_of(score_on, score_mom, 1) + [none] * 3)
    own = jnp.sum(jnp.where(diagonal, score_on, 0.0), axis=0)
    col_parts = jnp.stack(stats_of(score_on, score_mom, 0) + [own] + [none[: n_column * rows]] * 2)
    col_got = share(col_parts, column, n_column)
    other = swap(jnp.concatenate([row_parts[:, half:], row_parts[:, :half]], axis=1))
    row_got = share_ring(jnp.concatenate([row_parts, other], axis=0)).reshape(n_plane, 8, n_plane * rows)
    row_on, row_mom, row_loss = combine(row_got)
    col_on, col_mom, col_loss = combine(col_got)
    col_loss = col_loss - 2.0 * (1.0 - mix_weight) * jnp.sum(col_got[:, 5])

    delta = jnp.where(diagonal, 1.0 - mix_weight, 0.0)
    target_row = mix_weight * jnp.exp(score_mom - row_mom[:, None]) + delta
    target_col = mix_weight * jnp.exp(score_mom - col_mom[None, :]) + delta
    prob_row = jnp.exp(score_on - row_on[:, None])
    prob_col = jnp.exp(score_on - col_on[None, :])
    grad = (0.5 * ((prob_row - target_row) + (prob_col - target_col))).astype(jnp.bfloat16)

    part_text = lax.dot_general(grad, images, (((0,), (0,)), ((), ())), preferred_element_type=jnp.float32)
    tail = jnp.full((n_column, rows, 128), row_loss)
    sent_text = jnp.concatenate([part_text.reshape(n_column, rows, width), tail], axis=2)
    got_text = lax.all_to_all(sent_text, column, 0, 0, tiled=True)

    part_image = jnp.dot(grad, texts, preferred_element_type=jnp.float32)
    got = swap(jnp.concatenate([part_image[half:], jnp.full((8, width), col_loss)], axis=0))
    part_image = part_image[:half] + got[:half]
    part_image, col_loss = scatter_ring(part_image, "y", col_loss + got[half, 0])
    grad_image, col_loss = scatter_ring(part_image, "x", col_loss)

    grad_text = jnp.sum(got_text[:, :, :width], axis=0)
    loss = (jnp.sum(got_text[:, 0, width]) + col_loss) / (2.0 * rows * n_plane * n_column)
    return grad_image, grad_text, loss


def solution(mesh):
    fine = Mesh(mesh.devices.reshape(8, 4, 2, 4, 2), ("zl", "y", "zh", "x", "c"))
    by_image = P(("zh", "x", "c", "zl", "y"), None)
    by_text = P(("zl", "y", "zh", "x", "c"), None)
    return jax.shard_map(
        local,
        mesh=fine,
        in_specs=(by_image, by_text, by_image, by_text),
        out_specs=(by_image, by_text, P()),
        check_vma=False,
    )
```

time: 193 us -> 145 us (0.75)
  the two profiles are of different devices: /device:TPU:32 before, /device:TPU:56 now
where the time goes in v2:
time: 145 us; the launch traced here: 144 us
  starting transfers between devices  64.9 us (45%)
  blocking collectives  49.2 us (34%)
  between operations  8.69 us (6%)
  waiting for transfers between devices  7.96 us (5%)
  local copies, waits for them, and re-layouts  6.98 us (5%)
  other arithmetic  5.08 us (4%)
  matrix products  1.54 us (1%)
    all_gather x4, blocking collectives, share_ring(): return lax.all_gather(lax.all_gather(block, 'x'), 'y')  49.2 us
    all_to_all x2, starting transfers between devices, share(): return lax.all_to_all(sent, axes, 0, 0, tiled=True)  27.4 us
    ppermute x6, starting transfers between devices, scatter_ring(): got.append(lax.ppermute(sent, axis, [(i, (i + k) % 4) for i in range(4)]))  19.6 us
    all_to_all x1, starting transfers between devices, local(): got_text = lax.all_to_all(sent_text, column, 0, 0, tiled=True)  12 us
    ppermute x3, starting transfers between devices, swap(): return lax.ppermute(block, 'c', [(0, 1), (1, 0)])  5.87 us
    ppermute x6, waiting for transfers between devices, scatter_ring(): got.append(lax.ppermute(sent, axis, [(i, (i + k) % 4) for i in range(4)]))  4.3 us
    ppermute x3, waiting for transfers between devices, swap(): return lax.ppermute(block, 'c', [(0, 1), (1, 0)])  3.65 us
    slice x6, local copies, waits for them, and re-layouts, scatter_ring(): extra = extra + piece[rows, 0]  3.07 us
  transfers between devices with their start and end apart: 12, of which 6 were waited for; matrix products, arithmetic and copies ran while one was open for 5% of the time, Pallas kernels for 0%

profile of v2, /device:TPU:56, one launch (start us, length us, event | category | flops | bytes accessed | tf_op | source)
XLA Modules:
  0.0 144.4 jit_solution(17721619021912495941)
XLA Ops:
  0.6 0.7 pad_maximum_fusion.1
  1.4 0.8 broadcast_in_dim.24
  2.2 15.3 %all-to-all-start = ((bf16[16,16,1024]{2,1,0:T(8,128)(2,1)}), bf16[16,16,1024]{2,1,0:T(8,128)(2,1)S(1)}, u32[]{:S(2)}, u32[]{:S(2)}) async-start(bf16[16,16,1024]{2,1,0:T(8,128)(2,1)} %broadcast_in_dim.24), calls=%async_computation | async-start | bytes 1048576 | tf_op jit(solution)/shard_map/all_to_all | solution.py:12
  17.6 12.3 %all-gather = bf16[64,1024]{1,0:T(8,128)(2,1)S(1)} all-gather(bf16[16,1024]{1,0:T(8,128)(2,1)S(1)} %pad_maximum_fusion), channel_id=2, replica_groups=mesh['zl'=8,'y'=4,'zh'=2,'x'=4,'c'=2] {'x'}, dimensions={0}, use_global_device_ids=true | all-gather | bytes 163840 | tf_op jit(solution)/shard_map/all_gather | solution.py:20
  29.9 12.8 %all-gather.1 = bf16[16,16,1024]{2,1,0:T(8,128)(2,1)S(1)} all-gather(bf16[4,16,1024]{2,1,0:T(8,128)(2,1)S(1)} %bitcast.135), channel_id=3, replica_groups=mesh['zl'=8,'y'=4,'zh'=2,'x'=4,'c'=2] {'y'}, dimensions={0}, use_global_device_ids=true | all-gather | bytes 655360 | tf_op jit(solution)/shard_map/all_gather | solution.py:20
  42.7 1.9 %collective-permute-start = (bf16[16,16,1024]{2,1,0:T(8,128)(2,1)S(1)}, bf16[16,16,1024]{2,1,0:T(8,128)(2,1)S(1)}, u32[]{:S(2)}, u32[]{:S(2)}) collective-permute-start(bf16[16,16,1024]{2,1,0:T(8,128)(2,1)S(1)} %all-gather.1), channel_id=1, source_target_pairs={{0,1},{1,0},{2,3},{3,2},{4,5},{5,4},{6,7},{7,6},{8,9},{9,8},{10,11... | collective-permute-start | bytes 1572872 | tf_op jit(solution)/shard_map/ppermute | solution.py:16
  44.7 1.8 %collective-permute-done = bf16[16,16,1024]{2,1,0:T(8,128)(2,1)S(1)} collective-permute-done((bf16[16,16,1024]{2,1,0:T(8,128)(2,1)S(1)}, bf16[16,16,1024]{2,1,0:T(8,128)(2,1)S(1)}, u32[]{:S(2)}, u32[]{:S(2)}) %collective-permute-start) | collective-permute-done | bytes 524320 | tf_op jit(solution)/shard_map/ppermute | solution.py:16
  47.7 2.0 %collective-permute-start.1 = (f32[8,256]{1,0:T(8,128)S(1)}, f32[8,256]{1,0:T(8,128)S(1)}, u32[]{:S(2)}, u32[]{:S(2)}) collective-permute-start(f32[8,256]{1,0:T(8,128)S(1)} %pad_maximum_fusion.2), channel_id=1, source_target_pairs={{0,1},{1,0},{2,3},{3,2},{4,5},{5,4},{6,7},{7,6},{8,9},{9,8},{10,11... | collective-permute-start | bytes 24584 | tf_op jit(solution)/shard_map/ppermute | solution.py:16
  50.4 12.0 %all-to-all-start.1 = ((f32[16,8,128]{2,1,0:T(8,128)}), f32[16,8,128]{2,1,0:T(8,128)S(1)}, u32[]{:S(2)}, u32[]{:S(2)}) async-start(f32[16,8,128]{2,1,0:T(8,128)} %broadcast_in_dim.31), calls=%async_computation.1 | async-start | bytes 131072 | tf_op jit(solution)/shard_map/all_to_all | solution.py:12
  62.5 11.9 %all-gather.2 = f32[64,256]{1,0:T(8,128)S(1)} all-gather(f32[16,256]{1,0:T(8,128)S(1)} %concatenate.44), channel_id=4, replica_groups=mesh['zl'=8,'y'=4,'zh'=2,'x'=4,'c'=2] {'x'}, dimensions={0}, use_global_device_ids=true | all-gather | bytes 81920 | tf_op jit(solution)/shard_map/all_gather | solution.py:20
  74.3 12.2 %all-gather.3 = f32[16,16,256]{2,1,0:T(8,128)S(1)} all-gather(f32[4,16,256]{2,1,0:T(8,128)S(1)} %bitcast.136), channel_id=5, replica_groups=mesh['zl'=8,'y'=4,'zh'=2,'x'=4,'c'=2] {'y'}, dimensions={0}, use_global_device_ids=true | all-gather | bytes 327680 | tf_op jit(solution)/shard_map/all_gather | solution.py:20
  88.4 1.5 %concatenate.52 = f32[16,8,1152]{2,1,0:T(8,128)} pad(f32[16,8,1024]{2,1,0:T(8,128)S(1)} %fusion, f32[]{:T(128)} %get-tuple-element.20), padding=0_0x0_0x0_128 | pad | bytes 1114116 | tf_op jit(solution)/shard_map/concatenate | solution.py:111
  89.9 12.0 %all-to-all-start.2 = ((f32[16,8,1152]{2,1,0:T(8,128)}), f32[16,8,1152]{2,1,0:T(8,128)S(1)}, u32[]{:S(2)}, u32[]{:S(2)}) async-start(f32[16,8,1152]{2,1,0:T(8,128)} %concatenate.52), calls=%async_computation.2 | async-start | bytes 1179648 | tf_op jit(solution)/shard_map/all_to_all | solution.py:112
  104.4 1.9 %collective-permute-start.2 = (f32[136,1024]{1,0:T(8,128)S(1)}, f32[136,1024]{1,0:T(8,128)S(1)}, u32[]{:S(2)}, u32[]{:S(2)}) collective-permute-start(f32[136,1024]{1,0:T(8,128)S(1)} %concatenate.45), channel_id=1, source_target_pairs={{0,1},{1,0},{2,3},{3,2},{4,5},{5,4},{6,7},{7,6},{8,9},{9,8},{10,11... | collective-permute-start | bytes 1671176 | tf_op jit(solution)/shard_map/ppermute | solution.py:16
  106.4 1.9 %collective-permute-done.2 = f32[136,1024]{1,0:T(8,128)S(1)} collective-permute-done((f32[136,1024]{1,0:T(8,128)S(1)}, f32[136,1024]{1,0:T(8,128)S(1)}, u32[]{:S(2)}, u32[]{:S(2)}) %collective-permute-start.2) | collective-permute-done | bytes 557088 | tf_op jit(solution)/shard_map/ppermute | solution.py:16
  109.5 3.4 %collective-permute-start.3 = (f32[40,1024]{1,0:T(8,128)S(1)}, f32[40,1024]{1,0:T(8,128)S(1)}, u32[]{:S(2)}, u32[]{:S(2)}) collective-permute-start(f32[40,1024]{1,0:T(8,128)S(1)} %concatenate.46), channel_id=1, source_target_pairs={{0,32},{16,48},{32,0},{48,16},{1,33},{17,49},{33,1},{49,17},{2,34}... | collective-permute-start | bytes 491528 | tf_op jit(solution)/shard_map/ppermute | solution.py:33
  112.9 3.3 %collective-permute-start.4 = (f32[40,1024]{1,0:T(8,128)S(1)}, f32[40,1024]{1,0:T(8,128)S(1)}, u32[]{:S(2)}, u32[]{:S(2)}) collective-permute-start(f32[40,1024]{1,0:T(8,128)S(1)} %concatenate.47), channel_id=1, source_target_pairs={{0,16},{16,32},{32,48},{48,0},{1,17},{17,33},{33,49},{49,1},{2,18}... | collective-permute-start | bytes 491528 | tf_op jit(solution)/shard_map/ppermute | solution.py:33
  116.3 2.5 %collective-permute-start.5 = (f32[40,1024]{1,0:T(8,128)S(1)}, f32[40,1024]{1,0:T(8,128)S(1)}, u32[]{:S(2)}, u32[]{:S(2)}) collective-permute-start(f32[40,1024]{1,0:T(8,128)S(1)} %concatenate.48), channel_id=1, source_target_pairs={{0,48},{16,0},{32,16},{48,32},{1,49},{17,1},{33,17},{49,33},{2,50}... | collective-permute-start | bytes 491528 | tf_op jit(solution)/shard_map/ppermute | solution.py:33
  120.3 1.1 collective-permute-done.4
  122.6 2.5 %collective-permute-done.5 = f32[40,1024]{1,0:T(8,128)S(1)} collective-permute-done((f32[40,1024]{1,0:T(8,128)S(1)}, f32[40,1024]{1,0:T(8,128)S(1)}, u32[]{:S(2)}, u32[]{:S(2)}) %collective-permute-start.5) | collective-permute-done | bytes 163872 | tf_op jit(solution)/shard_map/ppermute | solution.py:33
  126.3 3.4 %collective-permute-start.6 = (f32[16,1024]{1,0:T(8,128)S(1)}, f32[16,1024]{1,0:T(8,128)S(1)}, u32[]{:S(2)}, u32[]{:S(2)}) collective-permute-start(f32[16,1024]{1,0:T(8,128)S(1)} %concatenate.49), channel_id=1, source_target_pairs={{0,4},{2,6},{4,0},{6,2},{1,5},{3,7},{5,1},{7,3},{8,12},{10,14},{12... | collective-permute-start | bytes 196616 | tf_op jit(solution)/shard_map/ppermute | solution.py:33
  129.7 3.7 %collective-permute-start.7 = (f32[16,1024]{1,0:T(8,128)S(1)}, f32[16,1024]{1,0:T(8,128)S(1)}, u32[]{:S(2)}, u32[]{:S(2)}) collective-permute-start(f32[16,1024]{1,0:T(8,128)S(1)} %concatenate.50), channel_id=1, source_target_pairs={{0,2},{2,4},{4,6},{6,0},{1,3},{3,5},{5,7},{7,1},{8,10},{10,12},{12... | collective-permute-start | bytes 196616 | tf_op jit(solution)/shard_map/ppermute | solution.py:33
  133.4 3.4 %collective-permute-start.8 = (f32[16,1024]{1,0:T(8,128)S(1)}, f32[16,1024]{1,0:T(8,128)S(1)}, u32[]{:S(2)}, u32[]{:S(2)}) collective-permute-start(f32[16,1024]{1,0:T(8,128)S(1)} %concatenate.51), channel_id=1, source_target_pairs={{0,6},{2,0},{4,2},{6,4},{1,7},{3,1},{5,3},{7,5},{8,14},{10,8},{12,... | collective-permute-start | bytes 196616 | tf_op jit(solution)/shard_map/ppermute | solution.py:33
  142.6 0.6 slice_reduce_fusion
  (61 shorter events, 10.6 us)
Async XLA Ops:
  2.2 15.3 %copy-start = (bf16[8,1024]{1,0:T(8,128)(2,1)S(1)}, bf16[8,1024]{1,0:T(8,128)(2,1)}, u32[]{:S(2)}) copy-start(bf16[8,1024]{1,0:T(8,128)(2,1)} %param.6) | copy-start | bytes 49156
  2.2 15.4 %copy-start.1 = (bf16[8,1024]{1,0:T(8,128)(2,1)S(1)}, bf16[8,1024]{1,0:T(8,128)(2,1)}, u32[]{:S(2)}) copy-start(bf16[8,1024]{1,0:T(8,128)(2,1)} %param.4) | copy-start | bytes 49156
  2.2 44.3 %all-to-all-start = ((bf16[16,16,1024]{2,1,0:T(8,128)(2,1)}), bf16[16,16,1024]{2,1,0:T(8,128)(2,1)S(1)}, u32[]{:S(2)}, u32[]{:S(2)}) async-start(bf16[16,16,1024]{2,1,0:T(8,128)(2,1)} %broadcast_in_dim.24), calls=%async_computation | async-start | bytes 1048576 | tf_op jit(solution)/shard_map/all_to_all | solution.py:12
  42.7 3.8 %collective-permute-start = (bf16[16,16,1024]{2,1,0:T(8,128)(2,1)S(1)}, bf16[16,16,1024]{2,1,0:T(8,128)(2,1)S(1)}, u32[]{:S(2)}, u32[]{:S(2)}) collective-permute-start(bf16[16,16,1024]{2,1,0:T(8,128)(2,1)S(1)} %all-gather.1), channel_id=1, source_target_pairs={{0,1},{1,0},{2,3},{3,2},{4,5},{5,4},{6,7},{7,6},{8,9},{9,8},{10,11... | collective-permute-start | bytes 1572872 | tf_op jit(solution)/shard_map/ppermute | solution.py:16
  47.7 14.8 %collective-permute-start.1 = (f32[8,256]{1,0:T(8,128)S(1)}, f32[8,256]{1,0:T(8,128)S(1)}, u32[]{:S(2)}, u32[]{:S(2)}) collective-permute-start(f32[8,256]{1,0:T(8,128)S(1)} %pad_maximum_fusion.2), channel_id=1, source_target_pairs={{0,1},{1,0},{2,3},{3,2},{4,5},{5,4},{6,7},{7,6},{8,9},{9,8},{10,11... | collective-permute-start | bytes 24584 | tf_op jit(solution)/shard_map/ppermute | solution.py:16
  50.4 37.0 %all-to-all-start.1 = ((f32[16,8,128]{2,1,0:T(8,128)}), f32[16,8,128]{2,1,0:T(8,128)S(1)}, u32[]{:S(2)}, u32[]{:S(2)}) async-start(f32[16,8,128]{2,1,0:T(8,128)} %broadcast_in_dim.31), calls=%async_computation.1 | async-start | bytes 131072 | tf_op jit(solution)/shard_map/all_to_all | solution.py:12
  89.9 51.5 %all-to-all-start.2 = ((f32[16,8,1152]{2,1,0:T(8,128)}), f32[16,8,1152]{2,1,0:T(8,128)S(1)}, u32[]{:S(2)}, u32[]{:S(2)}) async-start(f32[16,8,1152]{2,1,0:T(8,128)} %concatenate.52), calls=%async_computation.2 | async-start | bytes 1179648 | tf_op jit(solution)/shard_map/all_to_all | solution.py:112
  104.4 3.9 %collective-permute-start.2 = (f32[136,1024]{1,0:T(8,128)S(1)}, f32[136,1024]{1,0:T(8,128)S(1)}, u32[]{:S(2)}, u32[]{:S(2)}) collective-permute-start(f32[136,1024]{1,0:T(8,128)S(1)} %concatenate.45), channel_id=1, source_target_pairs={{0,1},{1,0},{2,3},{3,2},{4,5},{5,4},{6,7},{7,6},{8,9},{9,8},{10,11... | collective-permute-start | bytes 1671176 | tf_op jit(solution)/shard_map/ppermute | solution.py:16
  109.5 9.6 %collective-permute-start.3 = (f32[40,1024]{1,0:T(8,128)S(1)}, f32[40,1024]{1,0:T(8,128)S(1)}, u32[]{:S(2)}, u32[]{:S(2)}) collective-permute-start(f32[40,1024]{1,0:T(8,128)S(1)} %concatenate.46), channel_id=1, source_target_pairs={{0,32},{16,48},{32,0},{48,16},{1,33},{17,49},{33,1},{49,17},{2,34}... | collective-permute-start | bytes 491528 | tf_op jit(solution)/shard_map/ppermute | solution.py:33
  112.9 8.5 %collective-permute-start.4 = (f32[40,1024]{1,0:T(8,128)S(1)}, f32[40,1024]{1,0:T(8,128)S(1)}, u32[]{:S(2)}, u32[]{:S(2)}) collective-permute-start(f32[40,1024]{1,0:T(8,128)S(1)} %concatenate.47), channel_id=1, source_target_pairs={{0,16},{16,32},{32,48},{48,0},{1,17},{17,33},{33,49},{49,1},{2,18}... | collective-permute-start | bytes 491528 | tf_op jit(solution)/shard_map/ppermute | solution.py:33
  116.3 8.8 %collective-permute-start.5 = (f32[40,1024]{1,0:T(8,128)S(1)}, f32[40,1024]{1,0:T(8,128)S(1)}, u32[]{:S(2)}, u32[]{:S(2)}) collective-permute-start(f32[40,1024]{1,0:T(8,128)S(1)} %concatenate.48), channel_id=1, source_target_pairs={{0,48},{16,0},{32,16},{48,32},{1,49},{17,1},{33,17},{49,33},{2,50}... | collective-permute-start | bytes 491528 | tf_op jit(solution)/shard_map/ppermute | solution.py:33
  126.3 10.5 %collective-permute-start.6 = (f32[16,1024]{1,0:T(8,128)S(1)}, f32[16,1024]{1,0:T(8,128)S(1)}, u32[]{:S(2)}, u32[]{:S(2)}) collective-permute-start(f32[16,1024]{1,0:T(8,128)S(1)} %concatenate.49), channel_id=1, source_target_pairs={{0,4},{2,6},{4,0},{6,2},{1,5},{3,7},{5,1},{7,3},{8,12},{10,14},{12... | collective-permute-start | bytes 196616 | tf_op jit(solution)/shard_map/ppermute | solution.py:33
  129.7 8.3 %collective-permute-start.7 = (f32[16,1024]{1,0:T(8,128)S(1)}, f32[16,1024]{1,0:T(8,128)S(1)}, u32[]{:S(2)}, u32[]{:S(2)}) collective-permute-start(f32[16,1024]{1,0:T(8,128)S(1)} %concatenate.50), channel_id=1, source_target_pairs={{0,2},{2,4},{4,6},{6,0},{1,3},{3,5},{5,7},{7,1},{8,10},{10,12},{12... | collective-permute-start | bytes 196616 | tf_op jit(solution)/shard_map/ppermute | solution.py:33
  133.4 6.2 %collective-permute-start.8 = (f32[16,1024]{1,0:T(8,128)S(1)}, f32[16,1024]{1,0:T(8,128)S(1)}, u32[]{:S(2)}, u32[]{:S(2)}) collective-permute-start(f32[16,1024]{1,0:T(8,128)S(1)} %concatenate.51), channel_id=1, source_target_pairs={{0,6},{2,0},{4,2},{6,4},{1,7},{3,1},{5,3},{7,5},{8,14},{10,8},{12,... | collective-permute-start | bytes 196616 | tf_op jit(solution)/shard_map/ppermute | solution.py:33

commit v3 on v1

v3 whole, which is shorter than its diff:
```python
import jax
import jax.numpy as jnp
from jax import lax
from jax.experimental import pallas as pl
from jax.experimental.pallas import tpu as pltpu
from jax.sharding import Mesh, PartitionSpec as P

mix_weight = 0.4
very_low = -1e30
column = ("zh", "zl")
n_plane, n_column, rows = 32, 16, 8
f32, bf16 = jnp.float32, jnp.bfloat16
side = 16 * rows


def call(body, outs, *args, flops=0, exps=0):
    whole = pl.BlockSpec(memory_space=pltpu.VMEM)
    specs = [pl.BlockSpec(memory_space=pltpu.SMEM) if a.dtype == jnp.int32 else whole for a in args]
    moved = sum(a.size * a.dtype.itemsize for a in list(args) + outs)
    return pl.pallas_call(
        body,
        out_shape=outs,
        in_specs=specs,
        out_specs=[whole] * len(outs),
        cost_estimate=pl.CostEstimate(flops=flops, bytes_accessed=moved, transcendentals=exps),
        compiler_params=pltpu.CompilerParams(vmem_limit_bytes=40 * 2**20),
    )(*args)


def shape(*dims, dtype=f32):
    return jax.ShapeDtypeStruct(dims, dtype)


def pack_kernel(text_ref, mtext_ref, image_ref, mimage_ref, send_ref, pair_ref):
    def pair(a_ref, b_ref):
        return jnp.concatenate([a_ref[...].astype(f32), b_ref[...].astype(f32)], axis=0).astype(bf16)

    both = pair(text_ref, mtext_ref)
    for peer in range(n_column):
        send_ref[peer] = both
    pair_ref[...] = pair(image_ref, mimage_ref)


def lanes(height):
    lane = lax.broadcasted_iota(jnp.int32, (height, 2 * side), 1)
    return lane, (lane & rows) == 0


def diagonal_of(pos_ref):
    x, y, c, zh, zl = (pos_ref[k] for k in range(5))
    row = lax.broadcasted_iota(jnp.int32, (2 * side, 2 * side), 0)
    lane, valid = lanes(2 * side)
    pc, py, px = row >> 7, (row >> 5) & 3, (row >> 3) & 3
    image_block = (zh * 8 + px * 2 + pc) * 32 + zl * 4 + py
    qh, ql = lane >> 7, (lane >> 4) & 7
    text_block = (ql * 4 + y) * 16 + qh * 8 + x * 2 + c
    return valid & (image_block == text_block) & ((row & 7) == (lane & 7))


def score_kernel(pos_ref, mine_ref, other_ref, text_ref, on_ref, mom_ref, row_ref, col_ref):
    width = text_ref.shape[-1]
    texts = text_ref[...].reshape(2 * side, width)

    def product(ref):
        out = lax.dot_general(
            ref[...].reshape(2 * side, width), texts, (((1,), (1,)), ((), ())), preferred_element_type=f32
        )
        return (out * width ** (-0.5)).reshape(16, 2, rows, 2 * side)

    mine, other = product(mine_ref), product(other_ref)
    first = pos_ref[2] == 0
    low, high = jnp.where(first, mine, other), jnp.where(first, other, mine)
    _, valid = lanes(2 * side)

    def both(which):
        return jnp.concatenate([part[:, which].reshape(side, 2 * side) for part in (low, high)], axis=0)

    on = jnp.where(valid, both(0), very_low)
    mom = jnp.where(valid, pltpu.roll(both(1), 2 * side - rows, 1), very_low)
    on_ref[...] = on
    mom_ref[...] = mom

    def stats(along):
        max_on = jnp.max(on, axis=along, keepdims=True)
        sum_on = jnp.sum(jnp.exp(on - max_on), axis=along, keepdims=True)
        max_mom = jnp.max(mom, axis=along, keepdims=True)
        weight = jnp.exp(mom - max_mom)
        sum_mom = jnp.sum(weight, axis=along, keepdims=True)
        return [max_on, sum_on, max_mom, sum_mom, jnp.sum(weight * on, axis=along, keepdims=True)]

    slot = lax.broadcasted_iota(jnp.int32, (2 * side, 128), 1)
    by_row = jnp.zeros((2 * side, 128), f32)
    for k, value in enumerate(stats(1)):
        by_row = jnp.where(slot == k, value, by_row)
    by_row = by_row.T[:8]
    for peer in range(n_plane):
        row_ref[peer] = by_row
    own = jnp.sum(jnp.where(diagonal_of(pos_ref), on, 0.0), axis=0, keepdims=True)
    slot = lax.broadcasted_iota(jnp.int32, (8, 2 * side), 0)
    by_col = jnp.zeros((8, 2 * side), f32)
    for k, value in enumerate(stats(0) + [own]):
        by_col = jnp.where(slot == k, value, by_col)
    col_ref[...] = by_col


def combine(got):
    max_on, sum_on, max_mom, sum_mom, cross = (got[:, k : k + 1] for k in range(5))
    top_on = jnp.max(max_on, axis=0)
    lse_on = top_on + jnp.log(jnp.sum(sum_on * jnp.exp(max_on - top_on), axis=0))
    top_mom = jnp.max(max_mom, axis=0)
    rescale = jnp.exp(max_mom - top_mom)
    total = jnp.sum(sum_mom * rescale, axis=0)
    return lse_on, top_mom + jnp.log(total), lse_on - mix_weight * jnp.sum(cross * rescale, axis=0) / total


def row_kernel(got_ref, col_ref, lse_ref, send_ref):
    lse_on, lse_mom, loss = combine(got_ref[...])
    slot = lax.broadcasted_iota(jnp.int32, (128, 2 * side), 0)
    lse_ref[...] = jnp.where(slot == 0, lse_on, lse_mom).T
    slot = lax.broadcasted_iota(jnp.int32, (8, 2 * side), 0)
    send = jnp.where(slot == 6, jnp.sum(loss), col_ref[...])
    for peer in range(n_column):
        send_ref[peer] = send


def grad_kernel(pos_ref, on_ref, mom_ref, lse_ref, got_ref, mine_ref, other_ref, text_ref, out_ref, keep_ref, send_ref):
    width = text_ref.shape[-1]
    got = got_ref[...]
    col_on, col_mom, loss = combine(got)
    loss = loss - 2.0 * (1.0 - mix_weight) * jnp.sum(got[:, 5:6], axis=0)
    _, valid_row = lanes(1)
    row_total = jnp.sum(jnp.sum(got[:, 6:7], axis=0)[:, :1])
    share_of_loss = jnp.sum(jnp.where(valid_row, loss, 0.0)) + row_total / n_plane

    _, valid = lanes(2 * side)
    on, mom = on_ref[...], mom_ref[...]
    row_on, row_mom = lse_ref[:, 0:1], lse_ref[:, 1:2]
    delta = jnp.where(diagonal_of(pos_ref), 1.0 - mix_weight, 0.0)
    target_row = mix_weight * jnp.exp(mom - row_mom) + delta
    target_col = mix_weight * jnp.exp(mom - col_mom) + delta
    grad = 0.5 * ((jnp.exp(on - row_on) - target_row) + (jnp.exp(on - col_on) - target_col))
    grad = jnp.where(valid, grad, 0.0)
    first = pos_ref[2] == 0
    low, high = grad[:side], grad[side:]
    mine, other = jnp.where(first, low, high), jnp.where(first, high, low)
    texts = text_ref[...].reshape(2 * side, width)

    def down(part, ref):
        part = part.reshape(16, 1, rows, 2 * side)
        part = jnp.concatenate([part, jnp.zeros_like(part)], axis=1).reshape(2 * side, 2 * side)
        return lax.dot_general(
            part.astype(bf16), ref[...].reshape(2 * side, width), (((0,), (0,)), ((), ())), preferred_element_type=f32
        )

    by_text = down(mine, mine_ref) + down(other, other_ref)
    out_ref[...] = by_text.reshape(16, 2, rows, width)[:, 0]
    for part, ref in ((mine, keep_ref), (other, send_ref)):
        ref[:, :width] = jnp.dot(part.astype(bf16), texts, preferred_element_type=f32)
        ref[:, width:] = jnp.full((side, 128), share_of_loss, f32)


def local(image, text, mimage, mtext):
    width = image.shape[1]
    pos = jnp.stack([lax.axis_index(a) for a in ("x", "y", "c", "zh", "zl")] + [0] * 3).astype(jnp.int32)

    def swap(block):
        return lax.ppermute(block, "c", [(0, 1), (1, 0)])

    sent, pair = call(
        pack_kernel, [shape(n_column, 16, width, dtype=bf16), shape(16, width, dtype=bf16)], text, mtext, image, mimage
    )
    texts = lax.all_to_all(sent, column, 0, 0, tiled=True)
    mine = lax.all_gather(lax.all_gather(pair, "x"), "y").reshape(16, 16, width)
    other = swap(mine)

    on, mom, row_parts, col_parts = call(
        score_kernel,
        [shape(256, 256), shape(256, 256), shape(n_plane, 8, 256), shape(8, 256)],
        pos, mine, other, texts,
        flops=2**28, exps=2**18,
    )
    row_got = lax.all_to_all(row_parts, ("x", "y", "c"), 0, 0, tiled=True)
    row_lse, col_sent = call(row_kernel, [shape(256, 128), shape(n_column, 8, 256)], row_got, col_parts, exps=2**14)
    col_got = lax.all_to_all(col_sent, column, 0, 0, tiled=True)

    by_text, keep, send = call(
        grad_kernel,
        [shape(n_column, rows, width), shape(side, width + 128), shape(side, width + 128)],
        pos, on, mom, row_lse, col_got, mine, other, texts,
        flops=2**29, exps=2**18,
    )
    got_text = lax.all_to_all(by_text, column, 0, 0, tiled=True)
    by_image = (keep + swap(send)).reshape(16, rows, width + 128)
    by_image, got_text = lax.optimization_barrier((by_image, got_text))
    grad_text = jnp.sum(got_text, axis=0)
    got_image = lax.all_to_all(by_image, ("y", "x"), 0, 0, tiled=True)
    grad_image = jnp.sum(got_image[:, :, :width], axis=0)
    loss = jnp.sum(got_image[:, 0, width]) / (2.0 * rows * n_plane * n_column)
    return grad_image, grad_text, loss


def solution(mesh):
    fine = Mesh(mesh.devices.reshape(8, 4, 2, 4, 2), ("zl", "y", "zh", "x", "c"))
    by_image = P(("zh", "x", "c", "zl", "y"), None)
    by_text = P(("zl", "y", "zh", "x", "c"), None)
    return jax.shard_map(
        local,
        mesh=fine,
        in_specs=(by_image, by_text, by_image, by_text),
        out_specs=(by_image, by_text, P()),
        check_vma=False,
    )
```

time: 193 us -> 145 us (0.75)
  waiting for transfers between devices: 123 us -> 37.2 us
  blocking collectives: 0 us -> 66.1 us
  starting transfers between devices: 49.5 us -> 27.7 us
  Pallas kernels: 0 us -> 4.95 us
  matrix products: 3.19 us -> 0 us
  other arithmetic: 5.94 us -> 2.78 us
  local copies, waits for them, and re-layouts: 5.37 us -> 2.95 us
  between operations: 4.46 us -> 2.49 us
    all_to_all x8 -> x3, waiting for transfers between devices: 123 us -> 33.5 us  [the longest x1 23.7 us: local(): got_text = lax.all_to_all(by_text, column, 0, 0, tiled=True)]
    all_to_all x0 -> x2, blocking collectives: none -> 40.1 us  [the longest x1 25.6 us: local(): col_got = lax.all_to_all(col_sent, column, 0, 0, tiled=True)]
    all_gather x0 -> x2, blocking collectives: none -> 26 us  [local(): mine = lax.all_gather(lax.all_gather(pair, 'x'), 'y').reshape(16, 16, width)]
    all_to_all x8 -> x3, starting transfers between devices: 49.5 us -> 23.9 us  [the longest x1 15.2 us: local(): texts = lax.all_to_all(sent, column, 0, 0, tiled=True)]
    pallas_call x0 -> x4, Pallas kernels: none -> 4.95 us  [call(): pl.pallas_call(body, out_shape=outs, in_specs=specs, out_specs=[whole] *...]
    ppermute x0 -> x2, starting transfers between devices: none -> 3.82 us  [swap(): return lax.ppermute(block, 'c', [(0, 1), (1, 0)])]
    ppermute x0 -> x2, waiting for transfers between devices: none -> 3.74 us  [swap(): return lax.ppermute(block, 'c', [(0, 1), (1, 0)])]
    broadcast_in_dim x4 -> x0, local copies, waits for them, and re-layouts: 3.31 us -> none  [share(): sent = jnp.broadcast_to(block[None], (count,) + block.shape)]
  transfers between devices with their start and end apart: 8 -> 5, of which waited for: 8 -> 4; matrix products, arithmetic and copies ran while one was open for 4% -> 1% of each run, Pallas kernels for 0% -> 0%
where the time goes in v3:
time: 145 us; the launch traced here: 144 us
  blocking collectives  66.1 us (46%)
  waiting for transfers between devices  37.2 us (26%)
  starting transfers between devices  27.7 us (19%)
  Pallas kernels  4.95 us (3%)
  local copies, waits for them, and re-layouts  2.95 us (2%)
  other arithmetic  2.78 us (2%)
  between operations  2.49 us (2%)
    all_gather x2, blocking collectives, local(): mine = lax.all_gather(lax.all_gather(pair, 'x'), 'y').reshape(16, 16, width)  26 us
    all_to_all x1, blocking collectives, local(): col_got = lax.all_to_all(col_sent, column, 0, 0, tiled=True)  25.6 us
    all_to_all x1, waiting for transfers between devices, local(): got_text = lax.all_to_all(by_text, column, 0, 0, tiled=True)  23.7 us
    all_to_all x1, starting transfers between devices, local(): texts = lax.all_to_all(sent, column, 0, 0, tiled=True)  15.2 us
    all_to_all x1, blocking collectives, local(): row_got = lax.all_to_all(row_parts, ('x', 'y', 'c'), 0, 0, tiled=True)  14.5 us
    all_to_all x1, waiting for transfers between devices, local(): got_image = lax.all_to_all(by_image, ('y', 'x'), 0, 0, tiled=True)  9.8 us
    all_to_all x1, starting transfers between devices, local(): got_text = lax.all_to_all(by_text, column, 0, 0, tiled=True)  5.12 us
    pallas_call x4, Pallas kernels, call(): pl.pallas_call(body, out_shape=outs, in_specs=specs, out_specs=[whole] *...  4.95 us
  transfers between devices with their start and end apart: 5, of which 4 were waited for; matrix products, arithmetic and copies ran while one was open for 1% of the time, Pallas kernels for 0%

profile of v3, /device:TPU:32, one launch (start us, length us, event | category | flops | bytes accessed | tf_op | source)
XLA Modules:
  0.0 144.2 jit_solution(5333806821703115561)
XLA Ops:
  0.6 0.7 copy-done
  1.4 0.7 copy-done.1
  2.1 0.7 copy-done.2
  2.8 0.7 copy-done.3
  3.5 0.8 shard_map.67
  4.3 15.2 %all-to-all-start = ((bf16[16,16,1024]{2,1,0:T(8,128)(2,1)}), bf16[16,16,1024]{2,1,0:T(8,128)(2,1)S(1)}, u32[]{:S(2)}, u32[]{:S(2)}) async-start(bf16[16,16,1024]{2,1,0:T(8,128)(2,1)} %get-tuple-element.17), calls=%async_computation | async-start | bytes 1048576 | tf_op jit(solution)/shard_map/all_to_all | solution.py:172
  19.6 12.3 %all-gather = bf16[64,1024]{1,0:T(8,128)(2,1)S(1)} all-gather(bf16[16,1024]{1,0:T(8,128)(2,1)S(1)} %get-tuple-element.16), channel_id=2, replica_groups=mesh['zl'=8,'y'=4,'zh'=2,'x'=4,'c'=2] {'x'}, dimensions={0}, use_global_device_ids=true | all-gather | bytes 163840 | tf_op jit(solution)/shard_map/all_gather | solution.py:173
  31.9 13.6 %all-gather.1.mine_ref = bf16[16,16,1024]{2,1,0:T(8,128)(2,1)S(1)} all-gather(bf16[4,16,1024]{2,1,0:T(8,128)(2,1)S(1)} %bitcast.8), channel_id=3, replica_groups=mesh['zl'=8,'y'=4,'zh'=2,'x'=4,'c'=2] {'y'}, dimensions={0}, use_global_device_ids=true | all-gather | bytes 655360 | tf_op jit(solution)/shard_map/all_gather | solution.py:173
  45.5 1.9 %collective-permute-start = (bf16[16,16,1024]{2,1,0:T(8,128)(2,1)S(1)}, bf16[16,16,1024]{2,1,0:T(8,128)(2,1)S(1)}, u32[]{:S(2)}, u32[]{:S(2)}) collective-permute-start(bf16[16,16,1024]{2,1,0:T(8,128)(2,1)S(1)} %all-gather.1.mine_ref), channel_id=1, source_target_pairs={{0,1},{1,0},{2,3},{3,2},{4,5},{5,4},{6,7},{7,6},{8,9},{9,8},{10,11... | collective-permute-start | bytes 1572872 | tf_op jit(solution)/shard_map/ppermute | solution.py:167
  47.6 1.8 %collective-permute-done.other_ref = bf16[16,16,1024]{2,1,0:T(8,128)(2,1)S(1)} collective-permute-done((bf16[16,16,1024]{2,1,0:T(8,128)(2,1)S(1)}, bf16[16,16,1024]{2,1,0:T(8,128)(2,1)S(1)}, u32[]{:S(2)}, u32[]{:S(2)}) %collective-permute-start) | collective-permute-done | bytes 524320 | tf_op jit(solution)/shard_map/ppermute | solution.py:167
  49.3 1.6 %shard_map.68 = (f32[256,256]{1,0:T(8,128)S(1)}, f32[256,256]{1,0:T(8,128)S(1)}, f32[32,8,256]{2,1,0:T(8,128)S(1)}, f32[8,256]{1,0:T(8,128)S(1)}) custom-call(s32[8]{0:T(128)S(1)} %stack.23.pos_ref, bf16[16,16,1024]{2,1,0:T(8,128)(2,1)S(1)} %all-gather.1.mine_ref, bf16[16,16,1024]{2,1,0:T(8,128)(2,1)S(1)} %collective-permute-done.other_ref, ...), custom_call_target="tpu_custom_call" | custom-call | flops 268435456 | bytes 2367520 | tf_op jit(solution)/shard_map/pallas_call | solution.py:20
  51.0 14.5 %all_to_all.25.got_ref = f32[32,8,256]{2,1,0:T(8,128)S(1)} all-to-all(f32[32,8,256]{2,1,0:T(8,128)S(1)} %get-tuple-element.20), channel_id=1, replica_groups=mesh['zl'=8,'y'=4,'zh'=2,'x'=4,'c'=2] {'x','y','c'}, dimensions={0} | all-to-all | bytes 524288 | tf_op jit(solution)/shard_map/all_to_all | solution.py:182
  65.8 25.6 %all_to_all.26.got_ref = f32[16,8,256]{2,1,0:T(8,128)S(1)} all-to-all(f32[16,8,256]{2,1,0:T(8,128)S(1)} %get-tuple-element.23), channel_id=1, replica_groups=mesh['zl'=8,'y'=4,'zh'=2,'x'=4,'c'=2] {'zh','zl'}, dimensions={0} | all-to-all | bytes 262144 | tf_op jit(solution)/shard_map/all_to_all | solution.py:184
  91.5 2.1 %shard_map.70 = (f32[16,8,1024]{2,1,0:T(8,128)}, f32[128,1152]{1,0:T(8,128)S(1)}, f32[128,1152]{1,0:T(8,128)S(1)}) custom-call(s32[8]{0:T(128)S(1)} %stack.23.pos_ref, f32[256,256]{1,0:T(8,128)S(1)} %get-tuple-element.18.on_ref, f32[256,256]{1,0:T(8,128)S(1)} %get-tuple-element.19.mom_ref, f32[256,128]{1,0:T(8,128)S(1)} %get-tuple-element.22.lse_ref, ...), custom_call_target="tpu_custom_call" | custom-call | flops 536870912 | bytes 4063264 | tf_op jit(solution)/shard_map/pallas_call | solution.py:20
  93.6 5.1 %all-to-all-start.3 = ((f32[16,8,1024]{2,1,0:T(8,128)}), f32[16,8,1024]{2,1,0:T(8,128)S(1)}, u32[]{:S(2)}, u32[]{:S(2)}) async-start(f32[16,8,1024]{2,1,0:T(8,128)} %get-tuple-element.26), calls=%async_computation.3 | async-start | bytes 1048576 | tf_op jit(solution)/shard_map/all_to_all | solution.py:192
  98.7 1.9 %collective-permute-start.1 = (f32[128,1152]{1,0:T(8,128)S(1)}, f32[128,1152]{1,0:T(8,128)S(1)}, u32[]{:S(2)}, u32[]{:S(2)}) collective-permute-start(f32[128,1152]{1,0:T(8,128)S(1)} %get-tuple-element.25), channel_id=1, source_target_pairs={{0,1},{1,0},{2,3},{3,2},{4,5},{5,4},{6,7},{7,6},{8,9},{9,8},{10,11... | collective-permute-start | bytes 1769480 | tf_op jit(solution)/shard_map/ppermute | solution.py:167
  100.6 2.0 %collective-permute-done.1 = f32[128,1152]{1,0:T(8,128)S(1)} collective-permute-done((f32[128,1152]{1,0:T(8,128)S(1)}, f32[128,1152]{1,0:T(8,128)S(1)}, u32[]{:S(2)}, u32[]{:S(2)}) %collective-permute-start.1) | collective-permute-done | bytes 589856 | tf_op jit(solution)/shard_map/ppermute | solution.py:167
  102.6 0.9 add_bitcast_fusion
  103.5 23.7 %all-to-all-done.3 = f32[16,8,1024]{2,1,0:T(8,128)S(1)} async-done(((f32[16,8,1024]{2,1,0:T(8,128)}), f32[16,8,1024]{2,1,0:T(8,128)S(1)}, u32[]{:S(2)}, u32[]{:S(2)}) %all-to-all-start.3) | async-done | bytes 524320 | tf_op jit(solution)/shard_map/all_to_all | solution.py:192
  127.1 3.6 %all-to-all-start.4 = ((f32[16,8,1152]{2,1,0:T(8,128)}), f32[16,8,1152]{2,1,0:T(8,128)S(1)}, u32[]{:S(2)}, u32[]{:S(2)}) async-start(f32[16,8,1152]{2,1,0:T(8,128)} %add_bitcast_fusion), calls=%async_computation.4 | async-start | bytes 1179648 | tf_op jit(solution)/shard_map/all_to_all | solution.py:196
  130.7 0.6 reduce_sum.28
  131.4 9.8 %all-to-all-done.4 = f32[16,8,1152]{2,1,0:T(8,128)S(1)} async-done(((f32[16,8,1152]{2,1,0:T(8,128)}), f32[16,8,1152]{2,1,0:T(8,128)S(1)}, u32[]{:S(2)}, u32[]{:S(2)}) %all-to-all-start.4) | async-done | bytes 589856 | tf_op jit(solution)/shard_map/all_to_all | solution.py:196
  141.2 0.6 slice_reduce_fusion.1
  142.5 0.6 slice_reduce_fusion
  (8 shorter events, 0.4 us)
Async XLA Ops:
  0.6 0.7 copy-start
  1.3 0.7 copy-start.1
  2.1 0.7 copy-start.2
  2.8 0.7 copy-start.3
  4.3 45.0 %all-to-all-start = ((bf16[16,16,1024]{2,1,0:T(8,128)(2,1)}), bf16[16,16,1024]{2,1,0:T(8,128)(2,1)S(1)}, u32[]{:S(2)}, u32[]{:S(2)}) async-start(bf16[16,16,1024]{2,1,0:T(8,128)(2,1)} %get-tuple-element.17), calls=%async_computation | async-start | bytes 1048576 | tf_op jit(solution)/shard_map/all_to_all | solution.py:172
  45.5 3.8 %collective-permute-start = (bf16[16,16,1024]{2,1,0:T(8,128)(2,1)S(1)}, bf16[16,16,1024]{2,1,0:T(8,128)(2,1)S(1)}, u32[]{:S(2)}, u32[]{:S(2)}) collective-permute-start(bf16[16,16,1024]{2,1,0:T(8,128)(2,1)S(1)} %all-gather.1.mine_ref), channel_id=1, source_target_pairs={{0,1},{1,0},{2,3},{3,2},{4,5},{5,4},{6,7},{7,6},{8,9},{9,8},{10,11... | collective-permute-start | bytes 1572872 | tf_op jit(solution)/shard_map/ppermute | solution.py:167
  93.6 33.5 %all-to-all-start.3 = ((f32[16,8,1024]{2,1,0:T(8,128)}), f32[16,8,1024]{2,1,0:T(8,128)S(1)}, u32[]{:S(2)}, u32[]{:S(2)}) async-start(f32[16,8,1024]{2,1,0:T(8,128)} %get-tuple-element.26), calls=%async_computation.3 | async-start | bytes 1048576 | tf_op jit(solution)/shard_map/all_to_all | solution.py:192
  98.7 3.9 %collective-permute-start.1 = (f32[128,1152]{1,0:T(8,128)S(1)}, f32[128,1152]{1,0:T(8,128)S(1)}, u32[]{:S(2)}, u32[]{:S(2)}) collective-permute-start(f32[128,1152]{1,0:T(8,128)S(1)} %get-tuple-element.25), channel_id=1, source_target_pairs={{0,1},{1,0},{2,3},{3,2},{4,5},{5,4},{6,7},{7,6},{8,9},{9,8},{10,11... | collective-permute-start | bytes 1769480 | tf_op jit(solution)/shard_map/ppermute | solution.py:167
  127.1 14.0 %all-to-all-start.4 = ((f32[16,8,1152]{2,1,0:T(8,128)}), f32[16,8,1152]{2,1,0:T(8,128)S(1)}, u32[]{:S(2)}, u32[]{:S(2)}) async-start(f32[16,8,1152]{2,1,0:T(8,128)} %add_bitcast_fusion), calls=%async_computation.4 | async-start | bytes 1179648 | tf_op jit(solution)/shard_map/all_to_all | solution.py:196

commit v4 on v3

--- a/solution.py
+++ b/solution.py
@@ -13,17 +13,18 @@
 side = 16 * rows
 
 
-def call(body, outs, *args, flops=0, exps=0):
+def call(body, outs, *args, flops=0, exps=0, **more):
     whole = pl.BlockSpec(memory_space=pltpu.VMEM)
     specs = [pl.BlockSpec(memory_space=pltpu.SMEM) if a.dtype == jnp.int32 else whole for a in args]
     moved = sum(a.size * a.dtype.itemsize for a in list(args) + outs)
+    params = dict(in_specs=specs, out_specs=[whole] * len(outs))
+    params.update(more)
     return pl.pallas_call(
         body,
         out_shape=outs,
-        in_specs=specs,
-        out_specs=[whole] * len(outs),
         cost_estimate=pl.CostEstimate(flops=flops, bytes_accessed=moved, transcendentals=exps),
         compiler_params=pltpu.CompilerParams(vmem_limit_bytes=40 * 2**20),
+        **params,
     )(*args)
 
 
@@ -31,14 +32,23 @@
     return jax.ShapeDtypeStruct(dims, dtype)
 
 
-def pack_kernel(text_ref, mtext_ref, image_ref, mimage_ref, send_ref, pair_ref):
-    def pair(a_ref, b_ref):
-        return jnp.concatenate([a_ref[...].astype(f32), b_ref[...].astype(f32)], axis=0).astype(bf16)
-
-    both = pair(text_ref, mtext_ref)
+def pack_kernel(text_ref, mtext_ref, image_ref, mimage_ref, send_ref, pair_ref, held, sems):
+    loads = [
+        pltpu.make_async_copy(ref, held.at[k], sems.at[k])
+        for k, ref in enumerate((text_ref, mtext_ref, image_ref, mimage_ref))
+    ]
+    for load in loads:
+        load.start()
+    for load in loads:
+        load.wait()
+
+    def pair(k):
+        return jnp.concatenate([held[k].astype(f32), held[k + 1].astype(f32)], axis=0).astype(bf16)
+
+    both = pair(0)
     for peer in range(n_column):
         send_ref[peer] = both
-    pair_ref[...] = pair(image_ref, mimage_ref)
+    pair_ref[...] = pair(2)
 
 
 def lanes(height):
@@ -86,13 +96,16 @@
         max_mom = jnp.max(mom, axis=along, keepdims=True)
         weight = jnp.exp(mom - max_mom)
         sum_mom = jnp.sum(weight, axis=along, keepdims=True)
-        return [max_on, sum_on, max_mom, sum_mom, jnp.sum(weight * on, axis=along, keepdims=True)]
+        mean = jnp.sum(weight * on, axis=along, keepdims=True) / sum_mom
+        return [max_on + jnp.log(sum_on), max_mom + jnp.log(sum_mom), mean]
 
     slot = lax.broadcasted_iota(jnp.int32, (2 * side, 128), 1)
     by_row = jnp.zeros((2 * side, 128), f32)
     for k, value in enumerate(stats(1)):
         by_row = jnp.where(slot == k, value, by_row)
     by_row = by_row.T[:8]
+    slot = lax.broadcasted_iota(jnp.int32, (8, side), 0)
+    by_row = jnp.where(slot < 4, by_row[:, :side], pltpu.roll(by_row[:, side:], 4, 0))
     for peer in range(n_plane):
         row_ref[peer] = by_row
     own = jnp.sum(jnp.where(diagonal_of(pos_ref), on, 0.0), axis=0, keepdims=True)
@@ -100,41 +113,53 @@
     by_col = jnp.zeros((8, 2 * side), f32)
     for k, value in enumerate(stats(0) + [own]):
         by_col = jnp.where(slot == k, value, by_col)
-    col_ref[...] = by_col
+    lane = lax.broadcasted_iota(jnp.int32, (8, side), 1)
+    col_ref[...] = jnp.where((lane & rows) == 0, by_col[:, :side], pltpu.roll(by_col[:, side:], rows, 1))
 
 
 def combine(got):
-    max_on, sum_on, max_mom, sum_mom, cross = (got[:, k : k + 1] for k in range(5))
-    top_on = jnp.max(max_on, axis=0)
-    lse_on = top_on + jnp.log(jnp.sum(sum_on * jnp.exp(max_on - top_on), axis=0))
-    top_mom = jnp.max(max_mom, axis=0)
-    rescale = jnp.exp(max_mom - top_mom)
-    total = jnp.sum(sum_mom * rescale, axis=0)
-    return lse_on, top_mom + jnp.log(total), lse_on - mix_weight * jnp.sum(cross * rescale, axis=0) / total
+    top = jnp.max(got, axis=0)
+    spread = jnp.exp(got - top[None])
+    total = jnp.sum(spread, axis=0)
+    lse = top + jnp.log(total)
+    weight = pltpu.roll(spread, 1, 1)
+    mean = jnp.sum(weight * got, axis=0) / pltpu.roll(total, 1, 0)
+    return lse, mean
 
 
 def row_kernel(got_ref, col_ref, lse_ref, send_ref):
-    lse_on, lse_mom, loss = combine(got_ref[...])
-    slot = lax.broadcasted_iota(jnp.int32, (128, 2 * side), 0)
-    lse_ref[...] = jnp.where(slot == 0, lse_on, lse_mom).T
-    slot = lax.broadcasted_iota(jnp.int32, (8, 2 * side), 0)
-    send = jnp.where(slot == 6, jnp.sum(loss), col_ref[...])
+    lse, mean = combine(got_ref[...])
+    slot = lax.broadcasted_iota(jnp.int32, (8, side), 0)
+    loss = jnp.sum(jnp.where((slot & 3) == 0, lse, jnp.where((slot & 3) == 2, -mix_weight * mean, 0.0)))
+    lse_ref[...] = jnp.concatenate([lse] + [jnp.zeros((8, side), f32)] * 15, axis=0).T
+    send = jnp.where(slot == 4, loss, col_ref[...])
     for peer in range(n_column):
         send_ref[peer] = send
 
 
-def grad_kernel(pos_ref, on_ref, mom_ref, lse_ref, got_ref, mine_ref, other_ref, text_ref, out_ref, keep_ref, send_ref):
+def grad_kernel(
+    pos_ref, on_ref, mom_ref, lse_ref, got_ref, mine_ref, other_ref, text_ref, out_ref, keep_ref, send_ref
+):
     width = text_ref.shape[-1]
     got = got_ref[...]
-    col_on, col_mom, loss = combine(got)
-    loss = loss - 2.0 * (1.0 - mix_weight) * jnp.sum(got[:, 5:6], axis=0)
-    _, valid_row = lanes(1)
-    row_total = jnp.sum(jnp.sum(got[:, 6:7], axis=0)[:, :1])
-    share_of_loss = jnp.sum(jnp.where(valid_row, loss, 0.0)) + row_total / n_plane
+    lse, mean = combine(got)
+    sums = jnp.sum(got, axis=0)
+    slot = lax.broadcasted_iota(jnp.int32, (8, side), 0)
+    loss = jnp.where(slot == 3, -2.0 * (1.0 - mix_weight) * sums, 0.0)
+    loss = jnp.where(slot == 0, lse, jnp.where(slot == 2, -mix_weight * mean, loss))
+    loss = jnp.where(slot == 4, sums * (1.0 / (n_plane * side)), loss)
+    share_of_loss = jnp.sum(loss)
 
     _, valid = lanes(2 * side)
     on, mom = on_ref[...], mom_ref[...]
-    row_on, row_mom = lse_ref[:, 0:1], lse_ref[:, 1:2]
+
+    def spread(row):
+        return jnp.concatenate([row, pltpu.roll(row, side - rows, 1)], axis=1)
+
+    both = spread(lse)
+    col_on, col_mom = both[0:1], both[1:2]
+    row_on = jnp.concatenate([lse_ref[:, 0:1], lse_ref[:, 4:5]], axis=0)
+    row_mom = jnp.concatenate([lse_ref[:, 1:2], lse_ref[:, 5:6]], axis=0)
     delta = jnp.where(diagonal_of(pos_ref), 1.0 - mix_weight, 0.0)
     target_row = mix_weight * jnp.exp(mom - row_mom) + delta
     target_col = mix_weight * jnp.exp(mom - col_mom) + delta
@@ -159,15 +184,40 @@
         ref[:, width:] = jnp.full((side, 128), share_of_loss, f32)
 
 
+def core_kernel(pos_ref, keep_ref, got_ref, own_ref, *send_refs):
+    for k, ref in enumerate((own_ref,) + send_refs):
+        at = pl.ds(pl.multiple_of(((pos_ref[1] + k) & 3) * 32, 32), 32)
+        ref[...] = keep_ref[at, :] + got_ref[at, :]
+
+
+def y_kernel(pos_ref, keep_ref, a_ref, b_ref, c_ref, own_ref, *send_refs):
+    for k, ref in enumerate((own_ref,) + send_refs):
+        at = pl.ds(pl.multiple_of(((pos_ref[0] + k) & 3) * rows, rows), rows)
+        ref[...] = (keep_ref[at, :] + a_ref[at, :]) + (b_ref[at, :] + c_ref[at, :])
+
+
+def x_kernel(keep_ref, a_ref, b_ref, c_ref, grad_ref, loss_ref):
+    total = (keep_ref[...] + a_ref[...]) + (b_ref[...] + c_ref[...])
+    width = grad_ref.shape[1]
+    grad_ref[...] = total[:, :width]
+    loss_ref[...] = total[:, width:] * (1.0 / (2.0 * rows * n_plane * n_column))
+
+
 def local(image, text, mimage, mtext):
     width = image.shape[1]
+    wide = width + 128
     pos = jnp.stack([lax.axis_index(a) for a in ("x", "y", "c", "zh", "zl")] + [0] * 3).astype(jnp.int32)
 
     def swap(block):
         return lax.ppermute(block, "c", [(0, 1), (1, 0)])
 
+    def ahead(blocks, axis):
+        return [lax.ppermute(block, axis, [(i, (i + k) % 4) for i in range(4)]) for k, block in enumerate(blocks, 1)]
+
     sent, pair = call(
-        pack_kernel, [shape(n_column, 16, width, dtype=bf16), shape(16, width, dtype=bf16)], text, mtext, image, mimage
+        pack_kernel, [shape(n_column, 16, width, dtype=bf16), shape(16, width, dtype=bf16)], text, mtext, image, mimage,
+        in_specs=[pl.BlockSpec(memory_space=pltpu.HBM)] * 4,
+        scratch_shapes=[pltpu.VMEM((4, rows, width), bf16), pltpu.SemaphoreType.DMA((4,))],
     )
     texts = lax.all_to_all(sent, column, 0, 0, tiled=True)
     mine = lax.all_gather(lax.all_gather(pair, "x"), "y").reshape(16, 16, width)
@@ -175,28 +225,26 @@
 
     on, mom, row_parts, col_parts = call(
         score_kernel,
-        [shape(256, 256), shape(256, 256), shape(n_plane, 8, 256), shape(8, 256)],
+        [shape(256, 256), shape(256, 256), shape(n_plane, 8, side), shape(8, side)],
         pos, mine, other, texts,
         flops=2**28, exps=2**18,
     )
     row_got = lax.all_to_all(row_parts, ("x", "y", "c"), 0, 0, tiled=True)
-    row_lse, col_sent = call(row_kernel, [shape(256, 128), shape(n_column, 8, 256)], row_got, col_parts, exps=2**14)
+    row_lse, col_sent = call(row_kernel, [shape(side, side), shape(n_column, 8, side)], row_got, col_parts, exps=2**14)
     col_got = lax.all_to_all(col_sent, column, 0, 0, tiled=True)
 
     by_text, keep, send = call(
         grad_kernel,
-        [shape(n_column, rows, width), shape(side, width + 128), shape(side, width + 128)],
+        [shape(n_column, rows, width), shape(side, wide), shape(side, wide)],
         pos, on, mom, row_lse, col_got, mine, other, texts,
         flops=2**29, exps=2**18,
     )
     got_text = lax.all_to_all(by_text, column, 0, 0, tiled=True)
-    by_image = (keep + swap(send)).reshape(16, rows, width + 128)
-    by_image, got_text = lax.optimization_barrier((by_image, got_text))
+    keep, *send = call(core_kernel, [shape(32, wide)] * 4, pos, keep, swap(send))
+    keep, *send = call(y_kernel, [shape(rows, wide)] * 4, pos, keep, *ahead(send, "y"))
+    grad_image, loss = call(x_kernel, [shape(rows, width), shape(rows, 128)], keep, *ahead(send, "x"))
     grad_text = jnp.sum(got_text, axis=0)
-    got_image = lax.all_to_all(by_image, ("y", "x"), 0, 0, tiled=True)
-    grad_image = jnp.sum(got_image[:, :, :width], axis=0)
-    loss = jnp.sum(got_image[:, 0, width]) / (2.0 * rows * n_plane * n_column)
-    return grad_image, grad_text, loss
+    return grad_image, grad_text, loss[0, 0]
 
 
 def solution(mesh):

time: 145 us -> 130 us (0.90)
  the two profiles are of different devices: /device:TPU:32 before, /device:TPU:2 now
where the time goes in v4:
time: 130 us; the launch traced here: 129 us
  blocking collectives  63.3 us (49%)
  starting transfers between devices  41.7 us (32%)
  waiting for transfers between devices  12.4 us (10%)
  Pallas kernels  6.68 us (5%)
  local copies, waits for them, and re-layouts  3.46 us (3%)
    all_gather x2, blocking collectives, local(): mine = lax.all_gather(lax.all_gather(pair, 'x'), 'y').reshape(16, 16, width)  25.7 us
    all_to_all x1, blocking collectives, local(): col_got = lax.all_to_all(col_sent, column, 0, 0, tiled=True)  23.9 us
    ppermute x6, starting transfers between devices, ahead(): lax.ppermute(block, axis, [(i, (i + k) % 4) for i in range(4)])  19.1 us
    all_to_all x1, starting transfers between devices, local(): texts = lax.all_to_all(sent, column, 0, 0, tiled=True)  15.2 us
    all_to_all x1, blocking collectives, local(): row_got = lax.all_to_all(row_parts, ('x', 'y', 'c'), 0, 0, tiled=True)  13.7 us
    ppermute x6, waiting for transfers between devices, ahead(): lax.ppermute(block, axis, [(i, (i + k) % 4) for i in range(4)])  8.69 us
    pallas_call x7, Pallas kernels, call(): pl.pallas_call(body, out_shape=outs, cost_estimate=pl.CostEstimate(flops=...  6.68 us
    ppermute x2, starting transfers between devices, swap(): return lax.ppermute(block, 'c', [(0, 1), (1, 0)])  3.83 us
  transfers between devices with their start and end apart: 10, of which 6 were waited for; matrix products, arithmetic and copies ran while one was open for 0% of the time, Pallas kernels for 1%

profile of v4, /device:TPU:2, one launch (start us, length us, event | category | flops | bytes accessed | tf_op | source)
XLA Modules:
  0.0 129.0 jit_solution(6966579172311027527)
XLA Ops:
  1.4 0.7 copy-done.1
  2.1 0.7 copy-done.2
  3.5 0.9 shard_map.67
  4.5 15.2 %all-to-all-start = ((bf16[16,16,1024]{2,1,0:T(8,128)(2,1)}), bf16[16,16,1024]{2,1,0:T(8,128)(2,1)S(1)}, u32[]{:S(2)}, u32[]{:S(2)}) async-start(bf16[16,16,1024]{2,1,0:T(8,128)(2,1)} %get-tuple-element.25), calls=%async_computation | async-start | bytes 1048576 | tf_op jit(solution)/shard_map/all_to_all | solution.py:222
  19.7 12.1 %all-gather = bf16[64,1024]{1,0:T(8,128)(2,1)S(1)} all-gather(bf16[16,1024]{1,0:T(8,128)(2,1)S(1)} %get-tuple-element.24), channel_id=2, replica_groups=mesh['zl'=8,'y'=4,'zh'=2,'x'=4,'c'=2] {'x'}, dimensions={0}, use_global_device_ids=true | all-gather | bytes 163840 | tf_op jit(solution)/shard_map/all_gather | solution.py:223
  31.8 13.6 %all-gather.1.mine_ref = bf16[16,16,1024]{2,1,0:T(8,128)(2,1)S(1)} all-gather(bf16[4,16,1024]{2,1,0:T(8,128)(2,1)S(1)} %bitcast.7), channel_id=3, replica_groups=mesh['zl'=8,'y'=4,'zh'=2,'x'=4,'c'=2] {'y'}, dimensions={0}, use_global_device_ids=true | all-gather | bytes 655360 | tf_op jit(solution)/shard_map/all_gather | solution.py:223
  45.3 1.9 %collective-permute-start = (bf16[16,16,1024]{2,1,0:T(8,128)(2,1)S(1)}, bf16[16,16,1024]{2,1,0:T(8,128)(2,1)S(1)}, u32[]{:S(2)}, u32[]{:S(2)}) collective-permute-start(bf16[16,16,1024]{2,1,0:T(8,128)(2,1)S(1)} %all-gather.1.mine_ref), channel_id=1, source_target_pairs={{0,1},{1,0},{2,3},{3,2},{4,5},{5,4},{6,7},{7,6},{8,9},{9,8},{10,11... | collective-permute-start | bytes 1572872 | tf_op jit(solution)/shard_map/ppermute | solution.py:212
  47.4 1.8 %collective-permute-done.other_ref = bf16[16,16,1024]{2,1,0:T(8,128)(2,1)S(1)} collective-permute-done((bf16[16,16,1024]{2,1,0:T(8,128)(2,1)S(1)}, bf16[16,16,1024]{2,1,0:T(8,128)(2,1)S(1)}, u32[]{:S(2)}, u32[]{:S(2)}) %collective-permute-start) | collective-permute-done | bytes 524320 | tf_op jit(solution)/shard_map/ppermute | solution.py:212
  49.1 1.6 %shard_map.68 = (f32[256,256]{1,0:T(8,128)S(1)}, f32[256,256]{1,0:T(8,128)S(1)}, f32[32,8,128]{2,1,0:T(8,128)S(1)}, f32[8,128]{1,0:T(8,128)S(1)}) custom-call(s32[8]{0:T(128)S(1)} %stack.23.pos_ref, bf16[16,16,1024]{2,1,0:T(8,128)(2,1)S(1)} %all-gather.1.mine_ref, bf16[16,16,1024]{2,1,0:T(8,128)(2,1)S(1)} %collective-permute-done.other_ref, ...), custom_call_target="tpu_custom_call" | custom-call | flops 268435456 | bytes 2232352 | tf_op jit(solution)/shard_map/pallas_call | solution.py:22
  50.8 13.7 %all_to_all.20.got_ref = f32[32,8,128]{2,1,0:T(8,128)S(1)} all-to-all(f32[32,8,128]{2,1,0:T(8,128)S(1)} %get-tuple-element.28), channel_id=1, replica_groups=mesh['zl'=8,'y'=4,'zh'=2,'x'=4,'c'=2] {'x','y','c'}, dimensions={0} | all-to-all | bytes 262144 | tf_op jit(solution)/shard_map/all_to_all | solution.py:232
  64.7 23.9 %all_to_all.21.got_ref = f32[16,8,128]{2,1,0:T(8,128)S(1)} all-to-all(f32[16,8,128]{2,1,0:T(8,128)S(1)} %get-tuple-element.31), channel_id=1, replica_groups=mesh['zl'=8,'y'=4,'zh'=2,'x'=4,'c'=2] {'zh','zl'}, dimensions={0} | all-to-all | bytes 131072 | tf_op jit(solution)/shard_map/all_to_all | solution.py:234
  88.6 2.1 %shard_map.70 = (f32[16,8,1024]{2,1,0:T(8,128)}, f32[128,1152]{1,0:T(8,128)S(1)}, f32[128,1152]{1,0:T(8,128)S(1)}) custom-call(s32[8]{0:T(128)S(1)} %stack.23.pos_ref, f32[256,256]{1,0:T(8,128)S(1)} %get-tuple-element.26.on_ref, f32[256,256]{1,0:T(8,128)S(1)} %get-tuple-element.27.mom_ref, f32[128,128]{1,0:T(8,128)S(1)} %get-tuple-element.30.lse_ref, ...), custom_call_target="tpu_custom_call" | custom-call | flops 536870912 | bytes 3932192 | tf_op jit(solution)/shard_map/pallas_call | solution.py:22
  90.7 3.6 %all-to-all-start.3 = ((f32[16,8,1024]{2,1,0:T(8,128)}), f32[16,8,1024]{2,1,0:T(8,128)S(1)}, u32[]{:S(2)}, u32[]{:S(2)}) async-start(f32[16,8,1024]{2,1,0:T(8,128)} %get-tuple-element.43), calls=%async_computation.3 | async-start | bytes 1048576 | tf_op jit(solution)/shard_map/all_to_all | solution.py:242
  94.2 1.9 %collective-permute-start.1 = (f32[128,1152]{1,0:T(8,128)S(1)}, f32[128,1152]{1,0:T(8,128)S(1)}, u32[]{:S(2)}, u32[]{:S(2)}) collective-permute-start(f32[128,1152]{1,0:T(8,128)S(1)} %get-tuple-element.33), channel_id=1, source_target_pairs={{0,1},{1,0},{2,3},{3,2},{4,5},{5,4},{6,7},{7,6},{8,9},{9,8},{10,11... | collective-permute-start | bytes 1769480 | tf_op jit(solution)/shard_map/ppermute | solution.py:212
  96.2 2.0 %collective-permute-done.1.got_ref = f32[128,1152]{1,0:T(8,128)S(1)} collective-permute-done((f32[128,1152]{1,0:T(8,128)S(1)}, f32[128,1152]{1,0:T(8,128)S(1)}, u32[]{:S(2)}, u32[]{:S(2)}) %collective-permute-start.1) | collective-permute-done | bytes 589856 | tf_op jit(solution)/shard_map/ppermute | solution.py:212
  98.8 2.5 %collective-permute-start.2 = (f32[32,1152]{1,0:T(8,128)S(1)}, f32[32,1152]{1,0:T(8,128)S(1)}, u32[]{:S(2)}, u32[]{:S(2)}) collective-permute-start(f32[32,1152]{1,0:T(8,128)S(1)} %get-tuple-element.35), channel_id=1, source_target_pairs={{0,16},{16,32},{32,48},{48,0},{1,17},{17,33},{33,49},{49,1},{2,18}... | collective-permute-start | bytes 442376 | tf_op jit(solution)/shard_map/ppermute | solution.py:215
  101.3 4.0 %collective-permute-start.3 = (f32[32,1152]{1,0:T(8,128)S(1)}, f32[32,1152]{1,0:T(8,128)S(1)}, u32[]{:S(2)}, u32[]{:S(2)}) collective-permute-start(f32[32,1152]{1,0:T(8,128)S(1)} %get-tuple-element.36), channel_id=1, source_target_pairs={{0,32},{16,48},{32,0},{48,16},{1,33},{17,49},{33,1},{49,17},{2,34}... | collective-permute-start | bytes 442376 | tf_op jit(solution)/shard_map/ppermute | solution.py:215
  105.3 2.8 %collective-permute-start.4 = (f32[32,1152]{1,0:T(8,128)S(1)}, f32[32,1152]{1,0:T(8,128)S(1)}, u32[]{:S(2)}, u32[]{:S(2)}) collective-permute-start(f32[32,1152]{1,0:T(8,128)S(1)} %get-tuple-element.37), channel_id=1, source_target_pairs={{0,48},{16,0},{32,16},{48,32},{1,49},{17,1},{33,17},{49,33},{2,50}... | collective-permute-start | bytes 442376 | tf_op jit(solution)/shard_map/ppermute | solution.py:215
  108.1 2.8 %collective-permute-done.2.a_ref = f32[32,1152]{1,0:T(8,128)S(1)} collective-permute-done((f32[32,1152]{1,0:T(8,128)S(1)}, f32[32,1152]{1,0:T(8,128)S(1)}, u32[]{:S(2)}, u32[]{:S(2)}) %collective-permute-start.2) | collective-permute-done | bytes 147488 | tf_op jit(solution)/shard_map/ppermute | solution.py:215
  110.9 2.5 %collective-permute-done.4.c_ref = f32[32,1152]{1,0:T(8,128)S(1)} collective-permute-done((f32[32,1152]{1,0:T(8,128)S(1)}, f32[32,1152]{1,0:T(8,128)S(1)}, u32[]{:S(2)}, u32[]{:S(2)}) %collective-permute-start.4) | collective-permute-done | bytes 147488 | tf_op jit(solution)/shard_map/ppermute | solution.py:215
  114.0 2.6 %collective-permute-start.5 = (f32[8,1152]{1,0:T(8,128)S(1)}, f32[8,1152]{1,0:T(8,128)S(1)}, u32[]{:S(2)}, u32[]{:S(2)}) collective-permute-start(f32[8,1152]{1,0:T(8,128)S(1)} %get-tuple-element.39), channel_id=1, source_target_pairs={{0,2},{2,4},{4,6},{6,0},{1,3},{3,5},{5,7},{7,1},{8,10},{10,12},{12... | collective-permute-start | bytes 110600 | tf_op jit(solution)/shard_map/ppermute | solution.py:215
  116.6 4.8 %collective-permute-start.6 = (f32[8,1152]{1,0:T(8,128)S(1)}, f32[8,1152]{1,0:T(8,128)S(1)}, u32[]{:S(2)}, u32[]{:S(2)}) collective-permute-start(f32[8,1152]{1,0:T(8,128)S(1)} %get-tuple-element.40), channel_id=1, source_target_pairs={{0,4},{2,6},{4,0},{6,2},{1,5},{3,7},{5,1},{7,3},{8,12},{10,14},{12... | collective-permute-start | bytes 110600 | tf_op jit(solution)/shard_map/ppermute | solution.py:215
  121.3 2.4 %collective-permute-start.7 = (f32[8,1152]{1,0:T(8,128)S(1)}, f32[8,1152]{1,0:T(8,128)S(1)}, u32[]{:S(2)}, u32[]{:S(2)}) collective-permute-start(f32[8,1152]{1,0:T(8,128)S(1)} %get-tuple-element.41), channel_id=1, source_target_pairs={{0,6},{2,0},{4,2},{6,4},{1,7},{3,1},{5,3},{7,5},{8,14},{10,8},{12,... | collective-permute-start | bytes 110600 | tf_op jit(solution)/shard_map/ppermute | solution.py:215
  123.9 3.3 %collective-permute-done.7.c_ref = f32[8,1152]{1,0:T(8,128)S(1)} collective-permute-done((f32[8,1152]{1,0:T(8,128)S(1)}, f32[8,1152]{1,0:T(8,128)S(1)}, u32[]{:S(2)}, u32[]{:S(2)}) %collective-permute-start.7) | collective-permute-done | bytes 36896 | tf_op jit(solution)/shard_map/ppermute | solution.py:215
  (19 shorter events, 4.9 us)
Async XLA Ops:
  0.6 0.7 copy-start
  1.3 0.7 copy-start.1
  2.1 0.7 copy-start.2
  2.8 0.7 copy-start.3
  4.5 44.7 %all-to-all-start = ((bf16[16,16,1024]{2,1,0:T(8,128)(2,1)}), bf16[16,16,1024]{2,1,0:T(8,128)(2,1)S(1)}, u32[]{:S(2)}, u32[]{:S(2)}) async-start(bf16[16,16,1024]{2,1,0:T(8,128)(2,1)} %get-tuple-element.25), calls=%async_computation | async-start | bytes 1048576 | tf_op jit(solution)/shard_map/all_to_all | solution.py:222
  45.3 3.8 %collective-permute-start = (bf16[16,16,1024]{2,1,0:T(8,128)(2,1)S(1)}, bf16[16,16,1024]{2,1,0:T(8,128)(2,1)S(1)}, u32[]{:S(2)}, u32[]{:S(2)}) collective-permute-start(bf16[16,16,1024]{2,1,0:T(8,128)(2,1)S(1)} %all-gather.1.mine_ref), channel_id=1, source_target_pairs={{0,1},{1,0},{2,3},{3,2},{4,5},{5,4},{6,7},{7,6},{8,9},{9,8},{10,11... | collective-permute-start | bytes 1572872 | tf_op jit(solution)/shard_map/ppermute | solution.py:212
  90.7 37.7 %all-to-all-start.3 = ((f32[16,8,1024]{2,1,0:T(8,128)}), f32[16,8,1024]{2,1,0:T(8,128)S(1)}, u32[]{:S(2)}, u32[]{:S(2)}) async-start(f32[16,8,1024]{2,1,0:T(8,128)} %get-tuple-element.43), calls=%async_computation.3 | async-start | bytes 1048576 | tf_op jit(solution)/shard_map/all_to_all | solution.py:242
  94.2 3.9 %collective-permute-start.1 = (f32[128,1152]{1,0:T(8,128)S(1)}, f32[128,1152]{1,0:T(8,128)S(1)}, u32[]{:S(2)}, u32[]{:S(2)}) collective-permute-start(f32[128,1152]{1,0:T(8,128)S(1)} %get-tuple-element.33), channel_id=1, source_target_pairs={{0,1},{1,0},{2,3},{3,2},{4,5},{5,4},{6,7},{7,6},{8,9},{9,8},{10,11... | collective-permute-start | bytes 1769480 | tf_op jit(solution)/shard_map/ppermute | solution.py:212
  98.8 12.2 %collective-permute-start.2 = (f32[32,1152]{1,0:T(8,128)S(1)}, f32[32,1152]{1,0:T(8,128)S(1)}, u32[]{:S(2)}, u32[]{:S(2)}) collective-permute-start(f32[32,1152]{1,0:T(8,128)S(1)} %get-tuple-element.35), channel_id=1, source_target_pairs={{0,16},{16,32},{32,48},{48,0},{1,17},{17,33},{33,49},{49,1},{2,18}... | collective-permute-start | bytes 442376 | tf_op jit(solution)/shard_map/ppermute | solution.py:215
  101.3 9.7 %collective-permute-start.3 = (f32[32,1152]{1,0:T(8,128)S(1)}, f32[32,1152]{1,0:T(8,128)S(1)}, u32[]{:S(2)}, u32[]{:S(2)}) collective-permute-start(f32[32,1152]{1,0:T(8,128)S(1)} %get-tuple-element.36), channel_id=1, source_target_pairs={{0,32},{16,48},{32,0},{48,16},{1,33},{17,49},{33,1},{49,17},{2,34}... | collective-permute-start | bytes 442376 | tf_op jit(solution)/shard_map/ppermute | solution.py:215
  105.3 8.1 %collective-permute-start.4 = (f32[32,1152]{1,0:T(8,128)S(1)}, f32[32,1152]{1,0:T(8,128)S(1)}, u32[]{:S(2)}, u32[]{:S(2)}) collective-permute-start(f32[32,1152]{1,0:T(8,128)S(1)} %get-tuple-element.37), channel_id=1, source_target_pairs={{0,48},{16,0},{32,16},{48,32},{1,49},{17,1},{33,17},{49,33},{2,50}... | collective-permute-start | bytes 442376 | tf_op jit(solution)/shard_map/ppermute | solution.py:215
  114.0 9.8 %collective-permute-start.5 = (f32[8,1152]{1,0:T(8,128)S(1)}, f32[8,1152]{1,0:T(8,128)S(1)}, u32[]{:S(2)}, u32[]{:S(2)}) collective-permute-start(f32[8,1152]{1,0:T(8,128)S(1)} %get-tuple-element.39), channel_id=1, source_target_pairs={{0,2},{2,4},{4,6},{6,0},{1,3},{3,5},{5,7},{7,1},{8,10},{10,12},{12... | collective-permute-start | bytes 110600 | tf_op jit(solution)/shard_map/ppermute | solution.py:215
  116.6 7.4 %collective-permute-start.6 = (f32[8,1152]{1,0:T(8,128)S(1)}, f32[8,1152]{1,0:T(8,128)S(1)}, u32[]{:S(2)}, u32[]{:S(2)}) collective-permute-start(f32[8,1152]{1,0:T(8,128)S(1)} %get-tuple-element.40), channel_id=1, source_target_pairs={{0,4},{2,6},{4,0},{6,2},{1,5},{3,7},{5,1},{7,3},{8,12},{10,14},{12... | collective-permute-start | bytes 110600 | tf_op jit(solution)/shard_map/ppermute | solution.py:215
  121.3 5.9 %collective-permute-start.7 = (f32[8,1152]{1,0:T(8,128)S(1)}, f32[8,1152]{1,0:T(8,128)S(1)}, u32[]{:S(2)}, u32[]{:S(2)}) collective-permute-start(f32[8,1152]{1,0:T(8,128)S(1)} %get-tuple-element.41), channel_id=1, source_target_pairs={{0,6},{2,0},{4,2},{6,4},{1,7},{3,1},{5,3},{7,5},{8,14},{10,8},{12,... | collective-permute-start | bytes 110600 | tf_op jit(solution)/shard_map/ppermute | solution.py:215

commit v5 on v4

--- a/solution.py
+++ b/solution.py
@@ -30,25 +30,6 @@
 
 def shape(*dims, dtype=f32):
     return jax.ShapeDtypeStruct(dims, dtype)
-
-
-def pack_kernel(text_ref, mtext_ref, image_ref, mimage_ref, send_ref, pair_ref, held, sems):
-    loads = [
-        pltpu.make_async_copy(ref, held.at[k], sems.at[k])
-        for k, ref in enumerate((text_ref, mtext_ref, image_ref, mimage_ref))
-    ]
-    for load in loads:
-        load.start()
-    for load in loads:
-        load.wait()
-
-    def pair(k):
-        return jnp.concatenate([held[k].astype(f32), held[k + 1].astype(f32)], axis=0).astype(bf16)
-
-    both = pair(0)
-    for peer in range(n_column):
-        send_ref[peer] = both
-    pair_ref[...] = pair(2)
 
 
 def lanes(height):
@@ -178,29 +159,31 @@
         )
 
     by_text = down(mine, mine_ref) + down(other, other_ref)
-    out_ref[...] = by_text.reshape(16, 2, rows, width)[:, 0]
+    out_ref[...] = by_text.reshape(16, 2, rows, width)[:, 0].astype(bf16)
     for part, ref in ((mine, keep_ref), (other, send_ref)):
         ref[:, :width] = jnp.dot(part.astype(bf16), texts, preferred_element_type=f32)
         ref[:, width:] = jnp.full((side, 128), share_of_loss, f32)
 
 
-def core_kernel(pos_ref, keep_ref, got_ref, own_ref, *send_refs):
-    for k, ref in enumerate((own_ref,) + send_refs):
-        at = pl.ds(pl.multiple_of(((pos_ref[1] + k) & 3) * 32, 32), 32)
-        ref[...] = keep_ref[at, :] + got_ref[at, :]
-
-
-def y_kernel(pos_ref, keep_ref, a_ref, b_ref, c_ref, own_ref, *send_refs):
-    for k, ref in enumerate((own_ref,) + send_refs):
-        at = pl.ds(pl.multiple_of(((pos_ref[0] + k) & 3) * rows, rows), rows)
-        ref[...] = (keep_ref[at, :] + a_ref[at, :]) + (b_ref[at, :] + c_ref[at, :])
-
-
-def x_kernel(keep_ref, a_ref, b_ref, c_ref, grad_ref, loss_ref):
-    total = (keep_ref[...] + a_ref[...]) + (b_ref[...] + c_ref[...])
+def core_kernel(keep_ref, got_ref, out_ref):
+    total = keep_ref[...] + got_ref[...]
+    width = total.shape[1] - 128
+    loss = total[:, width:]
+    lane = lax.broadcasted_iota(jnp.int32, loss.shape, 1)
+    pieces = jnp.zeros_like(loss)
+    for k in range(3):
+        piece = loss.astype(bf16).astype(f32)
+        pieces = jnp.where(lane == k, piece, pieces)
+        loss = loss - piece
+    out_ref[:, :, :width] = total[:, :width].reshape(16, rows, width).astype(bf16)
+    out_ref[:, :, width:] = pieces.reshape(16, rows, 128).astype(bf16)
+
+
+def last_kernel(got_ref, grad_ref, loss_ref):
+    total = jnp.sum(got_ref[...].astype(f32), axis=0)
     width = grad_ref.shape[1]
     grad_ref[...] = total[:, :width]
-    loss_ref[...] = total[:, width:] * (1.0 / (2.0 * rows * n_plane * n_column))
+    loss_ref[0, 0] = jnp.sum(total[:1, width:]) * (1.0 / (2.0 * rows * n_plane * n_column))
 
 
 def local(image, text, mimage, mtext):
@@ -211,14 +194,9 @@
     def swap(block):
         return lax.ppermute(block, "c", [(0, 1), (1, 0)])
 
-    def ahead(blocks, axis):
-        return [lax.ppermute(block, axis, [(i, (i + k) % 4) for i in range(4)]) for k, block in enumerate(blocks, 1)]
-
-    sent, pair = call(
-        pack_kernel, [shape(n_column, 16, width, dtype=bf16), shape(16, width, dtype=bf16)], text, mtext, image, mimage,
-        in_specs=[pl.BlockSpec(memory_space=pltpu.HBM)] * 4,
-        scratch_shapes=[pltpu.VMEM((4, rows, width), bf16), pltpu.SemaphoreType.DMA((4,))],
-    )
+    both = jnp.concatenate([text, mtext], axis=0)
+    sent = jnp.broadcast_to(both[None], (n_column,) + both.shape)
+    pair = jnp.concatenate([image, mimage], axis=0)
     texts = lax.all_to_all(sent, column, 0, 0, tiled=True)
     mine = lax.all_gather(lax.all_gather(pair, "x"), "y").reshape(16, 16, width)
     other = swap(mine)
@@ -235,15 +213,19 @@
 
     by_text, keep, send = call(
         grad_kernel,
-        [shape(n_column, rows, width), shape(side, wide), shape(side, wide)],
+        [shape(n_column, rows, width, dtype=bf16), shape(side, wide), shape(side, wide)],
         pos, on, mom, row_lse, col_got, mine, other, texts,
         flops=2**29, exps=2**18,
     )
     got_text = lax.all_to_all(by_text, column, 0, 0, tiled=True)
-    keep, *send = call(core_kernel, [shape(32, wide)] * 4, pos, keep, swap(send))
-    keep, *send = call(y_kernel, [shape(rows, wide)] * 4, pos, keep, *ahead(send, "y"))
-    grad_image, loss = call(x_kernel, [shape(rows, width), shape(rows, 128)], keep, *ahead(send, "x"))
-    grad_text = jnp.sum(got_text, axis=0)
+    (by_image,) = call(core_kernel, [shape(16, rows, wide, dtype=bf16)], keep, swap(send))
+    by_image, got_text = lax.optimization_barrier((by_image, got_text))
+    got_image = lax.all_to_all(by_image, ("y", "x"), 0, 0, tiled=True)
+    grad_text = jnp.sum(got_text.astype(f32), axis=0)
+    grad_image, loss = call(
+        last_kernel, [shape(rows, width), shape(1, 1)], got_image,
+        out_specs=[pl.BlockSpec(memory_space=pltpu.VMEM), pl.BlockSpec(memory_space=pltpu.SMEM)],
+    )
     return grad_image, grad_text, loss[0, 0]
 
 

time: 130 us -> 124 us (0.954)
  the two profiles are of different devices: /device:TPU:2 before, /device:TPU:64 now
where the time goes in v5:
time: 124 us
  blocking collectives  62.6 us (50%)
  starting transfers between devices  27.2 us (22%)
  waiting for transfers between devices  25.5 us (21%)
  Pallas kernels  5.3 us (4%)
  other arithmetic  1.4 us (1%)
    all_gather x2, blocking collectives, local(): mine = lax.all_gather(lax.all_gather(pair, 'x'), 'y').reshape(16, 16, width)  26 us
    all_to_all x1, blocking collectives, local(): col_got = lax.all_to_all(col_sent, column, 0, 0, tiled=True)  23.3 us
    all_to_all x1, starting transfers between devices, local(): texts = lax.all_to_all(sent, column, 0, 0, tiled=True)  14.9 us
    all_to_all x1, waiting for transfers between devices, local(): got_text = lax.all_to_all(by_text, column, 0, 0, tiled=True)  13.6 us
    all_to_all x1, blocking collectives, local(): row_got = lax.all_to_all(row_parts, ('x', 'y', 'c'), 0, 0, tiled=True)  13.3 us
    all_to_all x1, waiting for transfers between devices, local(): got_image = lax.all_to_all(by_image, ('y', 'x'), 0, 0, tiled=True)  8.17 us
    pallas_call x5, Pallas kernels, call(): pl.pallas_call(body, out_shape=outs, cost_estimate=pl.CostEstimate(flops=...  5.3 us
    all_to_all x1, starting transfers between devices, local(): got_text = lax.all_to_all(by_text, column, 0, 0, tiled=True)  4.96 us
  transfers between devices with their start and end apart: 5, of which 4 were waited for; matrix products, arithmetic and copies ran while one was open for 1% of the time, Pallas kernels for 1%

profile of v5, /device:TPU:64, one launch (start us, length us, event | category | flops | bytes accessed | tf_op | source)
XLA Modules:
  0.0 123.7 jit_solution(16003734540004253921)
XLA Ops:
  0.6 0.7 pad_maximum_fusion.1
  1.4 0.8 broadcast_in_dim.2
  2.2 14.9 %all-to-all-start = ((bf16[16,16,1024]{2,1,0:T(8,128)(2,1)}), bf16[16,16,1024]{2,1,0:T(8,128)(2,1)S(1)}, u32[]{:S(2)}, u32[]{:S(2)}) async-start(bf16[16,16,1024]{2,1,0:T(8,128)(2,1)} %broadcast_in_dim.2), calls=%async_computation | async-start | bytes 1048576 | tf_op jit(solution)/shard_map/all_to_all | solution.py:200
  17.1 0.0 copy-done
  17.1 12.3 %all-gather = bf16[64,1024]{1,0:T(8,128)(2,1)S(1)} all-gather(bf16[16,1024]{1,0:T(8,128)(2,1)S(1)} %pad_maximum_fusion), channel_id=2, replica_groups=mesh['zl'=8,'y'=4,'zh'=2,'x'=4,'c'=2] {'x'}, dimensions={0}, use_global_device_ids=true | all-gather | bytes 163840 | tf_op jit(solution)/shard_map/all_gather | solution.py:201
  29.5 13.6 %all-gather.1.mine_ref = bf16[16,16,1024]{2,1,0:T(8,128)(2,1)S(1)} all-gather(bf16[4,16,1024]{2,1,0:T(8,128)(2,1)S(1)} %bitcast.7), channel_id=3, replica_groups=mesh['zl'=8,'y'=4,'zh'=2,'x'=4,'c'=2] {'y'}, dimensions={0}, use_global_device_ids=true | all-gather | bytes 655360 | tf_op jit(solution)/shard_map/all_gather | solution.py:201
  43.1 1.9 %collective-permute-start = (bf16[16,16,1024]{2,1,0:T(8,128)(2,1)S(1)}, bf16[16,16,1024]{2,1,0:T(8,128)(2,1)S(1)}, u32[]{:S(2)}, u32[]{:S(2)}) collective-permute-start(bf16[16,16,1024]{2,1,0:T(8,128)(2,1)S(1)} %all-gather.1.mine_ref), channel_id=1, source_target_pairs={{0,1},{1,0},{2,3},{3,2},{4,5},{5,4},{6,7},{7,6},{8,9},{9,8},{10,11... | collective-permute-start | bytes 1572872 | tf_op jit(solution)/shard_map/ppermute | solution.py:195
  45.1 0.1 stack.23.pos_ref
  45.2 1.8 %collective-permute-done.other_ref = bf16[16,16,1024]{2,1,0:T(8,128)(2,1)S(1)} collective-permute-done((bf16[16,16,1024]{2,1,0:T(8,128)(2,1)S(1)}, bf16[16,16,1024]{2,1,0:T(8,128)(2,1)S(1)}, u32[]{:S(2)}, u32[]{:S(2)}) %collective-permute-start) | collective-permute-done | bytes 524320 | tf_op jit(solution)/shard_map/ppermute | solution.py:195
  46.9 0.0 all-to-all-done.text_ref
  46.9 1.6 %shard_map.67 = (f32[256,256]{1,0:T(8,128)S(1)}, f32[256,256]{1,0:T(8,128)S(1)}, f32[32,8,128]{2,1,0:T(8,128)S(1)}, f32[8,128]{1,0:T(8,128)S(1)}) custom-call(s32[8]{0:T(128)S(1)} %stack.23.pos_ref, bf16[16,16,1024]{2,1,0:T(8,128)(2,1)S(1)} %all-gather.1.mine_ref, bf16[16,16,1024]{2,1,0:T(8,128)(2,1)S(1)} %collective-permute-done.other_ref, ...), custom_call_target="tpu_custom_call" | custom-call | flops 268435456 | bytes 2232352 | tf_op jit(solution)/shard_map/pallas_call | solution.py:22
  48.6 13.3 %all_to_all.25.got_ref = f32[32,8,128]{2,1,0:T(8,128)S(1)} all-to-all(f32[32,8,128]{2,1,0:T(8,128)S(1)} %get-tuple-element.18), channel_id=1, replica_groups=mesh['zl'=8,'y'=4,'zh'=2,'x'=4,'c'=2] {'x','y','c'}, dimensions={0} | all-to-all | bytes 262144 | tf_op jit(solution)/shard_map/all_to_all | solution.py:210
  61.9 0.2 shard_map.68
  62.1 23.3 %all_to_all.26.got_ref = f32[16,8,128]{2,1,0:T(8,128)S(1)} all-to-all(f32[16,8,128]{2,1,0:T(8,128)S(1)} %get-tuple-element.21), channel_id=1, replica_groups=mesh['zl'=8,'y'=4,'zh'=2,'x'=4,'c'=2] {'zh','zl'}, dimensions={0} | all-to-all | bytes 131072 | tf_op jit(solution)/shard_map/all_to_all | solution.py:212
  85.4 2.0 %shard_map.69 = (bf16[16,8,1024]{2,1,0:T(8,128)(2,1)}, f32[128,1152]{1,0:T(8,128)S(1)}, f32[128,1152]{1,0:T(8,128)S(1)}) custom-call(s32[8]{0:T(128)S(1)} %stack.23.pos_ref, f32[256,256]{1,0:T(8,128)S(1)} %get-tuple-element.16.on_ref, f32[256,256]{1,0:T(8,128)S(1)} %get-tuple-element.17.mom_ref, f32[128,128]{1,0:T(8,128)S(1)} %get-tuple-element.20.lse_ref, ...), custom_call_target="tpu_custom_call" | custom-call | flops 536870912 | bytes 3670048 | tf_op jit(solution)/shard_map/pallas_call | solution.py:22
  87.4 5.0 %all-to-all-start.3 = ((bf16[16,8,1024]{2,1,0:T(8,128)(2,1)}), bf16[16,8,1024]{2,1,0:T(8,128)(2,1)S(1)}, u32[]{:S(2)}, u32[]{:S(2)}) async-start(bf16[16,8,1024]{2,1,0:T(8,128)(2,1)} %get-tuple-element.24), calls=%async_computation.3 | async-start | bytes 524288 | tf_op jit(solution)/shard_map/all_to_all | solution.py:220
  92.4 1.9 %collective-permute-start.1 = (f32[128,1152]{1,0:T(8,128)S(1)}, f32[128,1152]{1,0:T(8,128)S(1)}, u32[]{:S(2)}, u32[]{:S(2)}) collective-permute-start(f32[128,1152]{1,0:T(8,128)S(1)} %get-tuple-element.23), channel_id=1, source_target_pairs={{0,1},{1,0},{2,3},{3,2},{4,5},{5,4},{6,7},{7,6},{8,9},{9,8},{10,11... | collective-permute-start | bytes 1769480 | tf_op jit(solution)/shard_map/ppermute | solution.py:195
  94.3 2.0 %collective-permute-done.1.got_ref = f32[128,1152]{1,0:T(8,128)S(1)} collective-permute-done((f32[128,1152]{1,0:T(8,128)S(1)}, f32[128,1152]{1,0:T(8,128)S(1)}, u32[]{:S(2)}, u32[]{:S(2)}) %collective-permute-start.1) | collective-permute-done | bytes 589856 | tf_op jit(solution)/shard_map/ppermute | solution.py:195
  96.3 0.8 shard_map.70
  97.0 13.6 %all-to-all-done.3 = bf16[16,8,1024]{2,1,0:T(8,128)(2,1)S(1)} async-done(((bf16[16,8,1024]{2,1,0:T(8,128)(2,1)}), bf16[16,8,1024]{2,1,0:T(8,128)(2,1)S(1)}, u32[]{:S(2)}, u32[]{:S(2)}) %all-to-all-start.3) | async-done | bytes 262176 | tf_op jit(solution)/shard_map/all_to_all | solution.py:220
  110.6 3.5 %all-to-all-start.4 = ((bf16[16,8,1152]{2,1,0:T(8,128)(2,1)}), bf16[16,8,1152]{2,1,0:T(8,128)(2,1)S(1)}, u32[]{:S(2)}, u32[]{:S(2)}) async-start(bf16[16,8,1152]{2,1,0:T(8,128)(2,1)} %shard_map.70), calls=%async_computation.4 | async-start | bytes 589824 | tf_op jit(solution)/shard_map/all_to_all | solution.py:223
  114.1 0.7 convert_reduce_fusion
  114.8 8.2 %all-to-all-done.4.got_ref = bf16[16,8,1152]{2,1,0:T(8,128)(2,1)S(1)} async-done(((bf16[16,8,1152]{2,1,0:T(8,128)(2,1)}), bf16[16,8,1152]{2,1,0:T(8,128)(2,1)S(1)}, u32[]{:S(2)}, u32[]{:S(2)}) %all-to-all-start.4) | async-done | bytes 294944 | tf_op jit(solution)/shard_map/all_to_all | solution.py:223
  123.0 0.7 shard_map.71
  (5 shorter events, 0.0 us)
Async XLA Ops:
  2.2 14.9 %copy-start = (bf16[8,1024]{1,0:T(8,128)(2,1)S(1)}, bf16[8,1024]{1,0:T(8,128)(2,1)}, u32[]{:S(2)}) copy-start(bf16[8,1024]{1,0:T(8,128)(2,1)} %param.6) | copy-start | bytes 49156
  2.2 14.9 %copy-start.1 = (bf16[8,1024]{1,0:T(8,128)(2,1)S(1)}, bf16[8,1024]{1,0:T(8,128)(2,1)}, u32[]{:S(2)}) copy-start(bf16[8,1024]{1,0:T(8,128)(2,1)} %param.4) | copy-start | bytes 49156
  2.2 44.7 %all-to-all-start = ((bf16[16,16,1024]{2,1,0:T(8,128)(2,1)}), bf16[16,16,1024]{2,1,0:T(8,128)(2,1)S(1)}, u32[]{:S(2)}, u32[]{:S(2)}) async-start(bf16[16,16,1024]{2,1,0:T(8,128)(2,1)} %broadcast_in_dim.2), calls=%async_computation | async-start | bytes 1048576 | tf_op jit(solution)/shard_map/all_to_all | solution.py:200
  43.1 3.8 %collective-permute-start = (bf16[16,16,1024]{2,1,0:T(8,128)(2,1)S(1)}, bf16[16,16,1024]{2,1,0:T(8,128)(2,1)S(1)}, u32[]{:S(2)}, u32[]{:S(2)}) collective-permute-start(bf16[16,16,1024]{2,1,0:T(8,128)(2,1)S(1)} %all-gather.1.mine_ref), channel_id=1, source_target_pairs={{0,1},{1,0},{2,3},{3,2},{4,5},{5,4},{6,7},{7,6},{8,9},{9,8},{10,11... | collective-permute-start | bytes 1572872 | tf_op jit(solution)/shard_map/ppermute | solution.py:195
  87.4 23.2 %all-to-all-start.3 = ((bf16[16,8,1024]{2,1,0:T(8,128)(2,1)}), bf16[16,8,1024]{2,1,0:T(8,128)(2,1)S(1)}, u32[]{:S(2)}, u32[]{:S(2)}) async-start(bf16[16,8,1024]{2,1,0:T(8,128)(2,1)} %get-tuple-element.24), calls=%async_computation.3 | async-start | bytes 524288 | tf_op jit(solution)/shard_map/all_to_all | solution.py:220
  92.4 3.9 %collective-permute-start.1 = (f32[128,1152]{1,0:T(8,128)S(1)}, f32[128,1152]{1,0:T(8,128)S(1)}, u32[]{:S(2)}, u32[]{:S(2)}) collective-permute-start(f32[128,1152]{1,0:T(8,128)S(1)} %get-tuple-element.23), channel_id=1, source_target_pairs={{0,1},{1,0},{2,3},{3,2},{4,5},{5,4},{6,7},{7,6},{8,9},{9,8},{10,11... | collective-permute-start | bytes 1769480 | tf_op jit(solution)/shard_map/ppermute | solution.py:195
  110.6 12.4 %all-to-all-start.4 = ((bf16[16,8,1152]{2,1,0:T(8,128)(2,1)}), bf16[16,8,1152]{2,1,0:T(8,128)(2,1)S(1)}, u32[]{:S(2)}, u32[]{:S(2)}) async-start(bf16[16,8,1152]{2,1,0:T(8,128)(2,1)} %shard_map.70), calls=%async_computation.4 | async-start | bytes 589824 | tf_op jit(solution)/shard_map/all_to_all | solution.py:223

commit v6 on v5

--- a/solution.py
+++ b/solution.py
@@ -151,15 +151,19 @@
     mine, other = jnp.where(first, low, high), jnp.where(first, high, low)
     texts = text_ref[...].reshape(2 * side, width)
 
+    lane = lax.broadcasted_iota(jnp.int32, (side, side), 1)
+
     def down(part, ref):
-        part = part.reshape(16, 1, rows, 2 * side)
-        part = jnp.concatenate([part, jnp.zeros_like(part)], axis=1).reshape(2 * side, 2 * side)
+        part = jnp.where((lane & rows) == 0, part[:, :side], pltpu.roll(part[:, side:], rows, 1))
+        part = part.reshape(16, 1, rows, side)
+        part = jnp.concatenate([part, jnp.zeros_like(part)], axis=1).reshape(2 * side, side)
         return lax.dot_general(
             part.astype(bf16), ref[...].reshape(2 * side, width), (((0,), (0,)), ((), ())), preferred_element_type=f32
         )
 
-    by_text = down(mine, mine_ref) + down(other, other_ref)
-    out_ref[...] = by_text.reshape(16, 2, rows, width)[:, 0].astype(bf16)
+    by_text = (down(mine, mine_ref) + down(other, other_ref)).reshape(8, 2, rows, width)
+    for k in range(2):
+        out_ref[8 * k : 8 * k + 8] = by_text[:, k].astype(bf16)
     for part, ref in ((mine, keep_ref), (other, send_ref)):
         ref[:, :width] = jnp.dot(part.astype(bf16), texts, preferred_element_type=f32)
         ref[:, width:] = jnp.full((side, 128), share_of_loss, f32)
@@ -198,7 +202,7 @@
     sent = jnp.broadcast_to(both[None], (n_column,) + both.shape)
     pair = jnp.concatenate([image, mimage], axis=0)
     texts = lax.all_to_all(sent, column, 0, 0, tiled=True)
-    mine = lax.all_gather(lax.all_gather(pair, "x"), "y").reshape(16, 16, width)
+    mine = lax.all_gather(pair, ("y", "x"))
     other = swap(mine)
 
     on, mom, row_parts, col_parts = call(

time: 124 us -> 122 us (0.984)
  blocking collectives: 62.6 us -> 60.5 us
    all_gather x2 -> x1, blocking collectives: 26 us -> 24.6 us  [local(): mine = lax.all_gather(pair, ('y', 'x'))]
    all_to_all x1, blocking collectives: 23.3 us -> 21.9 us  [local(): col_got = lax.all_to_all(col_sent, column, 0, 0, tiled=True)]
where the time goes in v6:
time: 122 us; the launch traced here: 121 us
  blocking collectives  60.5 us (50%)
  starting transfers between devices  27.2 us (22%)
  waiting for transfers between devices  25.5 us (21%)
  Pallas kernels  5.27 us (4%)
  other arithmetic  1.4 us (1%)
    all_gather x1, blocking collectives, local(): mine = lax.all_gather(pair, ('y', 'x'))  24.6 us
    all_to_all x1, blocking collectives, local(): col_got = lax.all_to_all(col_sent, column, 0, 0, tiled=True)  21.9 us
    all_to_all x1, starting transfers between devices, local(): texts = lax.all_to_all(sent, column, 0, 0, tiled=True)  14.9 us
    all_to_all x1, blocking collectives, local(): row_got = lax.all_to_all(row_parts, ('x', 'y', 'c'), 0, 0, tiled=True)  14 us
    all_to_all x1, waiting for transfers between devices, local(): got_text = lax.all_to_all(by_text, column, 0, 0, tiled=True)  13.6 us
    all_to_all x1, waiting for transfers between devices, local(): got_image = lax.all_to_all(by_image, ('y', 'x'), 0, 0, tiled=True)  8.17 us
    pallas_call x5, Pallas kernels, call(): pl.pallas_call(body, out_shape=outs, cost_estimate=pl.CostEstimate(flops=...  5.27 us
    all_to_all x1, starting transfers between devices, local(): got_text = lax.all_to_all(by_text, column, 0, 0, tiled=True)  4.96 us
  transfers between devices with their start and end apart: 5, of which 4 were waited for; matrix products, arithmetic and copies ran while one was open for 1% of the time, Pallas kernels for 1%

profile of v6, /device:TPU:64, one launch (start us, length us, event | category | flops | bytes accessed | tf_op | source)
XLA Modules:
  0.0 121.5 jit_solution(4439755627184528320)
XLA Ops:
  0.6 0.7 pad_maximum_fusion.1
  1.4 0.8 broadcast_in_dim.2
  2.2 14.9 %all-to-all-start = ((bf16[16,16,1024]{2,1,0:T(8,128)(2,1)}), bf16[16,16,1024]{2,1,0:T(8,128)(2,1)S(1)}, u32[]{:S(2)}, u32[]{:S(2)}) async-start(bf16[16,16,1024]{2,1,0:T(8,128)(2,1)} %broadcast_in_dim.2), calls=%async_computation | async-start | bytes 1048576 | tf_op jit(solution)/shard_map/all_to_all | solution.py:204
  17.1 0.0 copy-done
  17.1 0.0 copy-done.1
  17.1 24.6 %all-gather = bf16[256,1024]{1,0:T(8,128)(2,1)S(1)} all-gather(bf16[16,1024]{1,0:T(8,128)(2,1)S(1)} %pad_maximum_fusion), channel_id=2, replica_groups=mesh['zl'=8,'y'=4,'zh'=2,'x'=4,'c'=2] {'y','x'}, dimensions={0}, use_global_device_ids=true | all-gather | bytes 557056 | tf_op jit(solution)/shard_map/all_gather | solution.py:205
  41.7 1.9 %collective-permute-start = (bf16[16,16,1024]{2,1,0:T(8,128)(2,1)S(1)}, bf16[16,16,1024]{2,1,0:T(8,128)(2,1)S(1)}, u32[]{:S(2)}, u32[]{:S(2)}) collective-permute-start(bf16[16,16,1024]{2,1,0:T(8,128)(2,1)S(1)} %bitcast.7), channel_id=1, source_target_pairs={{0,1},{1,0},{2,3},{3,2},{4,5},{5,4},{6,7},{7,6},{8,9},{9,8},{10,11... | collective-permute-start | bytes 1572872 | tf_op jit(solution)/shard_map/ppermute | solution.py:199
  43.6 0.1 stack.23.pos_ref
  43.7 1.8 %collective-permute-done.other_ref = bf16[16,16,1024]{2,1,0:T(8,128)(2,1)S(1)} collective-permute-done((bf16[16,16,1024]{2,1,0:T(8,128)(2,1)S(1)}, bf16[16,16,1024]{2,1,0:T(8,128)(2,1)S(1)}, u32[]{:S(2)}, u32[]{:S(2)}) %collective-permute-start) | collective-permute-done | bytes 524320 | tf_op jit(solution)/shard_map/ppermute | solution.py:199
  45.5 0.0 all-to-all-done.text_ref
  45.5 1.6 %shard_map.67 = (f32[256,256]{1,0:T(8,128)S(1)}, f32[256,256]{1,0:T(8,128)S(1)}, f32[32,8,128]{2,1,0:T(8,128)S(1)}, f32[8,128]{1,0:T(8,128)S(1)}) custom-call(s32[8]{0:T(128)S(1)} %stack.23.pos_ref, bf16[16,16,1024]{2,1,0:T(8,128)(2,1)S(1)} %bitcast.8, bf16[16,16,1024]{2,1,0:T(8,128)(2,1)S(1)} %collective-permute-done.other_ref, ...), custom_call_target="tpu_custom_call" | custom-call | flops 268435456 | bytes 2232352 | tf_op jit(solution)/shard_map/pallas_call | solution.py:22
  47.1 14.0 %all_to_all.25.got_ref = f32[32,8,128]{2,1,0:T(8,128)S(1)} all-to-all(f32[32,8,128]{2,1,0:T(8,128)S(1)} %get-tuple-element.18), channel_id=1, replica_groups=mesh['zl'=8,'y'=4,'zh'=2,'x'=4,'c'=2] {'x','y','c'}, dimensions={0} | all-to-all | bytes 262144 | tf_op jit(solution)/shard_map/all_to_all | solution.py:214
  61.1 0.2 shard_map.68
  61.3 21.9 %all_to_all.26.got_ref = f32[16,8,128]{2,1,0:T(8,128)S(1)} all-to-all(f32[16,8,128]{2,1,0:T(8,128)S(1)} %get-tuple-element.21), channel_id=1, replica_groups=mesh['zl'=8,'y'=4,'zh'=2,'x'=4,'c'=2] {'zh','zl'}, dimensions={0} | all-to-all | bytes 131072 | tf_op jit(solution)/shard_map/all_to_all | solution.py:216
  83.3 2.0 %shard_map.69 = (bf16[16,8,1024]{2,1,0:T(8,128)(2,1)}, f32[128,1152]{1,0:T(8,128)S(1)}, f32[128,1152]{1,0:T(8,128)S(1)}) custom-call(s32[8]{0:T(128)S(1)} %stack.23.pos_ref, f32[256,256]{1,0:T(8,128)S(1)} %get-tuple-element.16.on_ref, f32[256,256]{1,0:T(8,128)S(1)} %get-tuple-element.17.mom_ref, f32[128,128]{1,0:T(8,128)S(1)} %get-tuple-element.20.lse_ref, ...), custom_call_target="tpu_custom_call" | custom-call | flops 536870912 | bytes 3670048 | tf_op jit(solution)/shard_map/pallas_call | solution.py:22
  85.2 5.0 %all-to-all-start.3 = ((bf16[16,8,1024]{2,1,0:T(8,128)(2,1)}), bf16[16,8,1024]{2,1,0:T(8,128)(2,1)S(1)}, u32[]{:S(2)}, u32[]{:S(2)}) async-start(bf16[16,8,1024]{2,1,0:T(8,128)(2,1)} %get-tuple-element.24), calls=%async_computation.3 | async-start | bytes 524288 | tf_op jit(solution)/shard_map/all_to_all | solution.py:224
  90.2 1.9 %collective-permute-start.1 = (f32[128,1152]{1,0:T(8,128)S(1)}, f32[128,1152]{1,0:T(8,128)S(1)}, u32[]{:S(2)}, u32[]{:S(2)}) collective-permute-start(f32[128,1152]{1,0:T(8,128)S(1)} %get-tuple-element.23), channel_id=1, source_target_pairs={{0,1},{1,0},{2,3},{3,2},{4,5},{5,4},{6,7},{7,6},{8,9},{9,8},{10,11... | collective-permute-start | bytes 1769480 | tf_op jit(solution)/shard_map/ppermute | solution.py:199
  92.1 2.0 %collective-permute-done.1.got_ref = f32[128,1152]{1,0:T(8,128)S(1)} collective-permute-done((f32[128,1152]{1,0:T(8,128)S(1)}, f32[128,1152]{1,0:T(8,128)S(1)}, u32[]{:S(2)}, u32[]{:S(2)}) %collective-permute-start.1) | collective-permute-done | bytes 589856 | tf_op jit(solution)/shard_map/ppermute | solution.py:199
  94.1 0.8 shard_map.70
  94.9 13.6 %all-to-all-done.3 = bf16[16,8,1024]{2,1,0:T(8,128)(2,1)S(1)} async-done(((bf16[16,8,1024]{2,1,0:T(8,128)(2,1)}), bf16[16,8,1024]{2,1,0:T(8,128)(2,1)S(1)}, u32[]{:S(2)}, u32[]{:S(2)}) %all-to-all-start.3) | async-done | bytes 262176 | tf_op jit(solution)/shard_map/all_to_all | solution.py:224
  108.4 3.5 %all-to-all-start.4 = ((bf16[16,8,1152]{2,1,0:T(8,128)(2,1)}), bf16[16,8,1152]{2,1,0:T(8,128)(2,1)S(1)}, u32[]{:S(2)}, u32[]{:S(2)}) async-start(bf16[16,8,1152]{2,1,0:T(8,128)(2,1)} %shard_map.70), calls=%async_computation.4 | async-start | bytes 589824 | tf_op jit(solution)/shard_map/all_to_all | solution.py:227
  112.0 0.7 convert_reduce_fusion
  112.6 8.2 %all-to-all-done.4.got_ref = bf16[16,8,1152]{2,1,0:T(8,128)(2,1)S(1)} async-done(((bf16[16,8,1152]{2,1,0:T(8,128)(2,1)}), bf16[16,8,1152]{2,1,0:T(8,128)(2,1)S(1)}, u32[]{:S(2)}, u32[]{:S(2)}) %all-to-all-start.4) | async-done | bytes 294944 | tf_op jit(solution)/shard_map/all_to_all | solution.py:227
  120.8 0.7 shard_map.71
  (4 shorter events, 0.0 us)
Async XLA Ops:
  2.2 14.9 %copy-start = (bf16[8,1024]{1,0:T(8,128)(2,1)S(1)}, bf16[8,1024]{1,0:T(8,128)(2,1)}, u32[]{:S(2)}) copy-start(bf16[8,1024]{1,0:T(8,128)(2,1)} %param.6) | copy-start | bytes 49156
  2.2 14.9 %copy-start.1 = (bf16[8,1024]{1,0:T(8,128)(2,1)S(1)}, bf16[8,1024]{1,0:T(8,128)(2,1)}, u32[]{:S(2)}) copy-start(bf16[8,1024]{1,0:T(8,128)(2,1)} %param.4) | copy-start | bytes 49156
  2.2 43.3 %all-to-all-start = ((bf16[16,16,1024]{2,1,0:T(8,128)(2,1)}), bf16[16,16,1024]{2,1,0:T(8,128)(2,1)S(1)}, u32[]{:S(2)}, u32[]{:S(2)}) async-start(bf16[16,16,1024]{2,1,0:T(8,128)(2,1)} %broadcast_in_dim.2), calls=%async_computation | async-start | bytes 1048576 | tf_op jit(solution)/shard_map/all_to_all | solution.py:204
  41.7 3.8 %collective-permute-start = (bf16[16,16,1024]{2,1,0:T(8,128)(2,1)S(1)}, bf16[16,16,1024]{2,1,0:T(8,128)(2,1)S(1)}, u32[]{:S(2)}, u32[]{:S(2)}) collective-permute-start(bf16[16,16,1024]{2,1,0:T(8,128)(2,1)S(1)} %bitcast.7), channel_id=1, source_target_pairs={{0,1},{1,0},{2,3},{3,2},{4,5},{5,4},{6,7},{7,6},{8,9},{9,8},{10,11... | collective-permute-start | bytes 1572872 | tf_op jit(solution)/shard_map/ppermute | solution.py:199
  85.2 23.2 %all-to-all-start.3 = ((bf16[16,8,1024]{2,1,0:T(8,128)(2,1)}), bf16[16,8,1024]{2,1,0:T(8,128)(2,1)S(1)}, u32[]{:S(2)}, u32[]{:S(2)}) async-start(bf16[16,8,1024]{2,1,0:T(8,128)(2,1)} %get-tuple-element.24), calls=%async_computation.3 | async-start | bytes 524288 | tf_op jit(solution)/shard_map/all_to_all | solution.py:224
  90.2 3.9 %collective-permute-start.1 = (f32[128,1152]{1,0:T(8,128)S(1)}, f32[128,1152]{1,0:T(8,128)S(1)}, u32[]{:S(2)}, u32[]{:S(2)}) collective-permute-start(f32[128,1152]{1,0:T(8,128)S(1)} %get-tuple-element.23), channel_id=1, source_target_pairs={{0,1},{1,0},{2,3},{3,2},{4,5},{5,4},{6,7},{7,6},{8,9},{9,8},{10,11... | collective-permute-start | bytes 1769480 | tf_op jit(solution)/shard_map/ppermute | solution.py:199
  108.4 12.4 %all-to-all-start.4 = ((bf16[16,8,1152]{2,1,0:T(8,128)(2,1)}), bf16[16,8,1152]{2,1,0:T(8,128)(2,1)S(1)}, u32[]{:S(2)}, u32[]{:S(2)}) async-start(bf16[16,8,1152]{2,1,0:T(8,128)(2,1)} %shard_map.70), calls=%async_computation.4 | async-start | bytes 589824 | tf_op jit(solution)/shard_map/all_to_all | solution.py:227

commit v7 on v6

--- a/solution.py
+++ b/solution.py
@@ -41,11 +41,18 @@
     x, y, c, zh, zl = (pos_ref[k] for k in range(5))
     row = lax.broadcasted_iota(jnp.int32, (2 * side, 2 * side), 0)
     lane, valid = lanes(2 * side)
-    pc, py, px = row >> 7, (row >> 5) & 3, (row >> 3) & 3
+    pc, px = row >> 7, (row >> 4) & 3
+    py = ((row >> 3) & 1) * 2 + ((row >> 6) & 1)
     image_block = (zh * 8 + px * 2 + pc) * 32 + zl * 4 + py
     qh, ql = lane >> 7, (lane >> 4) & 7
     text_block = (ql * 4 + y) * 16 + qh * 8 + x * 2 + c
     return valid & (image_block == text_block) & ((row & 7) == (lane & 7))
+
+
+def order_kernel(pos_ref, own_ref, other_ref, out_ref):
+    place = pos_ref[1] >> 1
+    out_ref[place] = own_ref[...]
+    out_ref[1 - place] = other_ref[...]
 
 
 def score_kernel(pos_ref, mine_ref, other_ref, text_ref, on_ref, mom_ref, row_ref, col_ref):
@@ -193,16 +200,20 @@
 def local(image, text, mimage, mtext):
     width = image.shape[1]
     wide = width + 128
-    pos = jnp.stack([lax.axis_index(a) for a in ("x", "y", "c", "zh", "zl")] + [0] * 3).astype(jnp.int32)
-
-    def swap(block):
-        return lax.ppermute(block, "c", [(0, 1), (1, 0)])
+    x, yh, yl, c, zh, zl = (lax.axis_index(a) for a in ("x", "yh", "yl", "c", "zh", "zl"))
+    pos = jnp.stack([x, yh * 2 + yl, c, zh, zl, 0, 0, 0]).astype(jnp.int32)
+
+    def swap(block, axis="c"):
+        return lax.ppermute(block, axis, [(0, 1), (1, 0)])
 
     both = jnp.concatenate([text, mtext], axis=0)
+    pair = jnp.concatenate([image, mimage], axis=0)
+    both, pair = lax.optimization_barrier((both, pair))
     sent = jnp.broadcast_to(both[None], (n_column,) + both.shape)
-    pair = jnp.concatenate([image, mimage], axis=0)
     texts = lax.all_to_all(sent, column, 0, 0, tiled=True)
-    mine = lax.all_gather(pair, ("y", "x"))
+    across = swap(pair, "yh")
+    (pair,) = call(order_kernel, [shape(2, 16, width, dtype=bf16)], pos, pair, across, flops=2**35)
+    mine = lax.all_gather(pair, ("yl", "x")).reshape(16, 16, width)
     other = swap(mine)
 
     on, mom, row_parts, col_parts = call(
@@ -211,7 +222,7 @@
         pos, mine, other, texts,
         flops=2**28, exps=2**18,
     )
-    row_got = lax.all_to_all(row_parts, ("x", "y", "c"), 0, 0, tiled=True)
+    row_got = lax.all_to_all(row_parts, ("x", "yh", "yl", "c"), 0, 0, tiled=True)
     row_lse, col_sent = call(row_kernel, [shape(side, side), shape(n_column, 8, side)], row_got, col_parts, exps=2**14)
     col_got = lax.all_to_all(col_sent, column, 0, 0, tiled=True)
 
@@ -224,7 +235,7 @@
     got_text = lax.all_to_all(by_text, column, 0, 0, tiled=True)
     (by_image,) = call(core_kernel, [shape(16, rows, wide, dtype=bf16)], keep, swap(send))
     by_image, got_text = lax.optimization_barrier((by_image, got_text))
-    got_image = lax.all_to_all(by_image, ("y", "x"), 0, 0, tiled=True)
+    got_image = lax.all_to_all(by_image, ("yl", "x", "yh"), 0, 0, tiled=True)
     grad_text = jnp.sum(got_text.astype(f32), axis=0)
     grad_image, loss = call(
         last_kernel, [shape(rows, width), shape(1, 1)], got_image,
@@ -234,9 +245,9 @@
 
 
 def solution(mesh):
-    fine = Mesh(mesh.devices.reshape(8, 4, 2, 4, 2), ("zl", "y", "zh", "x", "c"))
-    by_image = P(("zh", "x", "c", "zl", "y"), None)
-    by_text = P(("zl", "y", "zh", "x", "c"), None)
+    fine = Mesh(mesh.devices.reshape(8, 2, 2, 2, 4, 2), ("zl", "yh", "yl", "zh", "x", "c"))
+    by_image = P(("zh", "x", "c", "zl", "yh", "yl"), None)
+    by_text = P(("zl", "yh", "yl", "zh", "x", "c"), None)
     return jax.shard_map(
         local,
         mesh=fine,

time: 122 us -> 132 us (1.082)
  starting transfers between devices: 27.2 us -> 32.2 us
  blocking collectives: 60.5 us -> 65 us
    ppermute x2 -> x3, starting transfers between devices: 3.82 us -> 8.91 us  [swap(): return lax.ppermute(block, axis, [(0, 1), (1, 0)])]
    all_gather x1, blocking collectives: 24.6 us -> 29.1 us  [local(): mine = lax.all_gather(pair, ('yl', 'x')).reshape(16, 16, width)]
    all_to_all x1, blocking collectives: 14 us -> 12.5 us  [local(): lax.all_to_all(row_parts, ('x', 'yh', 'yl', 'c'), 0, 0, tiled=True)]
    all_to_all x1, blocking collectives: 21.9 us -> 23.3 us  [local(): col_got = lax.all_to_all(col_sent, column, 0, 0, tiled=True)]
    pallas_call x5 -> x6, Pallas kernels: 5.27 us -> 5.86 us  [call(): pl.pallas_call(body, out_shape=outs, cost_estimate=pl.CostEstimate(flops=...]
    ppermute x2 -> x3, waiting for transfers between devices: 3.74 us -> 3.85 us  [swap(): return lax.ppermute(block, axis, [(0, 1), (1, 0)])]
  transfers between devices with their start and end apart: 5 -> 6, of which waited for: 4 -> 4; matrix products, arithmetic and copies ran while one was open for 1% -> 1% of each run, Pallas kernels for 1% -> 1%
where the time goes in v7:
time: 132 us
  blocking collectives  65 us (49%)
  starting transfers between devices  32.2 us (24%)
  waiting for transfers between devices  25.6 us (19%)
  Pallas kernels  5.86 us (4%)
  other arithmetic  1.43 us (1%)
    all_gather x1, blocking collectives, local(): mine = lax.all_gather(pair, ('yl', 'x')).reshape(16, 16, width)  29.1 us
    all_to_all x1, blocking collectives, local(): col_got = lax.all_to_all(col_sent, column, 0, 0, tiled=True)  23.3 us
    all_to_all x1, starting transfers between devices, local(): texts = lax.all_to_all(sent, column, 0, 0, tiled=True)  14.8 us
    all_to_all x1, waiting for transfers between devices, local(): got_text = lax.all_to_all(by_text, column, 0, 0, tiled=True)  13.6 us
    all_to_all x1, blocking collectives, local(): lax.all_to_all(row_parts, ('x', 'yh', 'yl', 'c'), 0, 0, tiled=True)  12.5 us
    ppermute x3, starting transfers between devices, swap(): return lax.ppermute(block, axis, [(0, 1), (1, 0)])  8.91 us
    all_to_all x1, waiting for transfers between devices, local(): got_image = lax.all_to_all(by_image, ('yl', 'x', 'yh'), 0, 0, tiled=True)  8.21 us
    pallas_call x6, Pallas kernels, call(): pl.pallas_call(body, out_shape=outs, cost_estimate=pl.CostEstimate(flops=...  5.86 us
  transfers between devices with their start and end apart: 6, of which 4 were waited for; matrix products, arithmetic and copies ran while one was open for 1% of the time, Pallas kernels for 1%

profile of v7, /device:TPU:64, one launch (start us, length us, event | category | flops | bytes accessed | tf_op | source)
XLA Modules:
  0.0 131.7 jit_solution(5841204276039573334)
XLA Ops:
  0.6 0.8 pad_maximum_fusion
  1.4 5.1 %collective-permute-start = (bf16[16,1024]{1,0:T(8,128)(2,1)S(1)}, bf16[16,1024]{1,0:T(8,128)(2,1)S(1)}, u32[]{:S(2)}, u32[]{:S(2)}) collective-permute-start(bf16[16,1024]{1,0:T(8,128)(2,1)S(1)} %get-tuple-element.18.own_ref), channel_id=1, source_target_pairs={{0,32},{32,0},{1,33},{33,1},{2,34},{34,2},{3,35},{35,3},{4,36},{36... | collective-permute-start | bytes 98312 | tf_op jit(solution)/shard_map/ppermute | solution.py:207
  6.5 0.8 broadcast_in_dim.2
  7.4 14.8 %all-to-all-start = ((bf16[16,16,1024]{2,1,0:T(8,128)(2,1)}), bf16[16,16,1024]{2,1,0:T(8,128)(2,1)S(1)}, u32[]{:S(2)}, u32[]{:S(2)}) async-start(bf16[16,16,1024]{2,1,0:T(8,128)(2,1)} %broadcast_in_dim.2), calls=%async_computation | async-start | bytes 1048576 | tf_op jit(solution)/shard_map/all_to_all | solution.py:213
  22.1 0.1 stack.23.pos_ref
  22.2 0.6 shard_map.67
  22.8 29.1 %all-gather.mine_ref = bf16[16,16,1024]{2,1,0:T(8,128)(2,1)S(1)} all-gather(bf16[2,16,1024]{2,1,0:T(8,128)(2,1)S(1)} %shard_map.67), channel_id=2, replica_groups=mesh['zl'=8,'yh'=2,'yl'=2,'zh'=2,'x'=4,'c'=2] {'yl','x'}, dimensions={0}, use_global_device_ids=true | all-gather | bytes 589824 | tf_op jit(solution)/shard_map/all_gather | solution.py:216
  51.9 1.9 %collective-permute-start.1 = (bf16[16,16,1024]{2,1,0:T(8,128)(2,1)S(1)}, bf16[16,16,1024]{2,1,0:T(8,128)(2,1)S(1)}, u32[]{:S(2)}, u32[]{:S(2)}) collective-permute-start(bf16[16,16,1024]{2,1,0:T(8,128)(2,1)S(1)} %all-gather.mine_ref), channel_id=1, source_target_pairs={{0,1},{1,0},{2,3},{3,2},{4,5},{5,4},{6,7},{7,6},{8,9},{9,8},{10,11... | collective-permute-start | bytes 1572872 | tf_op jit(solution)/shard_map/ppermute | solution.py:207
  53.8 1.9 %collective-permute-done.1.other_ref = bf16[16,16,1024]{2,1,0:T(8,128)(2,1)S(1)} collective-permute-done((bf16[16,16,1024]{2,1,0:T(8,128)(2,1)S(1)}, bf16[16,16,1024]{2,1,0:T(8,128)(2,1)S(1)}, u32[]{:S(2)}, u32[]{:S(2)}) %collective-permute-start.1) | collective-permute-done | bytes 524320 | tf_op jit(solution)/shard_map/ppermute | solution.py:207
  55.7 0.0 all-to-all-done.text_ref
  55.7 1.6 %shard_map.68 = (f32[256,256]{1,0:T(8,128)S(1)}, f32[256,256]{1,0:T(8,128)S(1)}, f32[32,8,128]{2,1,0:T(8,128)S(1)}, f32[8,128]{1,0:T(8,128)S(1)}) custom-call(s32[8]{0:T(128)S(1)} %stack.23.pos_ref, bf16[16,16,1024]{2,1,0:T(8,128)(2,1)S(1)} %all-gather.mine_ref, bf16[16,16,1024]{2,1,0:T(8,128)(2,1)S(1)} %collective-permute-done.1.other_ref, ...), custom_call_target="tpu_custom_call" | custom-call | flops 268435456 | bytes 2232352 | tf_op jit(solution)/shard_map/pallas_call | solution.py:22
  57.3 12.5 %all_to_all.25.got_ref = f32[32,8,128]{2,1,0:T(8,128)S(1)} all-to-all(f32[32,8,128]{2,1,0:T(8,128)S(1)} %get-tuple-element.22), channel_id=1, replica_groups=mesh['zl'=8,'yh'=2,'yl'=2,'zh'=2,'x'=4,'c'=2] {'x','yh','yl','c'}, dimensions={0} | all-to-all | bytes 262144 | tf_op jit(solution)/shard_map/all_to_all | solution.py:225
  69.9 0.2 shard_map.69
  70.1 23.3 %all_to_all.26.got_ref = f32[16,8,128]{2,1,0:T(8,128)S(1)} all-to-all(f32[16,8,128]{2,1,0:T(8,128)S(1)} %get-tuple-element.25), channel_id=1, replica_groups=mesh['zl'=8,'yh'=2,'yl'=2,'zh'=2,'x'=4,'c'=2] {'zh','zl'}, dimensions={0} | all-to-all | bytes 131072 | tf_op jit(solution)/shard_map/all_to_all | solution.py:227
  93.4 2.0 %shard_map.70 = (bf16[16,8,1024]{2,1,0:T(8,128)(2,1)}, f32[128,1152]{1,0:T(8,128)S(1)}, f32[128,1152]{1,0:T(8,128)S(1)}) custom-call(s32[8]{0:T(128)S(1)} %stack.23.pos_ref, f32[256,256]{1,0:T(8,128)S(1)} %get-tuple-element.20.on_ref, f32[256,256]{1,0:T(8,128)S(1)} %get-tuple-element.21.mom_ref, f32[128,128]{1,0:T(8,128)S(1)} %get-tuple-element.24.lse_ref, ...), custom_call_target="tpu_custom_call" | custom-call | flops 536870912 | bytes 3670048 | tf_op jit(solution)/shard_map/pallas_call | solution.py:22
  95.4 5.0 %all-to-all-start.3 = ((bf16[16,8,1024]{2,1,0:T(8,128)(2,1)}), bf16[16,8,1024]{2,1,0:T(8,128)(2,1)S(1)}, u32[]{:S(2)}, u32[]{:S(2)}) async-start(bf16[16,8,1024]{2,1,0:T(8,128)(2,1)} %get-tuple-element.28), calls=%async_computation.3 | async-start | bytes 524288 | tf_op jit(solution)/shard_map/all_to_all | solution.py:235
  100.3 1.9 %collective-permute-start.2 = (f32[128,1152]{1,0:T(8,128)S(1)}, f32[128,1152]{1,0:T(8,128)S(1)}, u32[]{:S(2)}, u32[]{:S(2)}) collective-permute-start(f32[128,1152]{1,0:T(8,128)S(1)} %get-tuple-element.27), channel_id=1, source_target_pairs={{0,1},{1,0},{2,3},{3,2},{4,5},{5,4},{6,7},{7,6},{8,9},{9,8},{10,11... | collective-permute-start | bytes 1769480 | tf_op jit(solution)/shard_map/ppermute | solution.py:207
  102.3 2.0 %collective-permute-done.2.got_ref = f32[128,1152]{1,0:T(8,128)S(1)} collective-permute-done((f32[128,1152]{1,0:T(8,128)S(1)}, f32[128,1152]{1,0:T(8,128)S(1)}, u32[]{:S(2)}, u32[]{:S(2)}) %collective-permute-start.2) | collective-permute-done | bytes 589856 | tf_op jit(solution)/shard_map/ppermute | solution.py:207
  104.2 0.8 shard_map.71
  105.0 13.6 %all-to-all-done.3 = bf16[16,8,1024]{2,1,0:T(8,128)(2,1)S(1)} async-done(((bf16[16,8,1024]{2,1,0:T(8,128)(2,1)}), bf16[16,8,1024]{2,1,0:T(8,128)(2,1)S(1)}, u32[]{:S(2)}, u32[]{:S(2)}) %all-to-all-start.3) | async-done | bytes 262176 | tf_op jit(solution)/shard_map/all_to_all | solution.py:235
  118.6 3.5 %all-to-all-start.4 = ((bf16[16,8,1152]{2,1,0:T(8,128)(2,1)}), bf16[16,8,1152]{2,1,0:T(8,128)(2,1)S(1)}, u32[]{:S(2)}, u32[]{:S(2)}) async-start(bf16[16,8,1152]{2,1,0:T(8,128)(2,1)} %shard_map.71), calls=%async_computation.4 | async-start | bytes 589824 | tf_op jit(solution)/shard_map/all_to_all | solution.py:238
  122.1 0.7 convert_reduce_fusion
  122.8 8.2 %all-to-all-done.4.got_ref = bf16[16,8,1152]{2,1,0:T(8,128)(2,1)S(1)} async-done(((bf16[16,8,1152]{2,1,0:T(8,128)(2,1)}), bf16[16,8,1152]{2,1,0:T(8,128)(2,1)S(1)}, u32[]{:S(2)}, u32[]{:S(2)}) %all-to-all-start.4) | async-done | bytes 294944 | tf_op jit(solution)/shard_map/all_to_all | solution.py:238
  131.0 0.7 shard_map.72
  (2 shorter events, 0.0 us)
Async XLA Ops:
  1.4 20.8 %collective-permute-start = (bf16[16,1024]{1,0:T(8,128)(2,1)S(1)}, bf16[16,1024]{1,0:T(8,128)(2,1)S(1)}, u32[]{:S(2)}, u32[]{:S(2)}) collective-permute-start(bf16[16,1024]{1,0:T(8,128)(2,1)S(1)} %get-tuple-element.18.own_ref), channel_id=1, source_target_pairs={{0,32},{32,0},{1,33},{33,1},{2,34},{34,2},{3,35},{35,3},{4,36},{36... | collective-permute-start | bytes 98312 | tf_op jit(solution)/shard_map/ppermute | solution.py:207
  7.4 48.3 %all-to-all-start = ((bf16[16,16,1024]{2,1,0:T(8,128)(2,1)}), bf16[16,16,1024]{2,1,0:T(8,128)(2,1)S(1)}, u32[]{:S(2)}, u32[]{:S(2)}) async-start(bf16[16,16,1024]{2,1,0:T(8,128)(2,1)} %broadcast_in_dim.2), calls=%async_computation | async-start | bytes 1048576 | tf_op jit(solution)/shard_map/all_to_all | solution.py:213
  51.9 3.8 %collective-permute-start.1 = (bf16[16,16,1024]{2,1,0:T(8,128)(2,1)S(1)}, bf16[16,16,1024]{2,1,0:T(8,128)(2,1)S(1)}, u32[]{:S(2)}, u32[]{:S(2)}) collective-permute-start(bf16[16,16,1024]{2,1,0:T(8,128)(2,1)S(1)} %all-gather.mine_ref), channel_id=1, source_target_pairs={{0,1},{1,0},{2,3},{3,2},{4,5},{5,4},{6,7},{7,6},{8,9},{9,8},{10,11... | collective-permute-start | bytes 1572872 | tf_op jit(solution)/shard_map/ppermute | solution.py:207
  95.4 23.2 %all-to-all-start.3 = ((bf16[16,8,1024]{2,1,0:T(8,128)(2,1)}), bf16[16,8,1024]{2,1,0:T(8,128)(2,1)S(1)}, u32[]{:S(2)}, u32[]{:S(2)}) async-start(bf16[16,8,1024]{2,1,0:T(8,128)(2,1)} %get-tuple-element.28), calls=%async_computation.3 | async-start | bytes 524288 | tf_op jit(solution)/shard_map/all_to_all | solution.py:235
  100.3 3.9 %collective-permute-start.2 = (f32[128,1152]{1,0:T(8,128)S(1)}, f32[128,1152]{1,0:T(8,128)S(1)}, u32[]{:S(2)}, u32[]{:S(2)}) collective-permute-start(f32[128,1152]{1,0:T(8,128)S(1)} %get-tuple-element.27), channel_id=1, source_target_pairs={{0,1},{1,0},{2,3},{3,2},{4,5},{5,4},{6,7},{7,6},{8,9},{9,8},{10,11... | collective-permute-start | bytes 1769480 | tf_op jit(solution)/shard_map/ppermute | solution.py:207
  118.6 12.4 %all-to-all-start.4 = ((bf16[16,8,1152]{2,1,0:T(8,128)(2,1)}), bf16[16,8,1152]{2,1,0:T(8,128)(2,1)S(1)}, u32[]{:S(2)}, u32[]{:S(2)}) async-start(bf16[16,8,1152]{2,1,0:T(8,128)(2,1)} %shard_map.71), calls=%async_computation.4 | async-start | bytes 589824 | tf_op jit(solution)/shard_map/all_to_all | solution.py:238

commit v8 on v7

--- a/solution.py
+++ b/solution.py
@@ -32,25 +32,23 @@
     return jax.ShapeDtypeStruct(dims, dtype)
 
 
-def lanes(height):
-    lane = lax.broadcasted_iota(jnp.int32, (height, 2 * side), 1)
-    return lane, (lane & rows) == 0
+def first_half(height):
+    return (lax.broadcasted_iota(jnp.int32, (height, side), 1) & rows) == 0
 
 
 def diagonal_of(pos_ref):
     x, y, c, zh, zl = (pos_ref[k] for k in range(5))
-    row = lax.broadcasted_iota(jnp.int32, (2 * side, 2 * side), 0)
-    lane, valid = lanes(2 * side)
-    pc, px = row >> 7, (row >> 4) & 3
-    py = ((row >> 3) & 1) * 2 + ((row >> 6) & 1)
-    image_block = (zh * 8 + px * 2 + pc) * 32 + zl * 4 + py
-    qh, ql = lane >> 7, (lane >> 4) & 7
-    text_block = (ql * 4 + y) * 16 + qh * 8 + x * 2 + c
-    return valid & (image_block == text_block) & ((row & 7) == (lane & 7))
+    row = lax.broadcasted_iota(jnp.int32, (2 * side, 1), 0)
+    pc, px, py = row >> 7, (row >> 5) & 3, ((row >> 3) & 1) * 2 + ((row >> 4) & 1)
+    image = ((zh * 8 + px * 2 + pc) * 32 + zl * 4 + py) * rows + (row & 7)
+    lane = lax.broadcasted_iota(jnp.int32, (1, side), 1)
+    qh, ql = (lane >> 3) & 1, lane >> 4
+    text = ((ql * 4 + y) * 16 + qh * 8 + x * 2 + c) * rows + (lane & 7)
+    return image == text
 
 
 def order_kernel(pos_ref, own_ref, other_ref, out_ref):
-    place = pos_ref[1] >> 1
+    place = pos_ref[0]
     out_ref[place] = own_ref[...]
     out_ref[1 - place] = other_ref[...]
 
@@ -68,13 +66,16 @@
     mine, other = product(mine_ref), product(other_ref)
     first = pos_ref[2] == 0
     low, high = jnp.where(first, mine, other), jnp.where(first, other, mine)
-    _, valid = lanes(2 * side)
+    packed = first_half(2 * side)
 
     def both(which):
-        return jnp.concatenate([part[:, which].reshape(side, 2 * side) for part in (low, high)], axis=0)
-
-    on = jnp.where(valid, both(0), very_low)
-    mom = jnp.where(valid, pltpu.roll(both(1), 2 * side - rows, 1), very_low)
+        whole = jnp.concatenate([part[:, which].reshape(side, 2 * side) for part in (low, high)], axis=0)
+        return whole[:, :side], whole[:, side:]
+
+    left, right = both(0)
+    on = jnp.where(packed, left, pltpu.roll(right, rows, 1))
+    left, right = both(1)
+    mom = jnp.where(packed, pltpu.roll(left, side - rows, 1), right)
     on_ref[...] = on
     mom_ref[...] = mom
 
@@ -97,12 +98,11 @@
     for peer in range(n_plane):
         row_ref[peer] = by_row
     own = jnp.sum(jnp.where(diagonal_of(pos_ref), on, 0.0), axis=0, keepdims=True)
-    slot = lax.broadcasted_iota(jnp.int32, (8, 2 * side), 0)
-    by_col = jnp.zeros((8, 2 * side), f32)
+    slot = lax.broadcasted_iota(jnp.int32, (8, side), 0)
+    by_col = jnp.zeros((8, side), f32)
     for k, value in enumerate(stats(0) + [own]):
         by_col = jnp.where(slot == k, value, by_col)
-    lane = lax.broadcasted_iota(jnp.int32, (8, side), 1)
-    col_ref[...] = jnp.where((lane & rows) == 0, by_col[:, :side], pltpu.roll(by_col[:, side:], rows, 1))
+    col_ref[...] = by_col
 
 
 def combine(got):
@@ -138,30 +138,20 @@
     loss = jnp.where(slot == 4, sums * (1.0 / (n_plane * side)), loss)
     share_of_loss = jnp.sum(loss)
 
-    _, valid = lanes(2 * side)
     on, mom = on_ref[...], mom_ref[...]
-
-    def spread(row):
-        return jnp.concatenate([row, pltpu.roll(row, side - rows, 1)], axis=1)
-
-    both = spread(lse)
-    col_on, col_mom = both[0:1], both[1:2]
+    col_on, col_mom = lse[0:1], lse[1:2]
     row_on = jnp.concatenate([lse_ref[:, 0:1], lse_ref[:, 4:5]], axis=0)
     row_mom = jnp.concatenate([lse_ref[:, 1:2], lse_ref[:, 5:6]], axis=0)
     delta = jnp.where(diagonal_of(pos_ref), 1.0 - mix_weight, 0.0)
     target_row = mix_weight * jnp.exp(mom - row_mom) + delta
     target_col = mix_weight * jnp.exp(mom - col_mom) + delta
     grad = 0.5 * ((jnp.exp(on - row_on) - target_row) + (jnp.exp(on - col_on) - target_col))
-    grad = jnp.where(valid, grad, 0.0)
     first = pos_ref[2] == 0
     low, high = grad[:side], grad[side:]
     mine, other = jnp.where(first, low, high), jnp.where(first, high, low)
     texts = text_ref[...].reshape(2 * side, width)
 
-    lane = lax.broadcasted_iota(jnp.int32, (side, side), 1)
-
     def down(part, ref):
-        part = jnp.where((lane & rows) == 0, part[:, :side], pltpu.roll(part[:, side:], rows, 1))
         part = part.reshape(16, 1, rows, side)
         part = jnp.concatenate([part, jnp.zeros_like(part)], axis=1).reshape(2 * side, side)
         return lax.dot_general(
@@ -171,7 +161,10 @@
     by_text = (down(mine, mine_ref) + down(other, other_ref)).reshape(8, 2, rows, width)
     for k in range(2):
         out_ref[8 * k : 8 * k + 8] = by_text[:, k].astype(bf16)
+    packed = first_half(side)
     for part, ref in ((mine, keep_ref), (other, send_ref)):
+        halves = [jnp.where(packed, half, 0.0) for half in (part, pltpu.roll(part, side - rows, 1))]
+        part = jnp.concatenate(halves, axis=1)
         ref[:, :width] = jnp.dot(part.astype(bf16), texts, preferred_element_type=f32)
         ref[:, width:] = jnp.full((side, 128), share_of_loss, f32)
 
@@ -200,8 +193,9 @@
 def local(image, text, mimage, mtext):
     width = image.shape[1]
     wide = width + 128
-    x, yh, yl, c, zh, zl = (lax.axis_index(a) for a in ("x", "yh", "yl", "c", "zh", "zl"))
-    pos = jnp.stack([x, yh * 2 + yl, c, zh, zl, 0, 0, 0]).astype(jnp.int32)
+    x, yh, yl, c, zh, zl = (lax.axis_index(a).astype(jnp.int32) for a in ("x", "yh", "yl", "c", "zh", "zl"))
+    pos = jnp.stack([x, yh * 2 + yl, c, zh, zl, 0, 0, 0])
+    yh, yl = yh[None], yl[None]
 
     def swap(block, axis="c"):
         return lax.ppermute(block, axis, [(0, 1), (1, 0)])
@@ -212,13 +206,14 @@
     sent = jnp.broadcast_to(both[None], (n_column,) + both.shape)
     texts = lax.all_to_all(sent, column, 0, 0, tiled=True)
     across = swap(pair, "yh")
-    (pair,) = call(order_kernel, [shape(2, 16, width, dtype=bf16)], pos, pair, across, flops=2**35)
-    mine = lax.all_gather(pair, ("yl", "x")).reshape(16, 16, width)
+    (pair,) = call(order_kernel, [shape(2, 16, width, dtype=bf16)], yh, pair, across, flops=2**35)
+    (pair,) = call(order_kernel, [shape(2, 2, 16, width, dtype=bf16)], yl, pair, swap(pair, "yl"))
+    mine = lax.all_gather(pair, "x").reshape(16, 16, width)
     other = swap(mine)
 
     on, mom, row_parts, col_parts = call(
         score_kernel,
-        [shape(256, 256), shape(256, 256), shape(n_plane, 8, side), shape(8, side)],
+        [shape(2 * side, side), shape(2 * side, side), shape(n_plane, 8, side), shape(8, side)],
         pos, mine, other, texts,
         flops=2**28, exps=2**18,
     )
@@ -235,7 +230,7 @@
     got_text = lax.all_to_all(by_text, column, 0, 0, tiled=True)
     (by_image,) = call(core_kernel, [shape(16, rows, wide, dtype=bf16)], keep, swap(send))
     by_image, got_text = lax.optimization_barrier((by_image, got_text))
-    got_image = lax.all_to_all(by_image, ("yl", "x", "yh"), 0, 0, tiled=True)
+    got_image = lax.all_to_all(by_image, ("x", "yl", "yh"), 0, 0, tiled=True)
     grad_text = jnp.sum(got_text.astype(f32), axis=0)
     grad_image, loss = call(
         last_kernel, [shape(rows, width), shape(1, 1)], got_image,

time: 132 us -> 122 us (0.924)
  blocking collectives: 65 us -> 45.7 us
  waiting for transfers between devices: 25.6 us -> 32.6 us
  starting transfers between devices: 32.2 us -> 34.8 us
    all_gather x1, blocking collectives: 29.1 us -> 13.8 us  [local(): mine = lax.all_gather(pair, 'x').reshape(16, 16, width)]
    all_to_all x1, blocking collectives: 23.3 us -> 19.1 us  [local(): col_got = lax.all_to_all(col_sent, column, 0, 0, tiled=True)]
    all_to_all x1, waiting for transfers between devices: 0.01 us -> 3.56 us  [local(): texts = lax.all_to_all(sent, column, 0, 0, tiled=True)]
    ppermute x3 -> x4, waiting for transfers between devices: 3.85 us -> 7.29 us  [swap(): return lax.ppermute(block, axis, [(0, 1), (1, 0)])]
    ppermute x3 -> x4, starting transfers between devices: 8.91 us -> 11.5 us  [swap(): return lax.ppermute(block, axis, [(0, 1), (1, 0)])]
    pallas_call x6 -> x7, Pallas kernels: 5.86 us -> 4.89 us  [call(): pl.pallas_call(body, out_shape=outs, cost_estimate=pl.CostEstimate(flops=...]
  transfers between devices with their start and end apart: 6 -> 7, of which waited for: 4 -> 6; matrix products, arithmetic and copies ran while one was open for 1% -> 1% of each run, Pallas kernels for 1% -> 1%
where the time goes in v8:
time: 122 us; the launch traced here: 121 us
  blocking collectives  45.7 us (37%)
  starting transfers between devices  34.8 us (29%)
  waiting for transfers between devices  32.6 us (27%)
  Pallas kernels  4.89 us (4%)
  other arithmetic  1.43 us (1%)
    all_to_all x1, blocking collectives, local(): col_got = lax.all_to_all(col_sent, column, 0, 0, tiled=True)  19.1 us
    all_to_all x1, starting transfers between devices, local(): texts = lax.all_to_all(sent, column, 0, 0, tiled=True)  14.8 us
    all_gather x1, blocking collectives, local(): mine = lax.all_gather(pair, 'x').reshape(16, 16, width)  13.8 us
    all_to_all x1, waiting for transfers between devices, local(): got_text = lax.all_to_all(by_text, column, 0, 0, tiled=True)  13.5 us
    all_to_all x1, blocking collectives, local(): lax.all_to_all(row_parts, ('x', 'yh', 'yl', 'c'), 0, 0, tiled=True)  12.8 us
    ppermute x4, starting transfers between devices, swap(): return lax.ppermute(block, axis, [(0, 1), (1, 0)])  11.5 us
    all_to_all x1, waiting for transfers between devices, local(): got_image = lax.all_to_all(by_image, ('x', 'yl', 'yh'), 0, 0, tiled=True)  8.23 us
    ppermute x4, waiting for transfers between devices, swap(): return lax.ppermute(block, axis, [(0, 1), (1, 0)])  7.29 us
  transfers between devices with their start and end apart: 7, of which 6 were waited for; matrix products, arithmetic and copies ran while one was open for 1% of the time, Pallas kernels for 1%

profile of v8, /device:TPU:64, one launch (start us, length us, event | category | flops | bytes accessed | tf_op | source)
XLA Modules:
  0.0 121.1 jit_solution(934102717535733499)
XLA Ops:
  0.6 0.8 pad_maximum_fusion
  1.4 5.1 %collective-permute-start = (bf16[16,1024]{1,0:T(8,128)(2,1)S(1)}, bf16[16,1024]{1,0:T(8,128)(2,1)S(1)}, u32[]{:S(2)}, u32[]{:S(2)}) collective-permute-start(bf16[16,1024]{1,0:T(8,128)(2,1)S(1)} %get-tuple-element.18.own_ref), channel_id=1, source_target_pairs={{0,32},{32,0},{1,33},{33,1},{2,34},{34,2},{3,35},{35,3},{4,36},{36... | collective-permute-start | bytes 98312 | tf_op jit(solution)/shard_map/ppermute | solution.py:201
  6.5 0.9 broadcast_in_dim.14
  7.4 14.8 %all-to-all-start = ((bf16[16,16,1024]{2,1,0:T(8,128)(2,1)}), bf16[16,16,1024]{2,1,0:T(8,128)(2,1)S(1)}, u32[]{:S(2)}, u32[]{:S(2)}) async-start(bf16[16,16,1024]{2,1,0:T(8,128)(2,1)} %broadcast_in_dim.14), calls=%async_computation | async-start | bytes 1048576 | tf_op jit(solution)/shard_map/all_to_all | solution.py:207
  22.1 2.6 %collective-permute-start.1 = (bf16[2,16,1024]{2,1,0:T(8,128)(2,1)S(1)}, bf16[2,16,1024]{2,1,0:T(8,128)(2,1)S(1)}, u32[]{:S(2)}, u32[]{:S(2)}) collective-permute-start(bf16[2,16,1024]{2,1,0:T(8,128)(2,1)S(1)} %shard_map.67.own_ref), channel_id=1, source_target_pairs={{0,16},{16,0},{1,17},{17,1},{2,18},{18,2},{3,19},{19,3},{4,20},{20... | collective-permute-start | bytes 196616 | tf_op jit(solution)/shard_map/ppermute | solution.py:201
  24.7 3.6 %collective-permute-done.1.other_ref = bf16[2,16,1024]{2,1,0:T(8,128)(2,1)S(1)} collective-permute-done((bf16[2,16,1024]{2,1,0:T(8,128)(2,1)S(1)}, bf16[2,16,1024]{2,1,0:T(8,128)(2,1)S(1)}, u32[]{:S(2)}, u32[]{:S(2)}) %collective-permute-start.1) | collective-permute-done | bytes 65568 | tf_op jit(solution)/shard_map/ppermute | solution.py:201
  28.3 13.8 %all-gather = bf16[8,2,16,1024]{3,2,1,0:T(8,128)(2,1)S(1)} all-gather(bf16[2,2,16,1024]{3,2,1,0:T(8,128)(2,1)S(1)} %shard_map.68), channel_id=2, replica_groups=mesh['zl'=8,'yh'=2,'yl'=2,'zh'=2,'x'=4,'c'=2] {'x'}, dimensions={0}, use_global_device_ids=true | all-gather | bytes 655360 | tf_op jit(solution)/shard_map/all_gather | solution.py:211
  42.1 1.9 %collective-permute-start.2 = (bf16[16,16,1024]{2,1,0:T(8,128)(2,1)S(1)}, bf16[16,16,1024]{2,1,0:T(8,128)(2,1)S(1)}, u32[]{:S(2)}, u32[]{:S(2)}) collective-permute-start(bf16[16,16,1024]{2,1,0:T(8,128)(2,1)S(1)} %bitcast.9), channel_id=1, source_target_pairs={{0,1},{1,0},{2,3},{3,2},{4,5},{5,4},{6,7},{7,6},{8,9},{9,8},{10,11... | collective-permute-start | bytes 1572872 | tf_op jit(solution)/shard_map/ppermute | solution.py:201
  44.1 1.8 %collective-permute-done.2.other_ref = bf16[16,16,1024]{2,1,0:T(8,128)(2,1)S(1)} collective-permute-done((bf16[16,16,1024]{2,1,0:T(8,128)(2,1)S(1)}, bf16[16,16,1024]{2,1,0:T(8,128)(2,1)S(1)}, u32[]{:S(2)}, u32[]{:S(2)}) %collective-permute-start.2) | collective-permute-done | bytes 524320 | tf_op jit(solution)/shard_map/ppermute | solution.py:201
  45.9 3.6 %all-to-all-done.text_ref = bf16[16,16,1024]{2,1,0:T(8,128)(2,1)S(1)} async-done(((bf16[16,16,1024]{2,1,0:T(8,128)(2,1)}), bf16[16,16,1024]{2,1,0:T(8,128)(2,1)S(1)}, u32[]{:S(2)}, u32[]{:S(2)}) %all-to-all-start) | async-done | bytes 524320 | tf_op jit(solution)/shard_map/all_to_all | solution.py:207
  49.4 1.4 %shard_map.69 = (f32[256,128]{1,0:T(8,128)S(1)}, f32[256,128]{1,0:T(8,128)S(1)}, f32[32,8,128]{2,1,0:T(8,128)S(1)}, f32[8,128]{1,0:T(8,128)S(1)}) custom-call(s32[8]{0:T(128)S(1)} %stack.23.pos_ref, bf16[16,16,1024]{2,1,0:T(8,128)(2,1)S(1)} %bitcast.10, bf16[16,16,1024]{2,1,0:T(8,128)(2,1)S(1)} %collective-permute-done.2.other_ref, ...), custom_call_target="tpu_custom_call" | custom-call | flops 268435456 | bytes 1970208 | tf_op jit(solution)/shard_map/pallas_call | solution.py:22
  50.8 12.8 %all_to_all.25.got_ref = f32[32,8,128]{2,1,0:T(8,128)S(1)} all-to-all(f32[32,8,128]{2,1,0:T(8,128)S(1)} %get-tuple-element.22), channel_id=1, replica_groups=mesh['zl'=8,'yh'=2,'yl'=2,'zh'=2,'x'=4,'c'=2] {'x','yh','yl','c'}, dimensions={0} | all-to-all | bytes 262144 | tf_op jit(solution)/shard_map/all_to_all | solution.py:220
  63.7 0.2 shard_map.70
  63.9 19.1 %all_to_all.26.got_ref = f32[16,8,128]{2,1,0:T(8,128)S(1)} all-to-all(f32[16,8,128]{2,1,0:T(8,128)S(1)} %get-tuple-element.25), channel_id=1, replica_groups=mesh['zl'=8,'yh'=2,'yl'=2,'zh'=2,'x'=4,'c'=2] {'zh','zl'}, dimensions={0} | all-to-all | bytes 131072 | tf_op jit(solution)/shard_map/all_to_all | solution.py:222
  83.0 1.8 %shard_map.71 = (bf16[16,8,1024]{2,1,0:T(8,128)(2,1)}, f32[128,1152]{1,0:T(8,128)S(1)}, f32[128,1152]{1,0:T(8,128)S(1)}) custom-call(s32[8]{0:T(128)S(1)} %stack.23.pos_ref, f32[256,128]{1,0:T(8,128)S(1)} %get-tuple-element.20.on_ref, f32[256,128]{1,0:T(8,128)S(1)} %get-tuple-element.21.mom_ref, f32[128,128]{1,0:T(8,128)S(1)} %get-tuple-element.24.lse_ref, ...), custom_call_target="tpu_custom_call" | custom-call | flops 536870912 | bytes 3407904 | tf_op jit(solution)/shard_map/pallas_call | solution.py:22
  84.8 5.0 %all-to-all-start.3 = ((bf16[16,8,1024]{2,1,0:T(8,128)(2,1)}), bf16[16,8,1024]{2,1,0:T(8,128)(2,1)S(1)}, u32[]{:S(2)}, u32[]{:S(2)}) async-start(bf16[16,8,1024]{2,1,0:T(8,128)(2,1)} %get-tuple-element.28), calls=%async_computation.3 | async-start | bytes 524288 | tf_op jit(solution)/shard_map/all_to_all | solution.py:230
  89.7 1.9 %collective-permute-start.3 = (f32[128,1152]{1,0:T(8,128)S(1)}, f32[128,1152]{1,0:T(8,128)S(1)}, u32[]{:S(2)}, u32[]{:S(2)}) collective-permute-start(f32[128,1152]{1,0:T(8,128)S(1)} %get-tuple-element.27), channel_id=1, source_target_pairs={{0,1},{1,0},{2,3},{3,2},{4,5},{5,4},{6,7},{7,6},{8,9},{9,8},{10,11... | collective-permute-start | bytes 1769480 | tf_op jit(solution)/shard_map/ppermute | solution.py:201
  91.6 2.0 %collective-permute-done.3.got_ref = f32[128,1152]{1,0:T(8,128)S(1)} collective-permute-done((f32[128,1152]{1,0:T(8,128)S(1)}, f32[128,1152]{1,0:T(8,128)S(1)}, u32[]{:S(2)}, u32[]{:S(2)}) %collective-permute-start.3) | collective-permute-done | bytes 589856 | tf_op jit(solution)/shard_map/ppermute | solution.py:201
  93.6 0.8 shard_map.72
  94.4 13.5 %all-to-all-done.3 = bf16[16,8,1024]{2,1,0:T(8,128)(2,1)S(1)} async-done(((bf16[16,8,1024]{2,1,0:T(8,128)(2,1)}), bf16[16,8,1024]{2,1,0:T(8,128)(2,1)S(1)}, u32[]{:S(2)}, u32[]{:S(2)}) %all-to-all-start.3) | async-done | bytes 262176 | tf_op jit(solution)/shard_map/all_to_all | solution.py:230
  107.9 3.5 %all-to-all-start.4 = ((bf16[16,8,1152]{2,1,0:T(8,128)(2,1)}), bf16[16,8,1152]{2,1,0:T(8,128)(2,1)S(1)}, u32[]{:S(2)}, u32[]{:S(2)}) async-start(bf16[16,8,1152]{2,1,0:T(8,128)(2,1)} %shard_map.72), calls=%async_computation.4 | async-start | bytes 589824 | tf_op jit(solution)/shard_map/all_to_all | solution.py:233
  111.5 0.7 convert_reduce_fusion
  112.1 8.2 %all-to-all-done.4.got_ref = bf16[16,8,1152]{2,1,0:T(8,128)(2,1)S(1)} async-done(((bf16[16,8,1152]{2,1,0:T(8,128)(2,1)}), bf16[16,8,1152]{2,1,0:T(8,128)(2,1)S(1)}, u32[]{:S(2)}, u32[]{:S(2)}) %all-to-all-start.4) | async-done | bytes 294944 | tf_op jit(solution)/shard_map/all_to_all | solution.py:233
  120.4 0.7 shard_map.73
  (5 shorter events, 0.1 us)
Async XLA Ops:
  1.4 20.7 %collective-permute-start = (bf16[16,1024]{1,0:T(8,128)(2,1)S(1)}, bf16[16,1024]{1,0:T(8,128)(2,1)S(1)}, u32[]{:S(2)}, u32[]{:S(2)}) collective-permute-start(bf16[16,1024]{1,0:T(8,128)(2,1)S(1)} %get-tuple-element.18.own_ref), channel_id=1, source_target_pairs={{0,32},{32,0},{1,33},{33,1},{2,34},{34,2},{3,35},{35,3},{4,36},{36... | collective-permute-start | bytes 98312 | tf_op jit(solution)/shard_map/ppermute | solution.py:201
  7.4 42.1 %all-to-all-start = ((bf16[16,16,1024]{2,1,0:T(8,128)(2,1)}), bf16[16,16,1024]{2,1,0:T(8,128)(2,1)S(1)}, u32[]{:S(2)}, u32[]{:S(2)}) async-start(bf16[16,16,1024]{2,1,0:T(8,128)(2,1)} %broadcast_in_dim.14), calls=%async_computation | async-start | bytes 1048576 | tf_op jit(solution)/shard_map/all_to_all | solution.py:207
  22.1 6.2 %collective-permute-start.1 = (bf16[2,16,1024]{2,1,0:T(8,128)(2,1)S(1)}, bf16[2,16,1024]{2,1,0:T(8,128)(2,1)S(1)}, u32[]{:S(2)}, u32[]{:S(2)}) collective-permute-start(bf16[2,16,1024]{2,1,0:T(8,128)(2,1)S(1)} %shard_map.67.own_ref), channel_id=1, source_target_pairs={{0,16},{16,0},{1,17},{17,1},{2,18},{18,2},{3,19},{19,3},{4,20},{20... | collective-permute-start | bytes 196616 | tf_op jit(solution)/shard_map/ppermute | solution.py:201
  42.1 3.8 %collective-permute-start.2 = (bf16[16,16,1024]{2,1,0:T(8,128)(2,1)S(1)}, bf16[16,16,1024]{2,1,0:T(8,128)(2,1)S(1)}, u32[]{:S(2)}, u32[]{:S(2)}) collective-permute-start(bf16[16,16,1024]{2,1,0:T(8,128)(2,1)S(1)} %bitcast.9), channel_id=1, source_target_pairs={{0,1},{1,0},{2,3},{3,2},{4,5},{5,4},{6,7},{7,6},{8,9},{9,8},{10,11... | collective-permute-start | bytes 1572872 | tf_op jit(solution)/shard_map/ppermute | solution.py:201
  84.8 23.2 %all-to-all-start.3 = ((bf16[16,8,1024]{2,1,0:T(8,128)(2,1)}), bf16[16,8,1024]{2,1,0:T(8,128)(2,1)S(1)}, u32[]{:S(2)}, u32[]{:S(2)}) async-start(bf16[16,8,1024]{2,1,0:T(8,128)(2,1)} %get-tuple-element.28), calls=%async_computation.3 | async-start | bytes 524288 | tf_op jit(solution)/shard_map/all_to_all | solution.py:230
  89.7 3.9 %collective-permute-start.3 = (f32[128,1152]{1,0:T(8,128)S(1)}, f32[128,1152]{1,0:T(8,128)S(1)}, u32[]{:S(2)}, u32[]{:S(2)}) collective-permute-start(f32[128,1152]{1,0:T(8,128)S(1)} %get-tuple-element.27), channel_id=1, source_target_pairs={{0,1},{1,0},{2,3},{3,2},{4,5},{5,4},{6,7},{7,6},{8,9},{9,8},{10,11... | collective-permute-start | bytes 1769480 | tf_op jit(solution)/shard_map/ppermute | solution.py:201
  107.9 12.4 %all-to-all-start.4 = ((bf16[16,8,1152]{2,1,0:T(8,128)(2,1)}), bf16[16,8,1152]{2,1,0:T(8,128)(2,1)S(1)}, u32[]{:S(2)}, u32[]{:S(2)}) async-start(bf16[16,8,1152]{2,1,0:T(8,128)(2,1)} %shard_map.72), calls=%async_computation.4 | async-start | bytes 589824 | tf_op jit(solution)/shard_map/all_to_all | solution.py:233

commit v9 on v8

--- a/solution.py
+++ b/solution.py
@@ -183,10 +183,11 @@
     out_ref[:, :, width:] = pieces.reshape(16, rows, 128).astype(bf16)
 
 
-def last_kernel(got_ref, grad_ref, loss_ref):
-    total = jnp.sum(got_ref[...].astype(f32), axis=0)
-    width = grad_ref.shape[1]
-    grad_ref[...] = total[:, :width]
+def last_kernel(image_ref, text_ref, grad_image_ref, grad_text_ref, loss_ref):
+    total = jnp.sum(image_ref[...].astype(f32), axis=0)
+    width = grad_image_ref.shape[1]
+    grad_image_ref[...] = total[:, :width]
+    grad_text_ref[...] = jnp.sum(text_ref[...].astype(f32), axis=0)
     loss_ref[0, 0] = jnp.sum(total[:1, width:]) * (1.0 / (2.0 * rows * n_plane * n_column))
 
 
@@ -227,14 +228,15 @@
         pos, on, mom, row_lse, col_got, mine, other, texts,
         flops=2**29, exps=2**18,
     )
+    got = swap(send)
     got_text = lax.all_to_all(by_text, column, 0, 0, tiled=True)
-    (by_image,) = call(core_kernel, [shape(16, rows, wide, dtype=bf16)], keep, swap(send))
+    (by_image,) = call(core_kernel, [shape(16, rows, wide, dtype=bf16)], keep, got)
     by_image, got_text = lax.optimization_barrier((by_image, got_text))
     got_image = lax.all_to_all(by_image, ("x", "yl", "yh"), 0, 0, tiled=True)
-    grad_text = jnp.sum(got_text.astype(f32), axis=0)
-    grad_image, loss = call(
-        last_kernel, [shape(rows, width), shape(1, 1)], got_image,
-        out_specs=[pl.BlockSpec(memory_space=pltpu.VMEM), pl.BlockSpec(memory_space=pltpu.SMEM)],
+    vmem = pl.BlockSpec(memory_space=pltpu.VMEM)
+    grad_image, grad_text, loss = call(
+        last_kernel, [shape(rows, width), shape(rows, width), shape(1, 1)], got_image, got_text,
+        out_specs=[vmem, vmem, pl.BlockSpec(memory_space=pltpu.SMEM)],
     )
     return grad_image, grad_text, loss[0, 0]
 

time: 122 us -> 121 us (level)
  blocking collectives: 45.7 us -> 57.6 us
  waiting for transfers between devices: 32.6 us -> 25.1 us
  starting transfers between devices: 34.8 us -> 31.2 us
    all_to_all x0 -> x1, blocking collectives: none -> 11.9 us  [local(): got_image = lax.all_to_all(by_image, ('x', 'yl', 'yh'), 0, 0, tiled=True)]
    all_to_all x1 -> x0, waiting for transfers between devices: 8.23 us -> none  [local(): got_image = lax.all_to_all(by_image, ('x', 'yl', 'yh'), 0, 0, tiled=True)]
    all_to_all x1 -> x0, starting transfers between devices: 3.54 us -> none  [local(): got_image = lax.all_to_all(by_image, ('x', 'yl', 'yh'), 0, 0, tiled=True)]
  transfers between devices with their start and end apart: 7 -> 6, of which waited for: 6 -> 5; matrix products, arithmetic and copies ran while one was open for 1% -> 1% of each run, Pallas kernels for 1% -> 0%
where the time goes in v9:
time: 121 us
  blocking collectives  57.6 us (48%)
  starting transfers between devices  31.2 us (26%)
  waiting for transfers between devices  25.1 us (21%)
  Pallas kernels  4.2 us (3%)
    all_to_all x1, blocking collectives, local(): col_got = lax.all_to_all(col_sent, column, 0, 0, tiled=True)  19.1 us
    all_to_all x1, starting transfers between devices, local(): texts = lax.all_to_all(sent, column, 0, 0, tiled=True)  14.8 us
    all_to_all x1, waiting for transfers between devices, local(): got_text = lax.all_to_all(by_text, column, 0, 0, tiled=True)  14.2 us
    all_gather x1, blocking collectives, local(): mine = lax.all_gather(pair, 'x').reshape(16, 16, width)  13.8 us
    all_to_all x1, blocking collectives, local(): lax.all_to_all(row_parts, ('x', 'yh', 'yl', 'c'), 0, 0, tiled=True)  12.9 us
    all_to_all x1, blocking collectives, local(): got_image = lax.all_to_all(by_image, ('x', 'yl', 'yh'), 0, 0, tiled=True)  11.9 us
    ppermute x4, starting transfers between devices, swap(): return lax.ppermute(block, axis, [(0, 1), (1, 0)])  11.5 us
    ppermute x4, waiting for transfers between devices, swap(): return lax.ppermute(block, axis, [(0, 1), (1, 0)])  7.29 us
  transfers between devices with their start and end apart: 6, of which 5 were waited for; matrix products, arithmetic and copies ran while one was open for 1% of the time, Pallas kernels for 0%

profile of v9, /device:TPU:64, one launch (start us, length us, event | category | flops | bytes accessed | tf_op | source)
XLA Modules:
  0.0 120.6 jit_solution(11270343493950871662)
XLA Ops:
  0.6 0.8 pad_maximum_fusion
  1.4 5.1 %collective-permute-start = (bf16[16,1024]{1,0:T(8,128)(2,1)S(1)}, bf16[16,1024]{1,0:T(8,128)(2,1)S(1)}, u32[]{:S(2)}, u32[]{:S(2)}) collective-permute-start(bf16[16,1024]{1,0:T(8,128)(2,1)S(1)} %get-tuple-element.19.own_ref), channel_id=1, source_target_pairs={{0,32},{32,0},{1,33},{33,1},{2,34},{34,2},{3,35},{35,3},{4,36},{36... | collective-permute-start | bytes 98312 | tf_op jit(solution)/shard_map/ppermute | solution.py:202
  6.5 0.9 broadcast_in_dim.14
  7.4 14.8 %all-to-all-start = ((bf16[16,16,1024]{2,1,0:T(8,128)(2,1)}), bf16[16,16,1024]{2,1,0:T(8,128)(2,1)S(1)}, u32[]{:S(2)}, u32[]{:S(2)}) async-start(bf16[16,16,1024]{2,1,0:T(8,128)(2,1)} %broadcast_in_dim.14), calls=%async_computation | async-start | bytes 1048576 | tf_op jit(solution)/shard_map/all_to_all | solution.py:208
  22.1 0.0 collective-permute-done.other_ref
  22.1 2.6 %collective-permute-start.1 = (bf16[2,16,1024]{2,1,0:T(8,128)(2,1)S(1)}, bf16[2,16,1024]{2,1,0:T(8,128)(2,1)S(1)}, u32[]{:S(2)}, u32[]{:S(2)}) collective-permute-start(bf16[2,16,1024]{2,1,0:T(8,128)(2,1)S(1)} %shard_map.67.own_ref), channel_id=1, source_target_pairs={{0,16},{16,0},{1,17},{17,1},{2,18},{18,2},{3,19},{19,3},{4,20},{20... | collective-permute-start | bytes 196616 | tf_op jit(solution)/shard_map/ppermute | solution.py:202
  24.7 3.6 %collective-permute-done.1.other_ref = bf16[2,16,1024]{2,1,0:T(8,128)(2,1)S(1)} collective-permute-done((bf16[2,16,1024]{2,1,0:T(8,128)(2,1)S(1)}, bf16[2,16,1024]{2,1,0:T(8,128)(2,1)S(1)}, u32[]{:S(2)}, u32[]{:S(2)}) %collective-permute-start.1) | collective-permute-done | bytes 65568 | tf_op jit(solution)/shard_map/ppermute | solution.py:202
  28.3 13.8 %all-gather = bf16[8,2,16,1024]{3,2,1,0:T(8,128)(2,1)S(1)} all-gather(bf16[2,2,16,1024]{3,2,1,0:T(8,128)(2,1)S(1)} %shard_map.68), channel_id=2, replica_groups=mesh['zl'=8,'yh'=2,'yl'=2,'zh'=2,'x'=4,'c'=2] {'x'}, dimensions={0}, use_global_device_ids=true | all-gather | bytes 655360 | tf_op jit(solution)/shard_map/all_gather | solution.py:212
  42.1 1.9 %collective-permute-start.2 = (bf16[16,16,1024]{2,1,0:T(8,128)(2,1)S(1)}, bf16[16,16,1024]{2,1,0:T(8,128)(2,1)S(1)}, u32[]{:S(2)}, u32[]{:S(2)}) collective-permute-start(bf16[16,16,1024]{2,1,0:T(8,128)(2,1)S(1)} %bitcast.9), channel_id=1, source_target_pairs={{0,1},{1,0},{2,3},{3,2},{4,5},{5,4},{6,7},{7,6},{8,9},{9,8},{10,11... | collective-permute-start | bytes 1572872 | tf_op jit(solution)/shard_map/ppermute | solution.py:202
  44.0 0.1 stack.23.pos_ref
  44.1 1.8 %collective-permute-done.2.other_ref = bf16[16,16,1024]{2,1,0:T(8,128)(2,1)S(1)} collective-permute-done((bf16[16,16,1024]{2,1,0:T(8,128)(2,1)S(1)}, bf16[16,16,1024]{2,1,0:T(8,128)(2,1)S(1)}, u32[]{:S(2)}, u32[]{:S(2)}) %collective-permute-start.2) | collective-permute-done | bytes 524320 | tf_op jit(solution)/shard_map/ppermute | solution.py:202
  45.9 3.6 %all-to-all-done.text_ref = bf16[16,16,1024]{2,1,0:T(8,128)(2,1)S(1)} async-done(((bf16[16,16,1024]{2,1,0:T(8,128)(2,1)}), bf16[16,16,1024]{2,1,0:T(8,128)(2,1)S(1)}, u32[]{:S(2)}, u32[]{:S(2)}) %all-to-all-start) | async-done | bytes 524320 | tf_op jit(solution)/shard_map/all_to_all | solution.py:208
  49.4 1.4 %shard_map.69 = (f32[256,128]{1,0:T(8,128)S(1)}, f32[256,128]{1,0:T(8,128)S(1)}, f32[32,8,128]{2,1,0:T(8,128)S(1)}, f32[8,128]{1,0:T(8,128)S(1)}) custom-call(s32[8]{0:T(128)S(1)} %stack.23.pos_ref, bf16[16,16,1024]{2,1,0:T(8,128)(2,1)S(1)} %bitcast.10, bf16[16,16,1024]{2,1,0:T(8,128)(2,1)S(1)} %collective-permute-done.2.other_ref, ...), custom_call_target="tpu_custom_call" | custom-call | flops 268435456 | bytes 1970208 | tf_op jit(solution)/shard_map/pallas_call | solution.py:22
  50.8 12.9 %all_to_all.25.got_ref = f32[32,8,128]{2,1,0:T(8,128)S(1)} all-to-all(f32[32,8,128]{2,1,0:T(8,128)S(1)} %get-tuple-element.23), channel_id=1, replica_groups=mesh['zl'=8,'yh'=2,'yl'=2,'zh'=2,'x'=4,'c'=2] {'x','yh','yl','c'}, dimensions={0} | all-to-all | bytes 262144 | tf_op jit(solution)/shard_map/all_to_all | solution.py:221
  63.7 0.2 shard_map.70
  63.9 19.1 %all_to_all.26.got_ref = f32[16,8,128]{2,1,0:T(8,128)S(1)} all-to-all(f32[16,8,128]{2,1,0:T(8,128)S(1)} %get-tuple-element.26), channel_id=1, replica_groups=mesh['zl'=8,'yh'=2,'yl'=2,'zh'=2,'x'=4,'c'=2] {'zh','zl'}, dimensions={0} | all-to-all | bytes 131072 | tf_op jit(solution)/shard_map/all_to_all | solution.py:223
  83.0 1.8 %shard_map.71 = (bf16[16,8,1024]{2,1,0:T(8,128)(2,1)}, f32[128,1152]{1,0:T(8,128)S(1)}, f32[128,1152]{1,0:T(8,128)S(1)}) custom-call(s32[8]{0:T(128)S(1)} %stack.23.pos_ref, f32[256,128]{1,0:T(8,128)S(1)} %get-tuple-element.21.on_ref, f32[256,128]{1,0:T(8,128)S(1)} %get-tuple-element.22.mom_ref, f32[128,128]{1,0:T(8,128)S(1)} %get-tuple-element.25.lse_ref, ...), custom_call_target="tpu_custom_call" | custom-call | flops 536870912 | bytes 3407904 | tf_op jit(solution)/shard_map/pallas_call | solution.py:22
  84.8 5.0 %all-to-all-start.3 = ((bf16[16,8,1024]{2,1,0:T(8,128)(2,1)}), bf16[16,8,1024]{2,1,0:T(8,128)(2,1)S(1)}, u32[]{:S(2)}, u32[]{:S(2)}) async-start(bf16[16,8,1024]{2,1,0:T(8,128)(2,1)} %get-tuple-element.29), calls=%async_computation.3 | async-start | bytes 524288 | tf_op jit(solution)/shard_map/all_to_all | solution.py:232
  89.7 1.9 %collective-permute-start.3 = (f32[128,1152]{1,0:T(8,128)S(1)}, f32[128,1152]{1,0:T(8,128)S(1)}, u32[]{:S(2)}, u32[]{:S(2)}) collective-permute-start(f32[128,1152]{1,0:T(8,128)S(1)} %get-tuple-element.28), channel_id=1, source_target_pairs={{0,1},{1,0},{2,3},{3,2},{4,5},{5,4},{6,7},{7,6},{8,9},{9,8},{10,11... | collective-permute-start | bytes 1769480 | tf_op jit(solution)/shard_map/ppermute | solution.py:202
  91.6 2.0 %collective-permute-done.3.got_ref = f32[128,1152]{1,0:T(8,128)S(1)} collective-permute-done((f32[128,1152]{1,0:T(8,128)S(1)}, f32[128,1152]{1,0:T(8,128)S(1)}, u32[]{:S(2)}, u32[]{:S(2)}) %collective-permute-start.3) | collective-permute-done | bytes 589856 | tf_op jit(solution)/shard_map/ppermute | solution.py:202
  93.6 0.1 shard_map.72
  93.7 14.2 %all-to-all-done.3.text_ref = bf16[16,8,1024]{2,1,0:T(8,128)(2,1)S(1)} async-done(((bf16[16,8,1024]{2,1,0:T(8,128)(2,1)}), bf16[16,8,1024]{2,1,0:T(8,128)(2,1)S(1)}, u32[]{:S(2)}, u32[]{:S(2)}) %all-to-all-start.3) | async-done | bytes 262176 | tf_op jit(solution)/shard_map/all_to_all | solution.py:232
  107.9 11.9 %all_to_all.27.image_ref = bf16[16,8,1152]{2,1,0:T(8,128)(2,1)S(1)} all-to-all(bf16[16,8,1152]{2,1,0:T(8,128)(2,1)S(1)} %shard_map.72), channel_id=1, replica_groups=mesh['zl'=8,'yh'=2,'yl'=2,'zh'=2,'x'=4,'c'=2] {'x','yl','yh'}, dimensions={0} | all-to-all | bytes 589824 | tf_op jit(solution)/shard_map/all_to_all | solution.py:235
  119.9 0.7 shard_map.73
  (3 shorter events, 0.0 us)
Async XLA Ops:
  1.4 20.7 %collective-permute-start = (bf16[16,1024]{1,0:T(8,128)(2,1)S(1)}, bf16[16,1024]{1,0:T(8,128)(2,1)S(1)}, u32[]{:S(2)}, u32[]{:S(2)}) collective-permute-start(bf16[16,1024]{1,0:T(8,128)(2,1)S(1)} %get-tuple-element.19.own_ref), channel_id=1, source_target_pairs={{0,32},{32,0},{1,33},{33,1},{2,34},{34,2},{3,35},{35,3},{4,36},{36... | collective-permute-start | bytes 98312 | tf_op jit(solution)/shard_map/ppermute | solution.py:202
  7.4 42.1 %all-to-all-start = ((bf16[16,16,1024]{2,1,0:T(8,128)(2,1)}), bf16[16,16,1024]{2,1,0:T(8,128)(2,1)S(1)}, u32[]{:S(2)}, u32[]{:S(2)}) async-start(bf16[16,16,1024]{2,1,0:T(8,128)(2,1)} %broadcast_in_dim.14), calls=%async_computation | async-start | bytes 1048576 | tf_op jit(solution)/shard_map/all_to_all | solution.py:208
  22.1 6.2 %collective-permute-start.1 = (bf16[2,16,1024]{2,1,0:T(8,128)(2,1)S(1)}, bf16[2,16,1024]{2,1,0:T(8,128)(2,1)S(1)}, u32[]{:S(2)}, u32[]{:S(2)}) collective-permute-start(bf16[2,16,1024]{2,1,0:T(8,128)(2,1)S(1)} %shard_map.67.own_ref), channel_id=1, source_target_pairs={{0,16},{16,0},{1,17},{17,1},{2,18},{18,2},{3,19},{19,3},{4,20},{20... | collective-permute-start | bytes 196616 | tf_op jit(solution)/shard_map/ppermute | solution.py:202
  42.1 3.8 %collective-permute-start.2 = (bf16[16,16,1024]{2,1,0:T(8,128)(2,1)S(1)}, bf16[16,16,1024]{2,1,0:T(8,128)(2,1)S(1)}, u32[]{:S(2)}, u32[]{:S(2)}) collective-permute-start(bf16[16,16,1024]{2,1,0:T(8,128)(2,1)S(1)} %bitcast.9), channel_id=1, source_target_pairs={{0,1},{1,0},{2,3},{3,2},{4,5},{5,4},{6,7},{7,6},{8,9},{9,8},{10,11... | collective-permute-start | bytes 1572872 | tf_op jit(solution)/shard_map/ppermute | solution.py:202
  84.8 23.2 %all-to-all-start.3 = ((bf16[16,8,1024]{2,1,0:T(8,128)(2,1)}), bf16[16,8,1024]{2,1,0:T(8,128)(2,1)S(1)}, u32[]{:S(2)}, u32[]{:S(2)}) async-start(bf16[16,8,1024]{2,1,0:T(8,128)(2,1)} %get-tuple-element.29), calls=%async_computation.3 | async-start | bytes 524288 | tf_op jit(solution)/shard_map/all_to_all | solution.py:232
  89.7 3.9 %collective-permute-start.3 = (f32[128,1152]{1,0:T(8,128)S(1)}, f32[128,1152]{1,0:T(8,128)S(1)}, u32[]{:S(2)}, u32[]{:S(2)}) collective-permute-start(f32[128,1152]{1,0:T(8,128)S(1)} %get-tuple-element.28), channel_id=1, source_target_pairs={{0,1},{1,0},{2,3},{3,2},{4,5},{5,4},{6,7},{7,6},{8,9},{9,8},{10,11... | collective-permute-start | bytes 1769480 | tf_op jit(solution)/shard_map/ppermute | solution.py:202

commit v10 on v9

--- a/solution.py
+++ b/solution.py
@@ -7,7 +7,7 @@
 
 mix_weight = 0.4
 very_low = -1e30
-column = ("zh", "zl")
+column = ("zq", "zh", "zp")
 n_plane, n_column, rows = 32, 16, 8
 f32, bf16 = jnp.float32, jnp.bfloat16
 side = 16 * rows
@@ -39,22 +39,26 @@
 def diagonal_of(pos_ref):
     x, y, c, zh, zl = (pos_ref[k] for k in range(5))
     row = lax.broadcasted_iota(jnp.int32, (2 * side, 1), 0)
-    pc, px, py = row >> 7, (row >> 5) & 3, ((row >> 3) & 1) * 2 + ((row >> 4) & 1)
+    pc, py, px = row >> 7, (row >> 5) & 3, (row >> 3) & 3
     image = ((zh * 8 + px * 2 + pc) * 32 + zl * 4 + py) * rows + (row & 7)
     lane = lax.broadcasted_iota(jnp.int32, (1, side), 1)
-    qh, ql = (lane >> 3) & 1, lane >> 4
+    part = (lane >> 4) & 3
+    qh, ql = part >> 1, (part & 1) * 4 + ((lane >> 3) & 1) * 2 + (lane >> 6)
     text = ((ql * 4 + y) * 16 + qh * 8 + x * 2 + c) * rows + (lane & 7)
     return image == text
 
 
-def order_kernel(pos_ref, own_ref, other_ref, out_ref):
-    place = pos_ref[0]
-    out_ref[place] = own_ref[...]
-    out_ref[1 - place] = other_ref[...]
-
-
-def score_kernel(pos_ref, mine_ref, other_ref, text_ref, on_ref, mom_ref, row_ref, col_ref):
+def order_kernel(place_ref, *refs):
+    for k, ref in enumerate(refs[:4]):
+        refs[4][(place_ref[0] - k) & 3] = ref[...]
+
+
+def score_kernel(
+    pos_ref, mine_ref, other_ref, a_ref, b_ref, c_ref, d_ref, on_ref, mom_ref, row_ref, col_ref, text_ref
+):
     width = text_ref.shape[-1]
+    for k, ref in enumerate((a_ref, b_ref, c_ref, d_ref)):
+        text_ref[(pos_ref[5] - k) & 3] = ref[...]
     texts = text_ref[...].reshape(2 * side, width)
 
     def product(ref):
@@ -194,31 +198,32 @@
 def local(image, text, mimage, mtext):
     width = image.shape[1]
     wide = width + 128
-    x, yh, yl, c, zh, zl = (lax.axis_index(a).astype(jnp.int32) for a in ("x", "yh", "yl", "c", "zh", "zl"))
-    pos = jnp.stack([x, yh * 2 + yl, c, zh, zl, 0, 0, 0])
-    yh, yl = yh[None], yl[None]
-
-    def swap(block, axis="c"):
-        return lax.ppermute(block, axis, [(0, 1), (1, 0)])
+    x, y, c, zh, zp, zq = (lax.axis_index(a).astype(jnp.int32) for a in ("x", "y", "c", "zh", "zp", "zq"))
+    pos = jnp.stack([x, y, c, zh, zp * 4 + zq, zq, zq, zq])
+
+    def swap(block):
+        return lax.ppermute(block, "c", [(0, 1), (1, 0)])
+
+    def group(block, axes, names):
+        return [block] + [lax.ppermute(block, axes, [(names[i], names[(i + k) % 4]) for i in range(4)]) for k in (1, 2, 3)]
 
     both = jnp.concatenate([text, mtext], axis=0)
     pair = jnp.concatenate([image, mimage], axis=0)
     both, pair = lax.optimization_barrier((both, pair))
-    sent = jnp.broadcast_to(both[None], (n_column,) + both.shape)
-    texts = lax.all_to_all(sent, column, 0, 0, tiled=True)
-    across = swap(pair, "yh")
-    (pair,) = call(order_kernel, [shape(2, 16, width, dtype=bf16)], yh, pair, across, flops=2**35)
-    (pair,) = call(order_kernel, [shape(2, 2, 16, width, dtype=bf16)], yl, pair, swap(pair, "yl"))
-    mine = lax.all_gather(pair, "x").reshape(16, 16, width)
+    sent = jnp.broadcast_to(pair[None], (16,) + pair.shape)
+    mine = lax.all_to_all(sent, ("y", "x"), 0, 0, tiled=True)
+    place = (zh * 2 + zp)[None]
+    (far,) = call(order_kernel, [shape(4, 16, width, dtype=bf16)], place, *group(both, ("zp", "zh"), (0, 2, 1, 3)), flops=2**35)
+    texts = group(far, "zq", (0, 1, 2, 3))
     other = swap(mine)
 
-    on, mom, row_parts, col_parts = call(
+    on, mom, row_parts, col_parts, texts = call(
         score_kernel,
-        [shape(2 * side, side), shape(2 * side, side), shape(n_plane, 8, side), shape(8, side)],
-        pos, mine, other, texts,
+        [shape(2 * side, side), shape(2 * side, side), shape(n_plane, 8, side), shape(8, side), shape(4, 4, 16, width, dtype=bf16)],
+        pos, mine, other, *texts,
         flops=2**28, exps=2**18,
     )
-    row_got = lax.all_to_all(row_parts, ("x", "yh", "yl", "c"), 0, 0, tiled=True)
+    row_got = lax.all_to_all(row_parts, ("x", "y", "c"), 0, 0, tiled=True)
     row_lse, col_sent = call(row_kernel, [shape(side, side), shape(n_column, 8, side)], row_got, col_parts, exps=2**14)
     col_got = lax.all_to_all(col_sent, column, 0, 0, tiled=True)
 
@@ -232,7 +237,7 @@
     got_text = lax.all_to_all(by_text, column, 0, 0, tiled=True)
     (by_image,) = call(core_kernel, [shape(16, rows, wide, dtype=bf16)], keep, got)
     by_image, got_text = lax.optimization_barrier((by_image, got_text))
-    got_image = lax.all_to_all(by_image, ("x", "yl", "yh"), 0, 0, tiled=True)
+    got_image = lax.all_to_all(by_image, ("y", "x"), 0, 0, tiled=True)
     vmem = pl.BlockSpec(memory_space=pltpu.VMEM)
     grad_image, grad_text, loss = call(
         last_kernel, [shape(rows, width), shape(rows, width), shape(1, 1)], got_image, got_text,
@@ -242,9 +247,9 @@
 
 
 def solution(mesh):
-    fine = Mesh(mesh.devices.reshape(8, 2, 2, 2, 4, 2), ("zl", "yh", "yl", "zh", "x", "c"))
-    by_image = P(("zh", "x", "c", "zl", "yh", "yl"), None)
-    by_text = P(("zl", "yh", "yl", "zh", "x", "c"), None)
+    fine = Mesh(mesh.devices.reshape(2, 4, 4, 2, 4, 2), ("zp", "zq", "y", "zh", "x", "c"))
+    by_image = P(("zh", "x", "c", "zp", "zq", "y"), None)
+    by_text = P(("zp", "zq", "y", "zh", "x", "c"), None)
     return jax.shard_map(
         local,
         mesh=fine,

time: 121 us -> 128 us (1.058)
  starting transfers between devices: 31.2 us -> 49.2 us
  blocking collectives: 57.6 us -> 46 us
    ppermute x4 -> x8, starting transfers between devices: 11.5 us -> 37.4 us  [the longest x6 33.6 us: group(): lax.ppermute(block, axes, [(names[i], names[(i + k) % 4]) for i in range(...]
    all_gather x1 -> x0, blocking collectives: 13.8 us -> none  [local(): mine = lax.all_gather(pair, 'x').reshape(16, 16, width)]
    all_to_all x1, starting transfers between devices: 14.8 us -> 7.03 us  [local(): mine = lax.all_to_all(sent, ('y', 'x'), 0, 0, tiled=True)]
    ppermute x4 -> x8, waiting for transfers between devices: 7.29 us -> 10.9 us  [the longest x6 8.88 us: group(): lax.ppermute(block, axes, [(names[i], names[(i + k) % 4]) for i in range(...]
    all_to_all x1, waiting for transfers between devices: 3.56 us -> 0.01 us  [local(): mine = lax.all_to_all(sent, ('y', 'x'), 0, 0, tiled=True)]
    pallas_call x7 -> x6, Pallas kernels: 4.2 us -> 4.21 us  [call(): pl.pallas_call(body, out_shape=outs, cost_estimate=pl.CostEstimate(flops=...]
  transfers between devices with their start and end apart: 6 -> 10, of which waited for: 5 -> 6; matrix products, arithmetic and copies ran while one was open for 1% -> 0% of each run, Pallas kernels for 0% -> 0%
where the time goes in v10:
time: 128 us
  starting transfers between devices  49.2 us (38%)
  blocking collectives  46 us (36%)
  waiting for transfers between devices  25.8 us (20%)
  Pallas kernels  4.21 us (3%)
    ppermute x6, starting transfers between devices, group(): lax.ppermute(block, axes, [(names[i], names[(i + k) % 4]) for i in range(...  33.6 us
    all_to_all x1, blocking collectives, local(): col_got = lax.all_to_all(col_sent, column, 0, 0, tiled=True)  20 us
    all_to_all x1, waiting for transfers between devices, local(): got_text = lax.all_to_all(by_text, column, 0, 0, tiled=True)  14.9 us
    all_to_all x1, blocking collectives, local(): row_got = lax.all_to_all(row_parts, ('x', 'y', 'c'), 0, 0, tiled=True)  14.2 us
    all_to_all x1, blocking collectives, local(): got_image = lax.all_to_all(by_image, ('y', 'x'), 0, 0, tiled=True)  11.8 us
    ppermute x6, waiting for transfers between devices, group(): lax.ppermute(block, axes, [(names[i], names[(i + k) % 4]) for i in range(...  8.88 us
    all_to_all x1, starting transfers between devices, local(): mine = lax.all_to_all(sent, ('y', 'x'), 0, 0, tiled=True)  7.03 us
    all_to_all x1, starting transfers between devices, local(): got_text = lax.all_to_all(by_text, column, 0, 0, tiled=True)  4.76 us
  transfers between devices with their start and end apart: 10, of which 6 were waited for; matrix products, arithmetic and copies ran while one was open for 0% of the time, Pallas kernels for 0%

profile of v10, /device:TPU:64, one launch (start us, length us, event | category | flops | bytes accessed | tf_op | source)
XLA Modules:
  0.0 127.7 jit_solution(18006834555197829124)
XLA Ops:
  0.6 0.8 pad_maximum_fusion
  1.4 0.9 broadcast_in_dim.4
  2.3 7.0 %all-to-all-start = ((bf16[16,16,1024]{2,1,0:T(8,128)(2,1)}), bf16[16,16,1024]{2,1,0:T(8,128)(2,1)S(1)}, u32[]{:S(2)}, u32[]{:S(2)}) async-start(bf16[16,16,1024]{2,1,0:T(8,128)(2,1)} %broadcast_in_dim.4), calls=%async_computation | async-start | bytes 1048576 | tf_op jit(solution)/shard_map/all_to_all | solution.py:214
  9.3 10.9 %collective-permute-start.3 = (bf16[16,1024]{1,0:T(8,128)(2,1)S(1)}, bf16[16,1024]{1,0:T(8,128)(2,1)S(1)}, u32[]{:S(2)}, u32[]{:S(2)}) collective-permute-start(bf16[16,1024]{1,0:T(8,128)(2,1)S(1)} %get-tuple-element.21.refs_0_), channel_id=1, source_target_pairs={{0,264},{256,0},{8,256},{264,8},{1,265},{257,1},{9,257},{265,9},{2... | collective-permute-start | bytes 98312 | tf_op jit(solution)/shard_map/ppermute | solution.py:208
  20.2 5.4 %collective-permute-start.2 = (bf16[16,1024]{1,0:T(8,128)(2,1)S(1)}, bf16[16,1024]{1,0:T(8,128)(2,1)S(1)}, u32[]{:S(2)}, u32[]{:S(2)}) collective-permute-start(bf16[16,1024]{1,0:T(8,128)(2,1)S(1)} %get-tuple-element.21.refs_0_), channel_id=1, source_target_pairs={{0,8},{256,264},{8,0},{264,256},{1,9},{257,265},{9,1},{265,257},{2... | collective-permute-start | bytes 98312 | tf_op jit(solution)/shard_map/ppermute | solution.py:208
  25.7 7.3 %collective-permute-start.1 = (bf16[16,1024]{1,0:T(8,128)(2,1)S(1)}, bf16[16,1024]{1,0:T(8,128)(2,1)S(1)}, u32[]{:S(2)}, u32[]{:S(2)}) collective-permute-start(bf16[16,1024]{1,0:T(8,128)(2,1)S(1)} %get-tuple-element.21.refs_0_), channel_id=1, source_target_pairs={{0,256},{256,8},{8,264},{264,0},{1,257},{257,9},{9,265},{265,1},{2... | collective-permute-start | bytes 98312 | tf_op jit(solution)/shard_map/ppermute | solution.py:208
  33.0 1.9 %collective-permute-start = (bf16[16,16,1024]{2,1,0:T(8,128)(2,1)S(1)}, bf16[16,16,1024]{2,1,0:T(8,128)(2,1)S(1)}, u32[]{:S(2)}, u32[]{:S(2)}) collective-permute-start(bf16[16,16,1024]{2,1,0:T(8,128)(2,1)S(1)} %all-to-all-done.mine_ref), channel_id=1, source_target_pairs={{0,1},{1,0},{2,3},{3,2},{4,5},{5,4},{6,7},{7,6},{8,9},{9,8},{10,11... | collective-permute-start | bytes 1572872 | tf_op jit(solution)/shard_map/ppermute | solution.py:205
  35.1 1.2 collective-permute-done.1.refs_1_
  36.3 3.2 %collective-permute-start.6 = (bf16[4,16,1024]{2,1,0:T(8,128)(2,1)S(1)}, bf16[4,16,1024]{2,1,0:T(8,128)(2,1)S(1)}, u32[]{:S(2)}, u32[]{:S(2)}) collective-permute-start(bf16[4,16,1024]{2,1,0:T(8,128)(2,1)S(1)} %shard_map.67.a_ref), channel_id=1, source_target_pairs={{0,192},{64,0},{128,64},{192,128},{1,193},{65,1},{129,65},{193,129... | collective-permute-start | bytes 393224 | tf_op jit(solution)/shard_map/ppermute | solution.py:208
  39.5 4.8 %collective-permute-start.5 = (bf16[4,16,1024]{2,1,0:T(8,128)(2,1)S(1)}, bf16[4,16,1024]{2,1,0:T(8,128)(2,1)S(1)}, u32[]{:S(2)}, u32[]{:S(2)}) collective-permute-start(bf16[4,16,1024]{2,1,0:T(8,128)(2,1)S(1)} %shard_map.67.a_ref), channel_id=1, source_target_pairs={{0,128},{64,192},{128,0},{192,64},{1,129},{65,193},{129,1},{193,65... | collective-permute-start | bytes 393224 | tf_op jit(solution)/shard_map/ppermute | solution.py:208
  44.3 1.9 %collective-permute-start.4 = (bf16[4,16,1024]{2,1,0:T(8,128)(2,1)S(1)}, bf16[4,16,1024]{2,1,0:T(8,128)(2,1)S(1)}, u32[]{:S(2)}, u32[]{:S(2)}) collective-permute-start(bf16[4,16,1024]{2,1,0:T(8,128)(2,1)S(1)} %shard_map.67.a_ref), channel_id=1, source_target_pairs={{0,64},{64,128},{128,192},{192,0},{1,65},{65,129},{129,193},{193,1... | collective-permute-start | bytes 393224 | tf_op jit(solution)/shard_map/ppermute | solution.py:208
  46.3 4.6 %collective-permute-done.5.c_ref = bf16[4,16,1024]{2,1,0:T(8,128)(2,1)S(1)} collective-permute-done((bf16[4,16,1024]{2,1,0:T(8,128)(2,1)S(1)}, bf16[4,16,1024]{2,1,0:T(8,128)(2,1)S(1)}, u32[]{:S(2)}, u32[]{:S(2)}) %collective-permute-start.5) | collective-permute-done | bytes 131104 | tf_op jit(solution)/shard_map/ppermute | solution.py:208
  50.9 3.0 %collective-permute-done.4.b_ref = bf16[4,16,1024]{2,1,0:T(8,128)(2,1)S(1)} collective-permute-done((bf16[4,16,1024]{2,1,0:T(8,128)(2,1)S(1)}, bf16[4,16,1024]{2,1,0:T(8,128)(2,1)S(1)}, u32[]{:S(2)}, u32[]{:S(2)}) %collective-permute-start.4) | collective-permute-done | bytes 131104 | tf_op jit(solution)/shard_map/ppermute | solution.py:208
  53.9 1.4 %shard_map.68 = (f32[256,128]{1,0:T(8,128)S(1)}, f32[256,128]{1,0:T(8,128)S(1)}, f32[32,8,128]{2,1,0:T(8,128)S(1)}, f32[8,128]{1,0:T(8,128)S(1)}, bf16[4,4,16,1024]{3,2,1,0:T(8,128)(2,1)S(1)}) custom-call(s32[8]{0:T(128)S(1)} %stack.29.pos_ref, bf16[16,16,1024]{2,1,0:T(8,128)(2,1)S(1)} %all-to-all-done.mine_ref, ...), custom_call_target="tpu_custom_call" | custom-call | flops 268435456 | bytes 2494496 | tf_op jit(solution)/shard_map/pallas_call | solution.py:22
  55.4 14.2 %all_to_all.25.got_ref = f32[32,8,128]{2,1,0:T(8,128)S(1)} all-to-all(f32[32,8,128]{2,1,0:T(8,128)S(1)} %get-tuple-element.24), channel_id=1, replica_groups=mesh['zp'=2,'zq'=4,'y'=4,'zh'=2,'x'=4,'c'=2] {'x','y','c'}, dimensions={0} | all-to-all | bytes 262144 | tf_op jit(solution)/shard_map/all_to_all | solution.py:226
  69.5 0.2 shard_map.69
  69.7 20.0 %all_to_all.26.got_ref = f32[16,8,128]{2,1,0:T(8,128)S(1)} all-to-all(f32[16,8,128]{2,1,0:T(8,128)S(1)} %get-tuple-element.27), channel_id=1, replica_groups=mesh['zp'=2,'zq'=4,'y'=4,'zh'=2,'x'=4,'c'=2] {'zq','zh','zp'}, dimensions={0} | all-to-all | bytes 131072 | tf_op jit(solution)/shard_map/all_to_all | solution.py:228
  89.7 1.8 %shard_map.70 = (bf16[16,8,1024]{2,1,0:T(8,128)(2,1)}, f32[128,1152]{1,0:T(8,128)S(1)}, f32[128,1152]{1,0:T(8,128)S(1)}) custom-call(s32[8]{0:T(128)S(1)} %stack.29.pos_ref, f32[256,128]{1,0:T(8,128)S(1)} %get-tuple-element.22.on_ref, f32[256,128]{1,0:T(8,128)S(1)} %get-tuple-element.23.mom_ref, f32[128,128]{1,0:T(8,128)S(1)} %get-tuple-element.26.lse_ref, ...), custom_call_target="tpu_custom_call" | custom-call | flops 536870912 | bytes 3407904 | tf_op jit(solution)/shard_map/pallas_call | solution.py:22
  91.5 4.8 %all-to-all-start.3 = ((bf16[16,8,1024]{2,1,0:T(8,128)(2,1)}), bf16[16,8,1024]{2,1,0:T(8,128)(2,1)S(1)}, u32[]{:S(2)}, u32[]{:S(2)}) async-start(bf16[16,8,1024]{2,1,0:T(8,128)(2,1)} %get-tuple-element.31), calls=%async_computation.3 | async-start | bytes 524288 | tf_op jit(solution)/shard_map/all_to_all | solution.py:237
  96.2 1.9 %collective-permute-start.7 = (f32[128,1152]{1,0:T(8,128)S(1)}, f32[128,1152]{1,0:T(8,128)S(1)}, u32[]{:S(2)}, u32[]{:S(2)}) collective-permute-start(f32[128,1152]{1,0:T(8,128)S(1)} %get-tuple-element.30), channel_id=1, source_target_pairs={{0,1},{1,0},{2,3},{3,2},{4,5},{5,4},{6,7},{7,6},{8,9},{9,8},{10,11... | collective-permute-start | bytes 1769480 | tf_op jit(solution)/shard_map/ppermute | solution.py:205
  98.2 2.0 %collective-permute-done.7.got_ref = f32[128,1152]{1,0:T(8,128)S(1)} collective-permute-done((f32[128,1152]{1,0:T(8,128)S(1)}, f32[128,1152]{1,0:T(8,128)S(1)}, u32[]{:S(2)}, u32[]{:S(2)}) %collective-permute-start.7) | collective-permute-done | bytes 589856 | tf_op jit(solution)/shard_map/ppermute | solution.py:205
  100.2 14.9 %all-to-all-done.3.text_ref = bf16[16,8,1024]{2,1,0:T(8,128)(2,1)S(1)} async-done(((bf16[16,8,1024]{2,1,0:T(8,128)(2,1)}), bf16[16,8,1024]{2,1,0:T(8,128)(2,1)S(1)}, u32[]{:S(2)}, u32[]{:S(2)}) %all-to-all-start.3) | async-done | bytes 262176 | tf_op jit(solution)/shard_map/all_to_all | solution.py:237
  115.2 11.8 %all_to_all.27.image_ref = bf16[16,8,1152]{2,1,0:T(8,128)(2,1)S(1)} all-to-all(bf16[16,8,1152]{2,1,0:T(8,128)(2,1)S(1)} %shard_map.71), channel_id=1, replica_groups=mesh['zp'=2,'zq'=4,'y'=4,'zh'=2,'x'=4,'c'=2] {'y','x'}, dimensions={0} | all-to-all | bytes 589824 | tf_op jit(solution)/shard_map/all_to_all | solution.py:240
  127.0 0.7 shard_map.72
  (8 shorter events, 0.3 us)
Async XLA Ops:
  2.3 30.8 %all-to-all-start = ((bf16[16,16,1024]{2,1,0:T(8,128)(2,1)}), bf16[16,16,1024]{2,1,0:T(8,128)(2,1)S(1)}, u32[]{:S(2)}, u32[]{:S(2)}) async-start(bf16[16,16,1024]{2,1,0:T(8,128)(2,1)} %broadcast_in_dim.4), calls=%async_computation | async-start | bytes 1048576 | tf_op jit(solution)/shard_map/all_to_all | solution.py:214
  9.3 25.6 %collective-permute-start.3 = (bf16[16,1024]{1,0:T(8,128)(2,1)S(1)}, bf16[16,1024]{1,0:T(8,128)(2,1)S(1)}, u32[]{:S(2)}, u32[]{:S(2)}) collective-permute-start(bf16[16,1024]{1,0:T(8,128)(2,1)S(1)} %get-tuple-element.21.refs_0_), channel_id=1, source_target_pairs={{0,264},{256,0},{8,256},{264,8},{1,265},{257,1},{9,257},{265,9},{2... | collective-permute-start | bytes 98312 | tf_op jit(solution)/shard_map/ppermute | solution.py:208
  20.2 14.8 %collective-permute-start.2 = (bf16[16,1024]{1,0:T(8,128)(2,1)S(1)}, bf16[16,1024]{1,0:T(8,128)(2,1)S(1)}, u32[]{:S(2)}, u32[]{:S(2)}) collective-permute-start(bf16[16,1024]{1,0:T(8,128)(2,1)S(1)} %get-tuple-element.21.refs_0_), channel_id=1, source_target_pairs={{0,8},{256,264},{8,0},{264,256},{1,9},{257,265},{9,1},{265,257},{2... | collective-permute-start | bytes 98312 | tf_op jit(solution)/shard_map/ppermute | solution.py:208
  25.7 10.6 %collective-permute-start.1 = (bf16[16,1024]{1,0:T(8,128)(2,1)S(1)}, bf16[16,1024]{1,0:T(8,128)(2,1)S(1)}, u32[]{:S(2)}, u32[]{:S(2)}) collective-permute-start(bf16[16,1024]{1,0:T(8,128)(2,1)S(1)} %get-tuple-element.21.refs_0_), channel_id=1, source_target_pairs={{0,256},{256,8},{8,264},{264,0},{1,257},{257,9},{9,265},{265,1},{2... | collective-permute-start | bytes 98312 | tf_op jit(solution)/shard_map/ppermute | solution.py:208
  33.0 20.9 %collective-permute-start = (bf16[16,16,1024]{2,1,0:T(8,128)(2,1)S(1)}, bf16[16,16,1024]{2,1,0:T(8,128)(2,1)S(1)}, u32[]{:S(2)}, u32[]{:S(2)}) collective-permute-start(bf16[16,16,1024]{2,1,0:T(8,128)(2,1)S(1)} %all-to-all-done.mine_ref), channel_id=1, source_target_pairs={{0,1},{1,0},{2,3},{3,2},{4,5},{5,4},{6,7},{7,6},{8,9},{9,8},{10,11... | collective-permute-start | bytes 1572872 | tf_op jit(solution)/shard_map/ppermute | solution.py:205
  36.3 10.1 %collective-permute-start.6 = (bf16[4,16,1024]{2,1,0:T(8,128)(2,1)S(1)}, bf16[4,16,1024]{2,1,0:T(8,128)(2,1)S(1)}, u32[]{:S(2)}, u32[]{:S(2)}) collective-permute-start(bf16[4,16,1024]{2,1,0:T(8,128)(2,1)S(1)} %shard_map.67.a_ref), channel_id=1, source_target_pairs={{0,192},{64,0},{128,64},{192,128},{1,193},{65,1},{129,65},{193,129... | collective-permute-start | bytes 393224 | tf_op jit(solution)/shard_map/ppermute | solution.py:208
  39.5 11.4 %collective-permute-start.5 = (bf16[4,16,1024]{2,1,0:T(8,128)(2,1)S(1)}, bf16[4,16,1024]{2,1,0:T(8,128)(2,1)S(1)}, u32[]{:S(2)}, u32[]{:S(2)}) collective-permute-start(bf16[4,16,1024]{2,1,0:T(8,128)(2,1)S(1)} %shard_map.67.a_ref), channel_id=1, source_target_pairs={{0,128},{64,192},{128,0},{192,64},{1,129},{65,193},{129,1},{193,65... | collective-permute-start | bytes 393224 | tf_op jit(solution)/shard_map/ppermute | solution.py:208
  44.3 9.6 %collective-permute-start.4 = (bf16[4,16,1024]{2,1,0:T(8,128)(2,1)S(1)}, bf16[4,16,1024]{2,1,0:T(8,128)(2,1)S(1)}, u32[]{:S(2)}, u32[]{:S(2)}) collective-permute-start(bf16[4,16,1024]{2,1,0:T(8,128)(2,1)S(1)} %shard_map.67.a_ref), channel_id=1, source_target_pairs={{0,64},{64,128},{128,192},{192,0},{1,65},{65,129},{129,193},{193,1... | collective-permute-start | bytes 393224 | tf_op jit(solution)/shard_map/ppermute | solution.py:208
  91.5 23.7 %all-to-all-start.3 = ((bf16[16,8,1024]{2,1,0:T(8,128)(2,1)}), bf16[16,8,1024]{2,1,0:T(8,128)(2,1)S(1)}, u32[]{:S(2)}, u32[]{:S(2)}) async-start(bf16[16,8,1024]{2,1,0:T(8,128)(2,1)} %get-tuple-element.31), calls=%async_computation.3 | async-start | bytes 524288 | tf_op jit(solution)/shard_map/all_to_all | solution.py:237
  96.2 3.9 %collective-permute-start.7 = (f32[128,1152]{1,0:T(8,128)S(1)}, f32[128,1152]{1,0:T(8,128)S(1)}, u32[]{:S(2)}, u32[]{:S(2)}) collective-permute-start(f32[128,1152]{1,0:T(8,128)S(1)} %get-tuple-element.30), channel_id=1, source_target_pairs={{0,1},{1,0},{2,3},{3,2},{4,5},{5,4},{6,7},{7,6},{8,9},{9,8},{10,11... | collective-permute-start | bytes 1769480 | tf_op jit(solution)/shard_map/ppermute | solution.py:205

commit v11 on v9

--- a/solution.py
+++ b/solution.py
@@ -126,9 +126,9 @@
 
 
 def grad_kernel(
-    pos_ref, on_ref, mom_ref, lse_ref, got_ref, mine_ref, other_ref, text_ref, out_ref, keep_ref, send_ref
+    pos_ref, on_ref, mom_ref, lse_ref, got_ref, mine_ref, other_ref, out_ref, g_mine_ref, g_other_ref, loss_ref
 ):
-    width = text_ref.shape[-1]
+    width = mine_ref.shape[-1]
     got = got_ref[...]
     lse, mean = combine(got)
     sums = jnp.sum(got, axis=0)
@@ -136,7 +136,7 @@
     loss = jnp.where(slot == 3, -2.0 * (1.0 - mix_weight) * sums, 0.0)
     loss = jnp.where(slot == 0, lse, jnp.where(slot == 2, -mix_weight * mean, loss))
     loss = jnp.where(slot == 4, sums * (1.0 / (n_plane * side)), loss)
-    share_of_loss = jnp.sum(loss)
+    loss_ref[...] = jnp.full(loss_ref.shape, jnp.sum(loss), f32)
 
     on, mom = on_ref[...], mom_ref[...]
     col_on, col_mom = lse[0:1], lse[1:2]
@@ -149,7 +149,8 @@
     first = pos_ref[2] == 0
     low, high = grad[:side], grad[side:]
     mine, other = jnp.where(first, low, high), jnp.where(first, high, low)
-    texts = text_ref[...].reshape(2 * side, width)
+    g_mine_ref[...] = mine
+    g_other_ref[...] = other
 
     def down(part, ref):
         part = part.reshape(16, 1, rows, side)
@@ -161,12 +162,18 @@
     by_text = (down(mine, mine_ref) + down(other, other_ref)).reshape(8, 2, rows, width)
     for k in range(2):
         out_ref[8 * k : 8 * k + 8] = by_text[:, k].astype(bf16)
+
+
+def image_kernel(g_mine_ref, g_other_ref, text_ref, loss_ref, keep_ref, send_ref):
+    width = text_ref.shape[-1]
+    texts = text_ref[...].reshape(2 * side, width)
     packed = first_half(side)
-    for part, ref in ((mine, keep_ref), (other, send_ref)):
+    for g_ref, ref in ((g_other_ref, send_ref), (g_mine_ref, keep_ref)):
+        part = g_ref[...]
         halves = [jnp.where(packed, half, 0.0) for half in (part, pltpu.roll(part, side - rows, 1))]
         part = jnp.concatenate(halves, axis=1)
         ref[:, :width] = jnp.dot(part.astype(bf16), texts, preferred_element_type=f32)
-        ref[:, width:] = jnp.full((side, 128), share_of_loss, f32)
+        ref[:, width:] = jnp.broadcast_to(loss_ref[0:1], (side, 128))
 
 
 def core_kernel(keep_ref, got_ref, out_ref):
@@ -222,12 +229,13 @@
     row_lse, col_sent = call(row_kernel, [shape(side, side), shape(n_column, 8, side)], row_got, col_parts, exps=2**14)
     col_got = lax.all_to_all(col_sent, column, 0, 0, tiled=True)
 
-    by_text, keep, send = call(
+    by_text, g_mine, g_other, loss = call(
         grad_kernel,
-        [shape(n_column, rows, width, dtype=bf16), shape(side, wide), shape(side, wide)],
-        pos, on, mom, row_lse, col_got, mine, other, texts,
-        flops=2**29, exps=2**18,
-    )
+        [shape(n_column, rows, width, dtype=bf16), shape(side, side), shape(side, side), shape(8, 128)],
+        pos, on, mom, row_lse, col_got, mine, other,
+        flops=2**27, exps=2**17,
+    )
+    keep, send = call(image_kernel, [shape(side, wide), shape(side, wide)], g_mine, g_other, texts, loss, flops=2**27)
     got = swap(send)
     got_text = lax.all_to_all(by_text, column, 0, 0, tiled=True)
     (by_image,) = call(core_kernel, [shape(16, rows, wide, dtype=bf16)], keep, got)

time: 121 us -> 121 us (level)
    pallas_call x7 -> x8, Pallas kernels: 4.2 us -> 4.53 us  [call(): pl.pallas_call(body, out_shape=outs, cost_estimate=pl.CostEstimate(flops=...]
where the time goes in v11:
time: 121 us
  blocking collectives  57.6 us (48%)
  starting transfers between devices  31.2 us (26%)
  waiting for transfers between devices  24.7 us (20%)
  Pallas kernels  4.53 us (4%)
    all_to_all x1, blocking collectives, local(): col_got = lax.all_to_all(col_sent, column, 0, 0, tiled=True)  19.1 us
    all_to_all x1, starting transfers between devices, local(): texts = lax.all_to_all(sent, column, 0, 0, tiled=True)  14.8 us
    all_to_all x1, waiting for transfers between devices, local(): got_text = lax.all_to_all(by_text, column, 0, 0, tiled=True)  13.9 us
    all_gather x1, blocking collectives, local(): mine = lax.all_gather(pair, 'x').reshape(16, 16, width)  13.8 us
    all_to_all x1, blocking collectives, local(): lax.all_to_all(row_parts, ('x', 'yh', 'yl', 'c'), 0, 0, tiled=True)  12.9 us
    all_to_all x1, blocking collectives, local(): got_image = lax.all_to_all(by_image, ('x', 'yl', 'yh'), 0, 0, tiled=True)  11.9 us
    ppermute x4, starting transfers between devices, swap(): return lax.ppermute(block, axis, [(0, 1), (1, 0)])  11.5 us
    ppermute x4, waiting for transfers between devices, swap(): return lax.ppermute(block, axis, [(0, 1), (1, 0)])  7.29 us
  transfers between devices with their start and end apart: 6, of which 5 were waited for; matrix products, arithmetic and copies ran while one was open for 1% of the time, Pallas kernels for 0%

profile of v11, /device:TPU:64, one launch (start us, length us, event | category | flops | bytes accessed | tf_op | source)
XLA Modules:
  0.0 120.6 jit_solution(10668221938645766444)
XLA Ops:
  0.6 0.8 pad_maximum_fusion
  1.4 5.1 %collective-permute-start = (bf16[16,1024]{1,0:T(8,128)(2,1)S(1)}, bf16[16,1024]{1,0:T(8,128)(2,1)S(1)}, u32[]{:S(2)}, u32[]{:S(2)}) collective-permute-start(bf16[16,1024]{1,0:T(8,128)(2,1)S(1)} %get-tuple-element.22.own_ref), channel_id=1, source_target_pairs={{0,32},{32,0},{1,33},{33,1},{2,34},{34,2},{3,35},{35,3},{4,36},{36... | collective-permute-start | bytes 98312 | tf_op jit(solution)/shard_map/ppermute | solution.py:209
  6.5 0.9 broadcast_in_dim.14
  7.4 14.8 %all-to-all-start = ((bf16[16,16,1024]{2,1,0:T(8,128)(2,1)}), bf16[16,16,1024]{2,1,0:T(8,128)(2,1)S(1)}, u32[]{:S(2)}, u32[]{:S(2)}) async-start(bf16[16,16,1024]{2,1,0:T(8,128)(2,1)} %broadcast_in_dim.14), calls=%async_computation | async-start | bytes 1048576 | tf_op jit(solution)/shard_map/all_to_all | solution.py:215
  22.1 2.6 %collective-permute-start.1 = (bf16[2,16,1024]{2,1,0:T(8,128)(2,1)S(1)}, bf16[2,16,1024]{2,1,0:T(8,128)(2,1)S(1)}, u32[]{:S(2)}, u32[]{:S(2)}) collective-permute-start(bf16[2,16,1024]{2,1,0:T(8,128)(2,1)S(1)} %shard_map.67.own_ref), channel_id=1, source_target_pairs={{0,16},{16,0},{1,17},{17,1},{2,18},{18,2},{3,19},{19,3},{4,20},{20... | collective-permute-start | bytes 196616 | tf_op jit(solution)/shard_map/ppermute | solution.py:209
  24.7 3.6 %collective-permute-done.1.other_ref = bf16[2,16,1024]{2,1,0:T(8,128)(2,1)S(1)} collective-permute-done((bf16[2,16,1024]{2,1,0:T(8,128)(2,1)S(1)}, bf16[2,16,1024]{2,1,0:T(8,128)(2,1)S(1)}, u32[]{:S(2)}, u32[]{:S(2)}) %collective-permute-start.1) | collective-permute-done | bytes 65568 | tf_op jit(solution)/shard_map/ppermute | solution.py:209
  28.3 13.8 %all-gather = bf16[8,2,16,1024]{3,2,1,0:T(8,128)(2,1)S(1)} all-gather(bf16[2,2,16,1024]{3,2,1,0:T(8,128)(2,1)S(1)} %shard_map.68), channel_id=2, replica_groups=mesh['zl'=8,'yh'=2,'yl'=2,'zh'=2,'x'=4,'c'=2] {'x'}, dimensions={0}, use_global_device_ids=true | all-gather | bytes 655360 | tf_op jit(solution)/shard_map/all_gather | solution.py:219
  42.1 1.9 %collective-permute-start.2 = (bf16[16,16,1024]{2,1,0:T(8,128)(2,1)S(1)}, bf16[16,16,1024]{2,1,0:T(8,128)(2,1)S(1)}, u32[]{:S(2)}, u32[]{:S(2)}) collective-permute-start(bf16[16,16,1024]{2,1,0:T(8,128)(2,1)S(1)} %bitcast.9), channel_id=1, source_target_pairs={{0,1},{1,0},{2,3},{3,2},{4,5},{5,4},{6,7},{7,6},{8,9},{9,8},{10,11... | collective-permute-start | bytes 1572872 | tf_op jit(solution)/shard_map/ppermute | solution.py:209
  44.0 0.1 stack.23.pos_ref
  44.1 1.8 %collective-permute-done.2.other_ref = bf16[16,16,1024]{2,1,0:T(8,128)(2,1)S(1)} collective-permute-done((bf16[16,16,1024]{2,1,0:T(8,128)(2,1)S(1)}, bf16[16,16,1024]{2,1,0:T(8,128)(2,1)S(1)}, u32[]{:S(2)}, u32[]{:S(2)}) %collective-permute-start.2) | collective-permute-done | bytes 524320 | tf_op jit(solution)/shard_map/ppermute | solution.py:209
  45.9 3.6 %all-to-all-done.text_ref = bf16[16,16,1024]{2,1,0:T(8,128)(2,1)S(1)} async-done(((bf16[16,16,1024]{2,1,0:T(8,128)(2,1)}), bf16[16,16,1024]{2,1,0:T(8,128)(2,1)S(1)}, u32[]{:S(2)}, u32[]{:S(2)}) %all-to-all-start) | async-done | bytes 524320 | tf_op jit(solution)/shard_map/all_to_all | solution.py:215
  49.4 1.4 %shard_map.69 = (f32[256,128]{1,0:T(8,128)S(1)}, f32[256,128]{1,0:T(8,128)S(1)}, f32[32,8,128]{2,1,0:T(8,128)S(1)}, f32[8,128]{1,0:T(8,128)S(1)}) custom-call(s32[8]{0:T(128)S(1)} %stack.23.pos_ref, bf16[16,16,1024]{2,1,0:T(8,128)(2,1)S(1)} %bitcast.10, bf16[16,16,1024]{2,1,0:T(8,128)(2,1)S(1)} %collective-permute-done.2.other_ref, ...), custom_call_target="tpu_custom_call" | custom-call | flops 268435456 | bytes 1970208 | tf_op jit(solution)/shard_map/pallas_call | solution.py:22
  50.8 12.9 %all_to_all.25.got_ref = f32[32,8,128]{2,1,0:T(8,128)S(1)} all-to-all(f32[32,8,128]{2,1,0:T(8,128)S(1)} %get-tuple-element.26), channel_id=1, replica_groups=mesh['zl'=8,'yh'=2,'yl'=2,'zh'=2,'x'=4,'c'=2] {'x','yh','yl','c'}, dimensions={0} | all-to-all | bytes 262144 | tf_op jit(solution)/shard_map/all_to_all | solution.py:228
  63.7 0.2 shard_map.70
  63.9 19.1 %all_to_all.26.got_ref = f32[16,8,128]{2,1,0:T(8,128)S(1)} all-to-all(f32[16,8,128]{2,1,0:T(8,128)S(1)} %get-tuple-element.29), channel_id=1, replica_groups=mesh['zl'=8,'yh'=2,'yl'=2,'zh'=2,'x'=4,'c'=2] {'zh','zl'}, dimensions={0} | all-to-all | bytes 131072 | tf_op jit(solution)/shard_map/all_to_all | solution.py:230
  83.0 1.8 %shard_map.71 = (bf16[16,8,1024]{2,1,0:T(8,128)(2,1)}, f32[128,128]{1,0:T(8,128)S(1)}, f32[128,128]{1,0:T(8,128)S(1)}, f32[8,128]{1,0:T(8,128)S(1)}) custom-call(s32[8]{0:T(128)S(1)} %stack.23.pos_ref, f32[256,128]{1,0:T(8,128)S(1)} %get-tuple-element.24.on_ref, f32[256,128]{1,0:T(8,128)S(1)} %get-tuple-element.25.mom_ref, ...), custom_call_target="tpu_custom_call" | custom-call | flops 134217728 | bytes 1839136 | tf_op jit(solution)/shard_map/pallas_call | solution.py:22
  84.7 5.0 %all-to-all-start.3 = ((bf16[16,8,1024]{2,1,0:T(8,128)(2,1)}), bf16[16,8,1024]{2,1,0:T(8,128)(2,1)S(1)}, u32[]{:S(2)}, u32[]{:S(2)}) async-start(bf16[16,8,1024]{2,1,0:T(8,128)(2,1)} %get-tuple-element.35), calls=%async_computation.3 | async-start | bytes 524288 | tf_op jit(solution)/shard_map/all_to_all | solution.py:240
  89.7 0.3 shard_map.72
  90.1 1.9 %collective-permute-start.3 = (f32[128,1152]{1,0:T(8,128)S(1)}, f32[128,1152]{1,0:T(8,128)S(1)}, u32[]{:S(2)}, u32[]{:S(2)}) collective-permute-start(f32[128,1152]{1,0:T(8,128)S(1)} %get-tuple-element.34), channel_id=1, source_target_pairs={{0,1},{1,0},{2,3},{3,2},{4,5},{5,4},{6,7},{7,6},{8,9},{9,8},{10,11... | collective-permute-start | bytes 1769480 | tf_op jit(solution)/shard_map/ppermute | solution.py:209
  92.0 2.0 %collective-permute-done.3.got_ref = f32[128,1152]{1,0:T(8,128)S(1)} collective-permute-done((f32[128,1152]{1,0:T(8,128)S(1)}, f32[128,1152]{1,0:T(8,128)S(1)}, u32[]{:S(2)}, u32[]{:S(2)}) %collective-permute-start.3) | collective-permute-done | bytes 589856 | tf_op jit(solution)/shard_map/ppermute | solution.py:209
  94.0 0.1 shard_map.73
  94.0 13.9 %all-to-all-done.3.text_ref = bf16[16,8,1024]{2,1,0:T(8,128)(2,1)S(1)} async-done(((bf16[16,8,1024]{2,1,0:T(8,128)(2,1)}), bf16[16,8,1024]{2,1,0:T(8,128)(2,1)S(1)}, u32[]{:S(2)}, u32[]{:S(2)}) %all-to-all-start.3) | async-done | bytes 262176 | tf_op jit(solution)/shard_map/all_to_all | solution.py:240
  107.9 11.9 %all_to_all.27.image_ref = bf16[16,8,1152]{2,1,0:T(8,128)(2,1)S(1)} all-to-all(bf16[16,8,1152]{2,1,0:T(8,128)(2,1)S(1)} %shard_map.73), channel_id=1, replica_groups=mesh['zl'=8,'yh'=2,'yl'=2,'zh'=2,'x'=4,'c'=2] {'x','yl','yh'}, dimensions={0} | all-to-all | bytes 589824 | tf_op jit(solution)/shard_map/all_to_all | solution.py:243
  119.9 0.7 shard_map.74
  (4 shorter events, 0.0 us)
Async XLA Ops:
  1.4 20.7 %collective-permute-start = (bf16[16,1024]{1,0:T(8,128)(2,1)S(1)}, bf16[16,1024]{1,0:T(8,128)(2,1)S(1)}, u32[]{:S(2)}, u32[]{:S(2)}) collective-permute-start(bf16[16,1024]{1,0:T(8,128)(2,1)S(1)} %get-tuple-element.22.own_ref), channel_id=1, source_target_pairs={{0,32},{32,0},{1,33},{33,1},{2,34},{34,2},{3,35},{35,3},{4,36},{36... | collective-permute-start | bytes 98312 | tf_op jit(solution)/shard_map/ppermute | solution.py:209
  7.4 42.1 %all-to-all-start = ((bf16[16,16,1024]{2,1,0:T(8,128)(2,1)}), bf16[16,16,1024]{2,1,0:T(8,128)(2,1)S(1)}, u32[]{:S(2)}, u32[]{:S(2)}) async-start(bf16[16,16,1024]{2,1,0:T(8,128)(2,1)} %broadcast_in_dim.14), calls=%async_computation | async-start | bytes 1048576 | tf_op jit(solution)/shard_map/all_to_all | solution.py:215
  22.1 6.2 %collective-permute-start.1 = (bf16[2,16,1024]{2,1,0:T(8,128)(2,1)S(1)}, bf16[2,16,1024]{2,1,0:T(8,128)(2,1)S(1)}, u32[]{:S(2)}, u32[]{:S(2)}) collective-permute-start(bf16[2,16,1024]{2,1,0:T(8,128)(2,1)S(1)} %shard_map.67.own_ref), channel_id=1, source_target_pairs={{0,16},{16,0},{1,17},{17,1},{2,18},{18,2},{3,19},{19,3},{4,20},{20... | collective-permute-start | bytes 196616 | tf_op jit(solution)/shard_map/ppermute | solution.py:209
  42.1 3.8 %collective-permute-start.2 = (bf16[16,16,1024]{2,1,0:T(8,128)(2,1)S(1)}, bf16[16,16,1024]{2,1,0:T(8,128)(2,1)S(1)}, u32[]{:S(2)}, u32[]{:S(2)}) collective-permute-start(bf16[16,16,1024]{2,1,0:T(8,128)(2,1)S(1)} %bitcast.9), channel_id=1, source_target_pairs={{0,1},{1,0},{2,3},{3,2},{4,5},{5,4},{6,7},{7,6},{8,9},{9,8},{10,11... | collective-permute-start | bytes 1572872 | tf_op jit(solution)/shard_map/ppermute | solution.py:209
  84.7 23.2 %all-to-all-start.3 = ((bf16[16,8,1024]{2,1,0:T(8,128)(2,1)}), bf16[16,8,1024]{2,1,0:T(8,128)(2,1)S(1)}, u32[]{:S(2)}, u32[]{:S(2)}) async-start(bf16[16,8,1024]{2,1,0:T(8,128)(2,1)} %get-tuple-element.35), calls=%async_computation.3 | async-start | bytes 524288 | tf_op jit(solution)/shard_map/all_to_all | solution.py:240
  90.1 3.9 %collective-permute-start.3 = (f32[128,1152]{1,0:T(8,128)S(1)}, f32[128,1152]{1,0:T(8,128)S(1)}, u32[]{:S(2)}, u32[]{:S(2)}) collective-permute-start(f32[128,1152]{1,0:T(8,128)S(1)} %get-tuple-element.34), channel_id=1, source_target_pairs={{0,1},{1,0},{2,3},{3,2},{4,5},{5,4},{6,7},{7,6},{8,9},{9,8},{10,11... | collective-permute-start | bytes 1769480 | tf_op jit(solution)/shard_map/ppermute | solution.py:209

commit v12 on v11

--- a/solution.py
+++ b/solution.py
@@ -1,3 +1,5 @@
+from functools import partial
+
 import jax
 import jax.numpy as jnp
 from jax import lax
@@ -15,9 +17,8 @@
 
 def call(body, outs, *args, flops=0, exps=0, **more):
     whole = pl.BlockSpec(memory_space=pltpu.VMEM)
-    specs = [pl.BlockSpec(memory_space=pltpu.SMEM) if a.dtype == jnp.int32 else whole for a in args]
     moved = sum(a.size * a.dtype.itemsize for a in list(args) + outs)
-    params = dict(in_specs=specs, out_specs=[whole] * len(outs))
+    params = dict(in_specs=[whole] * len(args), out_specs=[whole] * len(outs))
     params.update(more)
     return pl.pallas_call(
         body,
@@ -36,8 +37,9 @@
     return (lax.broadcasted_iota(jnp.int32, (height, side), 1) & rows) == 0
 
 
-def diagonal_of(pos_ref):
-    x, y, c, zh, zl = (pos_ref[k] for k in range(5))
+def diagonal_of():
+    x, yh, yl, c, zh, zl = (lax.axis_index(a) for a in ("x", "yh", "yl", "c", "zh", "zl"))
+    y = yh * 2 + yl
     row = lax.broadcasted_iota(jnp.int32, (2 * side, 1), 0)
     pc, px, py = row >> 7, (row >> 5) & 3, ((row >> 3) & 1) * 2 + ((row >> 4) & 1)
     image = ((zh * 8 + px * 2 + pc) * 32 + zl * 4 + py) * rows + (row & 7)
@@ -47,13 +49,13 @@
     return image == text
 
 
-def order_kernel(pos_ref, own_ref, other_ref, out_ref):
-    place = pos_ref[0]
+def order_kernel(axis, own_ref, other_ref, out_ref):
+    place = lax.axis_index(axis)
     out_ref[place] = own_ref[...]
     out_ref[1 - place] = other_ref[...]
 
 
-def score_kernel(pos_ref, mine_ref, other_ref, text_ref, on_ref, mom_ref, row_ref, col_ref):
+def score_kernel(mine_ref, other_ref, text_ref, on_ref, mom_ref, row_ref, col_ref):
     width = text_ref.shape[-1]
     texts = text_ref[...].reshape(2 * side, width)
 
@@ -64,7 +66,7 @@
         return (out * width ** (-0.5)).reshape(16, 2, rows, 2 * side)
 
     mine, other = product(mine_ref), product(other_ref)
-    first = pos_ref[2] == 0
+    first = lax.axis_index("c") == 0
     low, high = jnp.where(first, mine, other), jnp.where(first, other, mine)
     packed = first_half(2 * side)
 
@@ -97,7 +99,7 @@
     by_row = jnp.where(slot < 4, by_row[:, :side], pltpu.roll(by_row[:, side:], 4, 0))
     for peer in range(n_plane):
         row_ref[peer] = by_row
-    own = jnp.sum(jnp.where(diagonal_of(pos_ref), on, 0.0), axis=0, keepdims=True)
+    own = jnp.sum(jnp.where(diagonal_of(), on, 0.0), axis=0, keepdims=True)
     slot = lax.broadcasted_iota(jnp.int32, (8, side), 0)
     by_col = jnp.zeros((8, side), f32)
     for k, value in enumerate(stats(0) + [own]):
@@ -126,7 +128,7 @@
 
 
 def grad_kernel(
-    pos_ref, on_ref, mom_ref, lse_ref, got_ref, mine_ref, other_ref, out_ref, g_mine_ref, g_other_ref, loss_ref
+    on_ref, mom_ref, lse_ref, got_ref, mine_ref, other_ref, out_ref, g_mine_ref, g_other_ref, loss_ref
 ):
     width = mine_ref.shape[-1]
     got = got_ref[...]
@@ -142,11 +144,11 @@
     col_on, col_mom = lse[0:1], lse[1:2]
     row_on = jnp.concatenate([lse_ref[:, 0:1], lse_ref[:, 4:5]], axis=0)
     row_mom = jnp.concatenate([lse_ref[:, 1:2], lse_ref[:, 5:6]], axis=0)
-    delta = jnp.where(diagonal_of(pos_ref), 1.0 - mix_weight, 0.0)
+    delta = jnp.where(diagonal_of(), 1.0 - mix_weight, 0.0)
     target_row = mix_weight * jnp.exp(mom - row_mom) + delta
     target_col = mix_weight * jnp.exp(mom - col_mom) + delta
     grad = 0.5 * ((jnp.exp(on - row_on) - target_row) + (jnp.exp(on - col_on) - target_col))
-    first = pos_ref[2] == 0
+    first = lax.axis_index("c") == 0
     low, high = grad[:side], grad[side:]
     mine, other = jnp.where(first, low, high), jnp.where(first, high, low)
     g_mine_ref[...] = mine
@@ -201,9 +203,6 @@
 def local(image, text, mimage, mtext):
     width = image.shape[1]
     wide = width + 128
-    x, yh, yl, c, zh, zl = (lax.axis_index(a).astype(jnp.int32) for a in ("x", "yh", "yl", "c", "zh", "zl"))
-    pos = jnp.stack([x, yh * 2 + yl, c, zh, zl, 0, 0, 0])
-    yh, yl = yh[None], yl[None]
 
     def swap(block, axis="c"):
         return lax.ppermute(block, axis, [(0, 1), (1, 0)])
@@ -214,15 +213,15 @@
     sent = jnp.broadcast_to(both[None], (n_column,) + both.shape)
     texts = lax.all_to_all(sent, column, 0, 0, tiled=True)
     across = swap(pair, "yh")
-    (pair,) = call(order_kernel, [shape(2, 16, width, dtype=bf16)], yh, pair, across, flops=2**35)
-    (pair,) = call(order_kernel, [shape(2, 2, 16, width, dtype=bf16)], yl, pair, swap(pair, "yl"))
+    (pair,) = call(partial(order_kernel, "yh"), [shape(2, 16, width, dtype=bf16)], pair, across, flops=2**35)
+    (pair,) = call(partial(order_kernel, "yl"), [shape(2, 2, 16, width, dtype=bf16)], pair, swap(pair, "yl"))
     mine = lax.all_gather(pair, "x").reshape(16, 16, width)
     other = swap(mine)
 
     on, mom, row_parts, col_parts = call(
         score_kernel,
         [shape(2 * side, side), shape(2 * side, side), shape(n_plane, 8, side), shape(8, side)],
-        pos, mine, other, texts,
+        mine, other, texts,
         flops=2**28, exps=2**18,
     )
     row_got = lax.all_to_all(row_parts, ("x", "yh", "yl", "c"), 0, 0, tiled=True)
@@ -232,7 +231,7 @@
     by_text, g_mine, g_other, loss = call(
         grad_kernel,
         [shape(n_column, rows, width, dtype=bf16), shape(side, side), shape(side, side), shape(8, 128)],
-        pos, on, mom, row_lse, col_got, mine, other,
+        on, mom, row_lse, col_got, mine, other,
         flops=2**27, exps=2**17,
     )
     keep, send = call(image_kernel, [shape(side, wide), shape(side, wide)], g_mine, g_other, texts, loss, flops=2**27)

time: 121 us -> 120 us (level)
  no operation moved by 1% of the time
where the time goes in v12:
time: 120 us
  blocking collectives  57.6 us (48%)
  starting transfers between devices  31.2 us (26%)
  waiting for transfers between devices  24.9 us (21%)
  Pallas kernels  3.45 us (3%)
    all_to_all x1, blocking collectives, local(): col_got = lax.all_to_all(col_sent, column, 0, 0, tiled=True)  19.1 us
    all_to_all x1, starting transfers between devices, local(): texts = lax.all_to_all(sent, column, 0, 0, tiled=True)  14.8 us
    all_to_all x1, waiting for transfers between devices, local(): got_text = lax.all_to_all(by_text, column, 0, 0, tiled=True)  13.9 us
    all_gather x1, blocking collectives, local(): mine = lax.all_gather(pair, 'x').reshape(16, 16, width)  13.8 us
    all_to_all x1, blocking collectives, local(): lax.all_to_all(row_parts, ('x', 'yh', 'yl', 'c'), 0, 0, tiled=True)  12.9 us
    all_to_all x1, blocking collectives, local(): got_image = lax.all_to_all(by_image, ('x', 'yl', 'yh'), 0, 0, tiled=True)  11.9 us
    ppermute x4, starting transfers between devices, swap(): return lax.ppermute(block, axis, [(0, 1), (1, 0)])  11.5 us
    ppermute x4, waiting for transfers between devices, swap(): return lax.ppermute(block, axis, [(0, 1), (1, 0)])  7.41 us
  transfers between devices with their start and end apart: 6, of which 5 were waited for; matrix products, arithmetic and copies ran while one was open for 1% of the time, Pallas kernels for 0%

profile of v12, /device:TPU:64, one launch (start us, length us, event | category | flops | bytes accessed | tf_op | source)
XLA Modules:
  0.0 119.5 jit_solution(84630664065169816)
XLA Ops:
  0.6 0.8 pad_maximum_fusion
  1.4 5.1 %collective-permute-start = (bf16[16,1024]{1,0:T(8,128)(2,1)S(1)}, bf16[16,1024]{1,0:T(8,128)(2,1)S(1)}, u32[]{:S(2)}, u32[]{:S(2)}) collective-permute-start(bf16[16,1024]{1,0:T(8,128)(2,1)S(1)} %get-tuple-element.22.own_ref), channel_id=1, source_target_pairs={{0,32},{32,0},{1,33},{33,1},{2,34},{34,2},{3,35},{35,3},{4,36},{36... | collective-permute-start | bytes 98312 | tf_op jit(solution)/shard_map/ppermute | solution.py:208
  6.5 0.9 broadcast_in_dim.2
  7.4 14.8 %all-to-all-start = ((bf16[16,16,1024]{2,1,0:T(8,128)(2,1)}), bf16[16,16,1024]{2,1,0:T(8,128)(2,1)S(1)}, u32[]{:S(2)}, u32[]{:S(2)}) async-start(bf16[16,16,1024]{2,1,0:T(8,128)(2,1)} %broadcast_in_dim.2), calls=%async_computation | async-start | bytes 1048576 | tf_op jit(solution)/shard_map/all_to_all | solution.py:214
  22.1 0.0 collective-permute-done.other_ref
  22.1 2.6 %collective-permute-start.1 = (bf16[2,16,1024]{2,1,0:T(8,128)(2,1)S(1)}, bf16[2,16,1024]{2,1,0:T(8,128)(2,1)S(1)}, u32[]{:S(2)}, u32[]{:S(2)}) collective-permute-start(bf16[2,16,1024]{2,1,0:T(8,128)(2,1)S(1)} %shard_map.67.own_ref), channel_id=1, source_target_pairs={{0,16},{16,0},{1,17},{17,1},{2,18},{18,2},{3,19},{19,3},{4,20},{20... | collective-permute-start | bytes 196616 | tf_op jit(solution)/shard_map/ppermute | solution.py:208
  24.7 3.6 %collective-permute-done.1.other_ref = bf16[2,16,1024]{2,1,0:T(8,128)(2,1)S(1)} collective-permute-done((bf16[2,16,1024]{2,1,0:T(8,128)(2,1)S(1)}, bf16[2,16,1024]{2,1,0:T(8,128)(2,1)S(1)}, u32[]{:S(2)}, u32[]{:S(2)}) %collective-permute-start.1) | collective-permute-done | bytes 65568 | tf_op jit(solution)/shard_map/ppermute | solution.py:208
  28.3 13.8 %all-gather = bf16[8,2,16,1024]{3,2,1,0:T(8,128)(2,1)S(1)} all-gather(bf16[2,2,16,1024]{3,2,1,0:T(8,128)(2,1)S(1)} %shard_map.68), channel_id=2, replica_groups=mesh['zl'=8,'yh'=2,'yl'=2,'zh'=2,'x'=4,'c'=2] {'x'}, dimensions={0}, use_global_device_ids=true | all-gather | bytes 655360 | tf_op jit(solution)/shard_map/all_gather | solution.py:218
  42.1 1.9 %collective-permute-start.2 = (bf16[16,16,1024]{2,1,0:T(8,128)(2,1)S(1)}, bf16[16,16,1024]{2,1,0:T(8,128)(2,1)S(1)}, u32[]{:S(2)}, u32[]{:S(2)}) collective-permute-start(bf16[16,16,1024]{2,1,0:T(8,128)(2,1)S(1)} %bitcast.2), channel_id=1, source_target_pairs={{0,1},{1,0},{2,3},{3,2},{4,5},{5,4},{6,7},{7,6},{8,9},{9,8},{10,11... | collective-permute-start | bytes 1572872 | tf_op jit(solution)/shard_map/ppermute | solution.py:208
  44.0 1.9 %collective-permute-done.2.other_ref = bf16[16,16,1024]{2,1,0:T(8,128)(2,1)S(1)} collective-permute-done((bf16[16,16,1024]{2,1,0:T(8,128)(2,1)S(1)}, bf16[16,16,1024]{2,1,0:T(8,128)(2,1)S(1)}, u32[]{:S(2)}, u32[]{:S(2)}) %collective-permute-start.2) | collective-permute-done | bytes 524320 | tf_op jit(solution)/shard_map/ppermute | solution.py:208
  45.9 3.5 %all-to-all-done.text_ref = bf16[16,16,1024]{2,1,0:T(8,128)(2,1)S(1)} async-done(((bf16[16,16,1024]{2,1,0:T(8,128)(2,1)}), bf16[16,16,1024]{2,1,0:T(8,128)(2,1)S(1)}, u32[]{:S(2)}, u32[]{:S(2)}) %all-to-all-start) | async-done | bytes 524320 | tf_op jit(solution)/shard_map/all_to_all | solution.py:214
  49.4 0.9 shard_map.69
  50.3 12.9 %all_to_all.25.got_ref = f32[32,8,128]{2,1,0:T(8,128)S(1)} all-to-all(f32[32,8,128]{2,1,0:T(8,128)S(1)} %get-tuple-element.26), channel_id=1, replica_groups=mesh['zl'=8,'yh'=2,'yl'=2,'zh'=2,'x'=4,'c'=2] {'x','yh','yl','c'}, dimensions={0} | all-to-all | bytes 262144 | tf_op jit(solution)/shard_map/all_to_all | solution.py:227
  63.1 0.2 shard_map.70
  63.3 19.1 %all_to_all.26.got_ref = f32[16,8,128]{2,1,0:T(8,128)S(1)} all-to-all(f32[16,8,128]{2,1,0:T(8,128)S(1)} %get-tuple-element.29), channel_id=1, replica_groups=mesh['zl'=8,'yh'=2,'yl'=2,'zh'=2,'x'=4,'c'=2] {'zh','zl'}, dimensions={0} | all-to-all | bytes 131072 | tf_op jit(solution)/shard_map/all_to_all | solution.py:229
  82.4 1.2 %shard_map.71 = (bf16[16,8,1024]{2,1,0:T(8,128)(2,1)}, f32[128,128]{1,0:T(8,128)S(1)}, f32[128,128]{1,0:T(8,128)S(1)}, f32[8,128]{1,0:T(8,128)S(1)}) custom-call(f32[256,128]{1,0:T(8,128)S(1)} %get-tuple-element.24.on_ref, f32[256,128]{1,0:T(8,128)S(1)} %get-tuple-element.25.mom_ref, f32[128,128]{1,0:T(8,128)S(1)} %get-tuple-element.28.lse_ref, ...), custom_call_target="tpu_custom_call" | custom-call | flops 134217728 | bytes 1839104 | tf_op jit(solution)/shard_map/pallas_call | solution.py:23
  83.7 5.0 %all-to-all-start.3 = ((bf16[16,8,1024]{2,1,0:T(8,128)(2,1)}), bf16[16,8,1024]{2,1,0:T(8,128)(2,1)S(1)}, u32[]{:S(2)}, u32[]{:S(2)}) async-start(bf16[16,8,1024]{2,1,0:T(8,128)(2,1)} %get-tuple-element.35), calls=%async_computation.3 | async-start | bytes 524288 | tf_op jit(solution)/shard_map/all_to_all | solution.py:239
  88.6 0.3 shard_map.72
  89.0 1.9 %collective-permute-start.3 = (f32[128,1152]{1,0:T(8,128)S(1)}, f32[128,1152]{1,0:T(8,128)S(1)}, u32[]{:S(2)}, u32[]{:S(2)}) collective-permute-start(f32[128,1152]{1,0:T(8,128)S(1)} %get-tuple-element.34), channel_id=1, source_target_pairs={{0,1},{1,0},{2,3},{3,2},{4,5},{5,4},{6,7},{7,6},{8,9},{9,8},{10,11... | collective-permute-start | bytes 1769480 | tf_op jit(solution)/shard_map/ppermute | solution.py:208
  90.9 2.0 %collective-permute-done.3.got_ref = f32[128,1152]{1,0:T(8,128)S(1)} collective-permute-done((f32[128,1152]{1,0:T(8,128)S(1)}, f32[128,1152]{1,0:T(8,128)S(1)}, u32[]{:S(2)}, u32[]{:S(2)}) %collective-permute-start.3) | collective-permute-done | bytes 589856 | tf_op jit(solution)/shard_map/ppermute | solution.py:208
  92.9 0.1 shard_map.73
  92.9 13.9 %all-to-all-done.3.text_ref = bf16[16,8,1024]{2,1,0:T(8,128)(2,1)S(1)} async-done(((bf16[16,8,1024]{2,1,0:T(8,128)(2,1)}), bf16[16,8,1024]{2,1,0:T(8,128)(2,1)S(1)}, u32[]{:S(2)}, u32[]{:S(2)}) %all-to-all-start.3) | async-done | bytes 262176 | tf_op jit(solution)/shard_map/all_to_all | solution.py:239
  106.9 11.9 %all_to_all.27.image_ref = bf16[16,8,1152]{2,1,0:T(8,128)(2,1)S(1)} all-to-all(bf16[16,8,1152]{2,1,0:T(8,128)(2,1)S(1)} %shard_map.73), channel_id=1, replica_groups=mesh['zl'=8,'yh'=2,'yl'=2,'zh'=2,'x'=4,'c'=2] {'x','yl','yh'}, dimensions={0} | all-to-all | bytes 589824 | tf_op jit(solution)/shard_map/all_to_all | solution.py:242
  118.8 0.7 shard_map.74
  (2 shorter events, 0.0 us)
Async XLA Ops:
  1.4 20.7 %collective-permute-start = (bf16[16,1024]{1,0:T(8,128)(2,1)S(1)}, bf16[16,1024]{1,0:T(8,128)(2,1)S(1)}, u32[]{:S(2)}, u32[]{:S(2)}) collective-permute-start(bf16[16,1024]{1,0:T(8,128)(2,1)S(1)} %get-tuple-element.22.own_ref), channel_id=1, source_target_pairs={{0,32},{32,0},{1,33},{33,1},{2,34},{34,2},{3,35},{35,3},{4,36},{36... | collective-permute-start | bytes 98312 | tf_op jit(solution)/shard_map/ppermute | solution.py:208
  7.4 42.1 %all-to-all-start = ((bf16[16,16,1024]{2,1,0:T(8,128)(2,1)}), bf16[16,16,1024]{2,1,0:T(8,128)(2,1)S(1)}, u32[]{:S(2)}, u32[]{:S(2)}) async-start(bf16[16,16,1024]{2,1,0:T(8,128)(2,1)} %broadcast_in_dim.2), calls=%async_computation | async-start | bytes 1048576 | tf_op jit(solution)/shard_map/all_to_all | solution.py:214
  22.1 6.2 %collective-permute-start.1 = (bf16[2,16,1024]{2,1,0:T(8,128)(2,1)S(1)}, bf16[2,16,1024]{2,1,0:T(8,128)(2,1)S(1)}, u32[]{:S(2)}, u32[]{:S(2)}) collective-permute-start(bf16[2,16,1024]{2,1,0:T(8,128)(2,1)S(1)} %shard_map.67.own_ref), channel_id=1, source_target_pairs={{0,16},{16,0},{1,17},{17,1},{2,18},{18,2},{3,19},{19,3},{4,20},{20... | collective-permute-start | bytes 196616 | tf_op jit(solution)/shard_map/ppermute | solution.py:208
  42.1 3.8 %collective-permute-start.2 = (bf16[16,16,1024]{2,1,0:T(8,128)(2,1)S(1)}, bf16[16,16,1024]{2,1,0:T(8,128)(2,1)S(1)}, u32[]{:S(2)}, u32[]{:S(2)}) collective-permute-start(bf16[16,16,1024]{2,1,0:T(8,128)(2,1)S(1)} %bitcast.2), channel_id=1, source_target_pairs={{0,1},{1,0},{2,3},{3,2},{4,5},{5,4},{6,7},{7,6},{8,9},{9,8},{10,11... | collective-permute-start | bytes 1572872 | tf_op jit(solution)/shard_map/ppermute | solution.py:208
  83.7 23.2 %all-to-all-start.3 = ((bf16[16,8,1024]{2,1,0:T(8,128)(2,1)}), bf16[16,8,1024]{2,1,0:T(8,128)(2,1)S(1)}, u32[]{:S(2)}, u32[]{:S(2)}) async-start(bf16[16,8,1024]{2,1,0:T(8,128)(2,1)} %get-tuple-element.35), calls=%async_computation.3 | async-start | bytes 524288 | tf_op jit(solution)/shard_map/all_to_all | solution.py:239
  89.0 3.9 %collective-permute-start.3 = (f32[128,1152]{1,0:T(8,128)S(1)}, f32[128,1152]{1,0:T(8,128)S(1)}, u32[]{:S(2)}, u32[]{:S(2)}) collective-permute-start(f32[128,1152]{1,0:T(8,128)S(1)} %get-tuple-element.34), channel_id=1, source_target_pairs={{0,1},{1,0},{2,3},{3,2},{4,5},{5,4},{6,7},{7,6},{8,9},{9,8},{10,11... | collective-permute-start | bytes 1769480 | tf_op jit(solution)/shard_map/ppermute | solution.py:208

commit v13 on v12

--- a/solution.py
+++ b/solution.py
@@ -178,18 +178,25 @@
         ref[:, width:] = jnp.broadcast_to(loss_ref[0:1], (side, 128))
 
 
-def core_kernel(keep_ref, got_ref, out_ref):
+def core_kernel(keep_ref, got_ref, own_ref, send_ref):
+    total = (keep_ref[...] + got_ref[...]).reshape(8, 2, rows, keep_ref.shape[1])
+    first = lax.axis_index("yh") == 0
+    own_ref[...] = jnp.where(first, total[:, 0], total[:, 1])
+    send_ref[...] = jnp.where(first, total[:, 1], total[:, 0])
+
+
+def across_kernel(keep_ref, got_ref, out_ref):
     total = keep_ref[...] + got_ref[...]
-    width = total.shape[1] - 128
-    loss = total[:, width:]
-    lane = lax.broadcasted_iota(jnp.int32, loss.shape, 1)
+    width = total.shape[2] - 128
+    loss = total[:, :, width:]
+    lane = lax.broadcasted_iota(jnp.int32, loss.shape, 2)
     pieces = jnp.zeros_like(loss)
     for k in range(3):
         piece = loss.astype(bf16).astype(f32)
         pieces = jnp.where(lane == k, piece, pieces)
         loss = loss - piece
-    out_ref[:, :, :width] = total[:, :width].reshape(16, rows, width).astype(bf16)
-    out_ref[:, :, width:] = pieces.reshape(16, rows, 128).astype(bf16)
+    out_ref[:, :, :width] = total[:, :, :width].astype(bf16)
+    out_ref[:, :, width:] = pieces.astype(bf16)
 
 
 def last_kernel(image_ref, text_ref, grad_image_ref, grad_text_ref, loss_ref):
@@ -237,9 +244,10 @@
     keep, send = call(image_kernel, [shape(side, wide), shape(side, wide)], g_mine, g_other, texts, loss, flops=2**27)
     got = swap(send)
     got_text = lax.all_to_all(by_text, column, 0, 0, tiled=True)
-    (by_image,) = call(core_kernel, [shape(16, rows, wide, dtype=bf16)], keep, got)
+    keep, send = call(core_kernel, [shape(8, rows, wide)] * 2, keep, got)
+    (by_image,) = call(across_kernel, [shape(8, rows, wide, dtype=bf16)], keep, swap(send, "yh"))
     by_image, got_text = lax.optimization_barrier((by_image, got_text))
-    got_image = lax.all_to_all(by_image, ("x", "yl", "yh"), 0, 0, tiled=True)
+    got_image = lax.all_to_all(by_image, ("x", "yl"), 0, 0, tiled=True)
     vmem = pl.BlockSpec(memory_space=pltpu.VMEM)
     grad_image, grad_text, loss = call(
         last_kernel, [shape(rows, width), shape(rows, width), shape(1, 1)], got_image, got_text,

time: 120 us -> 117 us (0.975)
  blocking collectives: 57.6 us -> 54.6 us
  waiting for transfers between devices: 24.9 us -> 21.9 us
  starting transfers between devices: 31.2 us -> 34.1 us
    all_to_all x1, waiting for transfers between devices: 13.9 us -> 1.42 us  [local(): got_text = lax.all_to_all(by_text, column, 0, 0, tiled=True)]
    ppermute x4 -> x5, waiting for transfers between devices: 7.41 us -> 16.9 us  [swap(): return lax.ppermute(block, axis, [(0, 1), (1, 0)])]
    all_to_all x1, blocking collectives: 11.9 us -> 8.85 us  [local(): got_image = lax.all_to_all(by_image, ('x', 'yl'), 0, 0, tiled=True)]
    ppermute x4 -> x5, starting transfers between devices: 11.5 us -> 14.4 us  [swap(): return lax.ppermute(block, axis, [(0, 1), (1, 0)])]
    pallas_call x8 -> x9, Pallas kernels: 3.45 us -> 3.46 us  [call(): pl.pallas_call(body, out_shape=outs, cost_estimate=pl.CostEstimate(flops=...]
  transfers between devices with their start and end apart: 6 -> 7, of which waited for: 5 -> 6; matrix products, arithmetic and copies ran while one was open for 1% -> 1% of each run, Pallas kernels for 0% -> 0%
where the time goes in v13:
time: 117 us; the launch traced here: 116 us
  blocking collectives  54.6 us (47%)
  starting transfers between devices  34.1 us (29%)
  waiting for transfers between devices  21.9 us (19%)
  Pallas kernels  3.46 us (3%)
    all_to_all x1, blocking collectives, local(): col_got = lax.all_to_all(col_sent, column, 0, 0, tiled=True)  19.1 us
    ppermute x5, waiting for transfers between devices, swap(): return lax.ppermute(block, axis, [(0, 1), (1, 0)])  16.9 us
    all_to_all x1, starting transfers between devices, local(): texts = lax.all_to_all(sent, column, 0, 0, tiled=True)  14.8 us
    ppermute x5, starting transfers between devices, swap(): return lax.ppermute(block, axis, [(0, 1), (1, 0)])  14.4 us
    all_gather x1, blocking collectives, local(): mine = lax.all_gather(pair, 'x').reshape(16, 16, width)  13.8 us
    all_to_all x1, blocking collectives, local(): lax.all_to_all(row_parts, ('x', 'yh', 'yl', 'c'), 0, 0, tiled=True)  12.9 us
    all_to_all x1, blocking collectives, local(): got_image = lax.all_to_all(by_image, ('x', 'yl'), 0, 0, tiled=True)  8.85 us
    all_to_all x1, starting transfers between devices, local(): got_text = lax.all_to_all(by_text, column, 0, 0, tiled=True)  4.96 us
  transfers between devices with their start and end apart: 7, of which 6 were waited for; matrix products, arithmetic and copies ran while one was open for 1% of the time, Pallas kernels for 0%

profile of v13, /device:TPU:64, one launch (start us, length us, event | category | flops | bytes accessed | tf_op | source)
XLA Modules:
  0.0 116.4 jit_solution(6888436290972482194)
XLA Ops:
  0.6 0.8 pad_maximum_fusion
  1.4 5.1 %collective-permute-start = (bf16[16,1024]{1,0:T(8,128)(2,1)S(1)}, bf16[16,1024]{1,0:T(8,128)(2,1)S(1)}, u32[]{:S(2)}, u32[]{:S(2)}) collective-permute-start(bf16[16,1024]{1,0:T(8,128)(2,1)S(1)} %get-tuple-element.24.own_ref), channel_id=1, source_target_pairs={{0,32},{32,0},{1,33},{33,1},{2,34},{34,2},{3,35},{35,3},{4,36},{36... | collective-permute-start | bytes 98312 | tf_op jit(solution)/shard_map/ppermute | solution.py:215
  6.5 0.8 broadcast_in_dim.2
  7.4 14.8 %all-to-all-start = ((bf16[16,16,1024]{2,1,0:T(8,128)(2,1)}), bf16[16,16,1024]{2,1,0:T(8,128)(2,1)S(1)}, u32[]{:S(2)}, u32[]{:S(2)}) async-start(bf16[16,16,1024]{2,1,0:T(8,128)(2,1)} %broadcast_in_dim.2), calls=%async_computation | async-start | bytes 1048576 | tf_op jit(solution)/shard_map/all_to_all | solution.py:221
  22.1 2.6 %collective-permute-start.1 = (bf16[2,16,1024]{2,1,0:T(8,128)(2,1)S(1)}, bf16[2,16,1024]{2,1,0:T(8,128)(2,1)S(1)}, u32[]{:S(2)}, u32[]{:S(2)}) collective-permute-start(bf16[2,16,1024]{2,1,0:T(8,128)(2,1)S(1)} %shard_map.67.own_ref), channel_id=1, source_target_pairs={{0,16},{16,0},{1,17},{17,1},{2,18},{18,2},{3,19},{19,3},{4,20},{20... | collective-permute-start | bytes 196616 | tf_op jit(solution)/shard_map/ppermute | solution.py:215
  24.7 3.6 %collective-permute-done.1.other_ref = bf16[2,16,1024]{2,1,0:T(8,128)(2,1)S(1)} collective-permute-done((bf16[2,16,1024]{2,1,0:T(8,128)(2,1)S(1)}, bf16[2,16,1024]{2,1,0:T(8,128)(2,1)S(1)}, u32[]{:S(2)}, u32[]{:S(2)}) %collective-permute-start.1) | collective-permute-done | bytes 65568 | tf_op jit(solution)/shard_map/ppermute | solution.py:215
  28.3 13.8 %all-gather = bf16[8,2,16,1024]{3,2,1,0:T(8,128)(2,1)S(1)} all-gather(bf16[2,2,16,1024]{3,2,1,0:T(8,128)(2,1)S(1)} %shard_map.68), channel_id=2, replica_groups=mesh['zl'=8,'yh'=2,'yl'=2,'zh'=2,'x'=4,'c'=2] {'x'}, dimensions={0}, use_global_device_ids=true | all-gather | bytes 655360 | tf_op jit(solution)/shard_map/all_gather | solution.py:225
  42.1 1.9 %collective-permute-start.2 = (bf16[16,16,1024]{2,1,0:T(8,128)(2,1)S(1)}, bf16[16,16,1024]{2,1,0:T(8,128)(2,1)S(1)}, u32[]{:S(2)}, u32[]{:S(2)}) collective-permute-start(bf16[16,16,1024]{2,1,0:T(8,128)(2,1)S(1)} %bitcast.2), channel_id=1, source_target_pairs={{0,1},{1,0},{2,3},{3,2},{4,5},{5,4},{6,7},{7,6},{8,9},{9,8},{10,11... | collective-permute-start | bytes 1572872 | tf_op jit(solution)/shard_map/ppermute | solution.py:215
  44.0 1.9 %collective-permute-done.2.other_ref = bf16[16,16,1024]{2,1,0:T(8,128)(2,1)S(1)} collective-permute-done((bf16[16,16,1024]{2,1,0:T(8,128)(2,1)S(1)}, bf16[16,16,1024]{2,1,0:T(8,128)(2,1)S(1)}, u32[]{:S(2)}, u32[]{:S(2)}) %collective-permute-start.2) | collective-permute-done | bytes 524320 | tf_op jit(solution)/shard_map/ppermute | solution.py:215
  45.9 3.5 %all-to-all-done.text_ref = bf16[16,16,1024]{2,1,0:T(8,128)(2,1)S(1)} async-done(((bf16[16,16,1024]{2,1,0:T(8,128)(2,1)}), bf16[16,16,1024]{2,1,0:T(8,128)(2,1)S(1)}, u32[]{:S(2)}, u32[]{:S(2)}) %all-to-all-start) | async-done | bytes 524320 | tf_op jit(solution)/shard_map/all_to_all | solution.py:221
  49.4 0.9 shard_map.69
  50.3 12.9 %all_to_all.25.got_ref = f32[32,8,128]{2,1,0:T(8,128)S(1)} all-to-all(f32[32,8,128]{2,1,0:T(8,128)S(1)} %get-tuple-element.28), channel_id=1, replica_groups=mesh['zl'=8,'yh'=2,'yl'=2,'zh'=2,'x'=4,'c'=2] {'x','yh','yl','c'}, dimensions={0} | all-to-all | bytes 262144 | tf_op jit(solution)/shard_map/all_to_all | solution.py:234
  63.1 0.2 shard_map.70
  63.3 19.1 %all_to_all.26.got_ref = f32[16,8,128]{2,1,0:T(8,128)S(1)} all-to-all(f32[16,8,128]{2,1,0:T(8,128)S(1)} %get-tuple-element.31), channel_id=1, replica_groups=mesh['zl'=8,'yh'=2,'yl'=2,'zh'=2,'x'=4,'c'=2] {'zh','zl'}, dimensions={0} | all-to-all | bytes 131072 | tf_op jit(solution)/shard_map/all_to_all | solution.py:236
  82.4 1.2 %shard_map.71 = (bf16[16,8,1024]{2,1,0:T(8,128)(2,1)}, f32[128,128]{1,0:T(8,128)S(1)}, f32[128,128]{1,0:T(8,128)S(1)}, f32[8,128]{1,0:T(8,128)S(1)}) custom-call(f32[256,128]{1,0:T(8,128)S(1)} %get-tuple-element.26.on_ref, f32[256,128]{1,0:T(8,128)S(1)} %get-tuple-element.27.mom_ref, f32[128,128]{1,0:T(8,128)S(1)} %get-tuple-element.30.lse_ref, ...), custom_call_target="tpu_custom_call" | custom-call | flops 134217728 | bytes 1839104 | tf_op jit(solution)/shard_map/pallas_call | solution.py:23
  83.7 5.0 %all-to-all-start.3 = ((bf16[16,8,1024]{2,1,0:T(8,128)(2,1)}), bf16[16,8,1024]{2,1,0:T(8,128)(2,1)S(1)}, u32[]{:S(2)}, u32[]{:S(2)}) async-start(bf16[16,8,1024]{2,1,0:T(8,128)(2,1)} %get-tuple-element.39), calls=%async_computation.3 | async-start | bytes 524288 | tf_op jit(solution)/shard_map/all_to_all | solution.py:246
  88.6 0.3 shard_map.72
  89.0 1.9 %collective-permute-start.3 = (f32[128,1152]{1,0:T(8,128)S(1)}, f32[128,1152]{1,0:T(8,128)S(1)}, u32[]{:S(2)}, u32[]{:S(2)}) collective-permute-start(f32[128,1152]{1,0:T(8,128)S(1)} %get-tuple-element.36), channel_id=1, source_target_pairs={{0,1},{1,0},{2,3},{3,2},{4,5},{5,4},{6,7},{7,6},{8,9},{9,8},{10,11... | collective-permute-start | bytes 1769480 | tf_op jit(solution)/shard_map/ppermute | solution.py:215
  90.9 2.0 %collective-permute-done.3.got_ref = f32[128,1152]{1,0:T(8,128)S(1)} collective-permute-done((f32[128,1152]{1,0:T(8,128)S(1)}, f32[128,1152]{1,0:T(8,128)S(1)}, u32[]{:S(2)}, u32[]{:S(2)}) %collective-permute-start.3) | collective-permute-done | bytes 589856 | tf_op jit(solution)/shard_map/ppermute | solution.py:215
  92.9 2.9 %collective-permute-start.4 = (f32[8,8,1152]{2,1,0:T(8,128)S(1)}, f32[8,8,1152]{2,1,0:T(8,128)S(1)}, u32[]{:S(2)}, u32[]{:S(2)}) collective-permute-start(f32[8,8,1152]{2,1,0:T(8,128)S(1)} %get-tuple-element.38), channel_id=1, source_target_pairs={{0,32},{32,0},{1,33},{33,1},{2,34},{34,2},{3,35},{35,3},{4,36},{36... | collective-permute-start | bytes 884744 | tf_op jit(solution)/shard_map/ppermute | solution.py:215
  95.8 9.5 %collective-permute-done.4.got_ref = f32[8,8,1152]{2,1,0:T(8,128)S(1)} collective-permute-done((f32[8,8,1152]{2,1,0:T(8,128)S(1)}, f32[8,8,1152]{2,1,0:T(8,128)S(1)}, u32[]{:S(2)}, u32[]{:S(2)}) %collective-permute-start.4) | collective-permute-done | bytes 294944 | tf_op jit(solution)/shard_map/ppermute | solution.py:215
  105.4 1.4 %all-to-all-done.3.text_ref = bf16[16,8,1024]{2,1,0:T(8,128)(2,1)S(1)} async-done(((bf16[16,8,1024]{2,1,0:T(8,128)(2,1)}), bf16[16,8,1024]{2,1,0:T(8,128)(2,1)S(1)}, u32[]{:S(2)}, u32[]{:S(2)}) %all-to-all-start.3) | async-done | bytes 262176 | tf_op jit(solution)/shard_map/all_to_all | solution.py:246
  106.8 8.9 %all_to_all.27.image_ref = bf16[8,8,1152]{2,1,0:T(8,128)(2,1)S(1)} all-to-all(bf16[8,8,1152]{2,1,0:T(8,128)(2,1)S(1)} %shard_map.74), channel_id=1, replica_groups=mesh['zl'=8,'yh'=2,'yl'=2,'zh'=2,'x'=4,'c'=2] {'x','yl'}, dimensions={0} | all-to-all | bytes 294912 | tf_op jit(solution)/shard_map/all_to_all | solution.py:250
  115.7 0.7 shard_map.75
  (5 shorter events, 0.1 us)
Async XLA Ops:
  1.4 20.7 %collective-permute-start = (bf16[16,1024]{1,0:T(8,128)(2,1)S(1)}, bf16[16,1024]{1,0:T(8,128)(2,1)S(1)}, u32[]{:S(2)}, u32[]{:S(2)}) collective-permute-start(bf16[16,1024]{1,0:T(8,128)(2,1)S(1)} %get-tuple-element.24.own_ref), channel_id=1, source_target_pairs={{0,32},{32,0},{1,33},{33,1},{2,34},{34,2},{3,35},{35,3},{4,36},{36... | collective-permute-start | bytes 98312 | tf_op jit(solution)/shard_map/ppermute | solution.py:215
  7.4 42.1 %all-to-all-start = ((bf16[16,16,1024]{2,1,0:T(8,128)(2,1)}), bf16[16,16,1024]{2,1,0:T(8,128)(2,1)S(1)}, u32[]{:S(2)}, u32[]{:S(2)}) async-start(bf16[16,16,1024]{2,1,0:T(8,128)(2,1)} %broadcast_in_dim.2), calls=%async_computation | async-start | bytes 1048576 | tf_op jit(solution)/shard_map/all_to_all | solution.py:221
  22.1 6.2 %collective-permute-start.1 = (bf16[2,16,1024]{2,1,0:T(8,128)(2,1)S(1)}, bf16[2,16,1024]{2,1,0:T(8,128)(2,1)S(1)}, u32[]{:S(2)}, u32[]{:S(2)}) collective-permute-start(bf16[2,16,1024]{2,1,0:T(8,128)(2,1)S(1)} %shard_map.67.own_ref), channel_id=1, source_target_pairs={{0,16},{16,0},{1,17},{17,1},{2,18},{18,2},{3,19},{19,3},{4,20},{20... | collective-permute-start | bytes 196616 | tf_op jit(solution)/shard_map/ppermute | solution.py:215
  42.1 3.8 %collective-permute-start.2 = (bf16[16,16,1024]{2,1,0:T(8,128)(2,1)S(1)}, bf16[16,16,1024]{2,1,0:T(8,128)(2,1)S(1)}, u32[]{:S(2)}, u32[]{:S(2)}) collective-permute-start(bf16[16,16,1024]{2,1,0:T(8,128)(2,1)S(1)} %bitcast.2), channel_id=1, source_target_pairs={{0,1},{1,0},{2,3},{3,2},{4,5},{5,4},{6,7},{7,6},{8,9},{9,8},{10,11... | collective-permute-start | bytes 1572872 | tf_op jit(solution)/shard_map/ppermute | solution.py:215
  83.7 23.2 %all-to-all-start.3 = ((bf16[16,8,1024]{2,1,0:T(8,128)(2,1)}), bf16[16,8,1024]{2,1,0:T(8,128)(2,1)S(1)}, u32[]{:S(2)}, u32[]{:S(2)}) async-start(bf16[16,8,1024]{2,1,0:T(8,128)(2,1)} %get-tuple-element.39), calls=%async_computation.3 | async-start | bytes 524288 | tf_op jit(solution)/shard_map/all_to_all | solution.py:246
  89.0 3.9 %collective-permute-start.3 = (f32[128,1152]{1,0:T(8,128)S(1)}, f32[128,1152]{1,0:T(8,128)S(1)}, u32[]{:S(2)}, u32[]{:S(2)}) collective-permute-start(f32[128,1152]{1,0:T(8,128)S(1)} %get-tuple-element.36), channel_id=1, source_target_pairs={{0,1},{1,0},{2,3},{3,2},{4,5},{5,4},{6,7},{7,6},{8,9},{9,8},{10,11... | collective-permute-start | bytes 1769480 | tf_op jit(solution)/shard_map/ppermute | solution.py:215
  92.9 12.4 %collective-permute-start.4 = (f32[8,8,1152]{2,1,0:T(8,128)S(1)}, f32[8,8,1152]{2,1,0:T(8,128)S(1)}, u32[]{:S(2)}, u32[]{:S(2)}) collective-permute-start(f32[8,8,1152]{2,1,0:T(8,128)S(1)} %get-tuple-element.38), channel_id=1, source_target_pairs={{0,32},{32,0},{1,33},{33,1},{2,34},{34,2},{3,35},{35,3},{4,36},{36... | collective-permute-start | bytes 884744 | tf_op jit(solution)/shard_map/ppermute | solution.py:215

commit v14 on v13

--- a/solution.py
+++ b/solution.py
@@ -179,10 +179,10 @@
 
 
 def core_kernel(keep_ref, got_ref, own_ref, send_ref):
-    total = (keep_ref[...] + got_ref[...]).reshape(8, 2, rows, keep_ref.shape[1])
-    first = lax.axis_index("yh") == 0
-    own_ref[...] = jnp.where(first, total[:, 0], total[:, 1])
-    send_ref[...] = jnp.where(first, total[:, 1], total[:, 0])
+    total = (keep_ref[...] + got_ref[...]).reshape(4, 2, 2 * rows, keep_ref.shape[1])
+    first = lax.axis_index("yl") == 0
+    own_ref[...] = jnp.where(first, total[:, 0], total[:, 1]).reshape(own_ref.shape)
+    send_ref[...] = jnp.where(first, total[:, 1], total[:, 0]).reshape(own_ref.shape)
 
 
 def across_kernel(keep_ref, got_ref, out_ref):
@@ -245,9 +245,9 @@
     got = swap(send)
     got_text = lax.all_to_all(by_text, column, 0, 0, tiled=True)
     keep, send = call(core_kernel, [shape(8, rows, wide)] * 2, keep, got)
-    (by_image,) = call(across_kernel, [shape(8, rows, wide, dtype=bf16)], keep, swap(send, "yh"))
+    (by_image,) = call(across_kernel, [shape(8, rows, wide, dtype=bf16)], keep, swap(send, "yl"))
     by_image, got_text = lax.optimization_barrier((by_image, got_text))
-    got_image = lax.all_to_all(by_image, ("x", "yl"), 0, 0, tiled=True)
+    got_image = lax.all_to_all(by_image, ("x", "yh"), 0, 0, tiled=True)
     vmem = pl.BlockSpec(memory_space=pltpu.VMEM)
     grad_image, grad_text, loss = call(
         last_kernel, [shape(rows, width), shape(rows, width), shape(1, 1)], got_image, got_text,

time: 117 us -> 119 us (1.017)
  blocking collectives: 54.6 us -> 56.4 us
    all_to_all x1, blocking collectives: 8.85 us -> 10.8 us  [local(): got_image = lax.all_to_all(by_image, ('x', 'yh'), 0, 0, tiled=True)]
    all_to_all x1, waiting for transfers between devices: 1.42 us -> 2.92 us  [local(): got_text = lax.all_to_all(by_text, column, 0, 0, tiled=True)]
where the time goes in v14:
time: 119 us; the launch traced here: 118 us
  blocking collectives  56.4 us (47%)
  starting transfers between devices  33.7 us (28%)
  waiting for transfers between devices  22.4 us (19%)
  Pallas kernels  3.46 us (3%)
    all_to_all x1, blocking collectives, local(): col_got = lax.all_to_all(col_sent, column, 0, 0, tiled=True)  19.1 us
    ppermute x5, waiting for transfers between devices, swap(): return lax.ppermute(block, axis, [(0, 1), (1, 0)])  15.9 us
    all_to_all x1, starting transfers between devices, local(): texts = lax.all_to_all(sent, column, 0, 0, tiled=True)  14.8 us
    ppermute x5, starting transfers between devices, swap(): return lax.ppermute(block, axis, [(0, 1), (1, 0)])  13.9 us
    all_gather x1, blocking collectives, local(): mine = lax.all_gather(pair, 'x').reshape(16, 16, width)  13.8 us
    all_to_all x1, blocking collectives, local(): lax.all_to_all(row_parts, ('x', 'yh', 'yl', 'c'), 0, 0, tiled=True)  12.9 us
    all_to_all x1, blocking collectives, local(): got_image = lax.all_to_all(by_image, ('x', 'yh'), 0, 0, tiled=True)  10.8 us
    all_to_all x1, starting transfers between devices, local(): got_text = lax.all_to_all(by_text, column, 0, 0, tiled=True)  4.96 us
  transfers between devices with their start and end apart: 7, of which 6 were waited for; matrix products, arithmetic and copies ran while one was open for 1% of the time, Pallas kernels for 0%

profile of v14, /device:TPU:64, one launch (start us, length us, event | category | flops | bytes accessed | tf_op | source)
XLA Modules:
  0.0 118.3 jit_solution(5123697239496157269)
XLA Ops:
  0.6 0.8 pad_maximum_fusion
  1.4 5.1 %collective-permute-start = (bf16[16,1024]{1,0:T(8,128)(2,1)S(1)}, bf16[16,1024]{1,0:T(8,128)(2,1)S(1)}, u32[]{:S(2)}, u32[]{:S(2)}) collective-permute-start(bf16[16,1024]{1,0:T(8,128)(2,1)S(1)} %get-tuple-element.24.own_ref), channel_id=1, source_target_pairs={{0,32},{32,0},{1,33},{33,1},{2,34},{34,2},{3,35},{35,3},{4,36},{36... | collective-permute-start | bytes 98312 | tf_op jit(solution)/shard_map/ppermute | solution.py:215
  6.5 0.8 broadcast_in_dim.2
  7.4 14.8 %all-to-all-start = ((bf16[16,16,1024]{2,1,0:T(8,128)(2,1)}), bf16[16,16,1024]{2,1,0:T(8,128)(2,1)S(1)}, u32[]{:S(2)}, u32[]{:S(2)}) async-start(bf16[16,16,1024]{2,1,0:T(8,128)(2,1)} %broadcast_in_dim.2), calls=%async_computation | async-start | bytes 1048576 | tf_op jit(solution)/shard_map/all_to_all | solution.py:221
  22.1 2.6 %collective-permute-start.1 = (bf16[2,16,1024]{2,1,0:T(8,128)(2,1)S(1)}, bf16[2,16,1024]{2,1,0:T(8,128)(2,1)S(1)}, u32[]{:S(2)}, u32[]{:S(2)}) collective-permute-start(bf16[2,16,1024]{2,1,0:T(8,128)(2,1)S(1)} %shard_map.67.own_ref), channel_id=1, source_target_pairs={{0,16},{16,0},{1,17},{17,1},{2,18},{18,2},{3,19},{19,3},{4,20},{20... | collective-permute-start | bytes 196616 | tf_op jit(solution)/shard_map/ppermute | solution.py:215
  24.7 3.6 %collective-permute-done.1.other_ref = bf16[2,16,1024]{2,1,0:T(8,128)(2,1)S(1)} collective-permute-done((bf16[2,16,1024]{2,1,0:T(8,128)(2,1)S(1)}, bf16[2,16,1024]{2,1,0:T(8,128)(2,1)S(1)}, u32[]{:S(2)}, u32[]{:S(2)}) %collective-permute-start.1) | collective-permute-done | bytes 65568 | tf_op jit(solution)/shard_map/ppermute | solution.py:215
  28.3 13.8 %all-gather = bf16[8,2,16,1024]{3,2,1,0:T(8,128)(2,1)S(1)} all-gather(bf16[2,2,16,1024]{3,2,1,0:T(8,128)(2,1)S(1)} %shard_map.68), channel_id=2, replica_groups=mesh['zl'=8,'yh'=2,'yl'=2,'zh'=2,'x'=4,'c'=2] {'x'}, dimensions={0}, use_global_device_ids=true | all-gather | bytes 655360 | tf_op jit(solution)/shard_map/all_gather | solution.py:225
  42.1 1.9 %collective-permute-start.2 = (bf16[16,16,1024]{2,1,0:T(8,128)(2,1)S(1)}, bf16[16,16,1024]{2,1,0:T(8,128)(2,1)S(1)}, u32[]{:S(2)}, u32[]{:S(2)}) collective-permute-start(bf16[16,16,1024]{2,1,0:T(8,128)(2,1)S(1)} %bitcast.2), channel_id=1, source_target_pairs={{0,1},{1,0},{2,3},{3,2},{4,5},{5,4},{6,7},{7,6},{8,9},{9,8},{10,11... | collective-permute-start | bytes 1572872 | tf_op jit(solution)/shard_map/ppermute | solution.py:215
  44.0 1.9 %collective-permute-done.2.other_ref = bf16[16,16,1024]{2,1,0:T(8,128)(2,1)S(1)} collective-permute-done((bf16[16,16,1024]{2,1,0:T(8,128)(2,1)S(1)}, bf16[16,16,1024]{2,1,0:T(8,128)(2,1)S(1)}, u32[]{:S(2)}, u32[]{:S(2)}) %collective-permute-start.2) | collective-permute-done | bytes 524320 | tf_op jit(solution)/shard_map/ppermute | solution.py:215
  45.9 3.5 %all-to-all-done.text_ref = bf16[16,16,1024]{2,1,0:T(8,128)(2,1)S(1)} async-done(((bf16[16,16,1024]{2,1,0:T(8,128)(2,1)}), bf16[16,16,1024]{2,1,0:T(8,128)(2,1)S(1)}, u32[]{:S(2)}, u32[]{:S(2)}) %all-to-all-start) | async-done | bytes 524320 | tf_op jit(solution)/shard_map/all_to_all | solution.py:221
  49.4 0.9 shard_map.69
  50.3 12.9 %all_to_all.25.got_ref = f32[32,8,128]{2,1,0:T(8,128)S(1)} all-to-all(f32[32,8,128]{2,1,0:T(8,128)S(1)} %get-tuple-element.28), channel_id=1, replica_groups=mesh['zl'=8,'yh'=2,'yl'=2,'zh'=2,'x'=4,'c'=2] {'x','yh','yl','c'}, dimensions={0} | all-to-all | bytes 262144 | tf_op jit(solution)/shard_map/all_to_all | solution.py:234
  63.1 0.2 shard_map.70
  63.3 19.1 %all_to_all.26.got_ref = f32[16,8,128]{2,1,0:T(8,128)S(1)} all-to-all(f32[16,8,128]{2,1,0:T(8,128)S(1)} %get-tuple-element.31), channel_id=1, replica_groups=mesh['zl'=8,'yh'=2,'yl'=2,'zh'=2,'x'=4,'c'=2] {'zh','zl'}, dimensions={0} | all-to-all | bytes 131072 | tf_op jit(solution)/shard_map/all_to_all | solution.py:236
  82.4 1.2 %shard_map.71 = (bf16[16,8,1024]{2,1,0:T(8,128)(2,1)}, f32[128,128]{1,0:T(8,128)S(1)}, f32[128,128]{1,0:T(8,128)S(1)}, f32[8,128]{1,0:T(8,128)S(1)}) custom-call(f32[256,128]{1,0:T(8,128)S(1)} %get-tuple-element.26.on_ref, f32[256,128]{1,0:T(8,128)S(1)} %get-tuple-element.27.mom_ref, f32[128,128]{1,0:T(8,128)S(1)} %get-tuple-element.30.lse_ref, ...), custom_call_target="tpu_custom_call" | custom-call | flops 134217728 | bytes 1839104 | tf_op jit(solution)/shard_map/pallas_call | solution.py:23
  83.7 5.0 %all-to-all-start.3 = ((bf16[16,8,1024]{2,1,0:T(8,128)(2,1)}), bf16[16,8,1024]{2,1,0:T(8,128)(2,1)S(1)}, u32[]{:S(2)}, u32[]{:S(2)}) async-start(bf16[16,8,1024]{2,1,0:T(8,128)(2,1)} %get-tuple-element.39), calls=%async_computation.3 | async-start | bytes 524288 | tf_op jit(solution)/shard_map/all_to_all | solution.py:246
  88.6 0.3 shard_map.72
  89.0 1.9 %collective-permute-start.3 = (f32[128,1152]{1,0:T(8,128)S(1)}, f32[128,1152]{1,0:T(8,128)S(1)}, u32[]{:S(2)}, u32[]{:S(2)}) collective-permute-start(f32[128,1152]{1,0:T(8,128)S(1)} %get-tuple-element.36), channel_id=1, source_target_pairs={{0,1},{1,0},{2,3},{3,2},{4,5},{5,4},{6,7},{7,6},{8,9},{9,8},{10,11... | collective-permute-start | bytes 1769480 | tf_op jit(solution)/shard_map/ppermute | solution.py:215
  90.9 2.0 %collective-permute-done.3.got_ref = f32[128,1152]{1,0:T(8,128)S(1)} collective-permute-done((f32[128,1152]{1,0:T(8,128)S(1)}, f32[128,1152]{1,0:T(8,128)S(1)}, u32[]{:S(2)}, u32[]{:S(2)}) %collective-permute-start.3) | collective-permute-done | bytes 589856 | tf_op jit(solution)/shard_map/ppermute | solution.py:215
  92.9 2.4 %collective-permute-start.4 = (f32[8,8,1152]{2,1,0:T(8,128)S(1)}, f32[8,8,1152]{2,1,0:T(8,128)S(1)}, u32[]{:S(2)}, u32[]{:S(2)}) collective-permute-start(f32[8,8,1152]{2,1,0:T(8,128)S(1)} %get-tuple-element.38), channel_id=1, source_target_pairs={{0,16},{16,0},{1,17},{17,1},{2,18},{18,2},{3,19},{19,3},{4,20},{20... | collective-permute-start | bytes 884744 | tf_op jit(solution)/shard_map/ppermute | solution.py:215
  95.4 8.5 %collective-permute-done.4.got_ref = f32[8,8,1152]{2,1,0:T(8,128)S(1)} collective-permute-done((f32[8,8,1152]{2,1,0:T(8,128)S(1)}, f32[8,8,1152]{2,1,0:T(8,128)S(1)}, u32[]{:S(2)}, u32[]{:S(2)}) %collective-permute-start.4) | collective-permute-done | bytes 294944 | tf_op jit(solution)/shard_map/ppermute | solution.py:215
  103.9 2.9 %all-to-all-done.3.text_ref = bf16[16,8,1024]{2,1,0:T(8,128)(2,1)S(1)} async-done(((bf16[16,8,1024]{2,1,0:T(8,128)(2,1)}), bf16[16,8,1024]{2,1,0:T(8,128)(2,1)S(1)}, u32[]{:S(2)}, u32[]{:S(2)}) %all-to-all-start.3) | async-done | bytes 262176 | tf_op jit(solution)/shard_map/all_to_all | solution.py:246
  106.8 10.8 %all_to_all.27.image_ref = bf16[8,8,1152]{2,1,0:T(8,128)(2,1)S(1)} all-to-all(bf16[8,8,1152]{2,1,0:T(8,128)(2,1)S(1)} %shard_map.74), channel_id=1, replica_groups=mesh['zl'=8,'yh'=2,'yl'=2,'zh'=2,'x'=4,'c'=2] {'x','yh'}, dimensions={0} | all-to-all | bytes 294912 | tf_op jit(solution)/shard_map/all_to_all | solution.py:250
  117.6 0.7 shard_map.75
  (5 shorter events, 0.1 us)
Async XLA Ops:
  1.4 20.7 %collective-permute-start = (bf16[16,1024]{1,0:T(8,128)(2,1)S(1)}, bf16[16,1024]{1,0:T(8,128)(2,1)S(1)}, u32[]{:S(2)}, u32[]{:S(2)}) collective-permute-start(bf16[16,1024]{1,0:T(8,128)(2,1)S(1)} %get-tuple-element.24.own_ref), channel_id=1, source_target_pairs={{0,32},{32,0},{1,33},{33,1},{2,34},{34,2},{3,35},{35,3},{4,36},{36... | collective-permute-start | bytes 98312 | tf_op jit(solution)/shard_map/ppermute | solution.py:215
  7.4 42.1 %all-to-all-start = ((bf16[16,16,1024]{2,1,0:T(8,128)(2,1)}), bf16[16,16,1024]{2,1,0:T(8,128)(2,1)S(1)}, u32[]{:S(2)}, u32[]{:S(2)}) async-start(bf16[16,16,1024]{2,1,0:T(8,128)(2,1)} %broadcast_in_dim.2), calls=%async_computation | async-start | bytes 1048576 | tf_op jit(solution)/shard_map/all_to_all | solution.py:221
  22.1 6.2 %collective-permute-start.1 = (bf16[2,16,1024]{2,1,0:T(8,128)(2,1)S(1)}, bf16[2,16,1024]{2,1,0:T(8,128)(2,1)S(1)}, u32[]{:S(2)}, u32[]{:S(2)}) collective-permute-start(bf16[2,16,1024]{2,1,0:T(8,128)(2,1)S(1)} %shard_map.67.own_ref), channel_id=1, source_target_pairs={{0,16},{16,0},{1,17},{17,1},{2,18},{18,2},{3,19},{19,3},{4,20},{20... | collective-permute-start | bytes 196616 | tf_op jit(solution)/shard_map/ppermute | solution.py:215
  42.1 3.8 %collective-permute-start.2 = (bf16[16,16,1024]{2,1,0:T(8,128)(2,1)S(1)}, bf16[16,16,1024]{2,1,0:T(8,128)(2,1)S(1)}, u32[]{:S(2)}, u32[]{:S(2)}) collective-permute-start(bf16[16,16,1024]{2,1,0:T(8,128)(2,1)S(1)} %bitcast.2), channel_id=1, source_target_pairs={{0,1},{1,0},{2,3},{3,2},{4,5},{5,4},{6,7},{7,6},{8,9},{9,8},{10,11... | collective-permute-start | bytes 1572872 | tf_op jit(solution)/shard_map/ppermute | solution.py:215
  83.7 23.2 %all-to-all-start.3 = ((bf16[16,8,1024]{2,1,0:T(8,128)(2,1)}), bf16[16,8,1024]{2,1,0:T(8,128)(2,1)S(1)}, u32[]{:S(2)}, u32[]{:S(2)}) async-start(bf16[16,8,1024]{2,1,0:T(8,128)(2,1)} %get-tuple-element.39), calls=%async_computation.3 | async-start | bytes 524288 | tf_op jit(solution)/shard_map/all_to_all | solution.py:246
  89.0 3.9 %collective-permute-start.3 = (f32[128,1152]{1,0:T(8,128)S(1)}, f32[128,1152]{1,0:T(8,128)S(1)}, u32[]{:S(2)}, u32[]{:S(2)}) collective-permute-start(f32[128,1152]{1,0:T(8,128)S(1)} %get-tuple-element.36), channel_id=1, source_target_pairs={{0,1},{1,0},{2,3},{3,2},{4,5},{5,4},{6,7},{7,6},{8,9},{9,8},{10,11... | collective-permute-start | bytes 1769480 | tf_op jit(solution)/shard_map/ppermute | solution.py:215
  92.9 10.9 %collective-permute-start.4 = (f32[8,8,1152]{2,1,0:T(8,128)S(1)}, f32[8,8,1152]{2,1,0:T(8,128)S(1)}, u32[]{:S(2)}, u32[]{:S(2)}) collective-permute-start(f32[8,8,1152]{2,1,0:T(8,128)S(1)} %get-tuple-element.38), channel_id=1, source_target_pairs={{0,16},{16,0},{1,17},{17,1},{2,18},{18,2},{3,19},{19,3},{4,20},{20... | collective-permute-start | bytes 884744 | tf_op jit(solution)/shard_map/ppermute | solution.py:215

commit v15 on v13

--- a/solution.py
+++ b/solution.py
@@ -178,15 +178,7 @@
         ref[:, width:] = jnp.broadcast_to(loss_ref[0:1], (side, 128))
 
 
-def core_kernel(keep_ref, got_ref, own_ref, send_ref):
-    total = (keep_ref[...] + got_ref[...]).reshape(8, 2, rows, keep_ref.shape[1])
-    first = lax.axis_index("yh") == 0
-    own_ref[...] = jnp.where(first, total[:, 0], total[:, 1])
-    send_ref[...] = jnp.where(first, total[:, 1], total[:, 0])
-
-
-def across_kernel(keep_ref, got_ref, out_ref):
-    total = keep_ref[...] + got_ref[...]
+def send_out(total, ref):
     width = total.shape[2] - 128
     loss = total[:, :, width:]
     lane = lax.broadcasted_iota(jnp.int32, loss.shape, 2)
@@ -195,8 +187,22 @@
         piece = loss.astype(bf16).astype(f32)
         pieces = jnp.where(lane == k, piece, pieces)
         loss = loss - piece
-    out_ref[:, :, :width] = total[:, :, :width].astype(bf16)
-    out_ref[:, :, width:] = pieces.astype(bf16)
+    ref[:, :, :width] = total[:, :, :width].astype(bf16)
+    ref[:, :, width:] = pieces.astype(bf16)
+
+
+def core_kernel(keep_ref, got_ref, own_ref, send_ref):
+    total = (keep_ref[...] + got_ref[...]).reshape(8, 2, rows, keep_ref.shape[1])
+    first = lax.axis_index("yh") == 0
+    own_ref[...] = jnp.where(first, total[:, 0], total[:, 1])
+    send_out(jnp.where(first, total[:, 1], total[:, 0]), send_ref)
+
+
+def across_kernel(keep_ref, got_ref, out_ref):
+    keep, got = keep_ref[...], got_ref[...].astype(f32)
+    width = keep.shape[2] - 128
+    loss = keep[:, :, width:] + jnp.sum(got[:, :, width:], axis=2, keepdims=True)
+    send_out(jnp.concatenate([keep[:, :, :width] + got[:, :, :width], loss], axis=2), out_ref)
 
 
 def last_kernel(image_ref, text_ref, grad_image_ref, grad_text_ref, loss_ref):
@@ -244,7 +250,7 @@
     keep, send = call(image_kernel, [shape(side, wide), shape(side, wide)], g_mine, g_other, texts, loss, flops=2**27)
     got = swap(send)
     got_text = lax.all_to_all(by_text, column, 0, 0, tiled=True)
-    keep, send = call(core_kernel, [shape(8, rows, wide)] * 2, keep, got)
+    keep, send = call(core_kernel, [shape(8, rows, wide), shape(8, rows, wide, dtype=bf16)], keep, got)
     (by_image,) = call(across_kernel, [shape(8, rows, wide, dtype=bf16)], keep, swap(send, "yh"))
     by_image, got_text = lax.optimization_barrier((by_image, got_text))
     got_image = lax.all_to_all(by_image, ("x", "yl"), 0, 0, tiled=True)

time: 117 us -> 117 us (level)
    ppermute x5, waiting for transfers between devices: 16.9 us -> 13.8 us  [swap(): return lax.ppermute(block, axis, [(0, 1), (1, 0)])]
    all_to_all x1, waiting for transfers between devices: 1.42 us -> 4.5 us  [local(): got_text = lax.all_to_all(by_text, column, 0, 0, tiled=True)]
where the time goes in v15:
time: 117 us; the launch traced here: 116 us
  blocking collectives  54.6 us (47%)
  starting transfers between devices  34.1 us (29%)
  waiting for transfers between devices  21.8 us (19%)
  Pallas kernels  3.54 us (3%)
    all_to_all x1, blocking collectives, local(): col_got = lax.all_to_all(col_sent, column, 0, 0, tiled=True)  19.1 us
    all_to_all x1, starting transfers between devices, local(): texts = lax.all_to_all(sent, column, 0, 0, tiled=True)  14.8 us
    ppermute x5, starting transfers between devices, swap(): return lax.ppermute(block, axis, [(0, 1), (1, 0)])  14.4 us
    ppermute x5, waiting for transfers between devices, swap(): return lax.ppermute(block, axis, [(0, 1), (1, 0)])  13.8 us
    all_gather x1, blocking collectives, local(): mine = lax.all_gather(pair, 'x').reshape(16, 16, width)  13.8 us
    all_to_all x1, blocking collectives, local(): lax.all_to_all(row_parts, ('x', 'yh', 'yl', 'c'), 0, 0, tiled=True)  12.9 us
    all_to_all x1, blocking collectives, local(): got_image = lax.all_to_all(by_image, ('x', 'yl'), 0, 0, tiled=True)  8.85 us
    all_to_all x1, starting transfers between devices, local(): got_text = lax.all_to_all(by_text, column, 0, 0, tiled=True)  4.96 us
  transfers between devices with their start and end apart: 7, of which 6 were waited for; matrix products, arithmetic and copies ran while one was open for 1% of the time, Pallas kernels for 0%

profile of v15, /device:TPU:64, one launch (start us, length us, event | category | flops | bytes accessed | tf_op | source)
XLA Modules:
  0.0 116.4 jit_solution(10358423454254455608)
XLA Ops:
  0.6 0.8 pad_maximum_fusion
  1.4 5.1 %collective-permute-start = (bf16[16,1024]{1,0:T(8,128)(2,1)S(1)}, bf16[16,1024]{1,0:T(8,128)(2,1)S(1)}, u32[]{:S(2)}, u32[]{:S(2)}) collective-permute-start(bf16[16,1024]{1,0:T(8,128)(2,1)S(1)} %get-tuple-element.24.own_ref), channel_id=1, source_target_pairs={{0,32},{32,0},{1,33},{33,1},{2,34},{34,2},{3,35},{35,3},{4,36},{36... | collective-permute-start | bytes 98312 | tf_op jit(solution)/shard_map/ppermute | solution.py:221
  6.5 0.8 broadcast_in_dim.2
  7.4 14.8 %all-to-all-start = ((bf16[16,16,1024]{2,1,0:T(8,128)(2,1)}), bf16[16,16,1024]{2,1,0:T(8,128)(2,1)S(1)}, u32[]{:S(2)}, u32[]{:S(2)}) async-start(bf16[16,16,1024]{2,1,0:T(8,128)(2,1)} %broadcast_in_dim.2), calls=%async_computation | async-start | bytes 1048576 | tf_op jit(solution)/shard_map/all_to_all | solution.py:227
  22.1 2.6 %collective-permute-start.1 = (bf16[2,16,1024]{2,1,0:T(8,128)(2,1)S(1)}, bf16[2,16,1024]{2,1,0:T(8,128)(2,1)S(1)}, u32[]{:S(2)}, u32[]{:S(2)}) collective-permute-start(bf16[2,16,1024]{2,1,0:T(8,128)(2,1)S(1)} %shard_map.67.own_ref), channel_id=1, source_target_pairs={{0,16},{16,0},{1,17},{17,1},{2,18},{18,2},{3,19},{19,3},{4,20},{20... | collective-permute-start | bytes 196616 | tf_op jit(solution)/shard_map/ppermute | solution.py:221
  24.7 3.6 %collective-permute-done.1.other_ref = bf16[2,16,1024]{2,1,0:T(8,128)(2,1)S(1)} collective-permute-done((bf16[2,16,1024]{2,1,0:T(8,128)(2,1)S(1)}, bf16[2,16,1024]{2,1,0:T(8,128)(2,1)S(1)}, u32[]{:S(2)}, u32[]{:S(2)}) %collective-permute-start.1) | collective-permute-done | bytes 65568 | tf_op jit(solution)/shard_map/ppermute | solution.py:221
  28.3 13.8 %all-gather = bf16[8,2,16,1024]{3,2,1,0:T(8,128)(2,1)S(1)} all-gather(bf16[2,2,16,1024]{3,2,1,0:T(8,128)(2,1)S(1)} %shard_map.68), channel_id=2, replica_groups=mesh['zl'=8,'yh'=2,'yl'=2,'zh'=2,'x'=4,'c'=2] {'x'}, dimensions={0}, use_global_device_ids=true | all-gather | bytes 655360 | tf_op jit(solution)/shard_map/all_gather | solution.py:231
  42.1 1.9 %collective-permute-start.2 = (bf16[16,16,1024]{2,1,0:T(8,128)(2,1)S(1)}, bf16[16,16,1024]{2,1,0:T(8,128)(2,1)S(1)}, u32[]{:S(2)}, u32[]{:S(2)}) collective-permute-start(bf16[16,16,1024]{2,1,0:T(8,128)(2,1)S(1)} %bitcast.2), channel_id=1, source_target_pairs={{0,1},{1,0},{2,3},{3,2},{4,5},{5,4},{6,7},{7,6},{8,9},{9,8},{10,11... | collective-permute-start | bytes 1572872 | tf_op jit(solution)/shard_map/ppermute | solution.py:221
  44.0 1.9 %collective-permute-done.2.other_ref = bf16[16,16,1024]{2,1,0:T(8,128)(2,1)S(1)} collective-permute-done((bf16[16,16,1024]{2,1,0:T(8,128)(2,1)S(1)}, bf16[16,16,1024]{2,1,0:T(8,128)(2,1)S(1)}, u32[]{:S(2)}, u32[]{:S(2)}) %collective-permute-start.2) | collective-permute-done | bytes 524320 | tf_op jit(solution)/shard_map/ppermute | solution.py:221
  45.9 3.5 %all-to-all-done.text_ref = bf16[16,16,1024]{2,1,0:T(8,128)(2,1)S(1)} async-done(((bf16[16,16,1024]{2,1,0:T(8,128)(2,1)}), bf16[16,16,1024]{2,1,0:T(8,128)(2,1)S(1)}, u32[]{:S(2)}, u32[]{:S(2)}) %all-to-all-start) | async-done | bytes 524320 | tf_op jit(solution)/shard_map/all_to_all | solution.py:227
  49.4 0.9 shard_map.69
  50.3 12.9 %all_to_all.25.got_ref = f32[32,8,128]{2,1,0:T(8,128)S(1)} all-to-all(f32[32,8,128]{2,1,0:T(8,128)S(1)} %get-tuple-element.28), channel_id=1, replica_groups=mesh['zl'=8,'yh'=2,'yl'=2,'zh'=2,'x'=4,'c'=2] {'x','yh','yl','c'}, dimensions={0} | all-to-all | bytes 262144 | tf_op jit(solution)/shard_map/all_to_all | solution.py:240
  63.1 0.2 shard_map.70
  63.3 19.1 %all_to_all.26.got_ref = f32[16,8,128]{2,1,0:T(8,128)S(1)} all-to-all(f32[16,8,128]{2,1,0:T(8,128)S(1)} %get-tuple-element.31), channel_id=1, replica_groups=mesh['zl'=8,'yh'=2,'yl'=2,'zh'=2,'x'=4,'c'=2] {'zh','zl'}, dimensions={0} | all-to-all | bytes 131072 | tf_op jit(solution)/shard_map/all_to_all | solution.py:242
  82.4 1.2 %shard_map.71 = (bf16[16,8,1024]{2,1,0:T(8,128)(2,1)}, f32[128,128]{1,0:T(8,128)S(1)}, f32[128,128]{1,0:T(8,128)S(1)}, f32[8,128]{1,0:T(8,128)S(1)}) custom-call(f32[256,128]{1,0:T(8,128)S(1)} %get-tuple-element.26.on_ref, f32[256,128]{1,0:T(8,128)S(1)} %get-tuple-element.27.mom_ref, f32[128,128]{1,0:T(8,128)S(1)} %get-tuple-element.30.lse_ref, ...), custom_call_target="tpu_custom_call" | custom-call | flops 134217728 | bytes 1839104 | tf_op jit(solution)/shard_map/pallas_call | solution.py:23
  83.7 5.0 %all-to-all-start.3 = ((bf16[16,8,1024]{2,1,0:T(8,128)(2,1)}), bf16[16,8,1024]{2,1,0:T(8,128)(2,1)S(1)}, u32[]{:S(2)}, u32[]{:S(2)}) async-start(bf16[16,8,1024]{2,1,0:T(8,128)(2,1)} %get-tuple-element.39), calls=%async_computation.3 | async-start | bytes 524288 | tf_op jit(solution)/shard_map/all_to_all | solution.py:252
  88.6 0.3 shard_map.72
  89.0 1.9 %collective-permute-start.3 = (f32[128,1152]{1,0:T(8,128)S(1)}, f32[128,1152]{1,0:T(8,128)S(1)}, u32[]{:S(2)}, u32[]{:S(2)}) collective-permute-start(f32[128,1152]{1,0:T(8,128)S(1)} %get-tuple-element.36), channel_id=1, source_target_pairs={{0,1},{1,0},{2,3},{3,2},{4,5},{5,4},{6,7},{7,6},{8,9},{9,8},{10,11... | collective-permute-start | bytes 1769480 | tf_op jit(solution)/shard_map/ppermute | solution.py:221
  90.9 2.0 %collective-permute-done.3.got_ref = f32[128,1152]{1,0:T(8,128)S(1)} collective-permute-done((f32[128,1152]{1,0:T(8,128)S(1)}, f32[128,1152]{1,0:T(8,128)S(1)}, u32[]{:S(2)}, u32[]{:S(2)}) %collective-permute-start.3) | collective-permute-done | bytes 589856 | tf_op jit(solution)/shard_map/ppermute | solution.py:221
  92.9 2.9 %collective-permute-start.4 = (bf16[8,8,1152]{2,1,0:T(8,128)(2,1)S(1)}, bf16[8,8,1152]{2,1,0:T(8,128)(2,1)S(1)}, u32[]{:S(2)}, u32[]{:S(2)}) collective-permute-start(bf16[8,8,1152]{2,1,0:T(8,128)(2,1)S(1)} %get-tuple-element.38), channel_id=1, source_target_pairs={{0,32},{32,0},{1,33},{33,1},{2,34},{34,2},{3,35},{35,3},{4,36},{36... | collective-permute-start | bytes 442376 | tf_op jit(solution)/shard_map/ppermute | solution.py:221
  95.9 6.4 %collective-permute-done.4.got_ref = bf16[8,8,1152]{2,1,0:T(8,128)(2,1)S(1)} collective-permute-done((bf16[8,8,1152]{2,1,0:T(8,128)(2,1)S(1)}, bf16[8,8,1152]{2,1,0:T(8,128)(2,1)S(1)}, u32[]{:S(2)}, u32[]{:S(2)}) %collective-permute-start.4) | collective-permute-done | bytes 147488 | tf_op jit(solution)/shard_map/ppermute | solution.py:221
  102.3 4.5 %all-to-all-done.3.text_ref = bf16[16,8,1024]{2,1,0:T(8,128)(2,1)S(1)} async-done(((bf16[16,8,1024]{2,1,0:T(8,128)(2,1)}), bf16[16,8,1024]{2,1,0:T(8,128)(2,1)S(1)}, u32[]{:S(2)}, u32[]{:S(2)}) %all-to-all-start.3) | async-done | bytes 262176 | tf_op jit(solution)/shard_map/all_to_all | solution.py:252
  106.8 8.9 %all_to_all.27.image_ref = bf16[8,8,1152]{2,1,0:T(8,128)(2,1)S(1)} all-to-all(bf16[8,8,1152]{2,1,0:T(8,128)(2,1)S(1)} %shard_map.74), channel_id=1, replica_groups=mesh['zl'=8,'yh'=2,'yl'=2,'zh'=2,'x'=4,'c'=2] {'x','yl'}, dimensions={0} | all-to-all | bytes 294912 | tf_op jit(solution)/shard_map/all_to_all | solution.py:256
  115.7 0.7 shard_map.75
  (5 shorter events, 0.2 us)
Async XLA Ops:
  1.4 20.7 %collective-permute-start = (bf16[16,1024]{1,0:T(8,128)(2,1)S(1)}, bf16[16,1024]{1,0:T(8,128)(2,1)S(1)}, u32[]{:S(2)}, u32[]{:S(2)}) collective-permute-start(bf16[16,1024]{1,0:T(8,128)(2,1)S(1)} %get-tuple-element.24.own_ref), channel_id=1, source_target_pairs={{0,32},{32,0},{1,33},{33,1},{2,34},{34,2},{3,35},{35,3},{4,36},{36... | collective-permute-start | bytes 98312 | tf_op jit(solution)/shard_map/ppermute | solution.py:221
  7.4 42.1 %all-to-all-start = ((bf16[16,16,1024]{2,1,0:T(8,128)(2,1)}), bf16[16,16,1024]{2,1,0:T(8,128)(2,1)S(1)}, u32[]{:S(2)}, u32[]{:S(2)}) async-start(bf16[16,16,1024]{2,1,0:T(8,128)(2,1)} %broadcast_in_dim.2), calls=%async_computation | async-start | bytes 1048576 | tf_op jit(solution)/shard_map/all_to_all | solution.py:227
  22.1 6.2 %collective-permute-start.1 = (bf16[2,16,1024]{2,1,0:T(8,128)(2,1)S(1)}, bf16[2,16,1024]{2,1,0:T(8,128)(2,1)S(1)}, u32[]{:S(2)}, u32[]{:S(2)}) collective-permute-start(bf16[2,16,1024]{2,1,0:T(8,128)(2,1)S(1)} %shard_map.67.own_ref), channel_id=1, source_target_pairs={{0,16},{16,0},{1,17},{17,1},{2,18},{18,2},{3,19},{19,3},{4,20},{20... | collective-permute-start | bytes 196616 | tf_op jit(solution)/shard_map/ppermute | solution.py:221
  42.1 3.8 %collective-permute-start.2 = (bf16[16,16,1024]{2,1,0:T(8,128)(2,1)S(1)}, bf16[16,16,1024]{2,1,0:T(8,128)(2,1)S(1)}, u32[]{:S(2)}, u32[]{:S(2)}) collective-permute-start(bf16[16,16,1024]{2,1,0:T(8,128)(2,1)S(1)} %bitcast.2), channel_id=1, source_target_pairs={{0,1},{1,0},{2,3},{3,2},{4,5},{5,4},{6,7},{7,6},{8,9},{9,8},{10,11... | collective-permute-start | bytes 1572872 | tf_op jit(solution)/shard_map/ppermute | solution.py:221
  83.7 23.2 %all-to-all-start.3 = ((bf16[16,8,1024]{2,1,0:T(8,128)(2,1)}), bf16[16,8,1024]{2,1,0:T(8,128)(2,1)S(1)}, u32[]{:S(2)}, u32[]{:S(2)}) async-start(bf16[16,8,1024]{2,1,0:T(8,128)(2,1)} %get-tuple-element.39), calls=%async_computation.3 | async-start | bytes 524288 | tf_op jit(solution)/shard_map/all_to_all | solution.py:252
  89.0 3.9 %collective-permute-start.3 = (f32[128,1152]{1,0:T(8,128)S(1)}, f32[128,1152]{1,0:T(8,128)S(1)}, u32[]{:S(2)}, u32[]{:S(2)}) collective-permute-start(f32[128,1152]{1,0:T(8,128)S(1)} %get-tuple-element.36), channel_id=1, source_target_pairs={{0,1},{1,0},{2,3},{3,2},{4,5},{5,4},{6,7},{7,6},{8,9},{9,8},{10,11... | collective-permute-start | bytes 1769480 | tf_op jit(solution)/shard_map/ppermute | solution.py:221
  92.9 9.3 %collective-permute-start.4 = (bf16[8,8,1152]{2,1,0:T(8,128)(2,1)S(1)}, bf16[8,8,1152]{2,1,0:T(8,128)(2,1)S(1)}, u32[]{:S(2)}, u32[]{:S(2)}) collective-permute-start(bf16[8,8,1152]{2,1,0:T(8,128)(2,1)S(1)} %get-tuple-element.38), channel_id=1, source_target_pairs={{0,32},{32,0},{1,33},{33,1},{2,34},{34,2},{3,35},{35,3},{4,36},{36... | collective-permute-start | bytes 442376 | tf_op jit(solution)/shard_map/ppermute | solution.py:221

commit v16 on v14

--- a/solution.py
+++ b/solution.py
@@ -178,15 +178,17 @@
         ref[:, width:] = jnp.broadcast_to(loss_ref[0:1], (side, 128))
 
 
-def core_kernel(keep_ref, got_ref, own_ref, send_ref):
-    total = (keep_ref[...] + got_ref[...]).reshape(4, 2, 2 * rows, keep_ref.shape[1])
-    first = lax.axis_index("yl") == 0
-    own_ref[...] = jnp.where(first, total[:, 0], total[:, 1]).reshape(own_ref.shape)
-    send_ref[...] = jnp.where(first, total[:, 1], total[:, 0]).reshape(own_ref.shape)
-
-
-def across_kernel(keep_ref, got_ref, out_ref):
-    total = keep_ref[...] + got_ref[...]
+def core_kernel(keep_ref, got_ref, own_ref, *send_refs):
+    y = lax.axis_index("yh") * 2 + lax.axis_index("yl")
+    for k, ref in enumerate((own_ref,) + send_refs):
+        to = (y + k) & 3
+        for x in range(4):
+            at = pl.ds(pl.multiple_of(x * 4 * rows + ((to & 1) * 2 + (to >> 1)) * rows, rows), rows)
+            ref[x] = keep_ref[at, :] + got_ref[at, :]
+
+
+def across_kernel(keep_ref, a_ref, b_ref, c_ref, out_ref):
+    total = (keep_ref[...] + a_ref[...]) + (b_ref[...] + c_ref[...])
     width = total.shape[2] - 128
     loss = total[:, :, width:]
     lane = lax.broadcasted_iota(jnp.int32, loss.shape, 2)
@@ -244,10 +246,13 @@
     keep, send = call(image_kernel, [shape(side, wide), shape(side, wide)], g_mine, g_other, texts, loss, flops=2**27)
     got = swap(send)
     got_text = lax.all_to_all(by_text, column, 0, 0, tiled=True)
-    keep, send = call(core_kernel, [shape(8, rows, wide)] * 2, keep, got)
-    (by_image,) = call(across_kernel, [shape(8, rows, wide, dtype=bf16)], keep, swap(send, "yl"))
+    keep, *send = call(core_kernel, [shape(4, rows, wide)] * 4, keep, got)
+    along = [
+        lax.ppermute(block, ("yh", "yl"), [(i, (i + k) % 4) for i in range(4)]) for k, block in enumerate(send, 1)
+    ]
+    (by_image,) = call(across_kernel, [shape(4, rows, wide, dtype=bf16)], keep, *along)
     by_image, got_text = lax.optimization_barrier((by_image, got_text))
-    got_image = lax.all_to_all(by_image, ("x", "yh"), 0, 0, tiled=True)
+    got_image = lax.all_to_all(by_image, "x", 0, 0, tiled=True)
     vmem = pl.BlockSpec(memory_space=pltpu.VMEM)
     grad_image, grad_text, loss = call(
         last_kernel, [shape(rows, width), shape(rows, width), shape(1, 1)], got_image, got_text,

time: 119 us -> 117 us (0.983)
  the two profiles are of different devices: /device:TPU:64 before, /device:TPU:32 now
where the time goes in v16:
time: 117 us
  blocking collectives  54 us (46%)
  starting transfers between devices  40.4 us (35%)
  waiting for transfers between devices  16.6 us (14%)
  Pallas kernels  3.43 us (3%)
    all_to_all x1, blocking collectives, local(): col_got = lax.all_to_all(col_sent, column, 0, 0, tiled=True)  19.3 us
    all_to_all x1, starting transfers between devices, local(): texts = lax.all_to_all(sent, column, 0, 0, tiled=True)  15.2 us
    all_gather x1, blocking collectives, local(): mine = lax.all_gather(pair, 'x').reshape(16, 16, width)  13.8 us
    all_to_all x1, blocking collectives, local(): lax.all_to_all(row_parts, ('x', 'yh', 'yl', 'c'), 0, 0, tiled=True)  12.8 us
    ppermute x4, starting transfers between devices, swap(): return lax.ppermute(block, axis, [(0, 1), (1, 0)])  11.5 us
    ppermute x3, starting transfers between devices, local(): lax.ppermute(block, ('yh', 'yl'), [(i, (i + k) % 4) for i in range(4)])  9.35 us
    all_to_all x1, blocking collectives, local(): got_image = lax.all_to_all(by_image, 'x', 0, 0, tiled=True)  8.04 us
    ppermute x4, waiting for transfers between devices, swap(): return lax.ppermute(block, axis, [(0, 1), (1, 0)])  7.41 us
  transfers between devices with their start and end apart: 9, of which 6 were waited for; matrix products, arithmetic and copies ran while one was open for 1% of the time, Pallas kernels for 0%

profile of v16, /device:TPU:32, one launch (start us, length us, event | category | flops | bytes accessed | tf_op | source)
XLA Modules:
  0.0 116.8 jit_solution(7780267747670508270)
XLA Ops:
  0.6 0.8 pad_maximum_fusion
  1.4 5.1 %collective-permute-start = (bf16[16,1024]{1,0:T(8,128)(2,1)S(1)}, bf16[16,1024]{1,0:T(8,128)(2,1)S(1)}, u32[]{:S(2)}, u32[]{:S(2)}) collective-permute-start(bf16[16,1024]{1,0:T(8,128)(2,1)S(1)} %get-tuple-element.26.own_ref), channel_id=1, source_target_pairs={{0,32},{32,0},{1,33},{33,1},{2,34},{34,2},{3,35},{35,3},{4,36},{36... | collective-permute-start | bytes 98312 | tf_op jit(solution)/shard_map/ppermute | solution.py:217
  6.5 0.8 broadcast_in_dim.2
  7.4 15.2 %all-to-all-start = ((bf16[16,16,1024]{2,1,0:T(8,128)(2,1)}), bf16[16,16,1024]{2,1,0:T(8,128)(2,1)S(1)}, u32[]{:S(2)}, u32[]{:S(2)}) async-start(bf16[16,16,1024]{2,1,0:T(8,128)(2,1)} %broadcast_in_dim.2), calls=%async_computation | async-start | bytes 1048576 | tf_op jit(solution)/shard_map/all_to_all | solution.py:223
  22.6 2.6 %collective-permute-start.1 = (bf16[2,16,1024]{2,1,0:T(8,128)(2,1)S(1)}, bf16[2,16,1024]{2,1,0:T(8,128)(2,1)S(1)}, u32[]{:S(2)}, u32[]{:S(2)}) collective-permute-start(bf16[2,16,1024]{2,1,0:T(8,128)(2,1)S(1)} %shard_map.67.own_ref), channel_id=1, source_target_pairs={{0,16},{16,0},{1,17},{17,1},{2,18},{18,2},{3,19},{19,3},{4,20},{20... | collective-permute-start | bytes 196616 | tf_op jit(solution)/shard_map/ppermute | solution.py:217
  25.2 3.6 %collective-permute-done.1.other_ref = bf16[2,16,1024]{2,1,0:T(8,128)(2,1)S(1)} collective-permute-done((bf16[2,16,1024]{2,1,0:T(8,128)(2,1)S(1)}, bf16[2,16,1024]{2,1,0:T(8,128)(2,1)S(1)}, u32[]{:S(2)}, u32[]{:S(2)}) %collective-permute-start.1) | collective-permute-done | bytes 65568 | tf_op jit(solution)/shard_map/ppermute | solution.py:217
  28.8 13.8 %all-gather = bf16[8,2,16,1024]{3,2,1,0:T(8,128)(2,1)S(1)} all-gather(bf16[2,2,16,1024]{3,2,1,0:T(8,128)(2,1)S(1)} %shard_map.68), channel_id=2, replica_groups=mesh['zl'=8,'yh'=2,'yl'=2,'zh'=2,'x'=4,'c'=2] {'x'}, dimensions={0}, use_global_device_ids=true | all-gather | bytes 655360 | tf_op jit(solution)/shard_map/all_gather | solution.py:227
  42.5 1.9 %collective-permute-start.2 = (bf16[16,16,1024]{2,1,0:T(8,128)(2,1)S(1)}, bf16[16,16,1024]{2,1,0:T(8,128)(2,1)S(1)}, u32[]{:S(2)}, u32[]{:S(2)}) collective-permute-start(bf16[16,16,1024]{2,1,0:T(8,128)(2,1)S(1)} %bitcast.2), channel_id=1, source_target_pairs={{0,1},{1,0},{2,3},{3,2},{4,5},{5,4},{6,7},{7,6},{8,9},{9,8},{10,11... | collective-permute-start | bytes 1572872 | tf_op jit(solution)/shard_map/ppermute | solution.py:217
  44.5 1.9 %collective-permute-done.2.other_ref = bf16[16,16,1024]{2,1,0:T(8,128)(2,1)S(1)} collective-permute-done((bf16[16,16,1024]{2,1,0:T(8,128)(2,1)S(1)}, bf16[16,16,1024]{2,1,0:T(8,128)(2,1)S(1)}, u32[]{:S(2)}, u32[]{:S(2)}) %collective-permute-start.2) | collective-permute-done | bytes 524320 | tf_op jit(solution)/shard_map/ppermute | solution.py:217
  46.3 3.9 %all-to-all-done.text_ref = bf16[16,16,1024]{2,1,0:T(8,128)(2,1)S(1)} async-done(((bf16[16,16,1024]{2,1,0:T(8,128)(2,1)}), bf16[16,16,1024]{2,1,0:T(8,128)(2,1)S(1)}, u32[]{:S(2)}, u32[]{:S(2)}) %all-to-all-start) | async-done | bytes 524320 | tf_op jit(solution)/shard_map/all_to_all | solution.py:223
  50.3 0.9 shard_map.69
  51.1 12.8 %all_to_all.25.got_ref = f32[32,8,128]{2,1,0:T(8,128)S(1)} all-to-all(f32[32,8,128]{2,1,0:T(8,128)S(1)} %get-tuple-element.30), channel_id=1, replica_groups=mesh['zl'=8,'yh'=2,'yl'=2,'zh'=2,'x'=4,'c'=2] {'x','yh','yl','c'}, dimensions={0} | all-to-all | bytes 262144 | tf_op jit(solution)/shard_map/all_to_all | solution.py:236
  64.2 19.3 %all_to_all.26.got_ref = f32[16,8,128]{2,1,0:T(8,128)S(1)} all-to-all(f32[16,8,128]{2,1,0:T(8,128)S(1)} %get-tuple-element.33), channel_id=1, replica_groups=mesh['zl'=8,'yh'=2,'yl'=2,'zh'=2,'x'=4,'c'=2] {'zh','zl'}, dimensions={0} | all-to-all | bytes 131072 | tf_op jit(solution)/shard_map/all_to_all | solution.py:238
  83.5 1.2 %shard_map.71 = (bf16[16,8,1024]{2,1,0:T(8,128)(2,1)}, f32[128,128]{1,0:T(8,128)S(1)}, f32[128,128]{1,0:T(8,128)S(1)}, f32[8,128]{1,0:T(8,128)S(1)}) custom-call(f32[256,128]{1,0:T(8,128)S(1)} %get-tuple-element.28.on_ref, f32[256,128]{1,0:T(8,128)S(1)} %get-tuple-element.29.mom_ref, f32[128,128]{1,0:T(8,128)S(1)} %get-tuple-element.32.lse_ref, ...), custom_call_target="tpu_custom_call" | custom-call | flops 134217728 | bytes 1839104 | tf_op jit(solution)/shard_map/pallas_call | solution.py:23
  84.7 4.4 %all-to-all-start.3 = ((bf16[16,8,1024]{2,1,0:T(8,128)(2,1)}), bf16[16,8,1024]{2,1,0:T(8,128)(2,1)S(1)}, u32[]{:S(2)}, u32[]{:S(2)}) async-start(bf16[16,8,1024]{2,1,0:T(8,128)(2,1)} %get-tuple-element.43), calls=%async_computation.3 | async-start | bytes 524288 | tf_op jit(solution)/shard_map/all_to_all | solution.py:248
  89.4 1.9 %collective-permute-start.3 = (f32[128,1152]{1,0:T(8,128)S(1)}, f32[128,1152]{1,0:T(8,128)S(1)}, u32[]{:S(2)}, u32[]{:S(2)}) collective-permute-start(f32[128,1152]{1,0:T(8,128)S(1)} %get-tuple-element.38), channel_id=1, source_target_pairs={{0,1},{1,0},{2,3},{3,2},{4,5},{5,4},{6,7},{7,6},{8,9},{9,8},{10,11... | collective-permute-start | bytes 1769480 | tf_op jit(solution)/shard_map/ppermute | solution.py:217
  91.3 2.0 %collective-permute-done.3.got_ref = f32[128,1152]{1,0:T(8,128)S(1)} collective-permute-done((f32[128,1152]{1,0:T(8,128)S(1)}, f32[128,1152]{1,0:T(8,128)S(1)}, u32[]{:S(2)}, u32[]{:S(2)}) %collective-permute-start.3) | collective-permute-done | bytes 589856 | tf_op jit(solution)/shard_map/ppermute | solution.py:217
  93.4 2.4 %collective-permute-start.4 = (f32[4,8,1152]{2,1,0:T(8,128)S(1)}, f32[4,8,1152]{2,1,0:T(8,128)S(1)}, u32[]{:S(2)}, u32[]{:S(2)}) collective-permute-start(f32[4,8,1152]{2,1,0:T(8,128)S(1)} %get-tuple-element.40), channel_id=1, source_target_pairs={{0,16},{16,32},{32,48},{48,0},{1,17},{17,33},{33,49},{49,1},{2,18}... | collective-permute-start | bytes 442376 | tf_op jit(solution)/shard_map/ppermute | solution.py:251
  95.8 4.0 %collective-permute-start.5 = (f32[4,8,1152]{2,1,0:T(8,128)S(1)}, f32[4,8,1152]{2,1,0:T(8,128)S(1)}, u32[]{:S(2)}, u32[]{:S(2)}) collective-permute-start(f32[4,8,1152]{2,1,0:T(8,128)S(1)} %get-tuple-element.41), channel_id=1, source_target_pairs={{0,32},{16,48},{32,0},{48,16},{1,33},{17,49},{33,1},{49,17},{2,34}... | collective-permute-start | bytes 442376 | tf_op jit(solution)/shard_map/ppermute | solution.py:251
  99.9 2.9 %collective-permute-start.6 = (f32[4,8,1152]{2,1,0:T(8,128)S(1)}, f32[4,8,1152]{2,1,0:T(8,128)S(1)}, u32[]{:S(2)}, u32[]{:S(2)}) collective-permute-start(f32[4,8,1152]{2,1,0:T(8,128)S(1)} %get-tuple-element.42), channel_id=1, source_target_pairs={{0,48},{16,0},{32,16},{48,32},{1,49},{17,1},{33,17},{49,33},{2,50}... | collective-permute-start | bytes 442376 | tf_op jit(solution)/shard_map/ppermute | solution.py:251
  102.7 2.8 %collective-permute-done.4.a_ref = f32[4,8,1152]{2,1,0:T(8,128)S(1)} collective-permute-done((f32[4,8,1152]{2,1,0:T(8,128)S(1)}, f32[4,8,1152]{2,1,0:T(8,128)S(1)}, u32[]{:S(2)}, u32[]{:S(2)}) %collective-permute-start.4) | collective-permute-done | bytes 147488 | tf_op jit(solution)/shard_map/ppermute | solution.py:251
  105.5 2.5 %collective-permute-done.6.c_ref = f32[4,8,1152]{2,1,0:T(8,128)S(1)} collective-permute-done((f32[4,8,1152]{2,1,0:T(8,128)S(1)}, f32[4,8,1152]{2,1,0:T(8,128)S(1)}, u32[]{:S(2)}, u32[]{:S(2)}) %collective-permute-start.6) | collective-permute-done | bytes 147488 | tf_op jit(solution)/shard_map/ppermute | solution.py:251
  108.1 8.0 %all_to_all.27.image_ref = bf16[4,8,1152]{2,1,0:T(8,128)(2,1)S(1)} all-to-all(bf16[4,8,1152]{2,1,0:T(8,128)(2,1)S(1)} %shard_map.74), channel_id=1, replica_groups=mesh['zl'=8,'yh'=2,'yl'=2,'zh'=2,'x'=4,'c'=2] {'x'}, dimensions={0} | all-to-all | bytes 147456 | tf_op jit(solution)/shard_map/all_to_all | solution.py:255
  116.1 0.7 shard_map.75
  (9 shorter events, 0.7 us)
Async XLA Ops:
  1.4 21.2 %collective-permute-start = (bf16[16,1024]{1,0:T(8,128)(2,1)S(1)}, bf16[16,1024]{1,0:T(8,128)(2,1)S(1)}, u32[]{:S(2)}, u32[]{:S(2)}) collective-permute-start(bf16[16,1024]{1,0:T(8,128)(2,1)S(1)} %get-tuple-element.26.own_ref), channel_id=1, source_target_pairs={{0,32},{32,0},{1,33},{33,1},{2,34},{34,2},{3,35},{35,3},{4,36},{36... | collective-permute-start | bytes 98312 | tf_op jit(solution)/shard_map/ppermute | solution.py:217
  7.4 42.9 %all-to-all-start = ((bf16[16,16,1024]{2,1,0:T(8,128)(2,1)}), bf16[16,16,1024]{2,1,0:T(8,128)(2,1)S(1)}, u32[]{:S(2)}, u32[]{:S(2)}) async-start(bf16[16,16,1024]{2,1,0:T(8,128)(2,1)} %broadcast_in_dim.2), calls=%async_computation | async-start | bytes 1048576 | tf_op jit(solution)/shard_map/all_to_all | solution.py:223
  22.6 6.2 %collective-permute-start.1 = (bf16[2,16,1024]{2,1,0:T(8,128)(2,1)S(1)}, bf16[2,16,1024]{2,1,0:T(8,128)(2,1)S(1)}, u32[]{:S(2)}, u32[]{:S(2)}) collective-permute-start(bf16[2,16,1024]{2,1,0:T(8,128)(2,1)S(1)} %shard_map.67.own_ref), channel_id=1, source_target_pairs={{0,16},{16,0},{1,17},{17,1},{2,18},{18,2},{3,19},{19,3},{4,20},{20... | collective-permute-start | bytes 196616 | tf_op jit(solution)/shard_map/ppermute | solution.py:217
  42.5 3.8 %collective-permute-start.2 = (bf16[16,16,1024]{2,1,0:T(8,128)(2,1)S(1)}, bf16[16,16,1024]{2,1,0:T(8,128)(2,1)S(1)}, u32[]{:S(2)}, u32[]{:S(2)}) collective-permute-start(bf16[16,16,1024]{2,1,0:T(8,128)(2,1)S(1)} %bitcast.2), channel_id=1, source_target_pairs={{0,1},{1,0},{2,3},{3,2},{4,5},{5,4},{6,7},{7,6},{8,9},{9,8},{10,11... | collective-permute-start | bytes 1572872 | tf_op jit(solution)/shard_map/ppermute | solution.py:217
  84.7 23.4 %all-to-all-start.3 = ((bf16[16,8,1024]{2,1,0:T(8,128)(2,1)}), bf16[16,8,1024]{2,1,0:T(8,128)(2,1)S(1)}, u32[]{:S(2)}, u32[]{:S(2)}) async-start(bf16[16,8,1024]{2,1,0:T(8,128)(2,1)} %get-tuple-element.43), calls=%async_computation.3 | async-start | bytes 524288 | tf_op jit(solution)/shard_map/all_to_all | solution.py:248
  89.4 3.9 %collective-permute-start.3 = (f32[128,1152]{1,0:T(8,128)S(1)}, f32[128,1152]{1,0:T(8,128)S(1)}, u32[]{:S(2)}, u32[]{:S(2)}) collective-permute-start(f32[128,1152]{1,0:T(8,128)S(1)} %get-tuple-element.38), channel_id=1, source_target_pairs={{0,1},{1,0},{2,3},{3,2},{4,5},{5,4},{6,7},{7,6},{8,9},{9,8},{10,11... | collective-permute-start | bytes 1769480 | tf_op jit(solution)/shard_map/ppermute | solution.py:217
  93.4 12.2 %collective-permute-start.4 = (f32[4,8,1152]{2,1,0:T(8,128)S(1)}, f32[4,8,1152]{2,1,0:T(8,128)S(1)}, u32[]{:S(2)}, u32[]{:S(2)}) collective-permute-start(f32[4,8,1152]{2,1,0:T(8,128)S(1)} %get-tuple-element.40), channel_id=1, source_target_pairs={{0,16},{16,32},{32,48},{48,0},{1,17},{17,33},{33,49},{49,1},{2,18}... | collective-permute-start | bytes 442376 | tf_op jit(solution)/shard_map/ppermute | solution.py:251
  95.8 9.7 %collective-permute-start.5 = (f32[4,8,1152]{2,1,0:T(8,128)S(1)}, f32[4,8,1152]{2,1,0:T(8,128)S(1)}, u32[]{:S(2)}, u32[]{:S(2)}) collective-permute-start(f32[4,8,1152]{2,1,0:T(8,128)S(1)} %get-tuple-element.41), channel_id=1, source_target_pairs={{0,32},{16,48},{32,0},{48,16},{1,33},{17,49},{33,1},{49,17},{2,34}... | collective-permute-start | bytes 442376 | tf_op jit(solution)/shard_map/ppermute | solution.py:251
  99.9 8.1 %collective-permute-start.6 = (f32[4,8,1152]{2,1,0:T(8,128)S(1)}, f32[4,8,1152]{2,1,0:T(8,128)S(1)}, u32[]{:S(2)}, u32[]{:S(2)}) collective-permute-start(f32[4,8,1152]{2,1,0:T(8,128)S(1)} %get-tuple-element.42), channel_id=1, source_target_pairs={{0,48},{16,0},{32,16},{48,32},{1,49},{17,1},{33,17},{49,33},{2,50}... | collective-permute-start | bytes 442376 | tf_op jit(solution)/shard_map/ppermute | solution.py:251

commit v17 on v15

--- a/solution.py
+++ b/solution.py
@@ -191,15 +191,25 @@
     ref[:, :, width:] = pieces.astype(bf16)
 
 
-def core_kernel(keep_ref, got_ref, own_ref, send_ref):
-    total = (keep_ref[...] + got_ref[...]).reshape(8, 2, rows, keep_ref.shape[1])
-    first = lax.axis_index("yh") == 0
-    own_ref[...] = jnp.where(first, total[:, 0], total[:, 1])
-    send_out(jnp.where(first, total[:, 1], total[:, 0]), send_ref)
-
-
-def across_kernel(keep_ref, got_ref, out_ref):
-    keep, got = keep_ref[...], got_ref[...].astype(f32)
+def core_kernel(keep_ref, got_ref, own_ref, *send_refs):
+    y = lax.axis_index("yh") * 2 + lax.axis_index("yl")
+
+    def block(k):
+        to = (y + k) & 3
+        parts = []
+        for x in range(4):
+            at = pl.ds(pl.multiple_of(x * 4 * rows + ((to & 1) * 2 + (to >> 1)) * rows, rows), rows)
+            parts.append(keep_ref[at, :] + got_ref[at, :])
+        return jnp.stack(parts)
+
+    own_ref[...] = block(0)
+    for k, ref in enumerate(send_refs, 1):
+        send_out(block(k), ref)
+
+
+def across_kernel(keep_ref, a_ref, b_ref, c_ref, out_ref):
+    keep = keep_ref[...]
+    got = (a_ref[...].astype(f32) + b_ref[...].astype(f32)) + c_ref[...].astype(f32)
     width = keep.shape[2] - 128
     loss = keep[:, :, width:] + jnp.sum(got[:, :, width:], axis=2, keepdims=True)
     send_out(jnp.concatenate([keep[:, :, :width] + got[:, :, :width], loss], axis=2), out_ref)
@@ -250,10 +260,13 @@
     keep, send = call(image_kernel, [shape(side, wide), shape(side, wide)], g_mine, g_other, texts, loss, flops=2**27)
     got = swap(send)
     got_text = lax.all_to_all(by_text, column, 0, 0, tiled=True)
-    keep, send = call(core_kernel, [shape(8, rows, wide), shape(8, rows, wide, dtype=bf16)], keep, got)
-    (by_image,) = call(across_kernel, [shape(8, rows, wide, dtype=bf16)], keep, swap(send, "yh"))
+    keep, *send = call(core_kernel, [shape(4, rows, wide)] + [shape(4, rows, wide, dtype=bf16)] * 3, keep, got)
+    along = [
+        lax.ppermute(block, ("yh", "yl"), [(i, (i + k) % 4) for i in range(4)]) for k, block in enumerate(send, 1)
+    ]
+    (by_image,) = call(across_kernel, [shape(4, rows, wide, dtype=bf16)], keep, *along)
     by_image, got_text = lax.optimization_barrier((by_image, got_text))
-    got_image = lax.all_to_all(by_image, ("x", "yl"), 0, 0, tiled=True)
+    got_image = lax.all_to_all(by_image, "x", 0, 0, tiled=True)
     vmem = pl.BlockSpec(memory_space=pltpu.VMEM)
     grad_image, grad_text, loss = call(
         last_kernel, [shape(rows, width), shape(rows, width), shape(1, 1)], got_image, got_text,

time: 117 us -> 116 us (level)
  starting transfers between devices: 34.1 us -> 40.6 us
  waiting for transfers between devices: 21.8 us -> 15.4 us
    ppermute x0 -> x3, starting transfers between devices: none -> 9.35 us  [local(): lax.ppermute(block, ('yh', 'yl'), [(i, (i + k) % 4) for i in range(4)])]
    ppermute x5 -> x4, waiting for transfers between devices: 13.8 us -> 7.41 us  [swap(): return lax.ppermute(block, axis, [(0, 1), (1, 0)])]
    all_to_all x1, waiting for transfers between devices: 4.5 us -> 1.04 us  [local(): got_text = lax.all_to_all(by_text, column, 0, 0, tiled=True)]
    ppermute x0 -> x3, waiting for transfers between devices: none -> 3.36 us  [local(): lax.ppermute(block, ('yh', 'yl'), [(i, (i + k) % 4) for i in range(4)])]
    ppermute x5 -> x4, starting transfers between devices: 14.4 us -> 11.5 us  [swap(): return lax.ppermute(block, axis, [(0, 1), (1, 0)])]
  transfers between devices with their start and end apart: 7 -> 9, of which waited for: 6 -> 7; matrix products, arithmetic and copies ran while one was open for 1% -> 1% of each run, Pallas kernels for 0% -> 0%
where the time goes in v17:
time: 116 us
  blocking collectives  53.7 us (46%)
  starting transfers between devices  40.6 us (35%)
  waiting for transfers between devices  15.4 us (13%)
  Pallas kernels  3.52 us (3%)
    all_to_all x1, blocking collectives, local(): col_got = lax.all_to_all(col_sent, column, 0, 0, tiled=True)  19.1 us
    all_to_all x1, starting transfers between devices, local(): texts = lax.all_to_all(sent, column, 0, 0, tiled=True)  14.8 us
    all_gather x1, blocking collectives, local(): mine = lax.all_gather(pair, 'x').reshape(16, 16, width)  13.8 us
    all_to_all x1, blocking collectives, local(): lax.all_to_all(row_parts, ('x', 'yh', 'yl', 'c'), 0, 0, tiled=True)  12.8 us
    ppermute x4, starting transfers between devices, swap(): return lax.ppermute(block, axis, [(0, 1), (1, 0)])  11.5 us
    ppermute x3, starting transfers between devices, local(): lax.ppermute(block, ('yh', 'yl'), [(i, (i + k) % 4) for i in range(4)])  9.35 us
    all_to_all x1, blocking collectives, local(): got_image = lax.all_to_all(by_image, 'x', 0, 0, tiled=True)  8.02 us
    ppermute x4, waiting for transfers between devices, swap(): return lax.ppermute(block, axis, [(0, 1), (1, 0)])  7.41 us
  transfers between devices with their start and end apart: 9, of which 7 were waited for; matrix products, arithmetic and copies ran while one was open for 1% of the time, Pallas kernels for 0%

profile of v17, /device:TPU:64, one launch (start us, length us, event | category | flops | bytes accessed | tf_op | source)
XLA Modules:
  0.0 115.5 jit_solution(844039332042568401)
XLA Ops:
  0.6 0.8 pad_maximum_fusion
  1.4 5.1 %collective-permute-start = (bf16[16,1024]{1,0:T(8,128)(2,1)S(1)}, bf16[16,1024]{1,0:T(8,128)(2,1)S(1)}, u32[]{:S(2)}, u32[]{:S(2)}) collective-permute-start(bf16[16,1024]{1,0:T(8,128)(2,1)S(1)} %get-tuple-element.26.own_ref), channel_id=1, source_target_pairs={{0,32},{32,0},{1,33},{33,1},{2,34},{34,2},{3,35},{35,3},{4,36},{36... | collective-permute-start | bytes 98312 | tf_op jit(solution)/shard_map/ppermute | solution.py:231
  6.5 0.8 broadcast_in_dim.2
  7.4 14.8 %all-to-all-start = ((bf16[16,16,1024]{2,1,0:T(8,128)(2,1)}), bf16[16,16,1024]{2,1,0:T(8,128)(2,1)S(1)}, u32[]{:S(2)}, u32[]{:S(2)}) async-start(bf16[16,16,1024]{2,1,0:T(8,128)(2,1)} %broadcast_in_dim.2), calls=%async_computation | async-start | bytes 1048576 | tf_op jit(solution)/shard_map/all_to_all | solution.py:237
  22.1 2.6 %collective-permute-start.1 = (bf16[2,16,1024]{2,1,0:T(8,128)(2,1)S(1)}, bf16[2,16,1024]{2,1,0:T(8,128)(2,1)S(1)}, u32[]{:S(2)}, u32[]{:S(2)}) collective-permute-start(bf16[2,16,1024]{2,1,0:T(8,128)(2,1)S(1)} %shard_map.67.own_ref), channel_id=1, source_target_pairs={{0,16},{16,0},{1,17},{17,1},{2,18},{18,2},{3,19},{19,3},{4,20},{20... | collective-permute-start | bytes 196616 | tf_op jit(solution)/shard_map/ppermute | solution.py:231
  24.7 3.6 %collective-permute-done.1.other_ref = bf16[2,16,1024]{2,1,0:T(8,128)(2,1)S(1)} collective-permute-done((bf16[2,16,1024]{2,1,0:T(8,128)(2,1)S(1)}, bf16[2,16,1024]{2,1,0:T(8,128)(2,1)S(1)}, u32[]{:S(2)}, u32[]{:S(2)}) %collective-permute-start.1) | collective-permute-done | bytes 65568 | tf_op jit(solution)/shard_map/ppermute | solution.py:231
  28.3 13.8 %all-gather = bf16[8,2,16,1024]{3,2,1,0:T(8,128)(2,1)S(1)} all-gather(bf16[2,2,16,1024]{3,2,1,0:T(8,128)(2,1)S(1)} %shard_map.68), channel_id=2, replica_groups=mesh['zl'=8,'yh'=2,'yl'=2,'zh'=2,'x'=4,'c'=2] {'x'}, dimensions={0}, use_global_device_ids=true | all-gather | bytes 655360 | tf_op jit(solution)/shard_map/all_gather | solution.py:241
  42.1 1.9 %collective-permute-start.2 = (bf16[16,16,1024]{2,1,0:T(8,128)(2,1)S(1)}, bf16[16,16,1024]{2,1,0:T(8,128)(2,1)S(1)}, u32[]{:S(2)}, u32[]{:S(2)}) collective-permute-start(bf16[16,16,1024]{2,1,0:T(8,128)(2,1)S(1)} %bitcast.2), channel_id=1, source_target_pairs={{0,1},{1,0},{2,3},{3,2},{4,5},{5,4},{6,7},{7,6},{8,9},{9,8},{10,11... | collective-permute-start | bytes 1572872 | tf_op jit(solution)/shard_map/ppermute | solution.py:231
  44.0 1.9 %collective-permute-done.2.other_ref = bf16[16,16,1024]{2,1,0:T(8,128)(2,1)S(1)} collective-permute-done((bf16[16,16,1024]{2,1,0:T(8,128)(2,1)S(1)}, bf16[16,16,1024]{2,1,0:T(8,128)(2,1)S(1)}, u32[]{:S(2)}, u32[]{:S(2)}) %collective-permute-start.2) | collective-permute-done | bytes 524320 | tf_op jit(solution)/shard_map/ppermute | solution.py:231
  45.9 3.5 %all-to-all-done.text_ref = bf16[16,16,1024]{2,1,0:T(8,128)(2,1)S(1)} async-done(((bf16[16,16,1024]{2,1,0:T(8,128)(2,1)}), bf16[16,16,1024]{2,1,0:T(8,128)(2,1)S(1)}, u32[]{:S(2)}, u32[]{:S(2)}) %all-to-all-start) | async-done | bytes 524320 | tf_op jit(solution)/shard_map/all_to_all | solution.py:237
  49.4 0.9 shard_map.69
  50.3 12.8 %all_to_all.25.got_ref = f32[32,8,128]{2,1,0:T(8,128)S(1)} all-to-all(f32[32,8,128]{2,1,0:T(8,128)S(1)} %get-tuple-element.30), channel_id=1, replica_groups=mesh['zl'=8,'yh'=2,'yl'=2,'zh'=2,'x'=4,'c'=2] {'x','yh','yl','c'}, dimensions={0} | all-to-all | bytes 262144 | tf_op jit(solution)/shard_map/all_to_all | solution.py:250
  63.3 19.1 %all_to_all.26.got_ref = f32[16,8,128]{2,1,0:T(8,128)S(1)} all-to-all(f32[16,8,128]{2,1,0:T(8,128)S(1)} %get-tuple-element.33), channel_id=1, replica_groups=mesh['zl'=8,'yh'=2,'yl'=2,'zh'=2,'x'=4,'c'=2] {'zh','zl'}, dimensions={0} | all-to-all | bytes 131072 | tf_op jit(solution)/shard_map/all_to_all | solution.py:252
  82.4 1.2 %shard_map.71 = (bf16[16,8,1024]{2,1,0:T(8,128)(2,1)}, f32[128,128]{1,0:T(8,128)S(1)}, f32[128,128]{1,0:T(8,128)S(1)}, f32[8,128]{1,0:T(8,128)S(1)}) custom-call(f32[256,128]{1,0:T(8,128)S(1)} %get-tuple-element.28.on_ref, f32[256,128]{1,0:T(8,128)S(1)} %get-tuple-element.29.mom_ref, f32[128,128]{1,0:T(8,128)S(1)} %get-tuple-element.32.lse_ref, ...), custom_call_target="tpu_custom_call" | custom-call | flops 134217728 | bytes 1839104 | tf_op jit(solution)/shard_map/pallas_call | solution.py:23
  83.6 5.0 %all-to-all-start.3 = ((bf16[16,8,1024]{2,1,0:T(8,128)(2,1)}), bf16[16,8,1024]{2,1,0:T(8,128)(2,1)S(1)}, u32[]{:S(2)}, u32[]{:S(2)}) async-start(bf16[16,8,1024]{2,1,0:T(8,128)(2,1)} %get-tuple-element.43), calls=%async_computation.3 | async-start | bytes 524288 | tf_op jit(solution)/shard_map/all_to_all | solution.py:262
  89.0 1.9 %collective-permute-start.3 = (f32[128,1152]{1,0:T(8,128)S(1)}, f32[128,1152]{1,0:T(8,128)S(1)}, u32[]{:S(2)}, u32[]{:S(2)}) collective-permute-start(f32[128,1152]{1,0:T(8,128)S(1)} %get-tuple-element.38), channel_id=1, source_target_pairs={{0,1},{1,0},{2,3},{3,2},{4,5},{5,4},{6,7},{7,6},{8,9},{9,8},{10,11... | collective-permute-start | bytes 1769480 | tf_op jit(solution)/shard_map/ppermute | solution.py:231
  90.9 2.0 %collective-permute-done.3.got_ref = f32[128,1152]{1,0:T(8,128)S(1)} collective-permute-done((f32[128,1152]{1,0:T(8,128)S(1)}, f32[128,1152]{1,0:T(8,128)S(1)}, u32[]{:S(2)}, u32[]{:S(2)}) %collective-permute-start.3) | collective-permute-done | bytes 589856 | tf_op jit(solution)/shard_map/ppermute | solution.py:231
  92.9 2.4 %collective-permute-start.4 = (bf16[4,8,1152]{2,1,0:T(8,128)(2,1)S(1)}, bf16[4,8,1152]{2,1,0:T(8,128)(2,1)S(1)}, u32[]{:S(2)}, u32[]{:S(2)}) collective-permute-start(bf16[4,8,1152]{2,1,0:T(8,128)(2,1)S(1)} %get-tuple-element.40), channel_id=1, source_target_pairs={{0,16},{16,32},{32,48},{48,0},{1,17},{17,33},{33,49},{49,1},{2,18}... | collective-permute-start | bytes 221192 | tf_op jit(solution)/shard_map/ppermute | solution.py:265
  95.4 4.0 %collective-permute-start.5 = (bf16[4,8,1152]{2,1,0:T(8,128)(2,1)S(1)}, bf16[4,8,1152]{2,1,0:T(8,128)(2,1)S(1)}, u32[]{:S(2)}, u32[]{:S(2)}) collective-permute-start(bf16[4,8,1152]{2,1,0:T(8,128)(2,1)S(1)} %get-tuple-element.41), channel_id=1, source_target_pairs={{0,32},{16,48},{32,0},{48,16},{1,33},{17,49},{33,1},{49,17},{2,34}... | collective-permute-start | bytes 221192 | tf_op jit(solution)/shard_map/ppermute | solution.py:265
  99.4 2.9 %collective-permute-start.6 = (bf16[4,8,1152]{2,1,0:T(8,128)(2,1)S(1)}, bf16[4,8,1152]{2,1,0:T(8,128)(2,1)S(1)}, u32[]{:S(2)}, u32[]{:S(2)}) collective-permute-start(bf16[4,8,1152]{2,1,0:T(8,128)(2,1)S(1)} %get-tuple-element.42), channel_id=1, source_target_pairs={{0,48},{16,0},{32,16},{48,32},{1,49},{17,1},{33,17},{49,33},{2,50}... | collective-permute-start | bytes 221192 | tf_op jit(solution)/shard_map/ppermute | solution.py:265
  102.3 0.8 collective-permute-done.5.b_ref
  103.1 2.5 %collective-permute-done.6.c_ref = bf16[4,8,1152]{2,1,0:T(8,128)(2,1)S(1)} collective-permute-done((bf16[4,8,1152]{2,1,0:T(8,128)(2,1)S(1)}, bf16[4,8,1152]{2,1,0:T(8,128)(2,1)S(1)}, u32[]{:S(2)}, u32[]{:S(2)}) %collective-permute-start.6) | collective-permute-done | bytes 73760 | tf_op jit(solution)/shard_map/ppermute | solution.py:265
  105.8 1.0 all-to-all-done.3.text_ref
  106.8 8.0 %all_to_all.27.image_ref = bf16[4,8,1152]{2,1,0:T(8,128)(2,1)S(1)} all-to-all(bf16[4,8,1152]{2,1,0:T(8,128)(2,1)S(1)} %shard_map.74), channel_id=1, replica_groups=mesh['zl'=8,'yh'=2,'yl'=2,'zh'=2,'x'=4,'c'=2] {'x'}, dimensions={0} | all-to-all | bytes 147456 | tf_op jit(solution)/shard_map/all_to_all | solution.py:269
  (9 shorter events, 1.4 us)
Async XLA Ops:
  1.4 20.7 %collective-permute-start = (bf16[16,1024]{1,0:T(8,128)(2,1)S(1)}, bf16[16,1024]{1,0:T(8,128)(2,1)S(1)}, u32[]{:S(2)}, u32[]{:S(2)}) collective-permute-start(bf16[16,1024]{1,0:T(8,128)(2,1)S(1)} %get-tuple-element.26.own_ref), channel_id=1, source_target_pairs={{0,32},{32,0},{1,33},{33,1},{2,34},{34,2},{3,35},{35,3},{4,36},{36... | collective-permute-start | bytes 98312 | tf_op jit(solution)/shard_map/ppermute | solution.py:231
  7.4 42.1 %all-to-all-start = ((bf16[16,16,1024]{2,1,0:T(8,128)(2,1)}), bf16[16,16,1024]{2,1,0:T(8,128)(2,1)S(1)}, u32[]{:S(2)}, u32[]{:S(2)}) async-start(bf16[16,16,1024]{2,1,0:T(8,128)(2,1)} %broadcast_in_dim.2), calls=%async_computation | async-start | bytes 1048576 | tf_op jit(solution)/shard_map/all_to_all | solution.py:237
  22.1 6.2 %collective-permute-start.1 = (bf16[2,16,1024]{2,1,0:T(8,128)(2,1)S(1)}, bf16[2,16,1024]{2,1,0:T(8,128)(2,1)S(1)}, u32[]{:S(2)}, u32[]{:S(2)}) collective-permute-start(bf16[2,16,1024]{2,1,0:T(8,128)(2,1)S(1)} %shard_map.67.own_ref), channel_id=1, source_target_pairs={{0,16},{16,0},{1,17},{17,1},{2,18},{18,2},{3,19},{19,3},{4,20},{20... | collective-permute-start | bytes 196616 | tf_op jit(solution)/shard_map/ppermute | solution.py:231
  42.1 3.8 %collective-permute-start.2 = (bf16[16,16,1024]{2,1,0:T(8,128)(2,1)S(1)}, bf16[16,16,1024]{2,1,0:T(8,128)(2,1)S(1)}, u32[]{:S(2)}, u32[]{:S(2)}) collective-permute-start(bf16[16,16,1024]{2,1,0:T(8,128)(2,1)S(1)} %bitcast.2), channel_id=1, source_target_pairs={{0,1},{1,0},{2,3},{3,2},{4,5},{5,4},{6,7},{7,6},{8,9},{9,8},{10,11... | collective-permute-start | bytes 1572872 | tf_op jit(solution)/shard_map/ppermute | solution.py:231
  83.6 23.2 %all-to-all-start.3 = ((bf16[16,8,1024]{2,1,0:T(8,128)(2,1)}), bf16[16,8,1024]{2,1,0:T(8,128)(2,1)S(1)}, u32[]{:S(2)}, u32[]{:S(2)}) async-start(bf16[16,8,1024]{2,1,0:T(8,128)(2,1)} %get-tuple-element.43), calls=%async_computation.3 | async-start | bytes 524288 | tf_op jit(solution)/shard_map/all_to_all | solution.py:262
  89.0 3.9 %collective-permute-start.3 = (f32[128,1152]{1,0:T(8,128)S(1)}, f32[128,1152]{1,0:T(8,128)S(1)}, u32[]{:S(2)}, u32[]{:S(2)}) collective-permute-start(f32[128,1152]{1,0:T(8,128)S(1)} %get-tuple-element.38), channel_id=1, source_target_pairs={{0,1},{1,0},{2,3},{3,2},{4,5},{5,4},{6,7},{7,6},{8,9},{9,8},{10,11... | collective-permute-start | bytes 1769480 | tf_op jit(solution)/shard_map/ppermute | solution.py:231
  92.9 9.4 %collective-permute-start.4 = (bf16[4,8,1152]{2,1,0:T(8,128)(2,1)S(1)}, bf16[4,8,1152]{2,1,0:T(8,128)(2,1)S(1)}, u32[]{:S(2)}, u32[]{:S(2)}) collective-permute-start(bf16[4,8,1152]{2,1,0:T(8,128)(2,1)S(1)} %get-tuple-element.40), channel_id=1, source_target_pairs={{0,16},{16,32},{32,48},{48,0},{1,17},{17,33},{33,49},{49,1},{2,18}... | collective-permute-start | bytes 221192 | tf_op jit(solution)/shard_map/ppermute | solution.py:265
  95.4 7.8 %collective-permute-start.5 = (bf16[4,8,1152]{2,1,0:T(8,128)(2,1)S(1)}, bf16[4,8,1152]{2,1,0:T(8,128)(2,1)S(1)}, u32[]{:S(2)}, u32[]{:S(2)}) collective-permute-start(bf16[4,8,1152]{2,1,0:T(8,128)(2,1)S(1)} %get-tuple-element.41), channel_id=1, source_target_pairs={{0,32},{16,48},{32,0},{48,16},{1,33},{17,49},{33,1},{49,17},{2,34}... | collective-permute-start | bytes 221192 | tf_op jit(solution)/shard_map/ppermute | solution.py:265
  99.4 6.2 %collective-permute-start.6 = (bf16[4,8,1152]{2,1,0:T(8,128)(2,1)S(1)}, bf16[4,8,1152]{2,1,0:T(8,128)(2,1)S(1)}, u32[]{:S(2)}, u32[]{:S(2)}) collective-permute-start(bf16[4,8,1152]{2,1,0:T(8,128)(2,1)S(1)} %get-tuple-element.42), channel_id=1, source_target_pairs={{0,48},{16,0},{32,16},{48,32},{1,49},{17,1},{33,17},{49,33},{2,50}... | collective-permute-start | bytes 221192 | tf_op jit(solution)/shard_map/ppermute | solution.py:265

commit v18 on v17

--- a/solution.py
+++ b/solution.py
@@ -220,7 +220,7 @@
     width = grad_image_ref.shape[1]
     grad_image_ref[...] = total[:, :width]
     grad_text_ref[...] = jnp.sum(text_ref[...].astype(f32), axis=0)
-    loss_ref[0, 0] = jnp.sum(total[:1, width:]) * (1.0 / (2.0 * rows * n_plane * n_column))
+    loss_ref[...] = jnp.sum(total[:1, width:], axis=1, keepdims=True) * (1.0 / (2.0 * rows * n_plane * n_column))
 
 
 def local(image, text, mimage, mtext):
@@ -267,10 +267,8 @@
     (by_image,) = call(across_kernel, [shape(4, rows, wide, dtype=bf16)], keep, *along)
     by_image, got_text = lax.optimization_barrier((by_image, got_text))
     got_image = lax.all_to_all(by_image, "x", 0, 0, tiled=True)
-    vmem = pl.BlockSpec(memory_space=pltpu.VMEM)
     grad_image, grad_text, loss = call(
-        last_kernel, [shape(rows, width), shape(rows, width), shape(1, 1)], got_image, got_text,
-        out_specs=[vmem, vmem, pl.BlockSpec(memory_space=pltpu.SMEM)],
+        last_kernel, [shape(rows, width), shape(rows, width), shape(1, 1)], got_image, got_text
     )
     return grad_image, grad_text, loss[0, 0]
 

time: 116 us -> 116 us (level)
  no operation moved by 1% of the time
where the time goes in v18:
time: 116 us
  blocking collectives  53.7 us (46%)
  starting transfers between devices  40.6 us (35%)
  waiting for transfers between devices  15.4 us (13%)
  Pallas kernels  3.51 us (3%)
    all_to_all x1, blocking collectives, local(): col_got = lax.all_to_all(col_sent, column, 0, 0, tiled=True)  19.1 us
    all_to_all x1, starting transfers between devices, local(): texts = lax.all_to_all(sent, column, 0, 0, tiled=True)  14.8 us
    all_gather x1, blocking collectives, local(): mine = lax.all_gather(pair, 'x').reshape(16, 16, width)  13.8 us
    all_to_all x1, blocking collectives, local(): lax.all_to_all(row_parts, ('x', 'yh', 'yl', 'c'), 0, 0, tiled=True)  12.8 us
    ppermute x4, starting transfers between devices, swap(): return lax.ppermute(block, axis, [(0, 1), (1, 0)])  11.5 us
    ppermute x3, starting transfers between devices, local(): lax.ppermute(block, ('yh', 'yl'), [(i, (i + k) % 4) for i in range(4)])  9.35 us
    all_to_all x1, blocking collectives, local(): got_image = lax.all_to_all(by_image, 'x', 0, 0, tiled=True)  8.02 us
    ppermute x4, waiting for transfers between devices, swap(): return lax.ppermute(block, axis, [(0, 1), (1, 0)])  7.41 us
  transfers between devices with their start and end apart: 9, of which 7 were waited for; matrix products, arithmetic and copies ran while one was open for 1% of the time, Pallas kernels for 0%

profile of v18, /device:TPU:64, one launch (start us, length us, event | category | flops | bytes accessed | tf_op | source)
XLA Modules:
  0.0 115.5 jit_solution(16346351495245300702)
XLA Ops:
  0.6 0.8 pad_maximum_fusion
  1.4 5.1 %collective-permute-start = (bf16[16,1024]{1,0:T(8,128)(2,1)S(1)}, bf16[16,1024]{1,0:T(8,128)(2,1)S(1)}, u32[]{:S(2)}, u32[]{:S(2)}) collective-permute-start(bf16[16,1024]{1,0:T(8,128)(2,1)S(1)} %get-tuple-element.26.own_ref), channel_id=1, source_target_pairs={{0,32},{32,0},{1,33},{33,1},{2,34},{34,2},{3,35},{35,3},{4,36},{36... | collective-permute-start | bytes 98312 | tf_op jit(solution)/shard_map/ppermute | solution.py:231
  6.5 0.8 broadcast_in_dim.2
  7.4 14.8 %all-to-all-start = ((bf16[16,16,1024]{2,1,0:T(8,128)(2,1)}), bf16[16,16,1024]{2,1,0:T(8,128)(2,1)S(1)}, u32[]{:S(2)}, u32[]{:S(2)}) async-start(bf16[16,16,1024]{2,1,0:T(8,128)(2,1)} %broadcast_in_dim.2), calls=%async_computation | async-start | bytes 1048576 | tf_op jit(solution)/shard_map/all_to_all | solution.py:237
  22.1 2.6 %collective-permute-start.1 = (bf16[2,16,1024]{2,1,0:T(8,128)(2,1)S(1)}, bf16[2,16,1024]{2,1,0:T(8,128)(2,1)S(1)}, u32[]{:S(2)}, u32[]{:S(2)}) collective-permute-start(bf16[2,16,1024]{2,1,0:T(8,128)(2,1)S(1)} %shard_map.67.own_ref), channel_id=1, source_target_pairs={{0,16},{16,0},{1,17},{17,1},{2,18},{18,2},{3,19},{19,3},{4,20},{20... | collective-permute-start | bytes 196616 | tf_op jit(solution)/shard_map/ppermute | solution.py:231
  24.7 3.6 %collective-permute-done.1.other_ref = bf16[2,16,1024]{2,1,0:T(8,128)(2,1)S(1)} collective-permute-done((bf16[2,16,1024]{2,1,0:T(8,128)(2,1)S(1)}, bf16[2,16,1024]{2,1,0:T(8,128)(2,1)S(1)}, u32[]{:S(2)}, u32[]{:S(2)}) %collective-permute-start.1) | collective-permute-done | bytes 65568 | tf_op jit(solution)/shard_map/ppermute | solution.py:231
  28.3 13.8 %all-gather = bf16[8,2,16,1024]{3,2,1,0:T(8,128)(2,1)S(1)} all-gather(bf16[2,2,16,1024]{3,2,1,0:T(8,128)(2,1)S(1)} %shard_map.68), channel_id=2, replica_groups=mesh['zl'=8,'yh'=2,'yl'=2,'zh'=2,'x'=4,'c'=2] {'x'}, dimensions={0}, use_global_device_ids=true | all-gather | bytes 655360 | tf_op jit(solution)/shard_map/all_gather | solution.py:241
  42.1 1.9 %collective-permute-start.2 = (bf16[16,16,1024]{2,1,0:T(8,128)(2,1)S(1)}, bf16[16,16,1024]{2,1,0:T(8,128)(2,1)S(1)}, u32[]{:S(2)}, u32[]{:S(2)}) collective-permute-start(bf16[16,16,1024]{2,1,0:T(8,128)(2,1)S(1)} %bitcast.2), channel_id=1, source_target_pairs={{0,1},{1,0},{2,3},{3,2},{4,5},{5,4},{6,7},{7,6},{8,9},{9,8},{10,11... | collective-permute-start | bytes 1572872 | tf_op jit(solution)/shard_map/ppermute | solution.py:231
  44.0 1.9 %collective-permute-done.2.other_ref = bf16[16,16,1024]{2,1,0:T(8,128)(2,1)S(1)} collective-permute-done((bf16[16,16,1024]{2,1,0:T(8,128)(2,1)S(1)}, bf16[16,16,1024]{2,1,0:T(8,128)(2,1)S(1)}, u32[]{:S(2)}, u32[]{:S(2)}) %collective-permute-start.2) | collective-permute-done | bytes 524320 | tf_op jit(solution)/shard_map/ppermute | solution.py:231
  45.9 3.5 %all-to-all-done.text_ref = bf16[16,16,1024]{2,1,0:T(8,128)(2,1)S(1)} async-done(((bf16[16,16,1024]{2,1,0:T(8,128)(2,1)}), bf16[16,16,1024]{2,1,0:T(8,128)(2,1)S(1)}, u32[]{:S(2)}, u32[]{:S(2)}) %all-to-all-start) | async-done | bytes 524320 | tf_op jit(solution)/shard_map/all_to_all | solution.py:237
  49.4 0.9 shard_map.69
  50.3 12.8 %all_to_all.25.got_ref = f32[32,8,128]{2,1,0:T(8,128)S(1)} all-to-all(f32[32,8,128]{2,1,0:T(8,128)S(1)} %get-tuple-element.30), channel_id=1, replica_groups=mesh['zl'=8,'yh'=2,'yl'=2,'zh'=2,'x'=4,'c'=2] {'x','yh','yl','c'}, dimensions={0} | all-to-all | bytes 262144 | tf_op jit(solution)/shard_map/all_to_all | solution.py:250
  63.3 19.1 %all_to_all.26.got_ref = f32[16,8,128]{2,1,0:T(8,128)S(1)} all-to-all(f32[16,8,128]{2,1,0:T(8,128)S(1)} %get-tuple-element.33), channel_id=1, replica_groups=mesh['zl'=8,'yh'=2,'yl'=2,'zh'=2,'x'=4,'c'=2] {'zh','zl'}, dimensions={0} | all-to-all | bytes 131072 | tf_op jit(solution)/shard_map/all_to_all | solution.py:252
  82.4 1.2 %shard_map.71 = (bf16[16,8,1024]{2,1,0:T(8,128)(2,1)}, f32[128,128]{1,0:T(8,128)S(1)}, f32[128,128]{1,0:T(8,128)S(1)}, f32[8,128]{1,0:T(8,128)S(1)}) custom-call(f32[256,128]{1,0:T(8,128)S(1)} %get-tuple-element.28.on_ref, f32[256,128]{1,0:T(8,128)S(1)} %get-tuple-element.29.mom_ref, f32[128,128]{1,0:T(8,128)S(1)} %get-tuple-element.32.lse_ref, ...), custom_call_target="tpu_custom_call" | custom-call | flops 134217728 | bytes 1839104 | tf_op jit(solution)/shard_map/pallas_call | solution.py:23
  83.6 5.0 %all-to-all-start.3 = ((bf16[16,8,1024]{2,1,0:T(8,128)(2,1)}), bf16[16,8,1024]{2,1,0:T(8,128)(2,1)S(1)}, u32[]{:S(2)}, u32[]{:S(2)}) async-start(bf16[16,8,1024]{2,1,0:T(8,128)(2,1)} %get-tuple-element.43), calls=%async_computation.3 | async-start | bytes 524288 | tf_op jit(solution)/shard_map/all_to_all | solution.py:262
  89.0 1.9 %collective-permute-start.3 = (f32[128,1152]{1,0:T(8,128)S(1)}, f32[128,1152]{1,0:T(8,128)S(1)}, u32[]{:S(2)}, u32[]{:S(2)}) collective-permute-start(f32[128,1152]{1,0:T(8,128)S(1)} %get-tuple-element.38), channel_id=1, source_target_pairs={{0,1},{1,0},{2,3},{3,2},{4,5},{5,4},{6,7},{7,6},{8,9},{9,8},{10,11... | collective-permute-start | bytes 1769480 | tf_op jit(solution)/shard_map/ppermute | solution.py:231
  90.9 2.0 %collective-permute-done.3.got_ref = f32[128,1152]{1,0:T(8,128)S(1)} collective-permute-done((f32[128,1152]{1,0:T(8,128)S(1)}, f32[128,1152]{1,0:T(8,128)S(1)}, u32[]{:S(2)}, u32[]{:S(2)}) %collective-permute-start.3) | collective-permute-done | bytes 589856 | tf_op jit(solution)/shard_map/ppermute | solution.py:231
  92.9 2.4 %collective-permute-start.4 = (bf16[4,8,1152]{2,1,0:T(8,128)(2,1)S(1)}, bf16[4,8,1152]{2,1,0:T(8,128)(2,1)S(1)}, u32[]{:S(2)}, u32[]{:S(2)}) collective-permute-start(bf16[4,8,1152]{2,1,0:T(8,128)(2,1)S(1)} %get-tuple-element.40), channel_id=1, source_target_pairs={{0,16},{16,32},{32,48},{48,0},{1,17},{17,33},{33,49},{49,1},{2,18}... | collective-permute-start | bytes 221192 | tf_op jit(solution)/shard_map/ppermute | solution.py:265
  95.4 4.0 %collective-permute-start.5 = (bf16[4,8,1152]{2,1,0:T(8,128)(2,1)S(1)}, bf16[4,8,1152]{2,1,0:T(8,128)(2,1)S(1)}, u32[]{:S(2)}, u32[]{:S(2)}) collective-permute-start(bf16[4,8,1152]{2,1,0:T(8,128)(2,1)S(1)} %get-tuple-element.41), channel_id=1, source_target_pairs={{0,32},{16,48},{32,0},{48,16},{1,33},{17,49},{33,1},{49,17},{2,34}... | collective-permute-start | bytes 221192 | tf_op jit(solution)/shard_map/ppermute | solution.py:265
  99.4 2.9 %collective-permute-start.6 = (bf16[4,8,1152]{2,1,0:T(8,128)(2,1)S(1)}, bf16[4,8,1152]{2,1,0:T(8,128)(2,1)S(1)}, u32[]{:S(2)}, u32[]{:S(2)}) collective-permute-start(bf16[4,8,1152]{2,1,0:T(8,128)(2,1)S(1)} %get-tuple-element.42), channel_id=1, source_target_pairs={{0,48},{16,0},{32,16},{48,32},{1,49},{17,1},{33,17},{49,33},{2,50}... | collective-permute-start | bytes 221192 | tf_op jit(solution)/shard_map/ppermute | solution.py:265
  102.3 0.8 collective-permute-done.5.b_ref
  103.1 2.5 %collective-permute-done.6.c_ref = bf16[4,8,1152]{2,1,0:T(8,128)(2,1)S(1)} collective-permute-done((bf16[4,8,1152]{2,1,0:T(8,128)(2,1)S(1)}, bf16[4,8,1152]{2,1,0:T(8,128)(2,1)S(1)}, u32[]{:S(2)}, u32[]{:S(2)}) %collective-permute-start.6) | collective-permute-done | bytes 73760 | tf_op jit(solution)/shard_map/ppermute | solution.py:265
  105.8 1.0 all-to-all-done.3.text_ref
  106.8 8.0 %all_to_all.27.image_ref = bf16[4,8,1152]{2,1,0:T(8,128)(2,1)S(1)} all-to-all(bf16[4,8,1152]{2,1,0:T(8,128)(2,1)S(1)} %shard_map.74), channel_id=1, replica_groups=mesh['zl'=8,'yh'=2,'yl'=2,'zh'=2,'x'=4,'c'=2] {'x'}, dimensions={0} | all-to-all | bytes 147456 | tf_op jit(solution)/shard_map/all_to_all | solution.py:269
  (9 shorter events, 1.4 us)
Async XLA Ops:
  1.4 20.7 %collective-permute-start = (bf16[16,1024]{1,0:T(8,128)(2,1)S(1)}, bf16[16,1024]{1,0:T(8,128)(2,1)S(1)}, u32[]{:S(2)}, u32[]{:S(2)}) collective-permute-start(bf16[16,1024]{1,0:T(8,128)(2,1)S(1)} %get-tuple-element.26.own_ref), channel_id=1, source_target_pairs={{0,32},{32,0},{1,33},{33,1},{2,34},{34,2},{3,35},{35,3},{4,36},{36... | collective-permute-start | bytes 98312 | tf_op jit(solution)/shard_map/ppermute | solution.py:231
  7.4 42.1 %all-to-all-start = ((bf16[16,16,1024]{2,1,0:T(8,128)(2,1)}), bf16[16,16,1024]{2,1,0:T(8,128)(2,1)S(1)}, u32[]{:S(2)}, u32[]{:S(2)}) async-start(bf16[16,16,1024]{2,1,0:T(8,128)(2,1)} %broadcast_in_dim.2), calls=%async_computation | async-start | bytes 1048576 | tf_op jit(solution)/shard_map/all_to_all | solution.py:237
  22.1 6.2 %collective-permute-start.1 = (bf16[2,16,1024]{2,1,0:T(8,128)(2,1)S(1)}, bf16[2,16,1024]{2,1,0:T(8,128)(2,1)S(1)}, u32[]{:S(2)}, u32[]{:S(2)}) collective-permute-start(bf16[2,16,1024]{2,1,0:T(8,128)(2,1)S(1)} %shard_map.67.own_ref), channel_id=1, source_target_pairs={{0,16},{16,0},{1,17},{17,1},{2,18},{18,2},{3,19},{19,3},{4,20},{20... | collective-permute-start | bytes 196616 | tf_op jit(solution)/shard_map/ppermute | solution.py:231
  42.1 3.8 %collective-permute-start.2 = (bf16[16,16,1024]{2,1,0:T(8,128)(2,1)S(1)}, bf16[16,16,1024]{2,1,0:T(8,128)(2,1)S(1)}, u32[]{:S(2)}, u32[]{:S(2)}) collective-permute-start(bf16[16,16,1024]{2,1,0:T(8,128)(2,1)S(1)} %bitcast.2), channel_id=1, source_target_pairs={{0,1},{1,0},{2,3},{3,2},{4,5},{5,4},{6,7},{7,6},{8,9},{9,8},{10,11... | collective-permute-start | bytes 1572872 | tf_op jit(solution)/shard_map/ppermute | solution.py:231
  83.6 23.2 %all-to-all-start.3 = ((bf16[16,8,1024]{2,1,0:T(8,128)(2,1)}), bf16[16,8,1024]{2,1,0:T(8,128)(2,1)S(1)}, u32[]{:S(2)}, u32[]{:S(2)}) async-start(bf16[16,8,1024]{2,1,0:T(8,128)(2,1)} %get-tuple-element.43), calls=%async_computation.3 | async-start | bytes 524288 | tf_op jit(solution)/shard_map/all_to_all | solution.py:262
  89.0 3.9 %collective-permute-start.3 = (f32[128,1152]{1,0:T(8,128)S(1)}, f32[128,1152]{1,0:T(8,128)S(1)}, u32[]{:S(2)}, u32[]{:S(2)}) collective-permute-start(f32[128,1152]{1,0:T(8,128)S(1)} %get-tuple-element.38), channel_id=1, source_target_pairs={{0,1},{1,0},{2,3},{3,2},{4,5},{5,4},{6,7},{7,6},{8,9},{9,8},{10,11... | collective-permute-start | bytes 1769480 | tf_op jit(solution)/shard_map/ppermute | solution.py:231
  92.9 9.4 %collective-permute-start.4 = (bf16[4,8,1152]{2,1,0:T(8,128)(2,1)S(1)}, bf16[4,8,1152]{2,1,0:T(8,128)(2,1)S(1)}, u32[]{:S(2)}, u32[]{:S(2)}) collective-permute-start(bf16[4,8,1152]{2,1,0:T(8,128)(2,1)S(1)} %get-tuple-element.40), channel_id=1, source_target_pairs={{0,16},{16,32},{32,48},{48,0},{1,17},{17,33},{33,49},{49,1},{2,18}... | collective-permute-start | bytes 221192 | tf_op jit(solution)/shard_map/ppermute | solution.py:265
  95.4 7.8 %collective-permute-start.5 = (bf16[4,8,1152]{2,1,0:T(8,128)(2,1)S(1)}, bf16[4,8,1152]{2,1,0:T(8,128)(2,1)S(1)}, u32[]{:S(2)}, u32[]{:S(2)}) collective-permute-start(bf16[4,8,1152]{2,1,0:T(8,128)(2,1)S(1)} %get-tuple-element.41), channel_id=1, source_target_pairs={{0,32},{16,48},{32,0},{48,16},{1,33},{17,49},{33,1},{49,17},{2,34}... | collective-permute-start | bytes 221192 | tf_op jit(solution)/shard_map/ppermute | solution.py:265
  99.4 6.2 %collective-permute-start.6 = (bf16[4,8,1152]{2,1,0:T(8,128)(2,1)S(1)}, bf16[4,8,1152]{2,1,0:T(8,128)(2,1)S(1)}, u32[]{:S(2)}, u32[]{:S(2)}) collective-permute-start(bf16[4,8,1152]{2,1,0:T(8,128)(2,1)S(1)} %get-tuple-element.42), channel_id=1, source_target_pairs={{0,48},{16,0},{32,16},{48,32},{1,49},{17,1},{33,17},{49,33},{2,50}... | collective-permute-start | bytes 221192 | tf_op jit(solution)/shard_map/ppermute | solution.py:265

commit v19 on v17

--- a/solution.py
+++ b/solution.py
@@ -41,7 +41,7 @@
     x, yh, yl, c, zh, zl = (lax.axis_index(a) for a in ("x", "yh", "yl", "c", "zh", "zl"))
     y = yh * 2 + yl
     row = lax.broadcasted_iota(jnp.int32, (2 * side, 1), 0)
-    pc, px, py = row >> 7, (row >> 5) & 3, ((row >> 3) & 1) * 2 + ((row >> 4) & 1)
+    pc, px, py = row >> 7, (row >> 5) & 3, (row >> 3) & 3
     image = ((zh * 8 + px * 2 + pc) * 32 + zl * 4 + py) * rows + (row & 7)
     lane = lax.broadcasted_iota(jnp.int32, (1, side), 1)
     qh, ql = (lane >> 3) & 1, lane >> 4
@@ -198,7 +198,7 @@
         to = (y + k) & 3
         parts = []
         for x in range(4):
-            at = pl.ds(pl.multiple_of(x * 4 * rows + ((to & 1) * 2 + (to >> 1)) * rows, rows), rows)
+            at = pl.ds(pl.multiple_of(x * 4 * rows + to * rows, rows), rows)
             parts.append(keep_ref[at, :] + got_ref[at, :])
         return jnp.stack(parts)
 
@@ -235,9 +235,9 @@
     both, pair = lax.optimization_barrier((both, pair))
     sent = jnp.broadcast_to(both[None], (n_column,) + both.shape)
     texts = lax.all_to_all(sent, column, 0, 0, tiled=True)
-    across = swap(pair, "yh")
-    (pair,) = call(partial(order_kernel, "yh"), [shape(2, 16, width, dtype=bf16)], pair, across, flops=2**35)
-    (pair,) = call(partial(order_kernel, "yl"), [shape(2, 2, 16, width, dtype=bf16)], pair, swap(pair, "yl"))
+    across = swap(pair, "yl")
+    (pair,) = call(partial(order_kernel, "yl"), [shape(2, 16, width, dtype=bf16)], pair, across, flops=2**35)
+    (pair,) = call(partial(order_kernel, "yh"), [shape(2, 2, 16, width, dtype=bf16)], pair, swap(pair, "yh"))
     mine = lax.all_gather(pair, "x").reshape(16, 16, width)
     other = swap(mine)
 

time: 116 us -> 117 us (level)
  blocking collectives: 53.7 us -> 56.4 us
  waiting for transfers between devices: 15.4 us -> 13.2 us
    all_to_all x1, blocking collectives: 12.8 us -> 14.7 us  [local(): lax.all_to_all(row_parts, ('x', 'yh', 'yl', 'c'), 0, 0, tiled=True)]
    all_to_all x1, waiting for transfers between devices: 3.54 us -> 2.11 us  [local(): texts = lax.all_to_all(sent, column, 0, 0, tiled=True)]
where the time goes in v19:
time: 117 us
  blocking collectives  56.4 us (48%)
  starting transfers between devices  41.2 us (35%)
  waiting for transfers between devices  13.2 us (11%)
  Pallas kernels  3.51 us (3%)
    all_to_all x1, blocking collectives, local(): col_got = lax.all_to_all(col_sent, column, 0, 0, tiled=True)  20 us
    all_to_all x1, starting transfers between devices, local(): texts = lax.all_to_all(sent, column, 0, 0, tiled=True)  14.8 us
    all_to_all x1, blocking collectives, local(): lax.all_to_all(row_parts, ('x', 'yh', 'yl', 'c'), 0, 0, tiled=True)  14.7 us
    all_gather x1, blocking collectives, local(): mine = lax.all_gather(pair, 'x').reshape(16, 16, width)  13.7 us
    ppermute x4, starting transfers between devices, swap(): return lax.ppermute(block, axis, [(0, 1), (1, 0)])  12.1 us
    ppermute x3, starting transfers between devices, local(): lax.ppermute(block, ('yh', 'yl'), [(i, (i + k) % 4) for i in range(4)])  9.35 us
    all_to_all x1, blocking collectives, local(): got_image = lax.all_to_all(by_image, 'x', 0, 0, tiled=True)  8.02 us
    ppermute x4, waiting for transfers between devices, swap(): return lax.ppermute(block, axis, [(0, 1), (1, 0)])  6.69 us
  transfers between devices with their start and end apart: 9, of which 7 were waited for; matrix products, arithmetic and copies ran while one was open for 1% of the time, Pallas kernels for 0%

profile of v19, /device:TPU:64, one launch (start us, length us, event | category | flops | bytes accessed | tf_op | source)
XLA Modules:
  0.0 116.7 jit_solution(1530014689721085513)
XLA Ops:
  0.6 0.8 pad_maximum_fusion
  1.4 3.5 %collective-permute-start = (bf16[16,1024]{1,0:T(8,128)(2,1)S(1)}, bf16[16,1024]{1,0:T(8,128)(2,1)S(1)}, u32[]{:S(2)}, u32[]{:S(2)}) collective-permute-start(bf16[16,1024]{1,0:T(8,128)(2,1)S(1)} %get-tuple-element.26.own_ref), channel_id=1, source_target_pairs={{0,16},{16,0},{1,17},{17,1},{2,18},{18,2},{3,19},{19,3},{4,20},{20... | collective-permute-start | bytes 98312 | tf_op jit(solution)/shard_map/ppermute | solution.py:231
  4.9 0.8 broadcast_in_dim.2
  5.7 14.8 %all-to-all-start = ((bf16[16,16,1024]{2,1,0:T(8,128)(2,1)}), bf16[16,16,1024]{2,1,0:T(8,128)(2,1)S(1)}, u32[]{:S(2)}, u32[]{:S(2)}) async-start(bf16[16,16,1024]{2,1,0:T(8,128)(2,1)} %broadcast_in_dim.2), calls=%async_computation | async-start | bytes 1048576 | tf_op jit(solution)/shard_map/all_to_all | solution.py:237
  20.5 4.8 %collective-permute-start.1 = (bf16[2,16,1024]{2,1,0:T(8,128)(2,1)S(1)}, bf16[2,16,1024]{2,1,0:T(8,128)(2,1)S(1)}, u32[]{:S(2)}, u32[]{:S(2)}) collective-permute-start(bf16[2,16,1024]{2,1,0:T(8,128)(2,1)S(1)} %shard_map.67.own_ref), channel_id=1, source_target_pairs={{0,32},{32,0},{1,33},{33,1},{2,34},{34,2},{3,35},{35,3},{4,36},{36... | collective-permute-start | bytes 196616 | tf_op jit(solution)/shard_map/ppermute | solution.py:231
  25.3 2.8 %collective-permute-done.1.other_ref = bf16[2,16,1024]{2,1,0:T(8,128)(2,1)S(1)} collective-permute-done((bf16[2,16,1024]{2,1,0:T(8,128)(2,1)S(1)}, bf16[2,16,1024]{2,1,0:T(8,128)(2,1)S(1)}, u32[]{:S(2)}, u32[]{:S(2)}) %collective-permute-start.1) | collective-permute-done | bytes 65568 | tf_op jit(solution)/shard_map/ppermute | solution.py:231
  28.2 13.7 %all-gather = bf16[8,2,16,1024]{3,2,1,0:T(8,128)(2,1)S(1)} all-gather(bf16[2,2,16,1024]{3,2,1,0:T(8,128)(2,1)S(1)} %shard_map.68), channel_id=2, replica_groups=mesh['zl'=8,'yh'=2,'yl'=2,'zh'=2,'x'=4,'c'=2] {'x'}, dimensions={0}, use_global_device_ids=true | all-gather | bytes 655360 | tf_op jit(solution)/shard_map/all_gather | solution.py:241
  41.9 1.9 %collective-permute-start.2 = (bf16[16,16,1024]{2,1,0:T(8,128)(2,1)S(1)}, bf16[16,16,1024]{2,1,0:T(8,128)(2,1)S(1)}, u32[]{:S(2)}, u32[]{:S(2)}) collective-permute-start(bf16[16,16,1024]{2,1,0:T(8,128)(2,1)S(1)} %bitcast.2), channel_id=1, source_target_pairs={{0,1},{1,0},{2,3},{3,2},{4,5},{5,4},{6,7},{7,6},{8,9},{9,8},{10,11... | collective-permute-start | bytes 1572872 | tf_op jit(solution)/shard_map/ppermute | solution.py:231
  43.8 1.9 %collective-permute-done.2.other_ref = bf16[16,16,1024]{2,1,0:T(8,128)(2,1)S(1)} collective-permute-done((bf16[16,16,1024]{2,1,0:T(8,128)(2,1)S(1)}, bf16[16,16,1024]{2,1,0:T(8,128)(2,1)S(1)}, u32[]{:S(2)}, u32[]{:S(2)}) %collective-permute-start.2) | collective-permute-done | bytes 524320 | tf_op jit(solution)/shard_map/ppermute | solution.py:231
  45.7 2.1 %all-to-all-done.text_ref = bf16[16,16,1024]{2,1,0:T(8,128)(2,1)S(1)} async-done(((bf16[16,16,1024]{2,1,0:T(8,128)(2,1)}), bf16[16,16,1024]{2,1,0:T(8,128)(2,1)S(1)}, u32[]{:S(2)}, u32[]{:S(2)}) %all-to-all-start) | async-done | bytes 524320 | tf_op jit(solution)/shard_map/all_to_all | solution.py:237
  47.8 0.8 shard_map.69
  48.7 14.7 %all_to_all.25.got_ref = f32[32,8,128]{2,1,0:T(8,128)S(1)} all-to-all(f32[32,8,128]{2,1,0:T(8,128)S(1)} %get-tuple-element.30), channel_id=1, replica_groups=mesh['zl'=8,'yh'=2,'yl'=2,'zh'=2,'x'=4,'c'=2] {'x','yh','yl','c'}, dimensions={0} | all-to-all | bytes 262144 | tf_op jit(solution)/shard_map/all_to_all | solution.py:250
  63.5 20.0 %all_to_all.26.got_ref = f32[16,8,128]{2,1,0:T(8,128)S(1)} all-to-all(f32[16,8,128]{2,1,0:T(8,128)S(1)} %get-tuple-element.33), channel_id=1, replica_groups=mesh['zl'=8,'yh'=2,'yl'=2,'zh'=2,'x'=4,'c'=2] {'zh','zl'}, dimensions={0} | all-to-all | bytes 131072 | tf_op jit(solution)/shard_map/all_to_all | solution.py:252
  83.6 1.2 %shard_map.71 = (bf16[16,8,1024]{2,1,0:T(8,128)(2,1)}, f32[128,128]{1,0:T(8,128)S(1)}, f32[128,128]{1,0:T(8,128)S(1)}, f32[8,128]{1,0:T(8,128)S(1)}) custom-call(f32[256,128]{1,0:T(8,128)S(1)} %get-tuple-element.28.on_ref, f32[256,128]{1,0:T(8,128)S(1)} %get-tuple-element.29.mom_ref, f32[128,128]{1,0:T(8,128)S(1)} %get-tuple-element.32.lse_ref, ...), custom_call_target="tpu_custom_call" | custom-call | flops 134217728 | bytes 1839104 | tf_op jit(solution)/shard_map/pallas_call | solution.py:23
  84.8 5.0 %all-to-all-start.3 = ((bf16[16,8,1024]{2,1,0:T(8,128)(2,1)}), bf16[16,8,1024]{2,1,0:T(8,128)(2,1)S(1)}, u32[]{:S(2)}, u32[]{:S(2)}) async-start(bf16[16,8,1024]{2,1,0:T(8,128)(2,1)} %get-tuple-element.43), calls=%async_computation.3 | async-start | bytes 524288 | tf_op jit(solution)/shard_map/all_to_all | solution.py:262
  90.1 1.9 %collective-permute-start.3 = (f32[128,1152]{1,0:T(8,128)S(1)}, f32[128,1152]{1,0:T(8,128)S(1)}, u32[]{:S(2)}, u32[]{:S(2)}) collective-permute-start(f32[128,1152]{1,0:T(8,128)S(1)} %get-tuple-element.38), channel_id=1, source_target_pairs={{0,1},{1,0},{2,3},{3,2},{4,5},{5,4},{6,7},{7,6},{8,9},{9,8},{10,11... | collective-permute-start | bytes 1769480 | tf_op jit(solution)/shard_map/ppermute | solution.py:231
  92.0 2.0 %collective-permute-done.3.got_ref = f32[128,1152]{1,0:T(8,128)S(1)} collective-permute-done((f32[128,1152]{1,0:T(8,128)S(1)}, f32[128,1152]{1,0:T(8,128)S(1)}, u32[]{:S(2)}, u32[]{:S(2)}) %collective-permute-start.3) | collective-permute-done | bytes 589856 | tf_op jit(solution)/shard_map/ppermute | solution.py:231
  94.1 2.4 %collective-permute-start.4 = (bf16[4,8,1152]{2,1,0:T(8,128)(2,1)S(1)}, bf16[4,8,1152]{2,1,0:T(8,128)(2,1)S(1)}, u32[]{:S(2)}, u32[]{:S(2)}) collective-permute-start(bf16[4,8,1152]{2,1,0:T(8,128)(2,1)S(1)} %get-tuple-element.40), channel_id=1, source_target_pairs={{0,16},{16,32},{32,48},{48,0},{1,17},{17,33},{33,49},{49,1},{2,18}... | collective-permute-start | bytes 221192 | tf_op jit(solution)/shard_map/ppermute | solution.py:265
  96.5 4.0 %collective-permute-start.5 = (bf16[4,8,1152]{2,1,0:T(8,128)(2,1)S(1)}, bf16[4,8,1152]{2,1,0:T(8,128)(2,1)S(1)}, u32[]{:S(2)}, u32[]{:S(2)}) collective-permute-start(bf16[4,8,1152]{2,1,0:T(8,128)(2,1)S(1)} %get-tuple-element.41), channel_id=1, source_target_pairs={{0,32},{16,48},{32,0},{48,16},{1,33},{17,49},{33,1},{49,17},{2,34}... | collective-permute-start | bytes 221192 | tf_op jit(solution)/shard_map/ppermute | solution.py:265
  100.6 2.9 %collective-permute-start.6 = (bf16[4,8,1152]{2,1,0:T(8,128)(2,1)S(1)}, bf16[4,8,1152]{2,1,0:T(8,128)(2,1)S(1)}, u32[]{:S(2)}, u32[]{:S(2)}) collective-permute-start(bf16[4,8,1152]{2,1,0:T(8,128)(2,1)S(1)} %get-tuple-element.42), channel_id=1, source_target_pairs={{0,48},{16,0},{32,16},{48,32},{1,49},{17,1},{33,17},{49,33},{2,50}... | collective-permute-start | bytes 221192 | tf_op jit(solution)/shard_map/ppermute | solution.py:265
  103.5 0.8 collective-permute-done.5.b_ref
  104.3 2.5 %collective-permute-done.6.c_ref = bf16[4,8,1152]{2,1,0:T(8,128)(2,1)S(1)} collective-permute-done((bf16[4,8,1152]{2,1,0:T(8,128)(2,1)S(1)}, bf16[4,8,1152]{2,1,0:T(8,128)(2,1)S(1)}, u32[]{:S(2)}, u32[]{:S(2)}) %collective-permute-start.6) | collective-permute-done | bytes 73760 | tf_op jit(solution)/shard_map/ppermute | solution.py:265
  107.0 1.0 all-to-all-done.3.text_ref
  108.0 8.0 %all_to_all.27.image_ref = bf16[4,8,1152]{2,1,0:T(8,128)(2,1)S(1)} all-to-all(bf16[4,8,1152]{2,1,0:T(8,128)(2,1)S(1)} %shard_map.74), channel_id=1, replica_groups=mesh['zl'=8,'yh'=2,'yl'=2,'zh'=2,'x'=4,'c'=2] {'x'}, dimensions={0} | all-to-all | bytes 147456 | tf_op jit(solution)/shard_map/all_to_all | solution.py:269
  (9 shorter events, 1.4 us)
Async XLA Ops:
  1.4 19.1 %collective-permute-start = (bf16[16,1024]{1,0:T(8,128)(2,1)S(1)}, bf16[16,1024]{1,0:T(8,128)(2,1)S(1)}, u32[]{:S(2)}, u32[]{:S(2)}) collective-permute-start(bf16[16,1024]{1,0:T(8,128)(2,1)S(1)} %get-tuple-element.26.own_ref), channel_id=1, source_target_pairs={{0,16},{16,0},{1,17},{17,1},{2,18},{18,2},{3,19},{19,3},{4,20},{20... | collective-permute-start | bytes 98312 | tf_op jit(solution)/shard_map/ppermute | solution.py:231
  5.7 42.1 %all-to-all-start = ((bf16[16,16,1024]{2,1,0:T(8,128)(2,1)}), bf16[16,16,1024]{2,1,0:T(8,128)(2,1)S(1)}, u32[]{:S(2)}, u32[]{:S(2)}) async-start(bf16[16,16,1024]{2,1,0:T(8,128)(2,1)} %broadcast_in_dim.2), calls=%async_computation | async-start | bytes 1048576 | tf_op jit(solution)/shard_map/all_to_all | solution.py:237
  20.5 7.7 %collective-permute-start.1 = (bf16[2,16,1024]{2,1,0:T(8,128)(2,1)S(1)}, bf16[2,16,1024]{2,1,0:T(8,128)(2,1)S(1)}, u32[]{:S(2)}, u32[]{:S(2)}) collective-permute-start(bf16[2,16,1024]{2,1,0:T(8,128)(2,1)S(1)} %shard_map.67.own_ref), channel_id=1, source_target_pairs={{0,32},{32,0},{1,33},{33,1},{2,34},{34,2},{3,35},{35,3},{4,36},{36... | collective-permute-start | bytes 196616 | tf_op jit(solution)/shard_map/ppermute | solution.py:231
  41.9 3.8 %collective-permute-start.2 = (bf16[16,16,1024]{2,1,0:T(8,128)(2,1)S(1)}, bf16[16,16,1024]{2,1,0:T(8,128)(2,1)S(1)}, u32[]{:S(2)}, u32[]{:S(2)}) collective-permute-start(bf16[16,16,1024]{2,1,0:T(8,128)(2,1)S(1)} %bitcast.2), channel_id=1, source_target_pairs={{0,1},{1,0},{2,3},{3,2},{4,5},{5,4},{6,7},{7,6},{8,9},{9,8},{10,11... | collective-permute-start | bytes 1572872 | tf_op jit(solution)/shard_map/ppermute | solution.py:231
  84.8 23.2 %all-to-all-start.3 = ((bf16[16,8,1024]{2,1,0:T(8,128)(2,1)}), bf16[16,8,1024]{2,1,0:T(8,128)(2,1)S(1)}, u32[]{:S(2)}, u32[]{:S(2)}) async-start(bf16[16,8,1024]{2,1,0:T(8,128)(2,1)} %get-tuple-element.43), calls=%async_computation.3 | async-start | bytes 524288 | tf_op jit(solution)/shard_map/all_to_all | solution.py:262
  90.1 3.9 %collective-permute-start.3 = (f32[128,1152]{1,0:T(8,128)S(1)}, f32[128,1152]{1,0:T(8,128)S(1)}, u32[]{:S(2)}, u32[]{:S(2)}) collective-permute-start(f32[128,1152]{1,0:T(8,128)S(1)} %get-tuple-element.38), channel_id=1, source_target_pairs={{0,1},{1,0},{2,3},{3,2},{4,5},{5,4},{6,7},{7,6},{8,9},{9,8},{10,11... | collective-permute-start | bytes 1769480 | tf_op jit(solution)/shard_map/ppermute | solution.py:231
  94.1 9.4 %collective-permute-start.4 = (bf16[4,8,1152]{2,1,0:T(8,128)(2,1)S(1)}, bf16[4,8,1152]{2,1,0:T(8,128)(2,1)S(1)}, u32[]{:S(2)}, u32[]{:S(2)}) collective-permute-start(bf16[4,8,1152]{2,1,0:T(8,128)(2,1)S(1)} %get-tuple-element.40), channel_id=1, source_target_pairs={{0,16},{16,32},{32,48},{48,0},{1,17},{17,33},{33,49},{49,1},{2,18}... | collective-permute-start | bytes 221192 | tf_op jit(solution)/shard_map/ppermute | solution.py:265
  96.5 7.8 %collective-permute-start.5 = (bf16[4,8,1152]{2,1,0:T(8,128)(2,1)S(1)}, bf16[4,8,1152]{2,1,0:T(8,128)(2,1)S(1)}, u32[]{:S(2)}, u32[]{:S(2)}) collective-permute-start(bf16[4,8,1152]{2,1,0:T(8,128)(2,1)S(1)} %get-tuple-element.41), channel_id=1, source_target_pairs={{0,32},{16,48},{32,0},{48,16},{1,33},{17,49},{33,1},{49,17},{2,34}... | collective-permute-start | bytes 221192 | tf_op jit(solution)/shard_map/ppermute | solution.py:265
  100.6 6.2 %collective-permute-start.6 = (bf16[4,8,1152]{2,1,0:T(8,128)(2,1)S(1)}, bf16[4,8,1152]{2,1,0:T(8,128)(2,1)S(1)}, u32[]{:S(2)}, u32[]{:S(2)}) collective-permute-start(bf16[4,8,1152]{2,1,0:T(8,128)(2,1)S(1)} %get-tuple-element.42), channel_id=1, source_target_pairs={{0,48},{16,0},{32,16},{48,32},{1,49},{17,1},{33,17},{49,33},{2,50}... | collective-permute-start | bytes 221192 | tf_op jit(solution)/shard_map/ppermute | solution.py:265

commit v20 on v17

--- a/solution.py
+++ b/solution.py
@@ -247,7 +247,7 @@
         mine, other, texts,
         flops=2**28, exps=2**18,
     )
-    row_got = lax.all_to_all(row_parts, ("x", "yh", "yl", "c"), 0, 0, tiled=True)
+    row_got = lax.all_to_all(row_parts, ("c", "yh", "yl", "x"), 0, 0, tiled=True)
     row_lse, col_sent = call(row_kernel, [shape(side, side), shape(n_column, 8, side)], row_got, col_parts, exps=2**14)
     col_got = lax.all_to_all(col_sent, column, 0, 0, tiled=True)
 

time: 116 us -> 116 us (level)
  no operation moved by 1% of the time
where the time goes in v20:
time: 116 us; the launch traced here: 115 us
  blocking collectives  53.9 us (46%)
  starting transfers between devices  41 us (35%)
  waiting for transfers between devices  14.4 us (12%)
  Pallas kernels  3.52 us (3%)
    all_to_all x1, blocking collectives, local(): col_got = lax.all_to_all(col_sent, column, 0, 0, tiled=True)  19 us
    all_to_all x1, starting transfers between devices, local(): texts = lax.all_to_all(sent, column, 0, 0, tiled=True)  14.8 us
    all_gather x1, blocking collectives, local(): mine = lax.all_gather(pair, 'x').reshape(16, 16, width)  13.8 us
    all_to_all x1, blocking collectives, local(): lax.all_to_all(row_parts, ('c', 'yh', 'yl', 'x'), 0, 0, tiled=True)  12.8 us
    ppermute x4, starting transfers between devices, swap(): return lax.ppermute(block, axis, [(0, 1), (1, 0)])  11.5 us
    ppermute x3, starting transfers between devices, local(): lax.ppermute(block, ('yh', 'yl'), [(i, (i + k) % 4) for i in range(4)])  9.72 us
    all_to_all x1, blocking collectives, local(): got_image = lax.all_to_all(by_image, 'x', 0, 0, tiled=True)  8.4 us
    ppermute x4, waiting for transfers between devices, swap(): return lax.ppermute(block, axis, [(0, 1), (1, 0)])  7.41 us
  transfers between devices with their start and end apart: 9, of which 7 were waited for; matrix products, arithmetic and copies ran while one was open for 1% of the time, Pallas kernels for 0%

profile of v20, /device:TPU:64, one launch (start us, length us, event | category | flops | bytes accessed | tf_op | source)
XLA Modules:
  0.0 115.2 jit_solution(3849550263190244528)
XLA Ops:
  0.6 0.8 pad_maximum_fusion
  1.4 5.1 %collective-permute-start = (bf16[16,1024]{1,0:T(8,128)(2,1)S(1)}, bf16[16,1024]{1,0:T(8,128)(2,1)S(1)}, u32[]{:S(2)}, u32[]{:S(2)}) collective-permute-start(bf16[16,1024]{1,0:T(8,128)(2,1)S(1)} %get-tuple-element.26.own_ref), channel_id=1, source_target_pairs={{0,32},{32,0},{1,33},{33,1},{2,34},{34,2},{3,35},{35,3},{4,36},{36... | collective-permute-start | bytes 98312 | tf_op jit(solution)/shard_map/ppermute | solution.py:231
  6.5 0.8 broadcast_in_dim.2
  7.4 14.8 %all-to-all-start = ((bf16[16,16,1024]{2,1,0:T(8,128)(2,1)}), bf16[16,16,1024]{2,1,0:T(8,128)(2,1)S(1)}, u32[]{:S(2)}, u32[]{:S(2)}) async-start(bf16[16,16,1024]{2,1,0:T(8,128)(2,1)} %broadcast_in_dim.2), calls=%async_computation | async-start | bytes 1048576 | tf_op jit(solution)/shard_map/all_to_all | solution.py:237
  22.1 2.6 %collective-permute-start.1 = (bf16[2,16,1024]{2,1,0:T(8,128)(2,1)S(1)}, bf16[2,16,1024]{2,1,0:T(8,128)(2,1)S(1)}, u32[]{:S(2)}, u32[]{:S(2)}) collective-permute-start(bf16[2,16,1024]{2,1,0:T(8,128)(2,1)S(1)} %shard_map.67.own_ref), channel_id=1, source_target_pairs={{0,16},{16,0},{1,17},{17,1},{2,18},{18,2},{3,19},{19,3},{4,20},{20... | collective-permute-start | bytes 196616 | tf_op jit(solution)/shard_map/ppermute | solution.py:231
  24.7 3.6 %collective-permute-done.1.other_ref = bf16[2,16,1024]{2,1,0:T(8,128)(2,1)S(1)} collective-permute-done((bf16[2,16,1024]{2,1,0:T(8,128)(2,1)S(1)}, bf16[2,16,1024]{2,1,0:T(8,128)(2,1)S(1)}, u32[]{:S(2)}, u32[]{:S(2)}) %collective-permute-start.1) | collective-permute-done | bytes 65568 | tf_op jit(solution)/shard_map/ppermute | solution.py:231
  28.3 13.8 %all-gather = bf16[8,2,16,1024]{3,2,1,0:T(8,128)(2,1)S(1)} all-gather(bf16[2,2,16,1024]{3,2,1,0:T(8,128)(2,1)S(1)} %shard_map.68), channel_id=2, replica_groups=mesh['zl'=8,'yh'=2,'yl'=2,'zh'=2,'x'=4,'c'=2] {'x'}, dimensions={0}, use_global_device_ids=true | all-gather | bytes 655360 | tf_op jit(solution)/shard_map/all_gather | solution.py:241
  42.1 1.9 %collective-permute-start.2 = (bf16[16,16,1024]{2,1,0:T(8,128)(2,1)S(1)}, bf16[16,16,1024]{2,1,0:T(8,128)(2,1)S(1)}, u32[]{:S(2)}, u32[]{:S(2)}) collective-permute-start(bf16[16,16,1024]{2,1,0:T(8,128)(2,1)S(1)} %bitcast.2), channel_id=1, source_target_pairs={{0,1},{1,0},{2,3},{3,2},{4,5},{5,4},{6,7},{7,6},{8,9},{9,8},{10,11... | collective-permute-start | bytes 1572872 | tf_op jit(solution)/shard_map/ppermute | solution.py:231
  44.0 1.9 %collective-permute-done.2.other_ref = bf16[16,16,1024]{2,1,0:T(8,128)(2,1)S(1)} collective-permute-done((bf16[16,16,1024]{2,1,0:T(8,128)(2,1)S(1)}, bf16[16,16,1024]{2,1,0:T(8,128)(2,1)S(1)}, u32[]{:S(2)}, u32[]{:S(2)}) %collective-permute-start.2) | collective-permute-done | bytes 524320 | tf_op jit(solution)/shard_map/ppermute | solution.py:231
  45.9 3.5 %all-to-all-done.text_ref = bf16[16,16,1024]{2,1,0:T(8,128)(2,1)S(1)} async-done(((bf16[16,16,1024]{2,1,0:T(8,128)(2,1)}), bf16[16,16,1024]{2,1,0:T(8,128)(2,1)S(1)}, u32[]{:S(2)}, u32[]{:S(2)}) %all-to-all-start) | async-done | bytes 524320 | tf_op jit(solution)/shard_map/all_to_all | solution.py:237
  49.4 0.9 shard_map.69
  50.3 12.8 %all_to_all.25.got_ref = f32[32,8,128]{2,1,0:T(8,128)S(1)} all-to-all(f32[32,8,128]{2,1,0:T(8,128)S(1)} %get-tuple-element.30), channel_id=1, replica_groups=mesh['zl'=8,'yh'=2,'yl'=2,'zh'=2,'x'=4,'c'=2] {'c','yh','yl','x'}, dimensions={0} | all-to-all | bytes 262144 | tf_op jit(solution)/shard_map/all_to_all | solution.py:250
  63.3 19.0 %all_to_all.26.got_ref = f32[16,8,128]{2,1,0:T(8,128)S(1)} all-to-all(f32[16,8,128]{2,1,0:T(8,128)S(1)} %get-tuple-element.33), channel_id=1, replica_groups=mesh['zl'=8,'yh'=2,'yl'=2,'zh'=2,'x'=4,'c'=2] {'zh','zl'}, dimensions={0} | all-to-all | bytes 131072 | tf_op jit(solution)/shard_map/all_to_all | solution.py:252
  82.2 1.2 %shard_map.71 = (bf16[16,8,1024]{2,1,0:T(8,128)(2,1)}, f32[128,128]{1,0:T(8,128)S(1)}, f32[128,128]{1,0:T(8,128)S(1)}, f32[8,128]{1,0:T(8,128)S(1)}) custom-call(f32[256,128]{1,0:T(8,128)S(1)} %get-tuple-element.28.on_ref, f32[256,128]{1,0:T(8,128)S(1)} %get-tuple-element.29.mom_ref, f32[128,128]{1,0:T(8,128)S(1)} %get-tuple-element.32.lse_ref, ...), custom_call_target="tpu_custom_call" | custom-call | flops 134217728 | bytes 1839104 | tf_op jit(solution)/shard_map/pallas_call | solution.py:23
  83.5 5.0 %all-to-all-start.3 = ((bf16[16,8,1024]{2,1,0:T(8,128)(2,1)}), bf16[16,8,1024]{2,1,0:T(8,128)(2,1)S(1)}, u32[]{:S(2)}, u32[]{:S(2)}) async-start(bf16[16,8,1024]{2,1,0:T(8,128)(2,1)} %get-tuple-element.43), calls=%async_computation.3 | async-start | bytes 524288 | tf_op jit(solution)/shard_map/all_to_all | solution.py:262
  88.8 1.9 %collective-permute-start.3 = (f32[128,1152]{1,0:T(8,128)S(1)}, f32[128,1152]{1,0:T(8,128)S(1)}, u32[]{:S(2)}, u32[]{:S(2)}) collective-permute-start(f32[128,1152]{1,0:T(8,128)S(1)} %get-tuple-element.38), channel_id=1, source_target_pairs={{0,1},{1,0},{2,3},{3,2},{4,5},{5,4},{6,7},{7,6},{8,9},{9,8},{10,11... | collective-permute-start | bytes 1769480 | tf_op jit(solution)/shard_map/ppermute | solution.py:231
  90.7 2.0 %collective-permute-done.3.got_ref = f32[128,1152]{1,0:T(8,128)S(1)} collective-permute-done((f32[128,1152]{1,0:T(8,128)S(1)}, f32[128,1152]{1,0:T(8,128)S(1)}, u32[]{:S(2)}, u32[]{:S(2)}) %collective-permute-start.3) | collective-permute-done | bytes 589856 | tf_op jit(solution)/shard_map/ppermute | solution.py:231
  92.8 2.4 %collective-permute-start.4 = (bf16[4,8,1152]{2,1,0:T(8,128)(2,1)S(1)}, bf16[4,8,1152]{2,1,0:T(8,128)(2,1)S(1)}, u32[]{:S(2)}, u32[]{:S(2)}) collective-permute-start(bf16[4,8,1152]{2,1,0:T(8,128)(2,1)S(1)} %get-tuple-element.40), channel_id=1, source_target_pairs={{0,16},{16,32},{32,48},{48,0},{1,17},{17,33},{33,49},{49,1},{2,18}... | collective-permute-start | bytes 221192 | tf_op jit(solution)/shard_map/ppermute | solution.py:265
  95.2 3.9 %collective-permute-start.5 = (bf16[4,8,1152]{2,1,0:T(8,128)(2,1)S(1)}, bf16[4,8,1152]{2,1,0:T(8,128)(2,1)S(1)}, u32[]{:S(2)}, u32[]{:S(2)}) collective-permute-start(bf16[4,8,1152]{2,1,0:T(8,128)(2,1)S(1)} %get-tuple-element.41), channel_id=1, source_target_pairs={{0,32},{16,48},{32,0},{48,16},{1,33},{17,49},{33,1},{49,17},{2,34}... | collective-permute-start | bytes 221192 | tf_op jit(solution)/shard_map/ppermute | solution.py:265
  99.1 3.4 %collective-permute-start.6 = (bf16[4,8,1152]{2,1,0:T(8,128)(2,1)S(1)}, bf16[4,8,1152]{2,1,0:T(8,128)(2,1)S(1)}, u32[]{:S(2)}, u32[]{:S(2)}) collective-permute-start(bf16[4,8,1152]{2,1,0:T(8,128)(2,1)S(1)} %get-tuple-element.42), channel_id=1, source_target_pairs={{0,48},{16,0},{32,16},{48,32},{1,49},{17,1},{33,17},{49,33},{2,50}... | collective-permute-start | bytes 221192 | tf_op jit(solution)/shard_map/ppermute | solution.py:265
  102.9 2.4 %collective-permute-done.6.c_ref = bf16[4,8,1152]{2,1,0:T(8,128)(2,1)S(1)} collective-permute-done((bf16[4,8,1152]{2,1,0:T(8,128)(2,1)S(1)}, bf16[4,8,1152]{2,1,0:T(8,128)(2,1)S(1)}, u32[]{:S(2)}, u32[]{:S(2)}) %collective-permute-start.6) | collective-permute-done | bytes 73760 | tf_op jit(solution)/shard_map/ppermute | solution.py:265
  105.5 0.7 all-to-all-done.3.text_ref
  106.1 8.4 %all_to_all.27.image_ref = bf16[4,8,1152]{2,1,0:T(8,128)(2,1)S(1)} all-to-all(bf16[4,8,1152]{2,1,0:T(8,128)(2,1)S(1)} %shard_map.74), channel_id=1, replica_groups=mesh['zl'=8,'yh'=2,'yl'=2,'zh'=2,'x'=4,'c'=2] {'x'}, dimensions={0} | all-to-all | bytes 147456 | tf_op jit(solution)/shard_map/all_to_all | solution.py:269
  114.5 0.7 shard_map.75
  (9 shorter events, 1.2 us)
Async XLA Ops:
  1.4 20.7 %collective-permute-start = (bf16[16,1024]{1,0:T(8,128)(2,1)S(1)}, bf16[16,1024]{1,0:T(8,128)(2,1)S(1)}, u32[]{:S(2)}, u32[]{:S(2)}) collective-permute-start(bf16[16,1024]{1,0:T(8,128)(2,1)S(1)} %get-tuple-element.26.own_ref), channel_id=1, source_target_pairs={{0,32},{32,0},{1,33},{33,1},{2,34},{34,2},{3,35},{35,3},{4,36},{36... | collective-permute-start | bytes 98312 | tf_op jit(solution)/shard_map/ppermute | solution.py:231
  7.4 42.1 %all-to-all-start = ((bf16[16,16,1024]{2,1,0:T(8,128)(2,1)}), bf16[16,16,1024]{2,1,0:T(8,128)(2,1)S(1)}, u32[]{:S(2)}, u32[]{:S(2)}) async-start(bf16[16,16,1024]{2,1,0:T(8,128)(2,1)} %broadcast_in_dim.2), calls=%async_computation | async-start | bytes 1048576 | tf_op jit(solution)/shard_map/all_to_all | solution.py:237
  22.1 6.2 %collective-permute-start.1 = (bf16[2,16,1024]{2,1,0:T(8,128)(2,1)S(1)}, bf16[2,16,1024]{2,1,0:T(8,128)(2,1)S(1)}, u32[]{:S(2)}, u32[]{:S(2)}) collective-permute-start(bf16[2,16,1024]{2,1,0:T(8,128)(2,1)S(1)} %shard_map.67.own_ref), channel_id=1, source_target_pairs={{0,16},{16,0},{1,17},{17,1},{2,18},{18,2},{3,19},{19,3},{4,20},{20... | collective-permute-start | bytes 196616 | tf_op jit(solution)/shard_map/ppermute | solution.py:231
  42.1 3.8 %collective-permute-start.2 = (bf16[16,16,1024]{2,1,0:T(8,128)(2,1)S(1)}, bf16[16,16,1024]{2,1,0:T(8,128)(2,1)S(1)}, u32[]{:S(2)}, u32[]{:S(2)}) collective-permute-start(bf16[16,16,1024]{2,1,0:T(8,128)(2,1)S(1)} %bitcast.2), channel_id=1, source_target_pairs={{0,1},{1,0},{2,3},{3,2},{4,5},{5,4},{6,7},{7,6},{8,9},{9,8},{10,11... | collective-permute-start | bytes 1572872 | tf_op jit(solution)/shard_map/ppermute | solution.py:231
  83.5 22.7 %all-to-all-start.3 = ((bf16[16,8,1024]{2,1,0:T(8,128)(2,1)}), bf16[16,8,1024]{2,1,0:T(8,128)(2,1)S(1)}, u32[]{:S(2)}, u32[]{:S(2)}) async-start(bf16[16,8,1024]{2,1,0:T(8,128)(2,1)} %get-tuple-element.43), calls=%async_computation.3 | async-start | bytes 524288 | tf_op jit(solution)/shard_map/all_to_all | solution.py:262
  88.8 3.9 %collective-permute-start.3 = (f32[128,1152]{1,0:T(8,128)S(1)}, f32[128,1152]{1,0:T(8,128)S(1)}, u32[]{:S(2)}, u32[]{:S(2)}) collective-permute-start(f32[128,1152]{1,0:T(8,128)S(1)} %get-tuple-element.38), channel_id=1, source_target_pairs={{0,1},{1,0},{2,3},{3,2},{4,5},{5,4},{6,7},{7,6},{8,9},{9,8},{10,11... | collective-permute-start | bytes 1769480 | tf_op jit(solution)/shard_map/ppermute | solution.py:231
  92.8 9.7 %collective-permute-start.4 = (bf16[4,8,1152]{2,1,0:T(8,128)(2,1)S(1)}, bf16[4,8,1152]{2,1,0:T(8,128)(2,1)S(1)}, u32[]{:S(2)}, u32[]{:S(2)}) collective-permute-start(bf16[4,8,1152]{2,1,0:T(8,128)(2,1)S(1)} %get-tuple-element.40), channel_id=1, source_target_pairs={{0,16},{16,32},{32,48},{48,0},{1,17},{17,33},{33,49},{49,1},{2,18}... | collective-permute-start | bytes 221192 | tf_op jit(solution)/shard_map/ppermute | solution.py:265
  95.2 7.8 %collective-permute-start.5 = (bf16[4,8,1152]{2,1,0:T(8,128)(2,1)S(1)}, bf16[4,8,1152]{2,1,0:T(8,128)(2,1)S(1)}, u32[]{:S(2)}, u32[]{:S(2)}) collective-permute-start(bf16[4,8,1152]{2,1,0:T(8,128)(2,1)S(1)} %get-tuple-element.41), channel_id=1, source_target_pairs={{0,32},{16,48},{32,0},{48,16},{1,33},{17,49},{33,1},{49,17},{2,34}... | collective-permute-start | bytes 221192 | tf_op jit(solution)/shard_map/ppermute | solution.py:265
  99.1 6.2 %collective-permute-start.6 = (bf16[4,8,1152]{2,1,0:T(8,128)(2,1)S(1)}, bf16[4,8,1152]{2,1,0:T(8,128)(2,1)S(1)}, u32[]{:S(2)}, u32[]{:S(2)}) collective-permute-start(bf16[4,8,1152]{2,1,0:T(8,128)(2,1)S(1)} %get-tuple-element.42), channel_id=1, source_target_pairs={{0,48},{16,0},{32,16},{48,32},{1,49},{17,1},{33,17},{49,33},{2,50}... | collective-permute-start | bytes 221192 | tf_op jit(solution)/shard_map/ppermute | solution.py:265
